TPU v7x, 32 devices: a whole 2x2x4 slice. The times are simulated.
32 devices in a mesh: rep: 4 (over z), grp: 8 (over y, x, core).
Axes of the slice: x: 2, y: 2, z: 4, core: 2. Of those that a mesh axis runs over, the one named last changes fastest.
Arguments:
- tokens: bfloat16 [8192, 2048], P(('rep', 'grp')), may hold values from -6 to 6
- response_sensitivity: bfloat16 [8192, 2048], P(('rep', 'grp')), may hold values from -6 to 6
- seq_lengths: int32 [8], replicated, may hold values from 1024 to 1024, as said below
- prefix_lengths: int32 [8], replicated, may hold values from 204 to 512, as said below
- adapter_ids: int32 [8], replicated, may hold values from 0 to 7, as said below
- attn_gain: float32 [2048], replicated, may hold values from 0.1 to 1.9
- mlp_gain: float32 [2048], replicated, may hold values from 0.1 to 1.9
- qkv_weight: bfloat16 [2048, 2560], P(None, 'grp'), may hold values from -0.125 to 0.125
- out_weight: bfloat16 [2048, 2048], P(None, 'grp'), may hold values from -2 to 2
- gate_up_weight: bfloat16 [2048, 11264], P(None, 'grp'), may hold values from -0.125 to 0.125
- down_weight: bfloat16 [5632, 2048], P(None, 'grp'), may hold values from -0.078125 to 0.078125
- query_in: bfloat16 [2048, 128], replicated, may hold values from -0.125 to 0.125
- asking_right_pieces: bfloat16 [128, 2048], replicated, may hold values from -0.75 to 0.75
- key_in: bfloat16 [2048, 128], replicated, may hold values from -0.125 to 0.125
- lookup_right_pieces: bfloat16 [128, 256], replicated, may hold values from -0.75 to 0.75
- value_in: bfloat16 [2048, 128], replicated, may hold values from -0.125 to 0.125
- content_right_pieces: bfloat16 [128, 256], replicated, may hold values from -0.75 to 0.75
- output_in: bfloat16 [2048, 128], replicated, may hold values from -2 to 2
- final_right_pieces: bfloat16 [128, 2048], replicated, may hold values from -0.75 to 0.75
- gate_in: bfloat16 [2048, 128], replicated, may hold values from -0.125 to 0.125
- switch_right_pieces: bfloat16 [128, 5632], replicated, may hold values from -0.75 to 0.75
- up_in: bfloat16 [2048, 128], replicated, may hold values from -0.125 to 0.125
- lift_right_pieces: bfloat16 [128, 5632], replicated, may hold values from -0.75 to 0.75
- down_in: bfloat16 [5632, 128], replicated, may hold values from -0.078125 to 0.078125
- lower_right_pieces: bfloat16 [128, 2048], replicated, may hold values from -0.75 to 0.75
Outputs:
- level_response: bfloat16 [8192, 2048], P(('rep', 'grp'))
- input_grad: bfloat16 [8192, 2048], P(('rep', 'grp'))
- query_in_grad: float32 [2048, 128], P('grp')
- asking_right_sens: float32 [128, 2048], P(None, 'grp')
- key_in_grad: float32 [2048, 128], P('grp')
- lookup_right_sens: float32 [128, 256], P(None, 'grp')
- value_in_grad: float32 [2048, 128], P('grp')
- content_right_sens: float32 [128, 256], P(None, 'grp')
- output_in_grad: float32 [2048, 128], P('grp')
- final_right_sens: float32 [128, 2048], P(None, 'grp')
- gate_in_grad: float32 [2048, 128], P('grp')
- switch_right_sens: float32 [128, 5632], P(None, 'grp')
- up_in_grad: float32 [2048, 128], P('grp')
- lift_right_sens: float32 [128, 5632], P(None, 'grp')
- down_in_grad: float32 [5632, 128], P('grp')
- lower_right_sens: float32 [128, 2048], P(None, 'grp')
Inputs may be any that keep to these rules, and one draw needn't show every extreme that they name: `seq_lengths`: entries 2r and 2r + 1 are the lengths of the two sequences of rep group r, in order; they sum to 2048. `prefix_lengths`: entry s is the prefix length of sequence s; it never exceeds half of that sequence's length. `adapter_ids`: each adapter serves exactly 1 sequence.
All inputs are finite; a program needn't handle non-finite values.
Results may differ from a plain program's by a relative error of at most 0.02.
The roundings to bfloat16 on the way count: a program that leaves them out, or rounds other values in their place, can miss the bound.
Values may be sent and summed in bfloat16 or wider, within the bound.
No kernel may reach another device: no remote copies, remote signals or barrier semaphores. Data moves between devices by JAX's collectives and lax.ppermute only.
A program may use at most 320 MiB of HBM per device.

v0:
```python
import jax
import jax.numpy as jnp
from jax import lax
from jax.sharding import PartitionSpec as P

HEADS = 32
KV_HEADS = 4
HEAD_DIM = 64
RANK = 16


EPS = 1e-05
LOWRANK_FACTOR = 2.0
MASKED = -1e30


def linear_compose(left, right):
    return jnp.dot(left, right, preferred_element_type=jnp.float32)


def left_with_flipped(left, right):
    return lax.dot_general(
        left, right, (((1,), (1,)), ((), ())), preferred_element_type=jnp.float32
    )


def flipped_with_right(left, right):
    return lax.dot_general(
        left, right, (((0,), (0,)), ((), ())), preferred_element_type=jnp.float32
    )


def inverse_rms(value):
    return lax.rsqrt(jnp.mean(value * value, axis=-1, keepdims=True) + EPS)


def norm_backward(value, scale, gain, grad):
    scaled = gain * grad
    return scale * scaled - value * (scale * scale * scale) * jnp.mean(
        scaled * value, axis=-1, keepdims=True
    )


def rotary_tables(positions, head_dim):
    half = head_dim // 2
    freqs = 10000.0 ** (-2.0 * jnp.arange(half).astype(jnp.float32) / head_dim)
    angles = positions.astype(jnp.float32)[:, None] * freqs[None, :]
    angles = jnp.concatenate([angles, angles], axis=1)
    return (jnp.cos(angles), jnp.sin(angles))


def rotate(value, cosines, sines):
    half = value.shape[-1] // 2
    turned = jnp.concatenate([-value[..., half:], value[..., :half]], axis=-1)
    return value * cosines[:, None, :] + turned * sines[:, None, :]


def unrotate(grad, cosines, sines):
    half = grad.shape[-1] // 2
    turned = grad * sines[:, None, :]
    return grad * cosines[:, None, :] + jnp.concatenate(
        [turned[..., half:], -turned[..., :half]], axis=-1
    )


def fold_parts(incoming_tokens, total_width):

    def accumulate(carry, piece, start):
        result = linear_compose(incoming_tokens, piece)
        return (result,)

    empty = jnp.zeros((incoming_tokens.shape[0], total_width), jnp.float32)
    return (accumulate, (empty,))


def fold_back(grads, in_width):

    def accumulate(total, piece, start):
        return left_with_flipped(grads, piece)

    return (accumulate, jnp.zeros((grads.shape[0], in_width), jnp.float32))


def shards(
    tokens,
    response_sensitivity,
    seq_lengths,
    prefix_lengths,
    adapter_ids,
    attn_gain,
    mlp_gain,
    qkv_weight,
    out_weight,
    gate_up_weight,
    down_weight,
    query_in,
    asking_right_pieces,
    key_in,
    lookup_right_pieces,
    value_in,
    content_right_pieces,
    output_in,
    final_right_pieces,
    gate_in,
    switch_right_pieces,
    up_in,
    lift_right_pieces,
    down_in,
    lower_right_pieces,
):
    count, width = tokens.shape
    members = lax.axis_size("grp")
    kv_width = lookup_right_pieces.shape[1]
    kv_heads = KV_HEADS
    head_dim = HEAD_DIM
    share = HEADS // KV_HEADS
    narrow_widths = query_in.shape[1]
    perceptron_part = down_weight.shape[0]
    scale = HEAD_DIM ** (-0.5)
    group = lax.axis_index("rep")
    member = lax.axis_index("grp")
    lengths = lax.dynamic_slice_in_dim(seq_lengths, 2 * group, 2)
    prefixes = lax.dynamic_slice_in_dim(prefix_lengths, 2 * group, 2)
    chosen_ids = lax.dynamic_slice_in_dim(adapter_ids, 2 * group, 2)
    key_count = count * members
    key_index = jnp.arange(key_count, dtype=jnp.int32)
    key_second = (key_index >= lengths[0]).astype(jnp.int32)
    key_position = key_index - key_second * lengths[0]
    own_index = member * count + jnp.arange(count, dtype=jnp.int32)
    own_second = (own_index >= lengths[0]).astype(jnp.int32)
    position = own_index - own_second * lengths[0]
    prefix = jnp.where(own_second == 0, prefixes[0], prefixes[1])
    chosen = jnp.where(own_second == 0, chosen_ids[0], chosen_ids[1])
    columns = jnp.arange(narrow_widths, dtype=jnp.int32) // RANK
    visibility_table = (chosen[:, None] == columns[None, :]).astype(jnp.float32)
    mask_two = jnp.concatenate([visibility_table, visibility_table], axis=1)
    mask_three = jnp.concatenate([visibility_table, visibility_table, visibility_table], axis=1)
    incoming_tokens = tokens.astype(jnp.float32)
    scale_one = inverse_rms(incoming_tokens)
    norm1 = (incoming_tokens * scale_one * attn_gain).astype(jnp.bfloat16)
    step_qkv, init_qkv = fold_parts(norm1, qkv_weight.shape[1] * members)
    folded_qkv = step_qkv(
        init_qkv, lax.all_gather(qkv_weight, "grp", axis=1, tiled=True), jnp.int32(0)
    )
    qkv_in = jnp.concatenate([query_in, key_in, value_in], axis=1)
    narrow_triple = (linear_compose(norm1, qkv_in) * mask_three).astype(jnp.bfloat16)
    adapted = jnp.concatenate(
        [
            LOWRANK_FACTOR * linear_compose(narrow_triple[:, :narrow_widths], asking_right_pieces),
            LOWRANK_FACTOR
            * linear_compose(
                narrow_triple[:, narrow_widths : 2 * narrow_widths], lookup_right_pieces
            ),
            LOWRANK_FACTOR
            * linear_compose(narrow_triple[:, 2 * narrow_widths :], content_right_pieces),
        ],
        axis=1,
    )
    qkv = folded_qkv[0] + adapted
    cosines, sines = rotary_tables(position, head_dim)
    query = rotate(qkv[:, :width].reshape(count, HEADS, head_dim), cosines, sines).astype(
        jnp.bfloat16
    )
    query = query.reshape(count, kv_heads, share, head_dim)
    key_own = rotate(
        qkv[:, width : width + kv_width].reshape(count, kv_heads, head_dim), cosines, sines
    )
    key_own = key_own.astype(jnp.bfloat16).reshape(count, kv_width)
    value_own = qkv[:, width + kv_width :].astype(jnp.bfloat16)
    keys, values = (
        lax.all_gather(key_own, "grp", axis=0, tiled=True),
        lax.all_gather(value_own, "grp", axis=0, tiled=True),
    )
    keys = keys.reshape(key_count, kv_heads, head_dim)
    values = values.reshape(key_count, kv_heads, head_dim)
    block = 512
    blocks = key_count // block

    def block_scores(start):
        key_block = lax.dynamic_slice_in_dim(keys, start, block, 0)
        scores = (
            jnp.einsum("qhgd,khd->hgqk", query, key_block, preferred_element_type=jnp.float32)
            * scale
        )
        other_pos = lax.dynamic_slice_in_dim(key_position, start, block, 0)
        other_seq = lax.dynamic_slice_in_dim(key_second, start, block, 0)
        allowed = (own_second[:, None] == other_seq[None, :]) & (
            (other_pos[None, :] <= position[:, None]) | (other_pos[None, :] < prefix[:, None])
        )
        return (jnp.where(allowed[None, None], scores, MASKED), key_block)

    def max_step(index, carry):
        peak, total = carry
        scores, unused = block_scores(index * block)
        new_peak = jnp.maximum(peak, jnp.max(scores, axis=-1))
        total = total * jnp.exp(peak - new_peak) + jnp.sum(
            jnp.exp(scores - new_peak[..., None]), axis=-1
        )
        return (new_peak, total)

    start_peak = jnp.full((kv_heads, share, count), MASKED, jnp.float32)
    start_total = jnp.zeros((kv_heads, share, count), jnp.float32)
    peak, total = lax.fori_loop(0, blocks, max_step, (start_peak, start_total))
    log_total = peak + jnp.log(total)

    def mix_step(index, mixed):
        start = index * block
        scores, unused = block_scores(start)
        probs = jnp.exp(scores - log_total[..., None]).astype(jnp.bfloat16)
        value_block = lax.dynamic_slice_in_dim(values, start, block, 0)
        return mixed + jnp.einsum(
            "hgqk,khd->qhgd", probs, value_block, preferred_element_type=jnp.float32
        )

    attended = lax.fori_loop(
        0, blocks, mix_step, jnp.zeros((count, kv_heads, share, head_dim), jnp.float32)
    )
    attended_low = attended.reshape(count, width).astype(jnp.bfloat16)
    step_out, init_out = fold_parts(attended_low, out_weight.shape[1] * members)
    combined_final = step_out(
        init_out, lax.all_gather(out_weight, "grp", axis=1, tiled=True), jnp.int32(0)
    )
    narrow_final = (linear_compose(attended_low, output_in) * visibility_table).astype(jnp.bfloat16)
    residual_stream = incoming_tokens + (
        combined_final[0] + LOWRANK_FACTOR * linear_compose(narrow_final, final_right_pieces)
    )
    scale_two = inverse_rms(residual_stream)
    norm2 = (residual_stream * scale_two * mlp_gain).astype(jnp.bfloat16)
    step_ffn, init_ffn = fold_parts(norm2, gate_up_weight.shape[1] * members)
    folded_ffn = step_ffn(
        init_ffn, lax.all_gather(gate_up_weight, "grp", axis=1, tiled=True), jnp.int32(0)
    )
    ffn_in = jnp.concatenate([gate_in, up_in], axis=1)
    narrow_perceptron = (linear_compose(norm2, ffn_in) * mask_two).astype(jnp.bfloat16)
    gate_up = folded_ffn[0] + jnp.concatenate(
        [
            LOWRANK_FACTOR
            * linear_compose(narrow_perceptron[:, :narrow_widths], switch_right_pieces),
            LOWRANK_FACTOR
            * linear_compose(narrow_perceptron[:, narrow_widths:], lift_right_pieces),
        ],
        axis=1,
    )
    gate = gate_up[:, :perceptron_part]
    up = gate_up[:, perceptron_part:]
    sigma = jax.nn.sigmoid(gate)
    act = (gate * sigma * up).astype(jnp.bfloat16)
    step_down, init_down = fold_parts(act, down_weight.shape[1] * members)
    combined_lower = step_down(
        init_down, lax.all_gather(down_weight, "grp", axis=1, tiled=True), jnp.int32(0)
    )
    narrow_lower = (linear_compose(act, down_in) * visibility_table).astype(jnp.bfloat16)
    level_response = (
        residual_stream
        + combined_lower[0]
        + LOWRANK_FACTOR * linear_compose(narrow_lower, lower_right_pieces)
    )
    lower_right_sens = LOWRANK_FACTOR * flipped_with_right(narrow_lower, response_sensitivity)
    sens_narrow_lower = (
        LOWRANK_FACTOR
        * left_with_flipped(response_sensitivity, lower_right_pieces)
        * visibility_table
    ).astype(jnp.bfloat16)
    down_in_grad = flipped_with_right(act, sens_narrow_lower)
    step_back, init_back = fold_back(response_sensitivity, perceptron_part)
    dact_base = step_back(
        init_back, lax.all_gather(down_weight, "grp", axis=1, tiled=True), jnp.int32(0)
    )
    dact = dact_base + left_with_flipped(sens_narrow_lower, down_in)
    dgate = dact * up * (sigma * (1.0 + gate * (1.0 - sigma)))
    dup = dact * gate * sigma
    sens_twin_lift = jnp.concatenate([dgate, dup], axis=1).astype(jnp.bfloat16)
    switch_right_sens = LOWRANK_FACTOR * flipped_with_right(
        narrow_perceptron[:, :narrow_widths], sens_twin_lift[:, :perceptron_part]
    )
    lift_right_sens = LOWRANK_FACTOR * flipped_with_right(
        narrow_perceptron[:, narrow_widths:], sens_twin_lift[:, perceptron_part:]
    )
    dlatent_ffn = (
        LOWRANK_FACTOR
        * jnp.concatenate(
            [
                left_with_flipped(sens_twin_lift[:, :perceptron_part], switch_right_pieces),
                left_with_flipped(sens_twin_lift[:, perceptron_part:], lift_right_pieces),
            ],
            axis=1,
        )
        * mask_two
    ).astype(jnp.bfloat16)
    gate_in_grad = flipped_with_right(norm2, dlatent_ffn[:, :narrow_widths])
    up_in_grad = flipped_with_right(norm2, dlatent_ffn[:, narrow_widths:])
    step_back, init_back = fold_back(sens_twin_lift, width)
    dnorm_base = step_back(
        init_back, lax.all_gather(gate_up_weight, "grp", axis=1, tiled=True), jnp.int32(0)
    )
    dnorm2 = dnorm_base + left_with_flipped(dlatent_ffn, ffn_in)
    dhidden = response_sensitivity.astype(jnp.float32) + norm_backward(
        residual_stream, scale_two, mlp_gain, dnorm2
    )
    side_path_sens = dhidden.astype(jnp.bfloat16)
    final_right_sens = LOWRANK_FACTOR * flipped_with_right(narrow_final, side_path_sens)
    sens_narrow_final = (
        LOWRANK_FACTOR * left_with_flipped(side_path_sens, final_right_pieces) * visibility_table
    ).astype(jnp.bfloat16)
    output_in_grad = flipped_with_right(attended_low, sens_narrow_final)
    step_back, init_back = fold_back(side_path_sens, width)
    dattended_base = step_back(
        init_back, lax.all_gather(out_weight, "grp", axis=1, tiled=True), jnp.int32(0)
    )
    dattended = (dattended_base + left_with_flipped(sens_narrow_final, output_in)).astype(
        jnp.bfloat16
    )
    dattended = dattended.reshape(count, kv_heads, share, head_dim)

    def delta_step(index, delta):
        start = index * block
        scores, unused = block_scores(start)
        probs = jnp.exp(scores - log_total[..., None])
        value_block = lax.dynamic_slice_in_dim(values, start, block, 0)
        dprobs = jnp.einsum(
            "qhgd,khd->hgqk", dattended, value_block, preferred_element_type=jnp.float32
        )
        return delta + jnp.sum(probs * dprobs, axis=-1)

    delta = lax.fori_loop(0, blocks, delta_step, jnp.zeros((kv_heads, share, count), jnp.float32))

    def grad_step(index, carry):
        dquery, dkeys, dvalues = carry
        start = index * block
        scores, key_block = block_scores(start)
        probs = jnp.exp(scores - log_total[..., None])
        value_block = lax.dynamic_slice_in_dim(values, start, block, 0)
        dprobs = jnp.einsum(
            "qhgd,khd->hgqk", dattended, value_block, preferred_element_type=jnp.float32
        )
        dscores = (probs * (dprobs - delta[..., None])).astype(jnp.bfloat16)
        dquery = (
            dquery
            + jnp.einsum("hgqk,khd->qhgd", dscores, key_block, preferred_element_type=jnp.float32)
            * scale
        )
        dkey_block = (
            jnp.einsum("hgqk,qhgd->khd", dscores, query, preferred_element_type=jnp.float32) * scale
        )
        dvalue_block = jnp.einsum(
            "hgqk,qhgd->khd",
            probs.astype(jnp.bfloat16),
            dattended,
            preferred_element_type=jnp.float32,
        )
        dkeys = lax.dynamic_update_slice_in_dim(
            dkeys, dkey_block.reshape(block, kv_width), start, 0
        )
        dvalues = lax.dynamic_update_slice_in_dim(
            dvalues, dvalue_block.reshape(block, kv_width), start, 0
        )
        return (dquery, dkeys, dvalues)

    start_grads = (
        jnp.zeros((count, kv_heads, share, head_dim), jnp.float32),
        jnp.zeros((key_count, kv_width), jnp.float32),
        jnp.zeros((key_count, kv_width), jnp.float32),
    )
    dquery, dkeys, dvalues = lax.fori_loop(0, blocks, grad_step, start_grads)
    dkey_own, dvalue_own = (
        lax.psum_scatter(dkeys.astype(jnp.bfloat16), "grp", scatter_dimension=0, tiled=True).astype(
            jnp.float32
        ),
        lax.psum_scatter(
            dvalues.astype(jnp.bfloat16), "grp", scatter_dimension=0, tiled=True
        ).astype(jnp.float32),
    )
    dquery_flat = unrotate(dquery.reshape(count, HEADS, head_dim), cosines, sines).reshape(
        count, width
    )
    dkey_flat = unrotate(dkey_own.reshape(count, kv_heads, head_dim), cosines, sines).reshape(
        count, kv_width
    )
    dqkv = jnp.concatenate([dquery_flat, dkey_flat, dvalue_own], axis=1).astype(jnp.bfloat16)
    sens_asking_part = dqkv[:, :width]
    sens_lookup_part = dqkv[:, width : width + kv_width]
    sens_content_part = dqkv[:, width + kv_width :]
    asking_right_sens = LOWRANK_FACTOR * flipped_with_right(
        narrow_triple[:, :narrow_widths], sens_asking_part
    )
    lookup_right_sens = LOWRANK_FACTOR * flipped_with_right(
        narrow_triple[:, narrow_widths : 2 * narrow_widths], sens_lookup_part
    )
    content_right_sens = LOWRANK_FACTOR * flipped_with_right(
        narrow_triple[:, 2 * narrow_widths :], sens_content_part
    )
    dlatent_qkv = (
        LOWRANK_FACTOR
        * jnp.concatenate(
            [
                left_with_flipped(sens_asking_part, asking_right_pieces),
                left_with_flipped(sens_lookup_part, lookup_right_pieces),
                left_with_flipped(sens_content_part, content_right_pieces),
            ],
            axis=1,
        )
        * mask_three
    ).astype(jnp.bfloat16)
    query_in_grad = flipped_with_right(norm1, dlatent_qkv[:, :narrow_widths])
    key_in_grad = flipped_with_right(norm1, dlatent_qkv[:, narrow_widths : 2 * narrow_widths])
    value_in_grad = flipped_with_right(norm1, dlatent_qkv[:, 2 * narrow_widths :])
    step_back, init_back = fold_back(dqkv, width)
    dnorm_first = step_back(
        init_back, lax.all_gather(qkv_weight, "grp", axis=1, tiled=True), jnp.int32(0)
    )
    dnorm1 = dnorm_first + left_with_flipped(dlatent_qkv, qkv_in)
    input_grad = (dhidden + norm_backward(incoming_tokens, scale_one, attn_gain, dnorm1)).astype(
        jnp.bfloat16
    )
    shares = (
        lax.psum_scatter(
            query_in_grad.astype(jnp.bfloat16), "grp", scatter_dimension=0, tiled=True
        ).astype(jnp.float32),
        lax.psum_scatter(
            asking_right_sens.astype(jnp.bfloat16), "grp", scatter_dimension=1, tiled=True
        ).astype(jnp.float32),
        lax.psum_scatter(
            key_in_grad.astype(jnp.bfloat16), "grp", scatter_dimension=0, tiled=True
        ).astype(jnp.float32),
        lax.psum_scatter(
            lookup_right_sens.astype(jnp.bfloat16), "grp", scatter_dimension=1, tiled=True
        ).astype(jnp.float32),
        lax.psum_scatter(
            value_in_grad.astype(jnp.bfloat16), "grp", scatter_dimension=0, tiled=True
        ).astype(jnp.float32),
        lax.psum_scatter(
            content_right_sens.astype(jnp.bfloat16), "grp", scatter_dimension=1, tiled=True
        ).astype(jnp.float32),
        lax.psum_scatter(
            output_in_grad.astype(jnp.bfloat16), "grp", scatter_dimension=0, tiled=True
        ).astype(jnp.float32),
        lax.psum_scatter(
            final_right_sens.astype(jnp.bfloat16), "grp", scatter_dimension=1, tiled=True
        ).astype(jnp.float32),
        lax.psum_scatter(
            gate_in_grad.astype(jnp.bfloat16), "grp", scatter_dimension=0, tiled=True
        ).astype(jnp.float32),
        lax.psum_scatter(
            switch_right_sens.astype(jnp.bfloat16), "grp", scatter_dimension=1, tiled=True
        ).astype(jnp.float32),
        lax.psum_scatter(
            up_in_grad.astype(jnp.bfloat16), "grp", scatter_dimension=0, tiled=True
        ).astype(jnp.float32),
        lax.psum_scatter(
            lift_right_sens.astype(jnp.bfloat16), "grp", scatter_dimension=1, tiled=True
        ).astype(jnp.float32),
        lax.psum_scatter(
            down_in_grad.astype(jnp.bfloat16), "grp", scatter_dimension=0, tiled=True
        ).astype(jnp.float32),
        lax.psum_scatter(
            lower_right_sens.astype(jnp.bfloat16), "grp", scatter_dimension=1, tiled=True
        ).astype(jnp.float32),
    )
    totals = (
        lax.psum(shares[0].astype(jnp.bfloat16), "rep").astype(jnp.float32),
        lax.psum(shares[1].astype(jnp.bfloat16), "rep").astype(jnp.float32),
        lax.psum(shares[2].astype(jnp.bfloat16), "rep").astype(jnp.float32),
        lax.psum(shares[3].astype(jnp.bfloat16), "rep").astype(jnp.float32),
        lax.psum(shares[4].astype(jnp.bfloat16), "rep").astype(jnp.float32),
        lax.psum(shares[5].astype(jnp.bfloat16), "rep").astype(jnp.float32),
        lax.psum(shares[6].astype(jnp.bfloat16), "rep").astype(jnp.float32),
        lax.psum(shares[7].astype(jnp.bfloat16), "rep").astype(jnp.float32),
        lax.psum(shares[8].astype(jnp.bfloat16), "rep").astype(jnp.float32),
        lax.psum(shares[9].astype(jnp.bfloat16), "rep").astype(jnp.float32),
        lax.psum(shares[10].astype(jnp.bfloat16), "rep").astype(jnp.float32),
        lax.psum(shares[11].astype(jnp.bfloat16), "rep").astype(jnp.float32),
        lax.psum(shares[12].astype(jnp.bfloat16), "rep").astype(jnp.float32),
        lax.psum(shares[13].astype(jnp.bfloat16), "rep").astype(jnp.float32),
    )
    return (
        level_response.astype(jnp.bfloat16),
        input_grad,
        totals[0],
        totals[1],
        totals[2],
        totals[3],
        totals[4],
        totals[5],
        totals[6],
        totals[7],
        totals[8],
        totals[9],
        totals[10],
        totals[11],
        totals[12],
        totals[13],
    )


def solution(mesh):
    in_specs = (
        P(("rep", "grp"), None),
        P(("rep", "grp"), None),
        P(),
        P(),
        P(),
        P(),
        P(),
        P(None, "grp"),
        P(None, "grp"),
        P(None, "grp"),
        P(None, "grp"),
        P(),
        P(),
        P(),
        P(),
        P(),
        P(),
        P(),
        P(),
        P(),
        P(),
        P(),
        P(),
        P(),
        P(),
    )
    out_specs = (
        P(("rep", "grp"), None),
        P(("rep", "grp"), None),
        P("grp", None),
        P(None, "grp"),
        P("grp", None),
        P(None, "grp"),
        P("grp", None),
        P(None, "grp"),
        P("grp", None),
        P(None, "grp"),
        P("grp", None),
        P(None, "grp"),
        P("grp", None),
        P(None, "grp"),
        P("grp", None),
        P(None, "grp"),
    )
    return jax.shard_map(shards, mesh=mesh, in_specs=in_specs, out_specs=out_specs, check_vma=False)
```

profile of v0, /device:TPU:0, one launch (start us, length us, event | category | flops | bytes accessed | tf_op | source)
XLA Modules:
  0.0 1529.3 jit_solution(14385701414066152637)
XLA Ops:
  18.4 57.5 %all-gather.7.cloned.1.call-done = bf16[2048,2560]{0,1:T(8,128)(2,1)} async-done(((bf16[2048,320]{0,1:T(8,128)(2,1)}), bf16[2048,2560]{0,1:T(8,128)(2,1)}) %all-gather.7.cloned.1.call-update) | async-done | bytes 10485776 | tf_op jit(solution)/shard_map/all_gather | solution.py:143
  112.9 23.7 %all-gather.9.cloned.1.call-done = bf16[2048,256]{1,0:T(8,128)(2,1)} async-done(((bf16[256,256]{1,0:T(8,128)(2,1)}), bf16[2048,256]{1,0:T(8,128)(2,1)}) %all-gather.9.cloned.1.call-update) | async-done | bytes 1048592 | tf_op jit(solution)/shard_map/all_gather | solution.py:172
  138.9 82.2 %while.70 = (s32[]{:T(128)}, f32[4,8,256]{2,1,0:T(8,128)S(1)}, f32[4,8,256]{2,1,0:T(8,128)S(1)}, s32[2048]{0:T(1024)S(1)}, s32[2048]{0:T(1024)}, /*index=5*/bf16...) while((s32[]{:T(128)}, f32[4,8,256]{2,1,0:T(8,128)S(1)}, ...), condition=%wide.region_4.5_spmd.clone.clone.clone, body=%wide.region_1.4_spmd.clone.clone.clone.sunk | while | flops 566929920 | bytes 35703016 | solution.py:203
  141.3 8.6 fusion.276
  150.0 9.2 exponential_reduce_fusion.2
  161.7 8.9 fusion.276
  170.6 9.3 exponential_reduce_fusion.2
  190.5 9.8 exponential_reduce_fusion.2
  202.8 8.7 fusion.276
  211.5 9.5 exponential_reduce_fusion.2
  221.2 53.4 %while.71 = (s32[]{:T(128)}, f32[256,4,8,64]{0,3,2,1:T(8,128)}, bf16[2048,4,64]{0,2,1:T(8,128)(2,1)}, s32[2048]{0:T(1024)S(1)}, s32[2048]{0:T(1024)}, /*index=5*...) while((s32[]{:T(128)}, f32[256,4,8,64]{0,3,2,1:T(8,128)}, ...), condition=%wide.region_6.7_spmd.clone.clone.clone, body=%wide.region_5.6_spmd.clone.clone.clone.sunk | while | flops 1092225536 | bytes 8177909 | solution.py:215
  224.9 9.3 bitcast_add_fusion.6
  237.9 9.6 bitcast_add_fusion.6
  251.2 9.7 bitcast_add_fusion.6
  264.6 9.6 bitcast_add_fusion.6
  295.2 21.9 %all-gather.17.cloned.1.call-done = bf16[5632,2048]{1,0:T(8,128)(2,1)} async-done(((bf16[5632,256]{1,0:T(8,128)(2,1)}), bf16[5632,2048]{1,0:T(8,128)(2,1)}) %all-gather.17.cloned.1.call-update) | async-done | bytes 23068688 | tf_op jit(solution)/shard_map/all_gather | solution.py:250
  317.1 12.8 fusion.166
  329.9 202.8 %all-gather.15.cloned.1.call-done = bf16[2048,11264]{1,0:T(8,128)(2,1)} async-done(((bf16[2048,1408]{1,0:T(8,128)(2,1)}), bf16[2048,11264]{1,0:T(8,128)(2,1)}) %all-gather.15.cloned.1.call-update) | async-done | bytes 46137360 | tf_op jit(solution)/shard_map/all_gather | solution.py:231
  532.7 26.9 %convolution_add_fusion = f32[256,11264]{1,0:T(8,128)} fusion(bf16[256,2048]{1,0:T(8,128)(2,1)S(1)} %multiply_convert_fusion.3, bf16[2048,11264]{1,0:T(8,128)(2,1)} %all-gather.15.cloned.1.call-done, f32[256,5632]{1,0:T(8,128)} %convolution_multiply_fusion, f32[256,5632]{1,0:T(8,128)} %convolution_multiply_fusion.1), kind=kOutput, calls=%fused_computation.99 | convolution fusion | flops 11816927232 | bytes 70254592 | tf_op jit(solution)/shard_map/dot_general | solution.py:18
  559.6 9.1 multiply_convert_fusion.1
  572.1 21.4 %fusion.86 = f32[256,2048]{1,0:T(8,128)} fusion(bf16[2048,11264]{1,0:T(8,128)(2,1)} %all-gather.15.cloned.1.call-done, bf16[256,5632]{1,0:T(8,128)(2,1)} %copy-done.18, bf16[256,5632]{1,0:T(8,128)(2,1)} %copy-done.19), kind=kOutput, calls=%fused_computation.108 | convolution fusion | flops 11822694400 | bytes 54001664 | tf_op jit(solution)/shard_map/dot_general | solution.py:22
  606.8 53.4 %while.72 = (s32[]{:T(128)}, f32[4,8,256]{2,1,0:T(8,128)}, s32[2048]{0:T(1024)S(1)}, s32[2048]{0:T(1024)}, bf16[2048,4,64]{0,2,1:T(8,128)(2,1)S(1)}, /*index=5*/...) while((s32[]{:T(128)}, f32[4,8,256]{2,1,0:T(8,128)}, ...), condition=%wide.region_11.12_spmd.clone.clone.clone, body=%wide.region_9.11_spmd.clone.clone.clone.sunk | while | flops 1095379456 | bytes 36751640 | solution.py:325
  662.4 174.8 %while.73 = (s32[]{:T(128)}, f32[256,4,8,64]{0,3,2,1:T(8,128)}, bf16[2048,256]{0,1:T(8,128)(2,1)}, bf16[2048,256]{0,1:T(8,128)(2,1)}, bf16[2048,4,64]{0,2,1:T(8,...) while((s32[]{:T(128)}, f32[256,4,8,64]{0,3,2,1:T(8,128)}, ...), condition=%wide.region_13.14_spmd.clone.clone.clone, body=%wide.region_12.13_spmd.clone.clone.clone.sunk | while | flops 2728790528 | bytes 196331952 | solution.py:364
  675.2 8.5 fusion.301
  693.5 10.6 fusion.303
  718.4 8.5 fusion.301
  737.3 10.6 fusion.303
  762.2 8.5 fusion.301
  781.1 10.6 fusion.303
  806.0 8.5 fusion.301
  824.8 10.6 fusion.303
  875.6 37.0 %reduce-scatter.19.cloned.1.call-done = bf16[256,256]{0,1:T(8,128)(2,1)} async-done(((bf16[2048,256]{0,1:T(8,128)(2,1)}), bf16[256,256]{0,1:T(8,128)(2,1)}) %reduce-scatter.19.cloned.1.call-update) | async-done | bytes 131088 | tf_op jit(solution)/shard_map/reduce_scatter | solution.py:369
  919.9 11.9 convolution_add_fusion.6
  949.8 37.4 %reduce-scatter.37.cloned.1.call-done = bf16[256,128]{1,0:T(8,128)(2,1)} async-done(((bf16[2048,128]{1,0:T(8,128)(2,1)}), bf16[256,128]{1,0:T(8,128)(2,1)}) %reduce-scatter.37.cloned.1.call-update) | async-done | bytes 65552 | tf_op jit(solution)/shard_map/reduce_scatter | solution.py:440
  987.3 37.2 %reduce-scatter.35.cloned.1.call-done = bf16[128,256]{1,0:T(8,128)(2,1)} async-done(((bf16[128,2048]{1,0:T(8,128)(2,1)}), bf16[128,256]{1,0:T(8,128)(2,1)}) %reduce-scatter.35.cloned.1.call-update) | async-done | bytes 65552 | tf_op jit(solution)/shard_map/reduce_scatter | solution.py:437
  1024.5 37.4 %reduce-scatter.33.cloned.1.call-done = bf16[256,128]{1,0:T(8,128)(2,1)} async-done(((bf16[2048,128]{1,0:T(8,128)(2,1)}), bf16[256,128]{1,0:T(8,128)(2,1)}) %reduce-scatter.33.cloned.1.call-update) | async-done | bytes 65552 | tf_op jit(solution)/shard_map/reduce_scatter | solution.py:434
  1061.9 37.2 %reduce-scatter.23.cloned.1.call-done = bf16[128,256]{1,0:T(8,128)(2,1)} async-done(((bf16[128,2048]{1,0:T(8,128)(2,1)}), bf16[128,256]{1,0:T(8,128)(2,1)}) %reduce-scatter.23.cloned.1.call-update) | async-done | bytes 65552 | tf_op jit(solution)/shard_map/reduce_scatter | solution.py:419
  1099.1 37.4 %reduce-scatter.47.cloned.1.call-done = bf16[128,256]{1,0:T(8,128)(2,1)} async-done(((bf16[128,2048]{1,0:T(8,128)(2,1)}), bf16[128,256]{1,0:T(8,128)(2,1)}) %reduce-scatter.47.cloned.1.call-update) | async-done | bytes 65552 | tf_op jit(solution)/shard_map/reduce_scatter | solution.py:455
  1136.6 41.0 %reduce-scatter.39.cloned.1.call-done = bf16[128,704]{0,1:T(8,128)(2,1)} async-done(((bf16[128,5632]{0,1:T(8,128)(2,1)}), bf16[128,704]{0,1:T(8,128)(2,1)}) %reduce-scatter.39.cloned.1.call-update) | async-done | bytes 180240 | tf_op jit(solution)/shard_map/reduce_scatter | solution.py:443
  1177.6 41.4 %reduce-scatter.43.cloned.1.call-done = bf16[128,704]{0,1:T(8,128)(2,1)} async-done(((bf16[128,5632]{0,1:T(8,128)(2,1)}), bf16[128,704]{0,1:T(8,128)(2,1)}) %reduce-scatter.43.cloned.1.call-update) | async-done | bytes 180240 | tf_op jit(solution)/shard_map/reduce_scatter | solution.py:449
  1219.0 41.1 %reduce-scatter.45.cloned.1.call-done = bf16[704,128]{1,0:T(8,128)(2,1)} async-done(((bf16[5632,128]{1,0:T(8,128)(2,1)}), bf16[704,128]{1,0:T(8,128)(2,1)}) %reduce-scatter.45.cloned.1.call-update) | async-done | bytes 180240 | tf_op jit(solution)/shard_map/reduce_scatter | solution.py:452
  1260.0 37.3 %reduce-scatter.21.cloned.1.call-done = bf16[256,128]{1,0:T(8,128)(2,1)} async-done(((bf16[2048,128]{1,0:T(8,128)(2,1)}), bf16[256,128]{1,0:T(8,128)(2,1)}) %reduce-scatter.21.cloned.1.call-update) | async-done | bytes 65552 | tf_op jit(solution)/shard_map/reduce_scatter | solution.py:416
  1297.4 37.2 %reduce-scatter.25.cloned.1.call-done = bf16[256,128]{1,0:T(8,128)(2,1)} async-done(((bf16[2048,128]{1,0:T(8,128)(2,1)}), bf16[256,128]{1,0:T(8,128)(2,1)}) %reduce-scatter.25.cloned.1.call-update) | async-done | bytes 65552 | tf_op jit(solution)/shard_map/reduce_scatter | solution.py:422
  1334.6 37.4 %reduce-scatter.29.cloned.1.call-done = bf16[256,128]{1,0:T(8,128)(2,1)} async-done(((bf16[2048,128]{1,0:T(8,128)(2,1)}), bf16[256,128]{1,0:T(8,128)(2,1)}) %reduce-scatter.29.cloned.1.call-update) | async-done | bytes 65552 | tf_op jit(solution)/shard_map/reduce_scatter | solution.py:428
  1376.7 32.1 %reduce-scatter.27.cloned.1.call-done = bf16[128,32]{0,1:T(8,128)(2,1)} async-done(((bf16[128,256]{0,1:T(8,128)(2,1)}), bf16[128,32]{0,1:T(8,128)(2,1)}) %reduce-scatter.27.cloned.1.call-update) | async-done | bytes 8208 | tf_op jit(solution)/shard_map/reduce_scatter | solution.py:425
  1408.8 37.1 %reduce-scatter.31.cloned.1.call-done = bf16[128,32]{0,1:T(8,128)(2,1)} async-done(((bf16[128,256]{0,1:T(8,128)(2,1)}), bf16[128,32]{0,1:T(8,128)(2,1)}) %reduce-scatter.31.cloned.1.call-update) | async-done | bytes 8208 | tf_op jit(solution)/shard_map/reduce_scatter | solution.py:431
  1445.9 19.9 %all-reduce = (bf16[128,32]{0,1:T(8,128)(2,1)S(1)}, bf16[128,32]{0,1:T(8,128)(2,1)S(1)}) all-reduce(bf16[128,32]{0,1:T(8,128)(2,1)} %reduce-scatter.27.cloned.1.call-done, bf16[128,32]{0,1:T(8,128)(2,1)} %reduce-scatter.31.cloned.1.call-done), channel_id=1, replica_groups=mesh['rep'=4,'grp'=8] {'rep'}, use_global_device_ids=true, to_apply=%region_24.25 | all-reduce | flops 8192 | bytes 32768 | tf_op jit(solution)/shard_map/psum | solution.py:463
  1466.9 42.0 %all-reduce.4.cloned.1.call-done = (bf16[256,128]{1,0:T(8,128)(2,1)}, bf16[128,256]{1,0:T(8,128)(2,1)}, bf16[256,128]{1,0:T(8,128)(2,1)}, bf16[256,128]{1,0:T(8,...) async-done(((bf16[256,128]{1,0:T(8,128)(2,1)}, ...) | async-done | bytes 1130512 | tf_op jit(solution)/shard_map/psum | solution.py:460
  (550 shorter events, 355.4 us)
Async XLA Ops:
  7.2 552.4 %copy-start = (bf16[5632,128]{1,0:T(8,128)(2,1)S(1)}, bf16[5632,128]{1,0:T(8,128)(2,1)}, u32[]{:S(2)}) copy-start(bf16[5632,128]{1,0:T(8,128)(2,1)} %param.56) | copy-start | bytes 4325380
  7.2 68.7 %all-gather.7.cloned.1.call-start = ((), (), s32[]{:S(2)}) async-start(), calls=%async_computation.16 | async-start | bytes 11796480 | tf_op jit(solution)/shard_map/all_gather | solution.py:143
  7.9 102.7 %all-gather.11.cloned.1.call-start = ((), (), s32[]{:S(2)}) async-start(), calls=%async_computation.18 | async-start | bytes 1179648 | tf_op jit(solution)/shard_map/all_gather | solution.py:171
  9.7 75.4 %copy-start.45 = (f32[256,64]{0,1:T(8,128)}, f32[256,64]{0,1:T(8,128)S(1)}, u32[]{:S(2)}) copy-start(f32[256,64]{0,1:T(8,128)S(1)} %get-tuple-element.1558) | copy-start | bytes 196612
  12.5 585.3 %copy-start.79 = (s32[256]{0:T(256)}, s32[256]{0:T(256)S(1)}, u32[]{:S(2)}) copy-start(s32[256]{0:T(256)S(1)} %compare_select_fusion.4) | copy-start | bytes 3076
  16.1 67.3 %copy-start.62 = (bf16[256,384]{1,0:T(8,128)(2,1)}, bf16[256,384]{1,0:T(8,128)(2,1)S(1)}, u32[]{:S(2)}) copy-start(bf16[256,384]{1,0:T(8,128)(2,1)S(1)} %fusion.116) | copy-start | bytes 589828
  16.1 59.8 %copy-start.98 = (f32[2048]{0:T(1024)S(1)}, f32[2048]{0:T(1024)}, u32[]{:S(2)}) copy-start(f32[2048]{0:T(1024)} %param.38) | copy-start | bytes 24580
  87.0 49.6 %all-gather.9.cloned.1.call-start = ((), (), s32[]{:S(2)}) async-start(), calls=%async_computation.17 | async-start | bytes 1179648 | tf_op jit(solution)/shard_map/all_gather | solution.py:172
  88.7 189.4 %all-gather.13.cloned.1.call-start = ((), (), s32[]{:S(2)}) async-start(), calls=%async_computation.19 | async-start | bytes 9437184 | tf_op jit(solution)/shard_map/all_gather | solution.py:221
  89.3 227.8 %all-gather.17.cloned.1.call-start = ((), (), s32[]{:S(2)}) async-start(), calls=%async_computation.21 | async-start | bytes 25952256 | tf_op jit(solution)/shard_map/all_gather | solution.py:250
  89.9 442.8 %all-gather.15.cloned.1.call-start = ((), (), s32[]{:S(2)}) async-start(), calls=%async_computation.20 | async-start | bytes 51904512 | tf_op jit(solution)/shard_map/all_gather | solution.py:231
  90.5 782.9 %reduce-scatter.17.cloned.1.call-start = ((), (), s32[]{:S(2)}) async-start(), calls=%async_computation.22 | async-start | bytes 1179648 | tf_op jit(solution)/shard_map/reduce_scatter | solution.py:366
  107.3 31.6 %copy-start.32 = (f32[4,8,256]{2,1,0:T(8,128)S(1)}, f32[4,8,256]{2,1,0:T(8,128)}, u32[]{:S(2)}) copy-start(f32[4,8,256]{2,1,0:T(8,128)} %custom-call) | copy-start | bytes 98308
  107.3 31.6 %copy-start.54 = (f32[4,8,256]{2,1,0:T(8,128)S(1)}, f32[4,8,256]{2,1,0:T(8,128)}, u32[]{:S(2)}) copy-start(f32[4,8,256]{2,1,0:T(8,128)} %custom-call.1) | copy-start | bytes 98308
  286.2 246.5 %copy-start.20 = (bf16[256,2048]{1,0:T(8,128)(2,1)}, bf16[256,2048]{1,0:T(8,128)(2,1)S(1)}, u32[]{:S(2)}) copy-start(bf16[256,2048]{1,0:T(8,128)(2,1)S(1)} %multiply_convert_fusion.3) | copy-start | bytes 3145732
  572.1 21.5 %copy-start.52 = (bf16[256,256]{1,0:T(8,128)(2,1)}, bf16[256,256]{1,0:T(8,128)(2,1)S(1)}, u32[]{:S(2)}) copy-start(bf16[256,256]{1,0:T(8,128)(2,1)S(1)} %fusion.129) | copy-start | bytes 393220
  572.1 21.5 %copy-start.88 = (f32[2048]{0:T(1024)S(1)}, f32[2048]{0:T(1024)}, u32[]{:S(2)}) copy-start(f32[2048]{0:T(1024)} %param.39) | copy-start | bytes 24580
  837.2 75.4 %reduce-scatter.19.cloned.1.call-start = ((), (), s32[]{:S(2)}) async-start(), calls=%async_computation.23 | async-start | bytes 1179648 | tf_op jit(solution)/shard_map/reduce_scatter | solution.py:369
  838.0 111.9 %reduce-scatter.41.cloned.1.call-start = ((), (), s32[]{:S(2)}) async-start(), calls=%async_computation.34 | async-start | bytes 589824 | tf_op jit(solution)/shard_map/reduce_scatter | solution.py:446
  839.7 147.5 %reduce-scatter.37.cloned.1.call-start = ((), (), s32[]{:S(2)}) async-start(), calls=%async_computation.32 | async-start | bytes 589824 | tf_op jit(solution)/shard_map/reduce_scatter | solution.py:440
  841.1 183.4 %reduce-scatter.35.cloned.1.call-start = ((), (), s32[]{:S(2)}) async-start(), calls=%async_computation.31 | async-start | bytes 589824 | tf_op jit(solution)/shard_map/reduce_scatter | solution.py:437
  844.6 217.3 %reduce-scatter.33.cloned.1.call-start = ((), (), s32[]{:S(2)}) async-start(), calls=%async_computation.30 | async-start | bytes 589824 | tf_op jit(solution)/shard_map/reduce_scatter | solution.py:434
  847.2 252.0 %reduce-scatter.23.cloned.1.call-start = ((), (), s32[]{:S(2)}) async-start(), calls=%async_computation.25 | async-start | bytes 589824 | tf_op jit(solution)/shard_map/reduce_scatter | solution.py:419
  853.0 283.6 %reduce-scatter.47.cloned.1.call-start = ((), (), s32[]{:S(2)}) async-start(), calls=%async_computation.37 | async-start | bytes 589824 | tf_op jit(solution)/shard_map/reduce_scatter | solution.py:455
  857.7 319.9 %reduce-scatter.39.cloned.1.call-start = ((), (), s32[]{:S(2)}) async-start(), calls=%async_computation.33 | async-start | bytes 1622016 | tf_op jit(solution)/shard_map/reduce_scatter | solution.py:443
  862.0 357.0 %reduce-scatter.43.cloned.1.call-start = ((), (), s32[]{:S(2)}) async-start(), calls=%async_computation.35 | async-start | bytes 1622016 | tf_op jit(solution)/shard_map/reduce_scatter | solution.py:449
  866.3 393.7 %reduce-scatter.45.cloned.1.call-start = ((), (), s32[]{:S(2)}) async-start(), calls=%async_computation.36 | async-start | bytes 1622016 | tf_op jit(solution)/shard_map/reduce_scatter | solution.py:452
  870.5 42.1 %copy-start.78 = (bf16[128,256]{1,0:T(8,128)(2,1)S(1)}, bf16[128,256]{1,0:T(8,128)(2,1)}, u32[]{:S(2)}) copy-start(bf16[128,256]{1,0:T(8,128)(2,1)} %param.49) | copy-start | bytes 196612
  870.5 43.3 %copy-start.60 = (f32[256,128]{1,0:T(8,128)S(1)}, f32[256,128]{1,0:T(8,128)}, u32[]{:S(2)}) copy-start(f32[256,128]{1,0:T(8,128)} %copy-done.57) | copy-start | bytes 393220
  870.5 426.9 %reduce-scatter.21.cloned.1.call-start = ((), (), s32[]{:S(2)}) async-start(), calls=%async_computation.24 | async-start | bytes 589824 | tf_op jit(solution)/shard_map/reduce_scatter | solution.py:416
  871.0 42.8 %copy-start.16 = (bf16[256,2048]{1,0:T(8,128)(2,1)S(1)}, bf16[256,2048]{1,0:T(8,128)(2,1)}, u32[]{:S(2)}) copy-start(bf16[256,2048]{1,0:T(8,128)(2,1)} %param.33) | copy-start | bytes 3145732
  871.0 42.7 %copy-start.99 = (f32[2048]{0:T(1024)S(1)}, f32[2048]{0:T(1024)}, u32[]{:S(2)}) copy-start(f32[2048]{0:T(1024)} %param.38) | copy-start | bytes 24580
  871.1 42.7 %copy-start.102 = (f32[256]{0:T(256)S(1)}, f32[256]{0:T(256)}, u32[]{:S(2)}) copy-start(f32[256]{0:T(256)} %copy-done.101) | copy-start | bytes 3076
  875.3 40.0 %copy-start.55 = (bf16[256,256]{0,1:T(8,128)(2,1)}, bf16[256,256]{0,1:T(8,128)(2,1)S(1)}, u32[]{:S(2)}) copy-start(bf16[256,256]{0,1:T(8,128)(2,1)S(1)} %fusion.130) | copy-start | bytes 393220
  915.3 419.3 %reduce-scatter.25.cloned.1.call-start = ((), (), s32[]{:S(2)}) async-start(), calls=%async_computation.26 | async-start | bytes 589824 | tf_op jit(solution)/shard_map/reduce_scatter | solution.py:422
  916.8 455.2 %reduce-scatter.29.cloned.1.call-start = ((), (), s32[]{:S(2)}) async-start(), calls=%async_computation.28 | async-start | bytes 589824 | tf_op jit(solution)/shard_map/reduce_scatter | solution.py:428
  919.6 489.2 %reduce-scatter.27.cloned.1.call-start = ((), (), s32[]{:S(2)}) async-start(), calls=%async_computation.27 | async-start | bytes 73728 | tf_op jit(solution)/shard_map/reduce_scatter | solution.py:425
  919.9 12.0 copy-start.40
  919.9 12.0 copy-start.65
  934.1 511.7 %reduce-scatter.31.cloned.1.call-start = ((), (), s32[]{:S(2)}) async-start(), calls=%async_computation.29 | async-start | bytes 73728 | tf_op jit(solution)/shard_map/reduce_scatter | solution.py:431
  935.0 437.0 %copy-start.17 = (bf16[256,2048]{1,0:T(8,128)(2,1)S(1)}, bf16[256,2048]{1,0:T(8,128)(2,1)}, u32[]{:S(2)}) copy-start(bf16[256,2048]{1,0:T(8,128)(2,1)} %param.33) | copy-start | bytes 3145732
  935.0 573.9 %all-reduce.4.cloned.1.call-start = ((), (), s32[]{:S(2)}) async-start(), calls=%async_computation.38 | async-start | bytes 2260992 | tf_op jit(solution)/shard_map/psum | solution.py:460
  1509.0 9.6 copy-start.86
  1509.0 10.3 copy-start.85
  1509.0 11.0 copy-start.84
  1509.0 11.6 copy-start.83
  1509.0 12.3 copy-start.82
  1509.0 13.0 copy-start.81
  (100 other events, 365.6 us)
Sparse Core Ops, SparseCore 0:
  9.9 65.9 all-gather.6
  87.1 23.4 all-gather.10
  113.1 23.4 all-gather.8
  138.4 55.9 all-gather.12
  196.1 120.9 all-gather.16
  318.9 213.8 all-gather.14
  837.3 36.0 reduce-scatter.16
  876.6 35.9 reduce-scatter.18
  915.7 34.1 reduce-scatter.40
  953.1 34.1 reduce-scatter.36
  990.3 34.1 reduce-scatter.34
  1027.7 34.1 reduce-scatter.32
  1065.0 34.1 reduce-scatter.22
  1102.4 34.1 reduce-scatter.46
  1139.7 37.8 reduce-scatter.38
  1181.1 37.8 reduce-scatter.42
  1222.1 37.9 reduce-scatter.44
  1263.3 34.0 reduce-scatter.20
  1300.5 34.1 reduce-scatter.24
  1337.8 34.0 reduce-scatter.28
  1375.6 33.1 reduce-scatter.26
  1412.6 33.1 reduce-scatter.30
  1449.3 59.6 all-reduce.3
where the time goes:
time: 1540 us; the launch traced here: 1530 us
  waiting for transfers between devices  891 us (58%)
  matrix products  409 us (27%)
  other arithmetic  102 us (7%)
  local copies, waits for them, and re-layouts  88.9 us (6%)
  blocking collectives  19.9 us (1%)
  between operations  15.6 us (1%)
    all_gather x1, waiting for transfers between devices, shards(): lax.all_gather(gate_up_weight, 'grp', axis=1, tiled=True)  203 us
    dot_general x12, matrix products, block_scores(): jnp.einsum('qhgd,khd->hgqk', query, key_block, preferred_element_type=jnp...  72.3 us
    dot_general x15, matrix products, linear_compose(): return jnp.dot(left, right, preferred_element_type=jnp.float32)  70.3 us
    dot_general x15, matrix products, left_with_flipped(): lax.dot_general(left, right, (((1,), (1,)), ((), ())), preferred_element_...  67.7 us
    all_gather x1, waiting for transfers between devices, shards(): lax.all_gather(qkv_weight, 'grp', axis=1, tiled=True)  57.5 us
    dot_general x4, matrix products, grad_step(): jnp.einsum('hgqk,qhgd->khd', probs.astype(jnp.bfloat16), dattended, prefe...  42.4 us
    psum x1, waiting for transfers between devices, shards(): lax.psum(shares[0].astype(jnp.bfloat16), 'rep').astype(jnp.float32)  42 us
    reduce_scatter x1, waiting for transfers between devices, shards(): lax.psum_scatter(lift_right_sens.astype(jnp.bfloat16), 'grp', scatter_dim...  41.4 us
  transfers between devices with their start and end apart: 23, of which 22 were waited for; matrix products, arithmetic and copies ran while one was open for 17% of the time, Pallas kernels for 0%

commit v1 on v0

v1 whole, which is shorter than its diff:
```python
import functools

import jax
import jax.numpy as jnp
from jax import lax
from jax.experimental import pallas as pl
from jax.experimental.pallas import tpu as pltpu
from jax.sharding import PartitionSpec as P

HEADS = 32
KV_HEADS = 4
HEAD_DIM = 64
RANK = 16
LANES = 128
KEY_BLOCK = 512

EPS = 1e-05
LOWRANK_FACTOR = 2.0
MASKED = -1e30
F32 = jnp.float32
BF16 = jnp.bfloat16


def mm(left, right):
    return jnp.dot(left, right, preferred_element_type=F32)


def mm_nt(left, right):
    return lax.dot_general(left, right, (((1,), (1,)), ((), ())), preferred_element_type=F32)


def mm_tn(left, right):
    return lax.dot_general(left, right, (((0,), (0,)), ((), ())), preferred_element_type=F32)


def inverse_rms(value):
    return lax.rsqrt(jnp.mean(value * value, axis=-1, keepdims=True) + EPS)


def norm_backward(value, scale, gain, grad):
    scaled = gain * grad
    return scale * scaled - value * (scale * scale * scale) * jnp.mean(
        scaled * value, axis=-1, keepdims=True
    )


def half_turn(value):
    half = HEAD_DIM // 2
    lane = lax.broadcasted_iota(jnp.int32, value.shape, 1) % HEAD_DIM
    return jnp.where(
        lane < half, -jnp.roll(value, -half, axis=1), jnp.roll(value, half, axis=1)
    )


def rotate(value, cosines, sines):
    return value * cosines + half_turn(value) * sines


def unrotate(grad, cosines, sines):
    return grad * cosines - half_turn(grad * sines)


def attention_forward_kernel(span, q_ref, k_ref, v_ref, bias_ref, out_ref, lse_ref):
    tokens = q_ref.shape[0]
    query = q_ref[...]

    def step(index, carry):
        start = pl.multiple_of(index * KEY_BLOCK, KEY_BLOCK)
        bias = bias_ref[pl.ds(start, KEY_BLOCK), :]
        mixed = carry[4]
        new, parts, decays = [], [], []
        for side in range(2):
            peak, total = carry[2 * side], carry[2 * side + 1]
            scores = mm_nt(k_ref[0, side, pl.ds(start, KEY_BLOCK), :], query) + bias
            top = jnp.maximum(peak, jnp.max(scores, axis=0, keepdims=True))
            decay = jnp.exp(peak - top)
            probs = jnp.exp(scores - top)
            total = total * decay + jnp.sum(probs, axis=0, keepdims=True)
            new += [top, total]
            decays.append(jnp.broadcast_to(decay, (HEAD_DIM, tokens)))
            parts.append(mm_tn(v_ref[0, side, pl.ds(start, KEY_BLOCK), :], probs.astype(BF16)))
        mixed = mixed * jnp.concatenate(decays, axis=0) + (parts[0] + parts[1])
        return (*new, mixed)

    low = jnp.full((1, tokens), MASKED, F32)
    none = jnp.zeros((1, tokens), F32)
    peak0, total0, peak1, total1, mixed = lax.fori_loop(
        span[0], span[1], step, (low, none, low, none, jnp.zeros((LANES, tokens), F32))
    )
    weight = jnp.concatenate(
        [
            jnp.broadcast_to(1.0 / total0, (HEAD_DIM, tokens)),
            jnp.broadcast_to(1.0 / total1, (HEAD_DIM, tokens)),
        ],
        axis=0,
    )
    out_ref[...] = (mixed * weight).T.astype(BF16)
    lse_ref[0] = jnp.concatenate([peak0 + jnp.log(total0), peak1 + jnp.log(total1)], axis=0)


def attention_forward(span, query, key_pairs, value_pairs, bias):
    tokens, width = query.shape
    keys = bias.shape[0]
    pairs = width // LANES
    per_kv = pairs // KV_HEADS
    pair_spec = pl.BlockSpec((tokens, LANES), lambda j, s: (0, j))
    kv_spec = pl.BlockSpec((1, 2, keys, LANES), lambda j, s: (j // per_kv, 0, 0, 0))
    return pl.pallas_call(
        attention_forward_kernel,
        out_shape=(
            jax.ShapeDtypeStruct((tokens, width), BF16),
            jax.ShapeDtypeStruct((pairs, 2, tokens), F32),
        ),
        grid_spec=pltpu.PrefetchScalarGridSpec(
            num_scalar_prefetch=1,
            grid=(pairs,),
            in_specs=[
                pair_spec,
                kv_spec,
                kv_spec,
                pl.BlockSpec((keys, tokens), lambda j, s: (0, 0)),
            ],
            out_specs=(pair_spec, pl.BlockSpec((1, 2, tokens), lambda j, s: (j, 0, 0))),
        ),
        compiler_params=pltpu.CompilerParams(
            dimension_semantics=("arbitrary",), vmem_limit_bytes=40 << 20
        ),
        cost_estimate=pl.CostEstimate(
            flops=4 * tokens * keys * width,
            transcendentals=tokens * keys * HEADS // 2,
            bytes_accessed=4 * tokens * width + 16 * keys * LANES * KV_HEADS,
        ),
        name="attention_forward",
    )(span, query, key_pairs, value_pairs, bias)


def attention_backward_kernel(
    span, q_ref, do_ref, o_ref, lse_ref, k_ref, v_ref, bias_ref, dq_ref, dk_ref, dv_ref
):
    tokens = q_ref.shape[0]
    per_kv = pl.num_programs(0) // KV_HEADS
    member = lax.rem(pl.program_id(0), per_kv)

    @pl.when(member == 0)
    def _():
        dk_ref[...] = jnp.zeros_like(dk_ref)
        dv_ref[...] = jnp.zeros_like(dv_ref)

    query = q_ref[...]
    grad = do_ref[...]
    lane = lax.broadcasted_iota(jnp.int32, (tokens, LANES), 1)
    none = jnp.zeros_like(query)
    query_stack = jnp.concatenate(
        [jnp.where(lane < HEAD_DIM, query, none), jnp.where(lane < HEAD_DIM, none, query)], axis=0
    )
    grad_stack = jnp.concatenate(
        [jnp.where(lane < HEAD_DIM, grad, none), jnp.where(lane < HEAD_DIM, none, grad)], axis=0
    )
    product = grad.astype(F32) * o_ref[...].astype(F32)
    row = lax.broadcasted_iota(jnp.int32, (8, LANES), 0)
    column = lax.broadcasted_iota(jnp.int32, (8, LANES), 1)
    chooser = jnp.where(row == column // HEAD_DIM, 1.0, 0.0).astype(F32)
    deltas = lax.dot_general(
        chooser,
        product,
        (((1,), (1,)), ((), ())),
        precision=lax.Precision.HIGHEST,
        preferred_element_type=F32,
    )

    def step(index, dquery):
        start = pl.multiple_of(index * KEY_BLOCK, KEY_BLOCK)
        rows = pl.ds(start, KEY_BLOCK)
        bias = bias_ref[rows, :]
        all_probs, all_dscores = [], []
        for side in range(2):
            scores = mm_nt(k_ref[0, side, rows, :], query) + bias
            probs = jnp.exp(scores - lse_ref[0, side : side + 1, :])
            dprobs = mm_nt(v_ref[0, side, rows, :], grad)
            dscores = (probs * (dprobs - deltas[side : side + 1, :])).astype(BF16)
            all_probs.append(probs.astype(BF16))
            all_dscores.append(dscores)
            dquery = dquery + mm_tn(k_ref[0, side, rows, :], dscores)
        dk_ref[0, rows, :] += mm(jnp.concatenate(all_dscores, axis=1), query_stack)
        dv_ref[0, rows, :] += mm(jnp.concatenate(all_probs, axis=1), grad_stack)
        return dquery

    dquery = lax.fori_loop(span[0], span[1], step, jnp.zeros((LANES, tokens), F32))
    dq_ref[...] = dquery.T * (HEAD_DIM**-0.5)


def attention_backward(span, query, grad, attended, lse, key_pairs, value_pairs, bias):
    tokens, width = query.shape
    keys = bias.shape[0]
    pairs = width // LANES
    per_kv = pairs // KV_HEADS
    pair_spec = pl.BlockSpec((tokens, LANES), lambda j, s: (0, j))
    kv_spec = pl.BlockSpec((1, 2, keys, LANES), lambda j, s: (j // per_kv, 0, 0, 0))
    dkv_spec = pl.BlockSpec((1, keys, LANES), lambda j, s: (j // per_kv, 0, 0))
    return pl.pallas_call(
        attention_backward_kernel,
        out_shape=(
            jax.ShapeDtypeStruct((tokens, width), F32),
            jax.ShapeDtypeStruct((KV_HEADS, keys, LANES), F32),
            jax.ShapeDtypeStruct((KV_HEADS, keys, LANES), F32),
        ),
        grid_spec=pltpu.PrefetchScalarGridSpec(
            num_scalar_prefetch=1,
            grid=(pairs,),
            in_specs=[
                pair_spec,
                pair_spec,
                pair_spec,
                pl.BlockSpec((1, 2, tokens), lambda j, s: (j, 0, 0)),
                kv_spec,
                kv_spec,
                pl.BlockSpec((keys, tokens), lambda j, s: (0, 0)),
            ],
            out_specs=(pair_spec, dkv_spec, dkv_spec),
        ),
        compiler_params=pltpu.CompilerParams(
            dimension_semantics=("arbitrary",), vmem_limit_bytes=48 << 20
        ),
        cost_estimate=pl.CostEstimate(
            flops=10 * tokens * keys * width,
            transcendentals=tokens * keys * HEADS // 2,
            bytes_accessed=10 * tokens * width + 24 * keys * LANES * KV_HEADS,
        ),
        name="attention_backward",
    )(span, query, grad, attended, lse, key_pairs, value_pairs, bias)


def side_pairs(array):
    keys = array.shape[0]
    heads = array.reshape(keys, KV_HEADS, HEAD_DIM).transpose(1, 0, 2)
    none = jnp.zeros_like(heads)
    return jnp.stack(
        [jnp.concatenate([heads, none], axis=2), jnp.concatenate([none, heads], axis=2)], axis=1
    )


def join_sides(array):
    summed = array[:, :, :HEAD_DIM] + array[:, :, HEAD_DIM:]
    return summed.transpose(1, 0, 2).reshape(array.shape[1], KV_HEADS * HEAD_DIM)


def exchange_sum(parts):
    received = lax.all_to_all(parts.astype(BF16), "grp", 0, 0, tiled=True)
    return jnp.sum(received.astype(F32), axis=0)


def shards(
    tokens,
    response_sensitivity,
    seq_lengths,
    prefix_lengths,
    adapter_ids,
    attn_gain,
    mlp_gain,
    qkv_weight,
    out_weight,
    gate_up_weight,
    down_weight,
    query_in,
    asking_right_pieces,
    key_in,
    lookup_right_pieces,
    value_in,
    content_right_pieces,
    output_in,
    final_right_pieces,
    gate_in,
    switch_right_pieces,
    up_in,
    lift_right_pieces,
    down_in,
    lower_right_pieces,
):
    count, width = tokens.shape
    members = lax.axis_size("grp")
    groups = lax.axis_size("rep")
    kv_width = lookup_right_pieces.shape[1]
    narrow = query_in.shape[1]
    hidden_width = down_weight.shape[0]
    group = lax.axis_index("rep")
    member = lax.axis_index("grp")
    lengths = lax.dynamic_slice_in_dim(seq_lengths, 2 * group, 2)
    prefixes = lax.dynamic_slice_in_dim(prefix_lengths, 2 * group, 2)
    chosen_ids = lax.dynamic_slice_in_dim(adapter_ids, 2 * group, 2)
    key_count = count * members

    qkv_full = lax.all_gather(qkv_weight, "grp", axis=1, tiled=True)
    out_full = lax.all_gather(out_weight, "grp", axis=1, tiled=True)
    down_full = lax.all_gather(down_weight, "grp", axis=1, tiled=True)
    gate_up_full = lax.all_gather(gate_up_weight, "grp", axis=1, tiled=True)

    key_index = jnp.arange(key_count, dtype=jnp.int32)
    key_second = (key_index >= lengths[0]).astype(jnp.int32)
    key_position = key_index - key_second * lengths[0]
    own_index = member * count + jnp.arange(count, dtype=jnp.int32)
    own_second = (own_index >= lengths[0]).astype(jnp.int32)
    position = own_index - own_second * lengths[0]
    prefix = jnp.where(own_second == 0, prefixes[0], prefixes[1])
    chosen = jnp.where(own_second == 0, chosen_ids[0], chosen_ids[1])
    allowed = (key_second[:, None] == own_second[None, :]) & (
        (key_position[:, None] <= position[None, :]) | (key_position[:, None] < prefix[None, :])
    )
    bias = jnp.where(allowed, 0.0, MASKED).astype(F32)
    first_key = own_second[0] * lengths[0]
    last_key = jnp.max(own_second * lengths[0] + jnp.maximum(position, prefix - 1))
    span = jnp.stack([first_key // KEY_BLOCK, last_key // KEY_BLOCK + 1]).astype(jnp.int32)

    columns = jnp.arange(narrow, dtype=jnp.int32)
    visible = (chosen[:, None] == columns[None, :] // RANK).astype(F32)
    mask_two = jnp.concatenate([visible, visible], axis=1)
    mask_three = jnp.concatenate([visible, visible, visible], axis=1)
    slots = 2 * RANK
    slot = jnp.arange(slots, dtype=jnp.int32)
    slot_column = chosen_ids[slot // RANK] * RANK + slot % RANK
    pick = (columns[:, None] == slot_column[None, :]).astype(BF16)
    slot_visible = (own_second[:, None] == slot[None, :] // RANK).astype(F32)

    def compact(latent):
        return (mm(latent, pick) * slot_visible).astype(BF16)

    incoming = tokens.astype(F32)
    scale_one = inverse_rms(incoming)
    norm1 = (incoming * scale_one * attn_gain).astype(BF16)
    qkv_in = jnp.concatenate([query_in, key_in, value_in], axis=1)
    latent_qkv = (mm(norm1, qkv_in) * mask_three).astype(BF16)
    latent_q, latent_k, latent_v = (
        latent_qkv[:, :narrow],
        latent_qkv[:, narrow : 2 * narrow],
        latent_qkv[:, 2 * narrow :],
    )
    adapted = LOWRANK_FACTOR * jnp.concatenate(
        [
            mm(latent_q, asking_right_pieces),
            mm(latent_k, lookup_right_pieces),
            mm(latent_v, content_right_pieces),
        ],
        axis=1,
    )
    half = HEAD_DIM // 2
    freqs = 10000.0 ** (-2.0 * jnp.arange(half).astype(F32) / HEAD_DIM)
    angles = position.astype(F32)[:, None] * jnp.concatenate([freqs, freqs])[None, :]
    cosines = jnp.cos(angles)
    sines = jnp.sin(angles)
    wide_cos, wide_sin = jnp.tile(cosines, (1, HEADS)), jnp.tile(sines, (1, HEADS))
    kv_cos, kv_sin = jnp.tile(cosines, (1, KV_HEADS)), jnp.tile(sines, (1, KV_HEADS))

    qkv = mm(norm1, qkv_full) + adapted
    scale = HEAD_DIM**-0.5
    query = (rotate(qkv[:, :width], wide_cos, wide_sin)).astype(BF16) * jnp.asarray(scale, BF16)
    key_own = rotate(qkv[:, width : width + kv_width], kv_cos, kv_sin).astype(BF16)
    value_own = qkv[:, width + kv_width :].astype(BF16)
    key_value = lax.all_gather(
        jnp.concatenate([key_own, value_own], axis=1), "grp", axis=0, tiled=True
    )
    key_pairs = side_pairs(key_value[:, :kv_width])
    value_pairs = side_pairs(key_value[:, kv_width:])
    attended_low, lse = attention_forward(span, query, key_pairs, value_pairs, bias)

    latent_o = (mm(attended_low, output_in) * visible).astype(BF16)
    stream = incoming + (
        mm(attended_low, out_full) + LOWRANK_FACTOR * mm(latent_o, final_right_pieces)
    )
    scale_two = inverse_rms(stream)
    norm2 = (stream * scale_two * mlp_gain).astype(BF16)
    ffn_in = jnp.concatenate([gate_in, up_in], axis=1)
    latent_gu = (mm(norm2, ffn_in) * mask_two).astype(BF16)
    latent_g, latent_u = latent_gu[:, :narrow], latent_gu[:, narrow:]
    gate_up = mm(norm2, gate_up_full) + LOWRANK_FACTOR * jnp.concatenate(
        [mm(latent_g, switch_right_pieces), mm(latent_u, lift_right_pieces)], axis=1
    )
    gate = gate_up[:, :hidden_width]
    up = gate_up[:, hidden_width:]
    sigma = jax.nn.sigmoid(gate)
    act = (gate * sigma * up).astype(BF16)
    latent_d = (mm(act, down_in) * visible).astype(BF16)
    level_response = (
        stream + mm(act, down_full) + LOWRANK_FACTOR * mm(latent_d, lower_right_pieces)
    ).astype(BF16)

    sens = response_sensitivity
    dlat_d = (LOWRANK_FACTOR * mm_nt(sens, lower_right_pieces) * visible).astype(BF16)
    dact = mm_nt(sens, down_full) + mm_nt(dlat_d, down_in)
    dgate = (dact * up * (sigma * (1.0 + gate * (1.0 - sigma)))).astype(BF16)
    dup = (dact * gate * sigma).astype(BF16)
    dlat_gu = (
        LOWRANK_FACTOR
        * jnp.concatenate(
            [mm_nt(dgate, switch_right_pieces), mm_nt(dup, lift_right_pieces)], axis=1
        )
        * mask_two
    ).astype(BF16)
    dnorm2 = (
        mm_nt(dgate, gate_up_full[:, :hidden_width])
        + mm_nt(dup, gate_up_full[:, hidden_width:])
        + mm_nt(dlat_gu, ffn_in)
    )
    dhidden = sens.astype(F32) + norm_backward(stream, scale_two, mlp_gain, dnorm2)
    dbranch = dhidden.astype(BF16)
    dlat_o = (LOWRANK_FACTOR * mm_nt(dbranch, final_right_pieces) * visible).astype(BF16)
    dattended = (mm_nt(dbranch, out_full) + mm_nt(dlat_o, output_in)).astype(BF16)

    def blocks(array):
        return array.reshape(members, array.shape[0] // members, array.shape[1])

    wide = jnp.concatenate(
        [
            LOWRANK_FACTOR * mm_tn(sens, compact(latent_d)),
            mm_tn(norm2, jnp.concatenate([compact(dlat_gu[:, :narrow]), compact(dlat_gu[:, narrow:])], axis=1)),
            mm_tn(attended_low, compact(dlat_o)),
        ],
        axis=1,
    ).astype(BF16)
    final_part = (LOWRANK_FACTOR * mm_tn(dbranch, compact(latent_o))).astype(BF16)
    deep = jnp.concatenate(
        [
            mm_tn(act, compact(dlat_d)),
            LOWRANK_FACTOR * mm_tn(dgate, compact(latent_g)),
            LOWRANK_FACTOR * mm_tn(dup, compact(latent_u)),
        ],
        axis=1,
    ).astype(BF16)
    wide_rows, deep_rows = width // members, hidden_width // members
    final_blocks = jnp.pad(blocks(final_part), ((0, 0), (0, deep_rows - wide_rows), (0, 0)))
    early = jnp.concatenate(
        [blocks(wide), jnp.concatenate([blocks(deep), final_blocks], axis=2)], axis=1
    )
    early_sum = lax.psum_scatter(early, "grp", scatter_dimension=0, tiled=True)
    early_sum = early_sum.reshape(wide_rows + deep_rows, 4 * slots)
    early_all = lax.all_gather(early_sum, "rep", axis=0)

    dquery, dkeys, dvalues = attention_backward(
        span, query, dattended, attended_low, lse, key_pairs, value_pairs, bias
    )
    dkv = jnp.concatenate([join_sides(dkeys), join_sides(dvalues)], axis=1)
    dkv_own = exchange_sum(dkv.reshape(members, count, 2 * kv_width))
    dq = unrotate(dquery, wide_cos, wide_sin).astype(BF16)
    dk = unrotate(dkv_own[:, :kv_width], kv_cos, kv_sin).astype(BF16)
    dv = dkv_own[:, kv_width:].astype(BF16)
    dlat_qkv = (
        LOWRANK_FACTOR
        * jnp.concatenate(
            [
                mm_nt(dq, asking_right_pieces),
                mm_nt(dk, lookup_right_pieces),
                mm_nt(dv, content_right_pieces),
            ],
            axis=1,
        )
        * mask_three
    ).astype(BF16)
    dqkv = jnp.concatenate([dq, dk, dv], axis=1)
    late_wide = jnp.concatenate(
        [
            mm_tn(
                norm1,
                jnp.concatenate(
                    [compact(dlat_qkv[:, i * narrow : (i + 1) * narrow]) for i in range(3)], axis=1
                ),
            ),
            LOWRANK_FACTOR * mm_tn(dq, compact(latent_q)),
        ],
        axis=1,
    ).astype(BF16)
    late_thin = jnp.concatenate(
        [
            LOWRANK_FACTOR * mm_tn(dk, compact(latent_k)),
            LOWRANK_FACTOR * mm_tn(dv, compact(latent_v)),
        ],
        axis=1,
    ).astype(BF16)
    thin_rows = kv_width // members
    late = jnp.concatenate(
        [blocks(late_wide), jnp.pad(blocks(late_thin), ((0, 0), (0, 0), (0, 2 * slots)))], axis=1
    )
    late_sum = exchange_sum(late).astype(BF16)
    late_all = lax.all_gather(late_sum, "rep", axis=0)
    dnorm1 = mm_nt(dqkv, qkv_full) + mm_nt(dlat_qkv, qkv_in)
    input_grad = (dhidden + norm_backward(incoming, scale_one, attn_gain, dnorm1)).astype(BF16)

    all_slot = jnp.arange(groups * slots, dtype=jnp.int32)
    all_column = adapter_ids[all_slot // RANK] * RANK + all_slot % RANK
    place = (all_column[:, None] == columns[None, :]).astype(BF16)

    def gathered(array, start, rows, index):
        piece = lax.slice_in_dim(array, start, start + rows, axis=1)
        piece = piece[:, :, index * slots : (index + 1) * slots]
        return piece.transpose(1, 0, 2).reshape(rows, groups * slots)

    def as_rows(array, start, rows, index):
        return mm(gathered(array, start, rows, index), place)

    def as_columns(array, start, rows, index):
        return lax.dot_general(
            place,
            gathered(array, start, rows, index),
            (((0,), (1,)), ((), ())),
            preferred_element_type=F32,
        )

    return (
        level_response,
        input_grad,
        as_rows(late_all, 0, wide_rows, 0),
        as_columns(late_all, 0, wide_rows, 3),
        as_rows(late_all, 0, wide_rows, 1),
        as_columns(late_all, wide_rows, thin_rows, 0),
        as_rows(late_all, 0, wide_rows, 2),
        as_columns(late_all, wide_rows, thin_rows, 1),
        as_rows(early_all, 0, wide_rows, 3),
        as_columns(early_all, wide_rows, wide_rows, 3),
        as_rows(early_all, 0, wide_rows, 1),
        as_columns(early_all, wide_rows, deep_rows, 1),
        as_rows(early_all, 0, wide_rows, 2),
        as_columns(early_all, wide_rows, deep_rows, 2),
        as_rows(early_all, wide_rows, deep_rows, 0),
        as_columns(early_all, 0, wide_rows, 0),
    )


def solution(mesh):
    rows = P(("rep", "grp"), None)
    split = P(None, "grp")
    in_specs = (rows, rows, *[P()] * 5, *[split] * 4, *[P()] * 14)
    out_specs = (rows, rows, *[P("grp", None), P(None, "grp")] * 7)
    return jax.shard_map(shards, mesh=mesh, in_specs=in_specs, out_specs=out_specs, check_vma=False)
```

time: 1540 us -> 847 us (0.55)
  waiting for transfers between devices: 891 us -> 400 us
  matrix products: 409 us -> 185 us
  other arithmetic: 102 us -> 49.4 us
  Pallas kernels: 0 us -> 44.9 us
  starting transfers between devices: 1.52 us -> 25.7 us
    reduce_scatter x16 -> x1, waiting for transfers between devices: 537 us -> 0.01 us  [shards(): early_sum = lax.psum_scatter(early, 'grp', scatter_dimension=0, tiled=True)]
    dot_general x80 -> x61, matrix products: 409 us -> 185 us  [the longest x27 80.3 us: mm(): return jnp.dot(left, right, preferred_element_type=F32)]
    all_gather x6 -> x5, waiting for transfers between devices: 309 us -> 378 us  [the longest x1 203 us: shards(): gate_up_full = lax.all_gather(gate_up_weight, 'grp', axis=1, tiled=True)]
    pallas_call x0 -> x2, Pallas kernels: none -> 44.9 us  [the longest x1 29.8 us: attention_backward(): pl.pallas_call(attention_backward_kernel, out_shape=(jax.ShapeDtypeStruct...]
    psum x1 -> x0, waiting for transfers between devices: 42 us -> none  [shards(): lax.psum(shares[0].astype(jnp.bfloat16), 'rep').astype(jnp.float32)]
    reduce_sum x4 -> x2, other arithmetic: 37.8 us -> 3.07 us  [exchange_sum(): return jnp.sum(received.astype(F32), axis=0)]
    all_gather x0 -> x2, blocking collectives: none -> 33.8 us  [the longest x1 19.8 us: shards(): early_all = lax.all_gather(early_sum, 'rep', axis=0)]
    all_to_all x0 -> x2, starting transfers between devices: none -> 25.2 us  [exchange_sum(): received = lax.all_to_all(parts.astype(BF16), 'grp', 0, 0, tiled=True)]
  transfers between devices with their start and end apart: 23 -> 8, of which waited for: 22 -> 6; matrix products, arithmetic and copies ran while one was open for 17% -> 19% of each run, Pallas kernels for 0% -> 2%
where the time goes in v1:
time: 847 us; the launch traced here: 839 us
  waiting for transfers between devices  400 us (47%)
  matrix products  185 us (22%)
  local copies, waits for them, and re-layouts  82.1 us (10%)
  other arithmetic  49.4 us (6%)
  Pallas kernels  44.9 us (5%)
  blocking collectives  33.8 us (4%)
  starting transfers between devices  25.7 us (3%)
  between operations  19.3 us (2%)
    all_gather x1, waiting for transfers between devices, shards(): gate_up_full = lax.all_gather(gate_up_weight, 'grp', axis=1, tiled=True)  203 us
    all_gather x1, waiting for transfers between devices, shards(): down_full = lax.all_gather(down_weight, 'grp', axis=1, tiled=True)  106 us
    dot_general x27, matrix products, mm(): return jnp.dot(left, right, preferred_element_type=F32)  80.3 us
    dot_general x16, matrix products, mm_nt(): lax.dot_general(left, right, (((1,), (1,)), ((), ())), preferred_element_...  71.5 us
    all_gather x1, waiting for transfers between devices, shards(): qkv_full = lax.all_gather(qkv_weight, 'grp', axis=1, tiled=True)  52.7 us
    pallas_call x1, Pallas kernels, attention_backward(): pl.pallas_call(attention_backward_kernel, out_shape=(jax.ShapeDtypeStruct...  29.8 us
    dot_general x11, matrix products, mm_tn(): lax.dot_general(left, right, (((0,), (0,)), ((), ())), preferred_element_...  25.4 us
    all_to_all x2, starting transfers between devices, exchange_sum(): received = lax.all_to_all(parts.astype(BF16), 'grp', 0, 0, tiled=True)  25.2 us
  transfers between devices with their start and end apart: 8, of which 6 were waited for; matrix products, arithmetic and copies ran while one was open for 19% of the time, Pallas kernels for 2%

profile of v1, /device:TPU:0, one launch (start us, length us, event | category | flops | bytes accessed | tf_op | source)
XLA Modules:
  0.0 839.5 jit_solution(3741880185636317054)
XLA Ops:
  23.3 52.7 %all-gather.7.cloned.1.call-done = bf16[2048,2560]{0,1:T(8,128)(2,1)} async-done(((bf16[2048,320]{0,1:T(8,128)(2,1)}), bf16[2048,2560]{0,1:T(8,128)(2,1)}) %all-gather.7.cloned.1.call-update) | async-done | bytes 10485776 | tf_op jit(solution)/shard_map/all_gather | solution.py:292
  75.9 7.5 convolution_add_fusion.2
  98.5 5.7 fusion.215
  114.3 2.6 and_select_fusion.bias_ref
  120.3 3.0 fusion.246
  130.0 3.5 pad_bitcast_fusion.1
  138.1 15.1 %attention_forward.1 = (bf16[256,2048]{1,0:T(8,128)(2,1)S(1)}, f32[16,2,256]{2,1,0:T(2,128)S(1)}) custom-call(s32[2]{0:T(128)S(1)} %pad_add_fusion.span, bf16[256,2048]{1,0:T(8,128)(2,1)S(1)} %fusion.71.q_ref, bf16[4,2,2048,128]{3,2,1,0:T(8,128)(2,1)S(1)} %pad_maximum_fusion.k_ref, bf16[4,2,2048,128]{3,2,1,0:T(8,128)(2,1)S(1)} %pad_maximum_fusion.1.v_ref, ...), custom_call_target="tpu_custom_call" | custom-call | flops 4294967296 | bytes 18874368 | tf_op jit(solution)/shard_map/attention_forward/pallas_call | solution.py:108
  154.9 17.0 %all-gather.11.cloned.1.call-done = bf16[2048,2048]{1,0:T(8,128)(2,1)} async-done(((bf16[2048,256]{1,0:T(8,128)(2,1)}), bf16[2048,2048]{1,0:T(8,128)(2,1)}) %all-gather.11.cloned.1.call-update) | async-done | bytes 8388624 | tf_op jit(solution)/shard_map/all_gather | solution.py:293
  171.9 5.9 fusion.253
  179.6 2.6 fusion.48
  182.3 3.4 fusion.116
  185.6 3.3 fusion.120
  189.0 105.8 %all-gather.15.cloned.1.call-done = bf16[5632,2048]{1,0:T(8,128)(2,1)} async-done(((bf16[5632,256]{1,0:T(8,128)(2,1)}), bf16[5632,2048]{1,0:T(8,128)(2,1)}) %all-gather.15.cloned.1.call-update) | async-done | bytes 23068688 | tf_op jit(solution)/shard_map/all_gather | solution.py:294
  294.7 12.8 %fusion.254 = f32[256,5632]{1,0:T(8,128)} fusion(bf16[256,2048]{1,0:T(8,128)(2,1)} %param.26, bf16[5632,2048]{1,0:T(8,128)(2,1)} %all-gather.15.cloned.1.call-done), kind=kOutput, calls=%fused_computation.386 | convolution fusion | flops 5905580032 | bytes 29884416 | tf_op jit(solution)/shard_map/dot_general | solution.py:29
  307.6 202.8 %all-gather.13.cloned.1.call-done = bf16[2048,11264]{1,0:T(8,128)(2,1)} async-done(((bf16[2048,1408]{1,0:T(8,128)(2,1)}), bf16[2048,11264]{1,0:T(8,128)(2,1)}) %all-gather.13.cloned.1.call-update) | async-done | bytes 46137360 | tf_op jit(solution)/shard_map/all_gather | solution.py:295
  510.4 27.1 %convolution_add_fusion = f32[256,11264]{1,0:T(8,128)} fusion(bf16[256,2048]{1,0:T(8,128)(2,1)} %copy-done.32, bf16[2048,11264]{1,0:T(8,128)(2,1)} %all-gather.13.cloned.1.call-done, f32[256,5632]{1,0:T(8,128)} %fusion.116, f32[256,5632]{1,0:T(8,128)} %fusion.120), kind=kOutput, calls=%fused_computation.4 | convolution fusion | flops 11819810816 | bytes 70254592 | tf_op jit(solution)/shard_map/dot_general | solution.py:25
  537.5 9.4 %multiply_convert_fusion.1 = (bf16[256,5632]{1,0:T(8,128)(2,1)S(1)}, bf16[256,5632]{1,0:T(8,128)(2,1)S(1)}, bf16[256,5632]{1,0:T(8,128)(2,1)}) fusion(f32[256,11264]{1,0:T(8,128)} %convolution_add_fusion, f32[256,5632]{1,0:T(8,128)} %fusion.254, bf16[256,128]{1,0:T(8,128)(2,1)} %fusion.53, bf16[5632,128]{1,0:T(8,128)(2,1)S(1)} %copy-done), kind=kOutput, calls=%fused_computation.13 | convolution fusion | flops 393609216 | bytes 27459584 | tf_op jit(solution)/shard_map/dot_general | solution.py:29
  551.8 3.4 fusion.4
  555.2 3.4 fusion.5
  558.6 12.7 %fusion = f32[256,2048]{1,0:T(8,128)} fusion(bf16[256,5632]{1,0:T(8,128)(2,1)} %copy-done.21, bf16[2048,11264]{1,0:T(8,128)(2,1)} %all-gather.13.cloned.1.call-done), kind=kOutput, calls=%fused_computation | convolution fusion | flops 5905580032 | bytes 28049408 | tf_op jit(solution)/shard_map/dot_general | solution.py:29
  571.3 13.6 %fusion.13 = f32[256,2048]{1,0:T(8,128)} fusion(f32[256,2048]{1,0:T(8,128)} %fusion, bf16[256,5632]{1,0:T(8,128)(2,1)} %copy-done.20, bf16[2048,11264]{1,0:T(8,128)(2,1)} %all-gather.13.cloned.1.call-done), kind=kOutput, calls=%fused_computation.41 | convolution fusion | flops 5906104320 | bytes 30146560 | tf_op jit(solution)/shard_map/dot_general | solution.py:29
  584.9 3.3 multiply_reduce_fusion
  591.5 2.8 fusion.20
  594.2 3.4 convolution_convert_fusion
  597.6 3.3 fusion.51
  601.0 2.0 convolution_convert_fusion.3
  602.9 6.4 fusion.227
  610.2 29.8 %attention_backward.1 = (f32[256,2048]{1,0:T(8,128)S(1)}, f32[4,2048,128]{2,1,0:T(8,128)}, f32[4,2048,128]{2,1,0:T(8,128)}) custom-call(s32[2]{0:T(128)S(1)} %pad_add_fusion.span, bf16[256,2048]{1,0:T(8,128)(2,1)S(1)} %fusion.71.q_ref, bf16[256,2048]{1,0:T(8,128)(2,1)S(1)} %fusion.17.do_ref, bf16[256,2048]{1,0:T(8,128)(2,1)S(1)} %get-tuple-element.21.o_ref, ...), custom_call_target="tpu_custom_call" | custom-call | flops 10737418240 | bytes 30408704 | tf_op jit(solution)/shard_map/attention_backward/pallas_call | solution.py:200
  644.0 2.0 fusion.19
  647.7 2.0 copy.238
  650.9 2.4 copy.241
  656.0 2.4 copy.240
  658.3 2.0 fusion.21
  661.5 5.1 fusion.40
  666.6 4.6 fusion.30
  672.8 2.5 copy.253
  675.3 4.6 fusion.31
  685.1 20.8 %all-to-all-start = ((bf16[8,256,512]{1,2,0:T(8,128)(2,1)}), bf16[8,256,512]{1,2,0:T(8,128)(2,1)}, u32[]{:S(2)}, u32[]{:S(2)}) async-start(bf16[8,256,512]{1,2,0:T(8,128)(2,1)} %copy.190), calls=%async_computation | async-start | bytes 4194304 | tf_op jit(solution)/shard_map/all_to_all | solution.py:248
  707.9 11.7 %convolution_add_fusion.6 = f32[256,2048]{1,0:T(8,128)S(1)} fusion(f32[256,2048]{1,0:T(8,128)S(1)} %copy-done.8, bf16[256,5632]{1,0:T(8,128)(2,1)} %get-tuple-element.28, bf16[5632,2048]{1,0:T(8,128)(2,1)} %all-gather.15.cloned.1.call-done), kind=kOutput, calls=%fused_computation.43 | convolution fusion | flops 5906104320 | bytes 30146560 | tf_op jit(solution)/shard_map/dot_general | solution.py:25
  721.0 17.5 %all-to-all-done = bf16[8,256,512]{1,2,0:T(8,128)(2,1)} async-done(((bf16[8,256,512]{1,2,0:T(8,128)(2,1)}), bf16[8,256,512]{1,2,0:T(8,128)(2,1)}, u32[]{:S(2)}, u32[]{:S(2)}) %all-to-all-start) | async-done | bytes 2097184 | tf_op jit(solution)/shard_map/all_to_all | solution.py:248
  751.6 2.1 copy.233
  756.9 2.3 pad_maximum_fusion.3
  759.2 4.4 all-to-all-start.1
  763.7 5.8 fusion.41
  775.2 14.0 %all-gather = bf16[1152,128]{1,0:T(8,128)(2,1)S(1)} all-gather(bf16[288,128]{1,0:T(8,128)(2,1)S(1)} %reduce_sum.62), channel_id=2, replica_groups=mesh['rep'=4,'grp'=8] {'rep'}, dimensions={0}, use_global_device_ids=true | all-gather | bytes 368640 | tf_op jit(solution)/shard_map/all_gather | solution.py:481
  795.6 19.8 %all_gather.31 = bf16[4,960,128]{2,1,0:T(8,128)(2,1)S(1)} all-gather(bf16[1,960,128]{2,1,0:T(8,128)(2,1)} %reduce-scatter.2.cloned.1.call-done), channel_id=1, replica_groups=mesh['rep'=4,'grp'=8] {'rep'}, dimensions={0}, use_global_device_ids=true | all-gather | bytes 1228800 | tf_op jit(solution)/shard_map/all_gather | solution.py:434
  817.9 2.0 copy.224
  822.8 2.0 fusion.102
  (373 shorter events, 126.1 us)
Async XLA Ops:
  7.2 530.3 %copy-start = (bf16[5632,128]{1,0:T(8,128)(2,1)S(1)}, bf16[5632,128]{1,0:T(8,128)(2,1)}, u32[]{:S(2)}) copy-start(bf16[5632,128]{1,0:T(8,128)(2,1)} %param.48) | copy-start | bytes 4325380
  7.2 9.9 %copy-start.17 = (bf16[256,2048]{1,0:T(8,128)(2,1)S(1)}, bf16[256,2048]{1,0:T(8,128)(2,1)}, u32[]{:S(2)}) copy-start(bf16[256,2048]{1,0:T(8,128)(2,1)} %param.25) | copy-start | bytes 3145732
  7.2 68.7 %all-gather.7.cloned.1.call-start = ((), (), s32[]{:S(2)}) async-start(), calls=%async_computation.3 | async-start | bytes 11796480 | tf_op jit(solution)/shard_map/all_gather | solution.py:292
  7.9 112.4 %all-gather.9.cloned.1.call-start = ((), (), s32[]{:S(2)}) async-start(), calls=%async_computation.4 | async-start | bytes 2359296 | tf_op jit(solution)/shard_map/all_gather | solution.py:357
  8.7 80.0 %copy-start.83 = (s32[2]{0:T(128)}, s32[2]{0:T(128)S(1)}, u32[]{:S(2)}) copy-start(s32[2]{0:T(128)S(1)} %dynamic_slice.9) | copy-start | bytes 28
  13.1 6.4 copy-start.59
  13.9 70.7 %copy-start.39 = (f32[256,256]{1,0:T(8,128)}, f32[256,256]{1,0:T(8,128)S(1)}, u32[]{:S(2)}) copy-start(f32[256,256]{1,0:T(8,128)S(1)} %copy.176) | copy-start | bytes 786436
  14.1 70.5 %copy-start.37 = (f32[256,256]{1,0:T(8,128)}, f32[256,256]{1,0:T(8,128)S(1)}, u32[]{:S(2)}) copy-start(f32[256,256]{1,0:T(8,128)S(1)} %copy.177) | copy-start | bytes 786436
  17.1 67.5 %copy-start.93 = (s32[256]{0:T(256)}, s32[256]{0:T(256)S(1)}, u32[]{:S(2)}) copy-start(s32[256]{0:T(256)S(1)} %get-tuple-element.93) | copy-start | bytes 3076
  21.0 54.9 %copy-start.101 = (f32[256]{0:T(256)S(1)}, f32[256]{0:T(256)}, u32[]{:S(2)}) copy-start(f32[256]{0:T(256)} %copy-done.100) | copy-start | bytes 3076
  86.0 85.9 %all-gather.11.cloned.1.call-start = ((), (), s32[]{:S(2)}) async-start(), calls=%async_computation.5 | async-start | bytes 9437184 | tf_op jit(solution)/shard_map/all_gather | solution.py:293
  86.7 208.0 %all-gather.15.cloned.1.call-start = ((), (), s32[]{:S(2)}) async-start(), calls=%async_computation.7 | async-start | bytes 25952256 | tf_op jit(solution)/shard_map/all_gather | solution.py:294
  87.3 423.1 %all-gather.13.cloned.1.call-start = ((), (), s32[]{:S(2)}) async-start(), calls=%async_computation.6 | async-start | bytes 51904512 | tf_op jit(solution)/shard_map/all_gather | solution.py:295
  87.9 707.7 %reduce-scatter.2.cloned.1.call-start = ((), (), s32[]{:S(2)}) async-start(), calls=%async_computation.8 | async-start | bytes 2211840 | tf_op jit(solution)/shard_map/reduce_scatter | solution.py:432
  97.8 15.4 %copy-start.22 = (bf16[256,2048]{1,0:T(8,128)(2,1)S(1)}, bf16[256,2048]{1,0:T(8,128)(2,1)}, u32[]{:S(2)}) copy-start(bf16[256,2048]{1,0:T(8,128)(2,1)} %param.26) | copy-start | bytes 3145732
  97.8 15.4 %copy-start.43 = (bf16[128,2048]{1,0:T(8,128)(2,1)S(1)}, bf16[128,2048]{1,0:T(8,128)(2,1)}, u32[]{:S(2)}) copy-start(bf16[128,2048]{1,0:T(8,128)(2,1)} %param.49) | copy-start | bytes 1572868
  97.8 15.4 %copy-start.87 = (s32[128]{0:T(128)S(1)}, s32[128]{0:T(128)}, u32[]{:S(2)}) copy-start(s32[128]{0:T(128)} %copy-done.86) | copy-start | bytes 1540
  106.1 11.6 %copy-start.84 = (pred[2048]{0:T(1024)(128)(4,1)}, pred[2048]{0:T(1024)(128)(4,1)S(1)}, u32[]{:S(2)}) copy-start(pred[2048]{0:T(1024)(128)(4,1)S(1)} %fusion.210) | copy-start | bytes 6148
  108.0 9.7 %copy-start.75 = (s32[2048]{0:T(1024)}, s32[2048]{0:T(1024)S(1)}, u32[]{:S(2)}) copy-start(s32[2048]{0:T(1024)S(1)} %fusion.207) | copy-start | bytes 24580
  108.0 9.6 %copy-start.77 = (s32[2048]{0:T(1024)}, s32[2048]{0:T(1024)S(1)}, u32[]{:S(2)}) copy-start(s32[2048]{0:T(1024)S(1)} %iota_and_fusion) | copy-start | bytes 24580
  138.0 15.1 %copy-start.2 = (bf16[4,2,2048,128]{3,2,1,0:T(8,128)(2,1)}, bf16[4,2,2048,128]{3,2,1,0:T(8,128)(2,1)S(1)}, u32[]{:S(2)}) copy-start(bf16[4,2,2048,128]{3,2,1,0:T(8,128)(2,1)S(1)} %pad_maximum_fusion.k_ref) | copy-start | bytes 12582916
  138.1 15.7 %copy-start.41 = (bf16[2048,128]{1,0:T(8,128)(2,1)S(1)}, bf16[2048,128]{1,0:T(8,128)(2,1)}, u32[]{:S(2)}) copy-start(bf16[2048,128]{1,0:T(8,128)(2,1)} %param.42) | copy-start | bytes 1572868
  138.1 15.7 %copy-start.88 = (s32[128]{0:T(128)S(1)}, s32[128]{0:T(128)}, u32[]{:S(2)}) copy-start(s32[128]{0:T(128)} %copy-done.86) | copy-start | bytes 1540
  171.9 5.9 copy-start.18
  171.9 5.9 copy-start.45
  171.9 5.9 copy-start.61
  179.6 6.0 copy-start.32
  537.5 9.4 %copy-start.29 = (bf16[128,5632]{1,0:T(8,128)(2,1)S(1)}, bf16[128,5632]{1,0:T(8,128)(2,1)}, u32[]{:S(2)}) copy-start(bf16[128,5632]{1,0:T(8,128)(2,1)} %param.45) | copy-start | bytes 4325380
  602.9 6.5 copy-start.42
  602.9 6.5 copy-start.58
  610.2 29.8 %copy-start.14 = (f32[256,2048]{1,0:T(8,128)S(1)}, f32[256,2048]{1,0:T(8,128)}, u32[]{:S(2)}) copy-start(f32[256,2048]{1,0:T(8,128)} %copy.175) | copy-start | bytes 6291460
  685.1 22.7 %copy-start.8 = (f32[256,2048]{1,0:T(8,128)S(1)}, f32[256,2048]{1,0:T(8,128)}, u32[]{:S(2)}) copy-start(f32[256,2048]{1,0:T(8,128)} %copy-done.6) | copy-start | bytes 6291460
  685.1 53.4 %all-to-all-start = ((bf16[8,256,512]{1,2,0:T(8,128)(2,1)}), bf16[8,256,512]{1,2,0:T(8,128)(2,1)}, u32[]{:S(2)}, u32[]{:S(2)}) async-start(bf16[8,256,512]{1,2,0:T(8,128)(2,1)} %copy.190), calls=%async_computation | async-start | bytes 4194304 | tf_op jit(solution)/shard_map/all_to_all | solution.py:248
  707.9 11.7 %copy-start.44 = (bf16[128,2048]{1,0:T(8,128)(2,1)S(1)}, bf16[128,2048]{1,0:T(8,128)(2,1)}, u32[]{:S(2)}) copy-start(bf16[128,2048]{1,0:T(8,128)(2,1)} %param.49) | copy-start | bytes 1572868
  707.9 11.8 %copy-start.57 = (bf16[256,128]{1,0:T(8,128)(2,1)S(1)}, bf16[256,128]{1,0:T(8,128)(2,1)}, u32[]{:S(2)}) copy-start(bf16[256,128]{1,0:T(8,128)(2,1)} %fusion.51) | copy-start | bytes 196612
  721.0 19.6 %copy-start.38 = (f32[256,256]{1,0:T(8,128)S(1)}, f32[256,256]{1,0:T(8,128)}, u32[]{:S(2)}) copy-start(f32[256,256]{1,0:T(8,128)} %copy-done.37) | copy-start | bytes 786436
  740.9 9.4 %copy-start.19 = (bf16[256,2048]{1,0:T(8,128)(2,1)S(1)}, bf16[256,2048]{1,0:T(8,128)(2,1)}, u32[]{:S(2)}) copy-start(bf16[256,2048]{1,0:T(8,128)(2,1)} %param.25) | copy-start | bytes 3145732
  741.6 8.7 %copy-start.97 = (f32[2048]{0:T(1024)S(1)}, f32[2048]{0:T(1024)}, u32[]{:S(2)}) copy-start(f32[2048]{0:T(1024)} %param.30) | copy-start | bytes 24580
  741.6 8.7 %copy-start.102 = (f32[256]{0:T(256)S(1)}, f32[256]{0:T(256)}, u32[]{:S(2)}) copy-start(f32[256]{0:T(256)} %copy-done.100) | copy-start | bytes 3076
  742.5 7.8 copy-start.69
  743.7 6.6 copy-start.68
  751.6 12.0 %copy-start.26 = (bf16[256,2048]{1,0:T(8,128)(2,1)S(1)}, bf16[256,2048]{1,0:T(8,128)(2,1)}, u32[]{:S(2)}) copy-start(bf16[256,2048]{1,0:T(8,128)(2,1)} %copy-done.25) | copy-start | bytes 3145732
  759.2 14.9 %all-to-all-start.1 = ((bf16[8,288,128]{2,1,0:T(8,128)(2,1)}), bf16[8,288,128]{2,1,0:T(8,128)(2,1)}, u32[]{:S(2)}, u32[]{:S(2)}) async-start(bf16[8,288,128]{2,1,0:T(8,128)(2,1)} %pad_maximum_fusion.3), calls=%async_computation.1 | async-start | bytes 1179648 | tf_op jit(solution)/shard_map/all_to_all | solution.py:248
  763.6 5.8 copy-start.36
  763.6 5.8 copy-start.56
  763.7 5.8 copy-start.98
  775.2 15.1 %copy-start.74 = (s32[128]{0:T(128)S(1)}, s32[128]{0:T(128)}, u32[]{:S(2)}) copy-start(s32[128]{0:T(128)} %fusion.215) | copy-start | bytes 1540
  822.8 6.3 copy-start.53
  (66 other events, 156.0 us)
Sparse Core Ops, SparseCore 0:
  9.9 65.9 all-gather.6
  86.1 27.8 all-gather.8
  115.9 55.9 all-gather.10
  173.6 121.0 all-gather.14
  296.5 213.8 all-gather.12
  666.7 69.3 reduce-scatter.1

commit v2 on v1

--- a/solution.py
+++ b/solution.py
@@ -249,6 +249,202 @@
     return jnp.sum(received.astype(F32), axis=0)
 
 
+CORE, ACROSS_X, ACROSS_Y = 1, 2, 4
+
+
+def flip(array, mask):
+    members = lax.axis_size("grp")
+    return lax.ppermute(array, "grp", [(i, i ^ mask) for i in range(members)])
+
+
+def flip_group(array):
+    groups = lax.axis_size("rep")
+    return lax.ppermute(array, "rep", [(i, i ^ 1) for i in range(groups)])
+
+
+def gather_same_core(weight):
+    rows = weight.shape[0] // 2
+    parity = lax.axis_index("rep") % 2
+    mine = lax.dynamic_slice_in_dim(weight, parity * rows, rows, 0)
+    over_x, over_y = yield flip(mine, ACROSS_X), flip(mine, ACROSS_Y)
+    both_low = flip(over_x[: rows // 2], ACROSS_Y)
+    both_high = flip(over_y[rows // 2 :], ACROSS_X)
+    other_x, both_low, both_high, over_y = yield flip_group(over_x), both_low, both_high, over_y
+    other_y, *_ = yield (flip_group(over_y),)
+    other_both = (flip_group(both_low), flip_group(both_high))
+    return (
+        ((over_x,), (other_x,)),
+        ((over_y,), (other_y,)),
+        ((both_low, both_high), other_both),
+    )
+
+
+def tie(value, transfers):
+    value, *transfers = lax.optimization_barrier((value, *transfers))
+    return value, tuple(transfers)
+
+
+def times_pieces(mine, other, pieces):
+    total = None
+    for value, part in zip((mine, other), pieces):
+        start = 0
+        for piece in part:
+            term = mm(value[:, start : start + piece.shape[0]], piece)
+            total = term if total is None else total + term
+            start += piece.shape[0]
+    return total
+
+
+def times_pieces_flipped(value, pieces):
+    return [
+        jnp.concatenate([mm_nt(value, piece) for piece in part], axis=1) for part in pieces
+    ]
+
+
+def feed_forward_alone(norm2, sens, gate_up_full, down_full, pieces, masks_of, compact_with):
+    ffn_in, switch_right_pieces, lift_right_pieces, down_in, lower_right_pieces = pieces
+    narrow = down_in.shape[1]
+    hidden_width = down_full.shape[0]
+    visible, seen = masks_of(lax.axis_index("grp"))
+    mask_two = jnp.concatenate([visible, visible], axis=1)
+    latent_gu = (mm(norm2, ffn_in) * mask_two).astype(BF16)
+    latent_g, latent_u = latent_gu[:, :narrow], latent_gu[:, narrow:]
+    gate_up = mm(norm2, gate_up_full) + LOWRANK_FACTOR * jnp.concatenate(
+        [mm(latent_g, switch_right_pieces), mm(latent_u, lift_right_pieces)], axis=1
+    )
+    gate = gate_up[:, :hidden_width]
+    up = gate_up[:, hidden_width:]
+    sigma = jax.nn.sigmoid(gate)
+    act = (gate * sigma * up).astype(BF16)
+    latent_d = (mm(act, down_in) * visible).astype(BF16)
+    response_part = mm(act, down_full) + LOWRANK_FACTOR * mm(latent_d, lower_right_pieces)
+    dlat_d = (LOWRANK_FACTOR * mm_nt(sens, lower_right_pieces) * visible).astype(BF16)
+    dact = mm_nt(sens, down_full) + mm_nt(dlat_d, down_in)
+    dgate = (dact * up * (sigma * (1.0 + gate * (1.0 - sigma)))).astype(BF16)
+    dup = (dact * gate * sigma).astype(BF16)
+    dlat_gu = (
+        LOWRANK_FACTOR
+        * jnp.concatenate(
+            [mm_nt(dgate, switch_right_pieces), mm_nt(dup, lift_right_pieces)], axis=1
+        )
+        * mask_two
+    ).astype(BF16)
+    dnorm2 = (
+        mm_nt(dgate, gate_up_full[:, :hidden_width])
+        + mm_nt(dup, gate_up_full[:, hidden_width:])
+        + mm_nt(dlat_gu, ffn_in)
+    )
+    deep = jnp.concatenate(
+        [
+            mm_tn(act, compact_with(dlat_d, seen)),
+            LOWRANK_FACTOR * mm_tn(dgate, compact_with(latent_g, seen)),
+            LOWRANK_FACTOR * mm_tn(dup, compact_with(latent_u, seen)),
+        ],
+        axis=1,
+    ).astype(BF16)
+    return response_part, dnorm2, latent_d, dlat_gu, deep
+
+
+def feed_forward_paired(
+    norm2, sens, sens_near, own_weight, far, down_full, pieces, masks_of, compact_with
+):
+    ffn_in, switch_right_pieces, lift_right_pieces, down_in, lower_right_pieces = pieces
+    count, width = norm2.shape
+    narrow = down_in.shape[1]
+    hidden_width = down_full.shape[0]
+    block = own_weight.shape[1]
+    member = lax.axis_index("grp")
+    parity = lax.axis_index("rep") % 2
+    owns_gate = member < ACROSS_Y
+    over_x, over_y, over_both = far
+
+    both = jnp.concatenate([norm2, flip(norm2, CORE)], axis=0)
+    sens_both = jnp.concatenate([sens, sens_near], axis=0)
+    visible, seen = (
+        jnp.concatenate(pair, axis=0) for pair in zip(masks_of(member), masks_of(member ^ CORE))
+    )
+    mask_two = jnp.concatenate([visible, visible], axis=1)
+    latent_gu = (mm(both, ffn_in) * mask_two).astype(BF16)
+    dlat_d = (LOWRANK_FACTOR * mm_nt(sens_both, lower_right_pieces) * visible).astype(BF16)
+    half = width // 2
+    mine = lax.dynamic_slice_in_dim(both, parity * half, half, 1)
+    other = lax.dynamic_slice_in_dim(both, (1 - parity) * half, half, 1)
+
+    def order(first, second):
+        return jnp.where(owns_gate, first, second), jnp.where(owns_gate, second, first)
+
+    latent_one, latent_two = order(latent_gu[:, :narrow], latent_gu[:, narrow:])
+    seen_d = compact_with(dlat_d, seen)
+    seen_one, seen_two = compact_with(latent_one, seen), compact_with(latent_two, seen)
+
+    response_part, latent_d, dlat_one, dlat_two, deep = 0.0, 0.0, 0.0, 0.0, None
+    dnorm_mine, dnorm_other = 0.0, 0.0
+    for index in range(2):
+        hidden = (member % ACROSS_Y) ^ (0 if index == 0 else ACROSS_X)
+        start = hidden * block
+        switch_block = lax.dynamic_slice_in_dim(switch_right_pieces, start, block, 1)
+        lift_block = lax.dynamic_slice_in_dim(lift_right_pieces, start, block, 1)
+        in_block = lax.dynamic_slice_in_dim(down_in, start, block, 0)
+        down_block = lax.dynamic_slice_in_dim(down_full, start, block, 0)
+        piece_one, piece_two = order(switch_block, lift_block)
+        if index == 0:
+            first = mm(both, own_weight)
+            second = times_pieces(mine, other, over_y)
+        else:
+            first = times_pieces(mine, other, over_x)
+            second = times_pieces(mine, other, over_both)
+        first = first + LOWRANK_FACTOR * mm(latent_one, piece_one)
+        second = second + LOWRANK_FACTOR * mm(latent_two, piece_two)
+        gate, up = order(first, second)
+        sigma = jax.nn.sigmoid(gate)
+        act = (gate * sigma * up).astype(BF16)
+        dact = mm_nt(sens_both, down_block) + mm_nt(dlat_d, in_block)
+        dgate = (dact * up * (sigma * (1.0 + gate * (1.0 - sigma)))).astype(BF16)
+        dup = (dact * gate * sigma).astype(BF16)
+        dfirst, dsecond = order(dgate, dup)
+        latent_d = latent_d + mm(act, in_block)
+        response_part = response_part + mm(act, down_block)
+        dlat_one = dlat_one + mm_nt(dfirst, piece_one)
+        dlat_two = dlat_two + mm_nt(dsecond, piece_two)
+        if index == 0:
+            dnorm_own = mm_nt(dfirst, own_weight)
+            terms = [times_pieces_flipped(dsecond, over_y)]
+        else:
+            terms = [
+                times_pieces_flipped(dfirst, over_x),
+                times_pieces_flipped(dsecond, over_both),
+            ]
+        for mine_part, other_part in terms:
+            dnorm_mine = dnorm_mine + mine_part
+            dnorm_other = dnorm_other + other_part
+        grad_one = LOWRANK_FACTOR * mm_tn(dfirst, seen_one)
+        grad_two = LOWRANK_FACTOR * mm_tn(dsecond, seen_two)
+        rows = jnp.concatenate([mm_tn(act, seen_d), *order(grad_one, grad_two)], axis=1)
+        if deep is None:
+            deep = jnp.zeros((hidden_width, rows.shape[1]), BF16)
+        deep = lax.dynamic_update_slice_in_dim(deep, rows.astype(BF16), start, 0)
+
+    low, high = jnp.where(parity == 0, dnorm_mine, dnorm_other), jnp.where(
+        parity == 0, dnorm_other, dnorm_mine
+    )
+    dnorm2 = dnorm_own + jnp.concatenate([low, high], axis=1)
+    dlat_g, dlat_u = order(dlat_one, dlat_two)
+
+    def meet(*parts):
+        joined = jnp.concatenate(parts, axis=1)
+        near = flip(joined[count:].astype(BF16), CORE)
+        return joined[:count] + near.astype(F32)
+
+    backward = meet(dnorm2, dlat_g, dlat_u)
+    own_mask = mask_two[:count]
+    dlat_gu = (LOWRANK_FACTOR * backward[:, width:] * own_mask).astype(BF16)
+    dnorm2 = backward[:, :width] + mm_nt(dlat_gu, ffn_in)
+    forward = meet(response_part, latent_d)
+    latent_d = (forward[:, width:] * visible[:count]).astype(BF16)
+    response_part = forward[:, :width] + LOWRANK_FACTOR * mm(latent_d, lower_right_pieces)
+    return response_part, dnorm2, latent_d, dlat_gu, deep
+
+
 def shards(
     tokens,
     response_sensitivity,
@@ -292,7 +488,13 @@
     qkv_full = lax.all_gather(qkv_weight, "grp", axis=1, tiled=True)
     out_full = lax.all_gather(out_weight, "grp", axis=1, tiled=True)
     down_full = lax.all_gather(down_weight, "grp", axis=1, tiled=True)
-    gate_up_full = lax.all_gather(gate_up_weight, "grp", axis=1, tiled=True)
+    paired = members == 8 and groups % 2 == 0
+    if paired:
+        steps = gather_same_core(gate_up_weight)
+        qkv_full, transfers = tie(qkv_full, next(steps))
+        sens_near = flip(response_sensitivity, CORE)
+    else:
+        gate_up_full = lax.all_gather(gate_up_weight, "grp", axis=1, tiled=True)
 
     key_index = jnp.arange(key_count, dtype=jnp.int32)
     key_second = (key_index >= lengths[0]).astype(jnp.int32)
@@ -301,7 +503,6 @@
     own_second = (own_index >= lengths[0]).astype(jnp.int32)
     position = own_index - own_second * lengths[0]
     prefix = jnp.where(own_second == 0, prefixes[0], prefixes[1])
-    chosen = jnp.where(own_second == 0, chosen_ids[0], chosen_ids[1])
     allowed = (key_second[:, None] == own_second[None, :]) & (
         (key_position[:, None] <= position[None, :]) | (key_position[:, None] < prefix[None, :])
     )
@@ -311,17 +512,25 @@
     span = jnp.stack([first_key // KEY_BLOCK, last_key // KEY_BLOCK + 1]).astype(jnp.int32)
 
     columns = jnp.arange(narrow, dtype=jnp.int32)
-    visible = (chosen[:, None] == columns[None, :] // RANK).astype(F32)
-    mask_two = jnp.concatenate([visible, visible], axis=1)
-    mask_three = jnp.concatenate([visible, visible, visible], axis=1)
     slots = 2 * RANK
     slot = jnp.arange(slots, dtype=jnp.int32)
     slot_column = chosen_ids[slot // RANK] * RANK + slot % RANK
     pick = (columns[:, None] == slot_column[None, :]).astype(BF16)
-    slot_visible = (own_second[:, None] == slot[None, :] // RANK).astype(F32)
+
+    def masks_of(device):
+        second = (device * count + jnp.arange(count, dtype=jnp.int32) >= lengths[0]).astype(jnp.int32)
+        chosen = jnp.where(second == 0, chosen_ids[0], chosen_ids[1])
+        visible = (chosen[:, None] == columns[None, :] // RANK).astype(F32)
+        return visible, (second[:, None] == slot[None, :] // RANK).astype(F32)
+
+    visible, slot_visible = masks_of(member)
+    mask_three = jnp.concatenate([visible, visible, visible], axis=1)
+
+    def compact_with(latent, seen):
+        return (mm(latent, pick) * seen).astype(BF16)
 
     def compact(latent):
-        return (mm(latent, pick) * slot_visible).astype(BF16)
+        return compact_with(latent, slot_visible)
 
     incoming = tokens.astype(F32)
     scale_one = inverse_rms(incoming)
@@ -359,7 +568,16 @@
     )
     key_pairs = side_pairs(key_value[:, :kv_width])
     value_pairs = side_pairs(key_value[:, kv_width:])
+    if paired:
+        key_pairs, transfers = tie(key_pairs, steps.send(transfers))
     attended_low, lse = attention_forward(span, query, key_pairs, value_pairs, bias)
+
+    if paired:
+        attended_low, transfers = tie(attended_low, steps.send(transfers))
+        try:
+            steps.send(transfers)
+        except StopIteration as stop:
+            far = stop.value
 
     latent_o = (mm(attended_low, output_in) * visible).astype(BF16)
     stream = incoming + (
@@ -367,38 +585,18 @@
     )
     scale_two = inverse_rms(stream)
     norm2 = (stream * scale_two * mlp_gain).astype(BF16)
+    sens = response_sensitivity
     ffn_in = jnp.concatenate([gate_in, up_in], axis=1)
-    latent_gu = (mm(norm2, ffn_in) * mask_two).astype(BF16)
-    latent_g, latent_u = latent_gu[:, :narrow], latent_gu[:, narrow:]
-    gate_up = mm(norm2, gate_up_full) + LOWRANK_FACTOR * jnp.concatenate(
-        [mm(latent_g, switch_right_pieces), mm(latent_u, lift_right_pieces)], axis=1
-    )
-    gate = gate_up[:, :hidden_width]
-    up = gate_up[:, hidden_width:]
-    sigma = jax.nn.sigmoid(gate)
-    act = (gate * sigma * up).astype(BF16)
-    latent_d = (mm(act, down_in) * visible).astype(BF16)
-    level_response = (
-        stream + mm(act, down_full) + LOWRANK_FACTOR * mm(latent_d, lower_right_pieces)
-    ).astype(BF16)
-
-    sens = response_sensitivity
-    dlat_d = (LOWRANK_FACTOR * mm_nt(sens, lower_right_pieces) * visible).astype(BF16)
-    dact = mm_nt(sens, down_full) + mm_nt(dlat_d, down_in)
-    dgate = (dact * up * (sigma * (1.0 + gate * (1.0 - sigma)))).astype(BF16)
-    dup = (dact * gate * sigma).astype(BF16)
-    dlat_gu = (
-        LOWRANK_FACTOR
-        * jnp.concatenate(
-            [mm_nt(dgate, switch_right_pieces), mm_nt(dup, lift_right_pieces)], axis=1
+    pieces = (ffn_in, switch_right_pieces, lift_right_pieces, down_in, lower_right_pieces)
+    if paired:
+        response_part, dnorm2, latent_d, dlat_gu, deep = feed_forward_paired(
+            norm2, sens, sens_near, gate_up_weight, far, down_full, pieces, masks_of, compact_with
         )
-        * mask_two
-    ).astype(BF16)
-    dnorm2 = (
-        mm_nt(dgate, gate_up_full[:, :hidden_width])
-        + mm_nt(dup, gate_up_full[:, hidden_width:])
-        + mm_nt(dlat_gu, ffn_in)
-    )
+    else:
+        response_part, dnorm2, latent_d, dlat_gu, deep = feed_forward_alone(
+            norm2, sens, gate_up_full, down_full, pieces, masks_of, compact_with
+        )
+    level_response = (stream + response_part).astype(BF16)
     dhidden = sens.astype(F32) + norm_backward(stream, scale_two, mlp_gain, dnorm2)
     dbranch = dhidden.astype(BF16)
     dlat_o = (LOWRANK_FACTOR * mm_nt(dbranch, final_right_pieces) * visible).astype(BF16)
@@ -416,14 +614,6 @@
         axis=1,
     ).astype(BF16)
     final_part = (LOWRANK_FACTOR * mm_tn(dbranch, compact(latent_o))).astype(BF16)
-    deep = jnp.concatenate(
-        [
-            mm_tn(act, compact(dlat_d)),
-            LOWRANK_FACTOR * mm_tn(dgate, compact(latent_g)),
-            LOWRANK_FACTOR * mm_tn(dup, compact(latent_u)),
-        ],
-        axis=1,
-    ).astype(BF16)
     wide_rows, deep_rows = width // members, hidden_width // members
     final_blocks = jnp.pad(blocks(final_part), ((0, 0), (0, deep_rows - wide_rows), (0, 0)))
     early = jnp.concatenate(

time: 847 us -> 727 us (0.86)
  waiting for transfers between devices: 400 us -> 210 us
  local copies, waits for them, and re-layouts: 82.1 us -> 108 us
  other arithmetic: 49.4 us -> 70.5 us
  starting transfers between devices: 25.7 us -> 37.8 us
  matrix products: 185 us -> 194 us
    all_gather x1 -> x0, waiting for transfers between devices: 203 us -> none  [shards(): gate_up_full = lax.all_gather(gate_up_weight, 'grp', axis=1, tiled=True)]
    ppermute x0 -> x12, waiting for transfers between devices: none -> 190 us  [the longest x8 110 us: flip(): return lax.ppermute(array, 'grp', [(i, i ^ mask) for i in range(members)])]
    all_gather x1, waiting for transfers between devices: 106 us -> 0.01 us  [shards(): down_full = lax.all_gather(down_weight, 'grp', axis=1, tiled=True)]
    all_gather x1, waiting for transfers between devices: 52.7 us -> 0.01 us  [shards(): qkv_full = lax.all_gather(qkv_weight, 'grp', axis=1, tiled=True)]
    all_gather x1, waiting for transfers between devices: 17 us -> 0.01 us  [shards(): out_full = lax.all_gather(out_weight, 'grp', axis=1, tiled=True)]
    dot_general x16 -> x27, matrix products: 71.5 us -> 86.3 us  [mm_nt(): lax.dot_general(left, right, (((1,), (1,)), ((), ())), preferred_element_...]
    ppermute x0 -> x12, starting transfers between devices: none -> 11.8 us  [the longest x8 6.68 us: flip(): return lax.ppermute(array, 'grp', [(i, i ^ mask) for i in range(members)])]
    dot_general x11 -> x14, matrix products: 25.4 us -> 16.2 us  [mm_tn(): lax.dot_general(left, right, (((0,), (0,)), ((), ())), preferred_element_...]
  transfers between devices with their start and end apart: 8 -> 19, of which waited for: 6 -> 10; matrix products, arithmetic and copies ran while one was open for 19% -> 34% of each run, Pallas kernels for 2% -> 6%
where the time goes in v2:
time: 727 us; the launch traced here: 720 us
  waiting for transfers between devices  210 us (29%)
  matrix products  194 us (27%)
  local copies, waits for them, and re-layouts  108 us (15%)
  other arithmetic  70.5 us (10%)
  Pallas kernels  45.1 us (6%)
  starting transfers between devices  37.8 us (5%)
  blocking collectives  35 us (5%)
  between operations  19.2 us (3%)
    ppermute x8, waiting for transfers between devices, flip(): return lax.ppermute(array, 'grp', [(i, i ^ mask) for i in range(members)])  110 us
    dot_general x27, matrix products, mm_nt(): lax.dot_general(left, right, (((1,), (1,)), ((), ())), preferred_element_...  86.3 us
    dot_general x42, matrix products, mm(): return jnp.dot(left, right, preferred_element_type=F32)  84.3 us
    ppermute x4, waiting for transfers between devices, flip_group(): return lax.ppermute(array, 'rep', [(i, i ^ 1) for i in range(groups)])  80.1 us
    pallas_call x1, Pallas kernels, attention_backward(): pl.pallas_call(attention_backward_kernel, out_shape=(jax.ShapeDtypeStruct...  30.1 us
    unnamed x295, local copies, waits for them, and re-layouts  29.5 us
    all_to_all x2, starting transfers between devices, exchange_sum(): received = lax.all_to_all(parts.astype(BF16), 'grp', 0, 0, tiled=True)  25.3 us
    all_gather x1, blocking collectives, shards(): early_all = lax.all_gather(early_sum, 'rep', axis=0)  20.8 us
  transfers between devices with their start and end apart: 19, of which 10 were waited for; matrix products, arithmetic and copies ran while one was open for 34% of the time, Pallas kernels for 6%

profile of v2, /device:TPU:0, one launch (start us, length us, event | category | flops | bytes accessed | tf_op | source)
XLA Modules:
  0.0 719.8 jit_solution(8917750417867196596)
XLA Ops:
  8.0 3.6 constant_dynamic-slice_fusion
  21.3 3.3 compare_select_fusion.10
  31.0 88.5 %collective-permute-done = bf16[1024,1408]{1,0:T(8,128)(2,1)} collective-permute-done((bf16[1024,1408]{1,0:T(8,128)(2,1)}, bf16[1024,1408]{1,0:T(8,128)(2,1)}, u32[]{:S(2)}, u32[]{:S(2)}) %collective-permute-start) | collective-permute-done | bytes 2883616 | tf_op jit(solution)/shard_map/ppermute | solution.py:257
  121.0 7.6 %convolution_add_fusion = f32[256,2560]{1,0:T(8,128)S(1)} fusion(bf16[2048,2560]{0,1:T(8,128)(2,1)} %all-gather.6.cloned.1.call-done, f32[256,256]{1,0:T(8,128)S(1)} %fusion.143, f32[256,256]{1,0:T(8,128)} %fusion.147, f32[256,2048]{1,0:T(8,128)} %fusion.151, bf16[256,2048]{1,0:T(8,128)(2,1)S(1)} %copy-done.36, f32[2048]{0:T(1024)} %param.30, ...), kind=kOutput, calls=%fused_computation.27 | convolution fusion | flops 2689073152 | bytes 16786432 | tf_op jit(solution)/shard_map/dot_general | solution.py:25
  148.0 3.7 and_select_fusion.bias_ref
  161.5 3.0 copy.198
  171.1 3.5 fusion.273
  177.8 3.3 pad_bitcast_fusion.3
  183.4 16.6 %collective-permute-done.3 = bf16[512,1408]{1,0:T(8,128)(2,1)} collective-permute-done((bf16[512,1408]{1,0:T(8,128)(2,1)}, bf16[512,1408]{1,0:T(8,128)(2,1)}, u32[]{:S(2)}, u32[]{:S(2)}) %collective-permute-start.3) | collective-permute-done | bytes 1441824 | tf_op jit(solution)/shard_map/ppermute | solution.py:257
  200.1 3.3 collective-permute-done.4
  206.1 5.4 fusion.240
  222.2 3.3 pad_bitcast_fusion.1
  228.4 15.0 %attention_forward.1 = (bf16[256,2048]{1,0:T(8,128)(2,1)S(1)}, f32[16,2,256]{2,1,0:T(2,128)S(1)}) custom-call(s32[2]{0:T(128)S(1)} %pad_add_fusion.1.span, bf16[256,2048]{1,0:T(8,128)(2,1)S(1)} %fusion.87.q_ref, bf16[4,2,2048,128]{3,2,1,0:T(8,128)(2,1)S(1)} %copy-done.1, bf16[4,2,2048,128]{3,2,1,0:T(8,128)(2,1)S(1)} %pad_maximum_fusion.2.v_ref, ...), custom_call_target="tpu_custom_call" | custom-call | flops 4294967296 | bytes 18874368 | tf_op jit(solution)/shard_map/attention_forward/pallas_call | solution.py:108
  244.1 24.9 %collective-permute-done.5 = bf16[1024,1408]{1,0:T(8,128)(2,1)} collective-permute-done((bf16[1024,1408]{1,0:T(8,128)(2,1)}, bf16[1024,1408]{1,0:T(8,128)(2,1)}, u32[]{:S(2)}, u32[]{:S(2)}) %collective-permute-start.5) | collective-permute-done | bytes 2883616 | tf_op jit(solution)/shard_map/ppermute | solution.py:262
  271.9 6.6 multiply_reduce_fusion.1
  296.7 25.5 %collective-permute-done.7 = bf16[512,1408]{1,0:T(8,128)(2,1)S(1)} collective-permute-done((bf16[512,1408]{1,0:T(8,128)(2,1)}, bf16[512,1408]{1,0:T(8,128)(2,1)S(1)}, u32[]{:S(2)}, u32[]{:S(2)}) %collective-permute-start.7) | collective-permute-done | bytes 1441824 | tf_op jit(solution)/shard_map/ppermute | solution.py:262
  323.5 28.5 %collective-permute-done.8 = bf16[512,1408]{1,0:T(8,128)(2,1)S(1)} collective-permute-done((bf16[512,1408]{1,0:T(8,128)(2,1)}, bf16[512,1408]{1,0:T(8,128)(2,1)S(1)}, u32[]{:S(2)}, u32[]{:S(2)}) %collective-permute-start.8) | collective-permute-done | bytes 1441824 | tf_op jit(solution)/shard_map/ppermute | solution.py:262
  353.0 3.6 fusion.281
  356.6 3.6 fusion.280
  360.2 5.5 fusion.19
  365.7 5.4 fusion.20
  371.1 4.2 fusion.21
  375.4 5.0 convolution_add_fusion.4
  380.4 10.4 %broadcast_select_fusion.1 = (bf16[512,1408]{1,0:T(8,128)(2,1)S(1)}, bf16[512,1408]{1,0:T(8,128)(2,1)S(1)}, bf16[512,1408]{1,0:T(8,128)(2,1)S(1)}, f32[512,1408]{1,0:T(8,128)S(1)}) fusion(pred[]{:T(512)S(6)} %lt.129, f32[512,1408]{1,0:T(8,128)} %fusion.21, f32[512,1408]{1,0:T(8,128)} %fusion.19, f32[512,1408]{1,0:T(8,128)} %fusion.97, ...), kind=kOutput, calls=%fused_computation.127 | convolution fusion | flops 2965045248 | bytes 23724036 | tf_op jit(solution)/shard_map/dot_general | solution.py:29
  393.3 3.3 fusion.284
  396.6 5.4 fusion.285
  402.0 5.1 fusion.282
  407.2 10.4 %broadcast_select_fusion.3 = (bf16[512,1408]{1,0:T(8,128)(2,1)S(1)}, bf16[512,1408]{1,0:T(8,128)(2,1)}, bf16[512,1408]{1,0:T(8,128)(2,1)}, f32[512,1408]{1,0:T(8,128)}) fusion(pred[]{:T(512)S(6)} %lt.129, f32[512,1408]{1,0:T(8,128)S(1)} %copy-done.26, f32[512,1408]{1,0:T(8,128)S(1)} %copy-done.41, f32[512,1408]{1,0:T(8,128)S(1)} %copy-done.40, ...), kind=kOutput, calls=%fused_computation.129 | convolution fusion | flops 2965045248 | bytes 23724036 | tf_op jit(solution)/shard_map/dot_general | solution.py:29
  424.7 3.8 maximum_add_fusion.2
  428.5 5.8 broadcast_select_fusion.9
  434.3 7.2 maximum_add_fusion
  451.0 5.6 fusion.2
  456.6 5.6 fusion.22
  471.6 3.7 fusion.31
  478.9 3.9 fusion.47
  496.0 4.2 fusion.34
  500.3 4.2 copy.243
  504.6 5.8 fusion.254
  512.0 30.1 %attention_backward.1 = (f32[256,2048]{1,0:T(8,128)S(1)}, f32[4,2048,128]{2,1,0:T(8,128)}, f32[4,2048,128]{2,1,0:T(8,128)}) custom-call(s32[2]{0:T(128)S(1)} %pad_add_fusion.1.span, bf16[256,2048]{1,0:T(8,128)(2,1)S(1)} %copy-done.7, bf16[256,2048]{1,0:T(8,128)(2,1)S(1)} %fusion.26.do_ref, bf16[256,2048]{1,0:T(8,128)(2,1)S(1)} %copy-done.4, ...), custom_call_target="tpu_custom_call" | custom-call | flops 10737418240 | bytes 30408704 | tf_op jit(solution)/shard_map/attention_backward/pallas_call | solution.py:200
  552.8 6.0 fusion.44
  565.0 21.1 %all-to-all-start = ((bf16[8,256,512]{1,2,0:T(8,128)(2,1)}), bf16[8,256,512]{1,2,0:T(8,128)(2,1)}, u32[]{:S(2)}, u32[]{:S(2)}) async-start(bf16[8,256,512]{1,2,0:T(8,128)(2,1)} %copy.222), calls=%async_computation | async-start | bytes 4194304 | tf_op jit(solution)/shard_map/all_to_all | solution.py:248
  587.2 3.1 fusion.272
  596.3 16.7 %all-to-all-done = bf16[8,256,512]{1,2,0:T(8,128)(2,1)} async-done(((bf16[8,256,512]{1,2,0:T(8,128)(2,1)}), bf16[8,256,512]{1,2,0:T(8,128)(2,1)}, u32[]{:S(2)}, u32[]{:S(2)}) %all-to-all-start) | async-done | bytes 2097184 | tf_op jit(solution)/shard_map/all_to_all | solution.py:248
  626.5 3.6 fusion.291
  638.9 4.2 all-to-all-start.1
  643.1 7.9 %fusion.42 = (f32[256]{0:T(256)S(1)}, f32[256,2048]{1,0:T(8,128)S(1)}) fusion(bf16[256,2048]{1,0:T(8,128)(2,1)S(1)} %copy-done.38, f32[256,2048]{1,0:T(8,128)} %fusion.291, bf16[2048,2560]{0,1:T(8,128)(2,1)} %all-gather.6.cloned.1.call-done, bf16[256,256]{1,0:T(8,128)(2,1)} %copy-done.84, bf16[256,256]{1,0:T(8,128)(2,1)} %copy-done.85, ...), kind=kOutput, calls=%fused_computation.95 | convolution fusion | flops 2690907904 | bytes 17048576 | tf_op jit(solution)/shard_map/dot_general | solution.py:29
  654.7 14.1 %all-gather = bf16[1152,128]{1,0:T(8,128)(2,1)S(1)} all-gather(bf16[288,128]{1,0:T(8,128)(2,1)S(1)} %reduce_sum.62), channel_id=2, replica_groups=mesh['rep'=4,'grp'=8] {'rep'}, dimensions={0}, use_global_device_ids=true | all-gather | bytes 368640 | tf_op jit(solution)/shard_map/all_gather | solution.py:671
  675.2 20.8 %all_gather.27 = bf16[4,960,128]{2,1,0:T(8,128)(2,1)S(1)} all-gather(bf16[1,960,128]{2,1,0:T(8,128)(2,1)} %reduce-scatter.2.cloned.1.call-done), channel_id=1, replica_groups=mesh['rep'=4,'grp'=8] {'rep'}, dimensions={0}, use_global_device_ids=true | all-gather | bytes 1228800 | tf_op jit(solution)/shard_map/all_gather | solution.py:624
  (514 shorter events, 215.7 us)
Async XLA Ops:
  7.2 276.2 %copy-start = (bf16[5632,128]{1,0:T(8,128)(2,1)S(1)}, bf16[5632,128]{1,0:T(8,128)(2,1)}, u32[]{:S(2)}) copy-start(bf16[5632,128]{1,0:T(8,128)(2,1)} %param.48) | copy-start | bytes 4325380
  7.2 113.8 %all-gather.6.cloned.1.call-start = ((), (), s32[]{:S(2)}) async-start(), calls=%async_computation.3 | async-start | bytes 11796480 | tf_op jit(solution)/shard_map/all_gather | solution.py:488
  7.9 163.1 %all-gather.8.cloned.1.call-start = ((), (), s32[]{:S(2)}) async-start(), calls=%async_computation.4 | async-start | bytes 2359296 | tf_op jit(solution)/shard_map/all_gather | solution.py:566
  8.0 8.1 %copy-start.131 = (s32[8]{0:T(128)S(1)}, s32[8]{0:T(128)}, u32[]{:S(2)}) copy-start(s32[8]{0:T(128)} %param.27) | copy-start | bytes 100
  8.0 10.3 %copy-start.104 = (s32[8]{0:T(128)S(1)}, s32[8]{0:T(128)}, u32[]{:S(2)}) copy-start(s32[8]{0:T(128)} %param.29) | copy-start | bytes 100
  8.0 10.3 %copy-start.132 = (s32[8]{0:T(128)S(1)}, s32[8]{0:T(128)}, u32[]{:S(2)}) copy-start(s32[8]{0:T(128)} %param.28) | copy-start | bytes 100
  11.6 12.9 %copy-start.36 = (bf16[256,2048]{1,0:T(8,128)(2,1)S(1)}, bf16[256,2048]{1,0:T(8,128)(2,1)}, u32[]{:S(2)}) copy-start(bf16[256,2048]{1,0:T(8,128)(2,1)} %param.25) | copy-start | bytes 3145732
  11.6 107.9 %collective-permute-start = (bf16[1024,1408]{1,0:T(8,128)(2,1)}, bf16[1024,1408]{1,0:T(8,128)(2,1)}, u32[]{:S(2)}, u32[]{:S(2)}) collective-permute-start(bf16[1024,1408]{1,0:T(8,128)(2,1)} %constant_dynamic-slice_fusion), channel_id=1, source_target_pairs={{0,2},{1,3},{2,0},{3,1},{4,6},{5,7},{6,4},{7,5},{8,10},{9,11},{10,... | collective-permute-start | bytes 8650760 | tf_op jit(solution)/shard_map/ppermute | solution.py:257
  14.6 106.4 %collective-permute-start.1 = (bf16[1024,1408]{1,0:T(8,128)(2,1)}, bf16[1024,1408]{1,0:T(8,128)(2,1)}, u32[]{:S(2)}, u32[]{:S(2)}) collective-permute-start(bf16[1024,1408]{1,0:T(8,128)(2,1)} %constant_dynamic-slice_fusion), channel_id=1, source_target_pairs={{0,4},{1,5},{2,6},{3,7},{4,0},{5,1},{6,2},{7,3},{8,12},{9,13},{10,... | collective-permute-start | bytes 8650760 | tf_op jit(solution)/shard_map/ppermute | solution.py:257
  16.2 10.6 %copy-start.113 = (s32[128]{0:T(128)}, s32[128]{0:T(128)S(1)}, u32[]{:S(2)}) copy-start(s32[128]{0:T(128)S(1)} %and_select_fusion.6) | copy-start | bytes 1540
  17.7 9.2 %copy-start.76 = (f32[256,64]{0,1:T(8,128)}, f32[256,64]{0,1:T(8,128)S(1)}, u32[]{:S(2)}) copy-start(f32[256,64]{0,1:T(8,128)S(1)} %get-tuple-element.103) | copy-start | bytes 196612
  18.6 111.1 %copy-start.49 = (f32[256,256]{1,0:T(8,128)}, f32[256,256]{1,0:T(8,128)S(1)}, u32[]{:S(2)}) copy-start(f32[256,256]{1,0:T(8,128)S(1)} %copy.200) | copy-start | bytes 786436
  18.8 111.0 %copy-start.47 = (f32[256,256]{1,0:T(8,128)}, f32[256,256]{1,0:T(8,128)S(1)}, u32[]{:S(2)}) copy-start(f32[256,256]{1,0:T(8,128)S(1)} %copy.201) | copy-start | bytes 786436
  18.8 8.0 %copy-start.82 = (bf16[2048,128]{1,0:T(8,128)(2,1)S(1)}, bf16[2048,128]{1,0:T(8,128)(2,1)}, u32[]{:S(2)}) copy-start(bf16[2048,128]{1,0:T(8,128)(2,1)} %param.38) | copy-start | bytes 1572868
  18.8 8.2 %copy-start.83 = (bf16[2048,128]{1,0:T(8,128)(2,1)S(1)}, bf16[2048,128]{1,0:T(8,128)(2,1)}, u32[]{:S(2)}) copy-start(bf16[2048,128]{1,0:T(8,128)(2,1)} %param.40) | copy-start | bytes 1572868
  25.5 119.8 %copy-start.54 = (f32[256,128]{1,0:T(8,128)}, f32[256,128]{1,0:T(8,128)S(1)}, u32[]{:S(2)}) copy-start(f32[256,128]{1,0:T(8,128)S(1)} %get-tuple-element.119) | copy-start | bytes 393220
  25.5 119.8 %copy-start.69 = (f32[256,128]{1,0:T(8,128)}, f32[256,128]{1,0:T(8,128)S(1)}, u32[]{:S(2)}) copy-start(f32[256,128]{1,0:T(8,128)S(1)} %get-tuple-element.118) | copy-start | bytes 393220
  28.3 92.7 %copy-start.120 = (f32[256]{0:T(256)S(1)}, f32[256]{0:T(256)}, u32[]{:S(2)}) copy-start(f32[256]{0:T(256)} %copy-done.119) | copy-start | bytes 3076
  131.1 140.8 %all-gather.10.cloned.1.call-start = ((), (), s32[]{:S(2)}) async-start(), calls=%async_computation.5 | async-start | bytes 9437184 | tf_op jit(solution)/shard_map/all_gather | solution.py:489
  131.8 248.5 %all-gather.12.cloned.1.call-start = ((), (), s32[]{:S(2)}) async-start(), calls=%async_computation.6 | async-start | bytes 25952256 | tf_op jit(solution)/shard_map/all_gather | solution.py:490
  132.4 542.8 %reduce-scatter.2.cloned.1.call-start = ((), (), s32[]{:S(2)}) async-start(), calls=%async_computation.7 | async-start | bytes 2211840 | tf_op jit(solution)/shard_map/reduce_scatter | solution.py:622
  133.0 79.6 %collective-permute-start.10 = (bf16[256,2048]{1,0:T(8,128)(2,1)S(1)}, bf16[256,2048]{1,0:T(8,128)(2,1)}, u32[]{:S(2)}, u32[]{:S(2)}) collective-permute-start(bf16[256,2048]{1,0:T(8,128)(2,1)S(1)} %copy-done.27), channel_id=1, source_target_pairs={{0,1},{1,0},{2,3},{3,2},{4,5},{5,4},{6,7},{7,6},{8,9},{9,8},{10,11... | collective-permute-start | bytes 3145736 | tf_op jit(solution)/shard_map/ppermute | solution.py:257
  135.0 19.2 %copy-start.102 = (s32[256]{0:T(256)}, s32[256]{0:T(256)S(1)}, u32[]{:S(2)}) copy-start(s32[256]{0:T(256)S(1)} %fusion.245) | copy-start | bytes 3076
  139.4 65.2 %collective-permute-start.2 = (bf16[1024,1408]{1,0:T(8,128)(2,1)}, bf16[1024,1408]{1,0:T(8,128)(2,1)}, u32[]{:S(2)}, u32[]{:S(2)}) collective-permute-start(bf16[1024,1408]{1,0:T(8,128)(2,1)} %collective-permute-done), channel_id=1, source_target_pairs={{0,8},{8,0},{16,24},{24,16},{1,9},{9,1},{17,25},{25,17},{2,10},{10... | collective-permute-start | bytes 8650760 | tf_op jit(solution)/shard_map/ppermute | solution.py:262
  154.2 45.8 %collective-permute-start.3 = (bf16[512,1408]{1,0:T(8,128)(2,1)}, bf16[512,1408]{1,0:T(8,128)(2,1)}, u32[]{:S(2)}, u32[]{:S(2)}) collective-permute-start(bf16[512,1408]{1,0:T(8,128)(2,1)} %slice.297), channel_id=1, source_target_pairs={{0,4},{1,5},{2,6},{3,7},{4,0},{5,1},{6,2},{7,3},{8,12},{9,13},{10,... | collective-permute-start | bytes 4325384 | tf_op jit(solution)/shard_map/ppermute | solution.py:257
  158.4 45.0 %collective-permute-start.4 = (bf16[512,1408]{1,0:T(8,128)(2,1)}, bf16[512,1408]{1,0:T(8,128)(2,1)}, u32[]{:S(2)}, u32[]{:S(2)}) collective-permute-start(bf16[512,1408]{1,0:T(8,128)(2,1)} %slice.298), channel_id=1, source_target_pairs={{0,2},{1,3},{2,0},{3,1},{4,6},{5,7},{6,4},{7,5},{8,10},{9,11},{10,... | collective-permute-start | bytes 4325384 | tf_op jit(solution)/shard_map/ppermute | solution.py:257
  204.6 64.4 %collective-permute-start.5 = (bf16[1024,1408]{1,0:T(8,128)(2,1)}, bf16[1024,1408]{1,0:T(8,128)(2,1)}, u32[]{:S(2)}, u32[]{:S(2)}) collective-permute-start(bf16[1024,1408]{1,0:T(8,128)(2,1)} %collective-permute-done.1), channel_id=1, source_target_pairs={{0,8},{8,0},{16,24},{24,16},{1,9},{9,1},{17,25},{25,17},{2,10},{10... | collective-permute-start | bytes 8650760 | tf_op jit(solution)/shard_map/ppermute | solution.py:262
  228.4 15.1 %copy-start.2 = (bf16[4,2,2048,128]{3,2,1,0:T(8,128)(2,1)}, bf16[4,2,2048,128]{3,2,1,0:T(8,128)(2,1)S(1)}, u32[]{:S(2)}) copy-start(bf16[4,2,2048,128]{3,2,1,0:T(8,128)(2,1)S(1)} %pad_maximum_fusion.2.v_ref) | copy-start | bytes 12582916
  228.4 40.6 %copy-start.52 = (bf16[2048,128]{1,0:T(8,128)(2,1)S(1)}, bf16[2048,128]{1,0:T(8,128)(2,1)}, u32[]{:S(2)}) copy-start(bf16[2048,128]{1,0:T(8,128)(2,1)} %param.42) | copy-start | bytes 1572868
  228.4 40.6 %copy-start.114 = (s32[128]{0:T(128)S(1)}, s32[128]{0:T(128)}, u32[]{:S(2)}) copy-start(s32[128]{0:T(128)} %copy-done.113) | copy-start | bytes 1540
  228.4 41.7 %copy-start.61 = (bf16[128,2048]{1,0:T(8,128)(2,1)S(1)}, bf16[128,2048]{1,0:T(8,128)(2,1)}, u32[]{:S(2)}) copy-start(bf16[128,2048]{1,0:T(8,128)(2,1)} %param.43) | copy-start | bytes 1572868
  244.1 250.5 %copy-start.3 = (bf16[256,2048]{1,0:T(8,128)(2,1)}, bf16[256,2048]{1,0:T(8,128)(2,1)S(1)}, u32[]{:S(2)}) copy-start(bf16[256,2048]{1,0:T(8,128)(2,1)S(1)} %get-tuple-element.37.o_ref) | copy-start | bytes 3145732
  279.3 96.1 %copy-start.29 = (bf16[256,2048]{1,0:T(8,128)(2,1)}, bf16[256,2048]{1,0:T(8,128)(2,1)S(1)}, u32[]{:S(2)}) copy-start(bf16[256,2048]{1,0:T(8,128)(2,1)S(1)} %multiply_convert_fusion.6) | copy-start | bytes 3145732
  279.3 10.3 %collective-permute-start.6 = (bf16[256,2048]{1,0:T(8,128)(2,1)S(1)}, bf16[256,2048]{1,0:T(8,128)(2,1)S(1)}, u32[]{:S(2)}, u32[]{:S(2)}) collective-permute-start(bf16[256,2048]{1,0:T(8,128)(2,1)S(1)} %multiply_convert_fusion.6), channel_id=1, source_target_pairs={{0,1},{1,0},{2,3},{3,2},{4,5},{5,4},{6,7},{7,6},{8,9},{9,8},{10,11... | collective-permute-start | bytes 3145736 | tf_op jit(solution)/shard_map/ppermute | solution.py:257
  287.6 34.7 %collective-permute-start.7 = (bf16[512,1408]{1,0:T(8,128)(2,1)}, bf16[512,1408]{1,0:T(8,128)(2,1)S(1)}, u32[]{:S(2)}, u32[]{:S(2)}) collective-permute-start(bf16[512,1408]{1,0:T(8,128)(2,1)} %collective-permute-done.3), channel_id=1, source_target_pairs={{0,8},{8,0},{16,24},{24,16},{1,9},{9,1},{17,25},{25,17},{2,10},{10... | collective-permute-start | bytes 4325384 | tf_op jit(solution)/shard_map/ppermute | solution.py:262
  289.1 62.8 %collective-permute-start.8 = (bf16[512,1408]{1,0:T(8,128)(2,1)}, bf16[512,1408]{1,0:T(8,128)(2,1)S(1)}, u32[]{:S(2)}, u32[]{:S(2)}) collective-permute-start(bf16[512,1408]{1,0:T(8,128)(2,1)} %collective-permute-done.4), channel_id=1, source_target_pairs={{0,8},{8,0},{16,24},{24,16},{1,9},{9,1},{17,25},{25,17},{2,10},{10... | collective-permute-start | bytes 4325384 | tf_op jit(solution)/shard_map/ppermute | solution.py:262
  365.7 9.6 %slice-start = ((s8[5767168]{0:T(1024)(128)(4,1)}), s8[1572864]{0:T(1024)(128)(4,1)S(1)}, s32[]{:S(2)}) async-start(s8[5767168]{0:T(1024)(128)(4,1)} %bitcast.261), calls=%async_computation.8 | async-start | bytes 3145728
  443.6 39.2 %collective-permute-start.11 = (bf16[256,2304]{1,0:T(8,128)(2,1)}, bf16[256,2304]{1,0:T(8,128)(2,1)}, u32[]{:S(2)}, u32[]{:S(2)}) collective-permute-start(bf16[256,2304]{1,0:T(8,128)(2,1)} %slice.523), channel_id=1, source_target_pairs={{0,1},{1,0},{2,3},{3,2},{4,5},{5,4},{6,7},{7,6},{8,9},{9,8},{10,11... | collective-permute-start | bytes 3538952 | tf_op jit(solution)/shard_map/ppermute | solution.py:257
  451.0 11.2 %copy-start.51 = (f32[512,128]{1,0:T(8,128)}, f32[512,128]{1,0:T(8,128)S(1)}, u32[]{:S(2)}) copy-start(f32[512,128]{1,0:T(8,128)S(1)} %convolution_add_fusion.10) | copy-start | bytes 786436
  464.6 7.0 collective-permute-start.9
  512.0 30.1 %copy-start.18 = (f32[256,2048]{1,0:T(8,128)S(1)}, f32[256,2048]{1,0:T(8,128)}, u32[]{:S(2)}) copy-start(f32[256,2048]{1,0:T(8,128)} %copy.199) | copy-start | bytes 6291460
  565.0 48.1 %all-to-all-start = ((bf16[8,256,512]{1,2,0:T(8,128)(2,1)}), bf16[8,256,512]{1,2,0:T(8,128)(2,1)}, u32[]{:S(2)}, u32[]{:S(2)}) async-start(bf16[8,256,512]{1,2,0:T(8,128)(2,1)} %copy.222), calls=%async_computation | async-start | bytes 4194304 | tf_op jit(solution)/shard_map/all_to_all | solution.py:248
  596.3 19.6 %copy-start.48 = (f32[256,256]{1,0:T(8,128)S(1)}, f32[256,256]{1,0:T(8,128)}, u32[]{:S(2)}) copy-start(f32[256,256]{1,0:T(8,128)} %copy-done.47) | copy-start | bytes 786436
  638.9 14.7 %all-to-all-start.1 = ((bf16[8,288,128]{2,1,0:T(8,128)(2,1)}), bf16[8,288,128]{2,1,0:T(8,128)(2,1)}, u32[]{:S(2)}, u32[]{:S(2)}) async-start(bf16[8,288,128]{2,1,0:T(8,128)(2,1)} %pad_maximum_fusion.12), calls=%async_computation.1 | async-start | bytes 1179648 | tf_op jit(solution)/shard_map/all_to_all | solution.py:248
  643.1 7.9 %copy-start.14 = (f32[256,2048]{1,0:T(8,128)S(1)}, f32[256,2048]{1,0:T(8,128)}, u32[]{:S(2)}) copy-start(f32[256,2048]{1,0:T(8,128)} %copy-done.12) | copy-start | bytes 6291460
  643.1 7.9 %copy-start.118 = (f32[256]{0:T(256)S(1)}, f32[256]{0:T(256)}, u32[]{:S(2)}) copy-start(f32[256]{0:T(256)} %get-tuple-element.104) | copy-start | bytes 3076
  643.1 7.9 %copy-start.122 = (f32[256]{0:T(256)S(1)}, f32[256]{0:T(256)}, u32[]{:S(2)}) copy-start(f32[256]{0:T(256)} %copy-done.119) | copy-start | bytes 3076
  654.7 15.2 %copy-start.95 = (s32[128]{0:T(128)S(1)}, s32[128]{0:T(128)}, u32[]{:S(2)}) copy-start(s32[128]{0:T(128)} %fusion.240) | copy-start | bytes 1540
  (110 other events, 315.4 us)
Sparse Core Ops, SparseCore 0:
  9.9 108.3 all-gather.5
  131.2 28.7 all-gather.7
  161.9 68.9 all-gather.9
  232.6 120.9 all-gather.11
  504.6 41.0 reduce-scatter.1

commit v3 on v1

v3 whole, which is shorter than its diff:
```python
import jax
import jax.numpy as jnp
from jax import lax
from jax.experimental import pallas as pl
from jax.experimental.pallas import tpu as pltpu
from jax.sharding import PartitionSpec as P

HEADS = 32
KV_HEADS = 4
HEAD_DIM = 64
RANK = 16
LANES = 128
KEY_BLOCK = 512

EPS = 1e-05
LOWRANK_FACTOR = 2.0
MASKED = -1e30
F32 = jnp.float32
BF16 = jnp.bfloat16


def mm(left, right):
    return jnp.dot(left, right, preferred_element_type=F32)


def mm_nt(left, right):
    return lax.dot_general(left, right, (((1,), (1,)), ((), ())), preferred_element_type=F32)


def mm_tn(left, right):
    return lax.dot_general(left, right, (((0,), (0,)), ((), ())), preferred_element_type=F32)


def inverse_rms(value):
    return lax.rsqrt(jnp.mean(value * value, axis=-1, keepdims=True) + EPS)


def norm_backward(value, scale, gain, grad):
    scaled = gain * grad
    return scale * scaled - value * (scale * scale * scale) * jnp.mean(
        scaled * value, axis=-1, keepdims=True
    )


def half_turn(value):
    half = HEAD_DIM // 2
    lane = lax.broadcasted_iota(jnp.int32, value.shape, 1) % HEAD_DIM
    return jnp.where(
        lane < half, -jnp.roll(value, -half, axis=1), jnp.roll(value, half, axis=1)
    )


def rotate(value, cosines, sines):
    return value * cosines + half_turn(value) * sines


def unrotate(grad, cosines, sines):
    return grad * cosines - half_turn(grad * sines)


def lane_of(shape):
    return lax.broadcasted_iota(jnp.int32, shape, 1)


def key_rows(span, index):
    return pl.ds(pl.multiple_of((index ^ span[2]) * KEY_BLOCK, KEY_BLOCK), KEY_BLOCK)


def spread_heads(span, odd, source_ref, pair_ref):
    def step(index, carry):
        rows = key_rows(span, index)
        value = source_ref[rows, :].astype(F32)
        turned = pltpu.roll(value, HEAD_DIM, 1)
        low = lane_of(value.shape) < HEAD_DIM
        none = jnp.zeros_like(value)
        pair_ref[0, rows, :] = jnp.where(low, jnp.where(odd, turned, value), none).astype(BF16)
        pair_ref[1, rows, :] = jnp.where(low, none, jnp.where(odd, value, turned)).astype(BF16)
        return carry

    lax.fori_loop(span[0], span[1], step, 0)


def attention_forward_kernel(span, q_ref, key_ref, value_ref, bias_ref, out_ref, lse_ref, k_ref, v_ref):
    tokens = q_ref.shape[0]
    per_kv = pl.num_programs(0) // KV_HEADS
    odd = lax.rem(pl.program_id(0) // per_kv, 2) == 1

    @pl.when(lax.rem(pl.program_id(0), per_kv) == 0)
    def _():
        spread_heads(span, odd, key_ref, k_ref)
        spread_heads(span, odd, value_ref, v_ref)

    query = q_ref[...]

    def step(index, carry):
        rows = key_rows(span, index)
        bias = bias_ref[rows, :]
        mixed = carry[4]
        new, parts, decays = [], [], []
        for side in range(2):
            peak, total = carry[2 * side], carry[2 * side + 1]
            scores = mm_nt(k_ref[side, rows, :], query) + bias
            top = jnp.maximum(peak, jnp.max(scores, axis=0, keepdims=True))
            decay = jnp.exp(peak - top)
            probs = jnp.exp(scores - top)
            total = total * decay + jnp.sum(probs, axis=0, keepdims=True)
            new += [top, total]
            decays.append(jnp.broadcast_to(decay, (HEAD_DIM, tokens)))
            parts.append(mm_tn(v_ref[side, rows, :], probs.astype(BF16)))
        mixed = mixed * jnp.concatenate(decays, axis=0) + (parts[0] + parts[1])
        return (*new, mixed)

    low = jnp.full((1, tokens), MASKED, F32)
    none = jnp.zeros((1, tokens), F32)
    peak0, total0, peak1, total1, mixed = lax.fori_loop(
        span[0], span[1], step, (low, none, low, none, jnp.zeros((LANES, tokens), F32))
    )
    weight = jnp.concatenate(
        [
            jnp.broadcast_to(1.0 / total0, (HEAD_DIM, tokens)),
            jnp.broadcast_to(1.0 / total1, (HEAD_DIM, tokens)),
        ],
        axis=0,
    )
    out_ref[...] = (mixed * weight).T.astype(BF16)
    lse_ref[0] = jnp.concatenate([peak0 + jnp.log(total0), peak1 + jnp.log(total1)], axis=0)


def key_value_specs(keys, per_kv):
    blocks = KV_HEADS * HEAD_DIM // LANES
    heads = LANES // HEAD_DIM
    return [
        pl.BlockSpec((keys, LANES), lambda j, s: (0, j // per_kv // heads)),
        pl.BlockSpec((keys, LANES), lambda j, s: (0, blocks + j // per_kv // heads)),
    ]


def attention_forward(span, query, key_value, bias):
    tokens, width = query.shape
    keys = bias.shape[0]
    pairs = width // LANES
    pair_spec = pl.BlockSpec((tokens, LANES), lambda j, s: (0, j))
    return pl.pallas_call(
        attention_forward_kernel,
        out_shape=(
            jax.ShapeDtypeStruct((tokens, width), BF16),
            jax.ShapeDtypeStruct((pairs, 2, tokens), F32),
        ),
        grid_spec=pltpu.PrefetchScalarGridSpec(
            num_scalar_prefetch=1,
            grid=(pairs,),
            in_specs=[
                pair_spec,
                *key_value_specs(keys, pairs // KV_HEADS),
                pl.BlockSpec((keys, tokens), lambda j, s: (0, 0)),
            ],
            out_specs=(pair_spec, pl.BlockSpec((1, 2, tokens), lambda j, s: (j, 0, 0))),
            scratch_shapes=[pltpu.VMEM((2, keys, LANES), BF16)] * 2,
        ),
        compiler_params=pltpu.CompilerParams(
            dimension_semantics=("arbitrary",), vmem_limit_bytes=40 << 20
        ),
        cost_estimate=pl.CostEstimate(
            flops=4 * tokens * keys * width,
            transcendentals=tokens * keys * HEADS // 2,
            bytes_accessed=4 * tokens * width + 16 * keys * LANES * KV_HEADS,
        ),
        name="attention_forward",
    )(span, query, key_value, key_value, bias)


def attention_backward_kernel(
    span,
    q_ref,
    do_ref,
    o_ref,
    lse_ref,
    key_ref,
    value_ref,
    bias_ref,
    cos_ref,
    sin_ref,
    dq_ref,
    dk_ref,
    dv_ref,
    k_ref,
    v_ref,
    dk_sum,
    dv_sum,
):
    tokens = q_ref.shape[0]
    per_kv = pl.num_programs(0) // KV_HEADS
    member = lax.rem(pl.program_id(0), per_kv)
    odd = lax.rem(pl.program_id(0) // per_kv, LANES // HEAD_DIM) == 1

    @pl.when(member == 0)
    def _():
        spread_heads(span, odd, key_ref, k_ref)
        spread_heads(span, odd, value_ref, v_ref)
        dk_sum[...] = jnp.zeros_like(dk_sum)
        dv_sum[...] = jnp.zeros_like(dv_sum)

    query = q_ref[...]
    grad = do_ref[...]
    low = lane_of((tokens, LANES)) < HEAD_DIM
    none = jnp.zeros_like(query)
    query_stack = jnp.concatenate(
        [jnp.where(low, query, none), jnp.where(low, none, query)], axis=0
    )
    grad_stack = jnp.concatenate([jnp.where(low, grad, none), jnp.where(low, none, grad)], axis=0)
    product = grad.astype(F32) * o_ref[...].astype(F32)
    row = lax.broadcasted_iota(jnp.int32, (8, LANES), 0)
    column = lax.broadcasted_iota(jnp.int32, (8, LANES), 1)
    chooser = jnp.where(row == column // HEAD_DIM, 1.0, 0.0).astype(F32)
    deltas = lax.dot_general(
        chooser,
        product,
        (((1,), (1,)), ((), ())),
        precision=lax.Precision.HIGHEST,
        preferred_element_type=F32,
    )

    def step(index, dquery):
        rows = key_rows(span, index)
        bias = bias_ref[rows, :]
        all_probs, all_dscores = [], []
        for side in range(2):
            scores = mm_nt(k_ref[side, rows, :], query) + bias
            probs = jnp.exp(scores - lse_ref[0, side : side + 1, :])
            dprobs = mm_nt(v_ref[side, rows, :], grad)
            dscores = (probs * (dprobs - deltas[side : side + 1, :])).astype(BF16)
            all_probs.append(probs.astype(BF16))
            all_dscores.append(dscores)
            dquery = dquery + mm_tn(k_ref[side, rows, :], dscores)
        dk_sum[rows, :] += mm(jnp.concatenate(all_dscores, axis=1), query_stack)
        dv_sum[rows, :] += mm(jnp.concatenate(all_probs, axis=1), grad_stack)
        return dquery

    dquery = lax.fori_loop(span[0], span[1], step, jnp.zeros((LANES, tokens), F32))
    dquery = dquery.T * (HEAD_DIM**-0.5)
    turned = dquery * sin_ref[...]
    half = HEAD_DIM // 2
    first = lax.rem(lane_of(turned.shape), HEAD_DIM) < half
    turned = jnp.where(
        first, pltpu.roll(turned, LANES - half, 1), -pltpu.roll(turned, half, 1)
    )
    dq_ref[...] = (dquery * cos_ref[...] + turned).astype(BF16)

    @pl.when(member == per_kv - 1)
    def _():
        def put(index, carry):
            place = pl.ds(pl.multiple_of((index ^ span[3]) * tokens, tokens), tokens)
            for sum_ref, out_ref in ((dk_sum, dk_ref), (dv_sum, dv_ref)):
                total = sum_ref[pl.ds(pl.multiple_of(index * tokens, tokens), tokens), :]
                total = total + pltpu.roll(total, HEAD_DIM, 1)
                keep = jnp.logical_and(odd, lane_of(total.shape) < HEAD_DIM)
                out_ref[place, :] = jnp.where(keep, out_ref[place, :], total.astype(BF16))
            return carry

        lax.fori_loop(0, dk_sum.shape[0] // tokens, put, 0)


def attention_backward(span, query, grad, attended, lse, key_value, bias, cosines, sines):
    tokens, width = query.shape
    keys = bias.shape[0]
    pairs = width // LANES
    per_kv = pairs // KV_HEADS
    heads = LANES // HEAD_DIM
    pair_spec = pl.BlockSpec((tokens, LANES), lambda j, s: (0, j))
    table_spec = pl.BlockSpec((tokens, LANES), lambda j, s: (0, 0))
    dkv_spec = pl.BlockSpec((keys, LANES), lambda j, s: (0, j // per_kv // heads))
    return pl.pallas_call(
        attention_backward_kernel,
        out_shape=(
            jax.ShapeDtypeStruct((tokens, width), BF16),
            jax.ShapeDtypeStruct((keys, KV_HEADS * HEAD_DIM), BF16),
            jax.ShapeDtypeStruct((keys, KV_HEADS * HEAD_DIM), BF16),
        ),
        grid_spec=pltpu.PrefetchScalarGridSpec(
            num_scalar_prefetch=1,
            grid=(pairs,),
            in_specs=[
                pair_spec,
                pair_spec,
                pair_spec,
                pl.BlockSpec((1, 2, tokens), lambda j, s: (j, 0, 0)),
                *key_value_specs(keys, per_kv),
                pl.BlockSpec((keys, tokens), lambda j, s: (0, 0)),
                table_spec,
                table_spec,
            ],
            out_specs=(pair_spec, dkv_spec, dkv_spec),
            scratch_shapes=[pltpu.VMEM((2, keys, LANES), BF16)] * 2
            + [pltpu.VMEM((keys, LANES), F32)] * 2,
        ),
        compiler_params=pltpu.CompilerParams(
            dimension_semantics=("arbitrary",), vmem_limit_bytes=48 << 20
        ),
        cost_estimate=pl.CostEstimate(
            flops=10 * tokens * keys * width,
            transcendentals=tokens * keys * HEADS // 2,
            bytes_accessed=10 * tokens * width + 24 * keys * LANES * KV_HEADS,
        ),
        name="attention_backward",
    )(span, query, grad, attended, lse, key_value, key_value, bias, cosines, sines)


CORE, ACROSS_X, ACROSS_Y = 1, 2, 4


def flip(array, mask):
    members = lax.axis_size("grp")
    return lax.ppermute(array, "grp", [(i, i ^ mask) for i in range(members)])


def flip_group(array):
    groups = lax.axis_size("rep")
    return lax.ppermute(array, "rep", [(i, i ^ 1) for i in range(groups)])


def gather_same_core(weight):
    rows = weight.shape[0] // 4
    parity = lax.axis_index("rep") % 2
    quarters = [
        lax.dynamic_slice_in_dim(weight, ((parity ^ (q // 2)) * 2 + q % 2) * rows, rows, 0)
        for q in range(4)
    ]
    x_low, y_low, next_quarter = yield quarters, (
        flip(quarters[0], ACROSS_X),
        flip(quarters[0], ACROSS_Y),
        quarters[1],
    )
    x_high, y_high, *others = yield (
        flip(next_quarter, ACROSS_X),
        flip(next_quarter, ACROSS_Y),
        flip_group(x_low),
        flip_group(y_low),
    )
    x_low_other, y_low_other = others
    both_low, both_high, x_high_other, y_high_other = yield (
        flip(x_low, ACROSS_Y),
        flip(y_high, ACROSS_X),
        flip_group(x_high),
        flip_group(y_high),
    )
    both_other = yield flip_group(both_low), flip_group(both_high)
    return (
        (x_low, x_high, x_low_other, x_high_other),
        (y_low, y_high, y_low_other, y_high_other),
        (both_low, both_high, *both_other),
    )


def gather_key_values(own):
    pieces = [own, flip(own, ACROSS_X), flip(own, ACROSS_Y), flip(own, ACROSS_X | ACROSS_Y)]
    return jnp.concatenate(
        [part for piece in pieces for part in (piece, flip(piece, CORE))], axis=0
    )


def tie(value, transfers):
    value, *transfers = lax.optimization_barrier((value, *transfers))
    return value, tuple(transfers)


def feed_forward_alone(norm2, sens, gate_up_full, down_full, small, seen):
    ffn_in, switch, lift, down_in, lower = small
    slots, hidden_width = switch.shape
    seen_two = jnp.concatenate([seen, seen], axis=1)
    latent_gu = (mm(norm2, ffn_in) * seen_two).astype(BF16)
    latent_g, latent_u = latent_gu[:, :slots], latent_gu[:, slots:]
    gate_up = mm(norm2, gate_up_full) + LOWRANK_FACTOR * jnp.concatenate(
        [mm(latent_g, switch), mm(latent_u, lift)], axis=1
    )
    gate = gate_up[:, :hidden_width]
    up = gate_up[:, hidden_width:]
    sigma = jax.nn.sigmoid(gate)
    act = (gate * sigma * up).astype(BF16)
    latent_d = (mm_nt(act, down_in) * seen).astype(BF16)
    response_part = mm(act, down_full) + LOWRANK_FACTOR * mm(latent_d, lower)
    dlat_d = (LOWRANK_FACTOR * mm_nt(sens, lower) * seen).astype(BF16)
    dact = mm_nt(sens, down_full) + mm(dlat_d, down_in)
    dgate = (dact * up * (sigma * (1.0 + gate * (1.0 - sigma)))).astype(BF16)
    dup = (dact * gate * sigma).astype(BF16)
    dlat_gu = (
        LOWRANK_FACTOR
        * jnp.concatenate([mm_nt(dgate, switch), mm_nt(dup, lift)], axis=1)
        * seen_two
    ).astype(BF16)
    dnorm2 = (
        mm_nt(dgate, gate_up_full[:, :hidden_width])
        + mm_nt(dup, gate_up_full[:, hidden_width:])
        + mm_nt(dlat_gu, ffn_in)
    )
    deep = jnp.concatenate(
        [
            mm_tn(dlat_d, act),
            LOWRANK_FACTOR * mm_tn(latent_g, dgate),
            LOWRANK_FACTOR * mm_tn(latent_u, dup),
        ],
        axis=0,
    ).astype(BF16)
    return response_part, dnorm2, latent_d, dlat_gu, deep


def feed_forward_kernel(
    meta, x_ref, g_ref, latent_ref, dlat_ref, stack_ref, *refs
):
    weights = [[refs[8 * b + 4 * t : 8 * b + 4 * t + 4] for t in range(2)] for b in range(2)]
    piece_refs = [refs[16 + 2 * b : 18 + 2 * b] for b in range(2)]
    in_refs = refs[20:22]
    down_refs = refs[22:24]
    back_own, back_near, front_own, front_near, deep_ref = refs[24:29]
    dnorm, response, dlat_sum, latent_sum = refs[29:33]
    tokens, width = x_ref.shape
    count = tokens // 2
    slots = dlat_ref.shape[1]
    quarter = width // 4
    parity = meta[0]
    owns_gate = meta[1] == 1
    starts = [
        pl.multiple_of((parity if q < 2 else 1 - parity) * (width // 2) + (q % 2) * quarter, quarter)
        for q in range(4)
    ]

    @pl.when(pl.program_id(0) == 0)
    def _():
        for ref in (dnorm, response, dlat_sum, latent_sum):
            ref[...] = jnp.zeros_like(ref)

    none = jnp.zeros((slots, LANES), BF16)
    firsts, seconds = ([piece_refs[b][t][...] for b in range(2)] for t in range(2))
    pieces = jnp.concatenate(
        [
            jnp.concatenate([firsts[0], none, firsts[1], none], axis=1),
            jnp.concatenate([none, seconds[0], none, seconds[1]], axis=1),
        ],
        axis=0,
    )

    def columns_of(q):
        return jnp.concatenate(
            [weights[b][t][q][...] for b in range(2) for t in range(2)], axis=1
        )

    total = mm(latent_ref[...], pieces)
    for q in range(4):
        total = total + mm(x_ref[:, pl.ds(starts[q], quarter)], columns_of(q))
    first = jnp.concatenate([total[:, :LANES], total[:, 2 * LANES : 3 * LANES]], axis=1)
    second = jnp.concatenate([total[:, LANES : 2 * LANES], total[:, 3 * LANES :]], axis=1)
    gate = jnp.where(owns_gate, first, second)
    up = jnp.where(owns_gate, second, first)
    down_in = jnp.concatenate([ref[...] for ref in in_refs], axis=1)
    sigma = jax.nn.sigmoid(gate)
    act = (gate * sigma * up).astype(BF16)
    dact = mm(dlat_ref[...], down_in)
    parts, _, columns = down_refs[0].shape
    for k in range(parts):
        down = jnp.concatenate([ref[k] for ref in down_refs], axis=0)
        lanes = slice(k * columns, (k + 1) * columns)
        dact = dact + mm_nt(g_ref[:, lanes], down)
        response[:, lanes] += mm(act, down)
    dgate = (dact * up * (sigma * (1.0 + gate * (1.0 - sigma)))).astype(BF16)
    dup = (dact * gate * sigma).astype(BF16)
    latent_sum[:, :slots] += mm_nt(act, down_in)
    act_grad = mm(stack_ref[:slots, :], act)
    dfirst = jnp.where(owns_gate, dgate, dup)
    dsecond = jnp.where(owns_gate, dup, dgate)
    both = jnp.concatenate(
        [dfirst[:, :LANES], dsecond[:, :LANES], dfirst[:, LANES:], dsecond[:, LANES:]], axis=1
    )
    for q in range(4):
        dnorm[:, q * quarter : (q + 1) * quarter] += mm_nt(both, columns_of(q))
    dlat_sum[:, : 2 * slots] += mm_nt(both, pieces)
    piece_grad = mm(stack_ref[slots:, :], both).astype(BF16)
    act_grad = act_grad.astype(BF16)
    for b in range(2):
        deep_ref[b, :slots, :] = act_grad[:, b * LANES : (b + 1) * LANES]
        start = 2 * b * LANES
        deep_ref[b, slots : 2 * slots, :] = piece_grad[:slots, start : start + LANES]
        deep_ref[b, 2 * slots :, :] = piece_grad[slots:, start + LANES : start + 2 * LANES]

    @pl.when(pl.program_id(0) == pl.num_programs(0) - 1)
    def _():
        for q in range(4):
            value = dnorm[:, q * quarter : (q + 1) * quarter]
            back_own[:, pl.ds(starts[q], quarter)] = value[:count]
            back_near[:, pl.ds(starts[q], quarter)] = value[count:].astype(BF16)
        back_own[:, width:] = dlat_sum[:count, :]
        back_near[:, width:] = dlat_sum[count:, :].astype(BF16)
        front_own[:, :width] = response[:count, :]
        front_near[:, :width] = response[count:, :].astype(BF16)
        front_own[:, width:] = latent_sum[:count, :]
        front_near[:, width:] = latent_sum[count:, :].astype(BF16)


def feed_forward_paired(norm2, sens, sens_near, own, far, down_parts, small, seen, seen_near):
    ffn_in, switch, lift, down_in, lower = small
    count, width = norm2.shape
    slots, hidden_width = switch.shape
    block = own[0].shape[1]
    steps = block // LANES
    member = lax.axis_index("grp")
    parity = lax.axis_index("rep") % 2
    owns_gate = member < ACROSS_Y
    hidden = member % ACROSS_Y
    over_x, over_y, over_both = far

    def order(first, second):
        return jnp.where(owns_gate, first, second), jnp.where(owns_gate, second, first)

    both = jnp.concatenate([norm2, flip(norm2, CORE)], axis=0)
    sens_both = jnp.concatenate([sens, sens_near], axis=0)
    seen_both = jnp.concatenate([seen, seen_near], axis=0)
    seen_two = jnp.concatenate([seen_both, seen_both], axis=1)
    latent_gu = (mm(both, ffn_in) * seen_two).astype(BF16)
    latent = jnp.concatenate(order(latent_gu[:, :slots], latent_gu[:, slots:]), axis=1)
    dlat_d = (LOWRANK_FACTOR * mm_nt(sens_both, lower) * seen_both).astype(BF16)
    stack = jnp.concatenate([dlat_d, latent], axis=1).T
    pieces = order(switch, lift)
    meta = jnp.stack([parity, owns_gate.astype(jnp.int32), hidden, hidden ^ ACROSS_X]).astype(
        jnp.int32
    )

    quarter = width // 4
    operands, specs = [], []

    def add(operand, shape, index_map, **how):
        operands.append(operand)
        specs.append(pl.BlockSpec(shape, index_map, **how))

    def whole(operand):
        add(operand, operand.shape, lambda j, m: (0,) * operand.ndim)

    def columns_of(piece):
        add(piece, (quarter, LANES), lambda j, m: (0, j))

    for operand in (both, sens_both, latent * jnp.asarray(LOWRANK_FACTOR, BF16), dlat_d, stack):
        whole(operand)
    for quarters in (own, over_y, over_x, over_both):
        for piece in quarters:
            columns_of(piece)
    for b in range(2):
        for piece in pieces:
            add(piece, (slots, LANES), lambda j, m, b=b: (0, m[2 + b] * steps + j))
    for b in range(2):
        add(down_in, (slots, LANES), lambda j, m, b=b: (0, m[2 + b] * steps + j))
    members, _, part_columns = down_parts.shape
    for b in range(2):
        add(
            down_parts,
            (members, LANES, part_columns),
            lambda j, m, b=b: (0, m[2 + b] * steps + j, 0),
        )
    wide = width + LANES
    result_spec = pl.BlockSpec((count, wide), lambda j, m: (0, 0))
    flops = 2 * 6 * 2 * count * width * 2 * block
    back_own, back_near, front_own, front_near, deep = pl.pallas_call(
        feed_forward_kernel,
        out_shape=(
            jax.ShapeDtypeStruct((count, wide), F32),
            jax.ShapeDtypeStruct((count, wide), BF16),
            jax.ShapeDtypeStruct((count, wide), F32),
            jax.ShapeDtypeStruct((count, wide), BF16),
            jax.ShapeDtypeStruct((2, 3 * slots, block), BF16),
        ),
        grid_spec=pltpu.PrefetchScalarGridSpec(
            num_scalar_prefetch=1,
            grid=(steps,),
            in_specs=specs,
            out_specs=(
                *[result_spec] * 4,
                pl.BlockSpec((2, 3 * slots, LANES), lambda j, m: (0, 0, j)),
            ),
            scratch_shapes=[
                pltpu.VMEM((2 * count, width), F32),
                pltpu.VMEM((2 * count, width), F32),
                pltpu.VMEM((2 * count, LANES), F32),
                pltpu.VMEM((2 * count, LANES), F32),
            ],
        ),
        compiler_params=pltpu.CompilerParams(
            dimension_semantics=("arbitrary",), vmem_limit_bytes=56 << 20
        ),
        cost_estimate=pl.CostEstimate(
            flops=flops,
            transcendentals=4 * count * block,
            bytes_accessed=2 * 6 * width * block + 40 * count * width,
        ),
        name="feed_forward",
    )(meta, *operands)

    backward = back_own + flip(back_near, CORE).astype(F32)
    forward = front_own + flip(front_near, CORE).astype(F32)
    dlat_one, dlat_two = (
        backward[:, width : width + slots],
        backward[:, width + slots : width + 2 * slots],
    )
    dlat_gu = (
        LOWRANK_FACTOR * jnp.concatenate(order(dlat_one, dlat_two), axis=1) * seen_two[:count]
    ).astype(BF16)
    dnorm2 = backward[:, :width] + mm_nt(dlat_gu, ffn_in)
    latent_d = (forward[:, width : width + slots] * seen).astype(BF16)
    response_part = forward[:, :width] + LOWRANK_FACTOR * mm(latent_d, lower)

    two = jnp.asarray(LOWRANK_FACTOR, BF16)
    grads = order(deep[:, slots : 2 * slots] * two, deep[:, 2 * slots :] * two)
    deep = jnp.concatenate([deep[:, :slots], *grads], axis=1)
    placed = jnp.zeros((3 * slots, hidden_width), BF16)
    for b in range(2):
        placed = lax.dynamic_update_slice_in_dim(
            placed, deep[b], (hidden ^ (b * ACROSS_X)) * block, 1
        )
    return response_part, dnorm2, latent_d, dlat_gu, placed


def exchange_sum(parts):
    received = lax.all_to_all(parts.astype(BF16), "grp", 0, 0, tiled=True)
    return jnp.sum(received.astype(F32), axis=0)


def round_groups(array):
    groups = lax.axis_size("rep")
    return [array] + [
        lax.ppermute(array, "rep", [(i, (i + shift) % groups) for i in range(groups)])
        for shift in range(1, groups)
    ]


def shards(
    tokens,
    response_sensitivity,
    seq_lengths,
    prefix_lengths,
    adapter_ids,
    attn_gain,
    mlp_gain,
    qkv_weight,
    out_weight,
    gate_up_weight,
    down_weight,
    query_in,
    asking_right_pieces,
    key_in,
    lookup_right_pieces,
    value_in,
    content_right_pieces,
    output_in,
    final_right_pieces,
    gate_in,
    switch_right_pieces,
    up_in,
    lift_right_pieces,
    down_in,
    lower_right_pieces,
):
    count, width = tokens.shape
    members = lax.axis_size("grp")
    groups = lax.axis_size("rep")
    kv_width = lookup_right_pieces.shape[1]
    narrow = query_in.shape[1]
    group = lax.axis_index("rep")
    member = lax.axis_index("grp")
    lengths = lax.dynamic_slice_in_dim(seq_lengths, 2 * group, 2)
    prefixes = lax.dynamic_slice_in_dim(prefix_lengths, 2 * group, 2)
    chosen_ids = lax.dynamic_slice_in_dim(adapter_ids, 2 * group, 2)
    key_count = count * members
    sens = response_sensitivity

    paired = members == 8 and groups % 2 == 0
    qkv_full = lax.all_gather(qkv_weight, "grp", axis=1, tiled=True)
    if paired:
        steps = gather_same_core(gate_up_weight)
        own, transfers = next(steps)
        sens_near = flip(sens, CORE)
    else:
        out_full = lax.all_gather(out_weight, "grp", axis=1, tiled=True)
        down_full = lax.all_gather(down_weight, "grp", axis=1, tiled=True)
        gate_up_full = lax.all_gather(gate_up_weight, "grp", axis=1, tiled=True)

    turn = member if paired else 0
    key_index = jnp.arange(key_count, dtype=jnp.int32)
    key_index = (key_index // count ^ turn) * count + key_index % count
    key_second = (key_index >= lengths[0]).astype(jnp.int32)
    key_position = key_index - key_second * lengths[0]
    own_index = member * count + jnp.arange(count, dtype=jnp.int32)
    own_second = (own_index >= lengths[0]).astype(jnp.int32)
    position = own_index - own_second * lengths[0]
    prefix = jnp.where(own_second == 0, prefixes[0], prefixes[1])
    allowed = (key_second[:, None] == own_second[None, :]) & (
        (key_position[:, None] <= position[None, :]) | (key_position[:, None] < prefix[None, :])
    )
    bias = jnp.where(allowed, 0.0, MASKED).astype(F32)
    first_key = own_second[0] * lengths[0]
    last_key = jnp.max(own_second * lengths[0] + jnp.maximum(position, prefix - 1))
    span = jnp.stack(
        [first_key // KEY_BLOCK, last_key // KEY_BLOCK + 1, turn * count // KEY_BLOCK, turn]
    ).astype(jnp.int32)

    slots = 2 * RANK
    columns = jnp.arange(narrow, dtype=jnp.int32)
    slot = jnp.arange(slots, dtype=jnp.int32)
    slot_column = chosen_ids[slot // RANK] * RANK + slot % RANK
    pick = (columns[:, None] == slot_column[None, :]).astype(BF16)

    def seen_by(device):
        index = device * count + jnp.arange(count, dtype=jnp.int32)
        second = (index >= lengths[0]).astype(jnp.int32)
        return (second[:, None] == slot[None, :] // RANK).astype(F32)

    def pick_in(weight):
        return mm(weight, pick).astype(BF16)

    def pick_right(weight):
        return mm_tn(pick, weight).astype(BF16)

    seen = seen_by(member)
    seen_three = jnp.concatenate([seen, seen, seen], axis=1)
    qkv_in = jnp.concatenate([pick_in(query_in), pick_in(key_in), pick_in(value_in)], axis=1)
    asking = pick_right(asking_right_pieces)
    lookup = pick_right(lookup_right_pieces)
    content = pick_right(content_right_pieces)
    none = jnp.zeros_like(lookup)
    kv_right = jnp.concatenate(
        [jnp.concatenate([lookup, none], axis=1), jnp.concatenate([none, content], axis=1)], axis=0
    )
    out_in = pick_in(output_in)
    final = pick_right(final_right_pieces)
    lower = pick_right(lower_right_pieces)
    small = (
        jnp.concatenate([pick_in(gate_in), pick_in(up_in)], axis=1),
        pick_right(switch_right_pieces),
        pick_right(lift_right_pieces),
        lax.dot_general(
            pick, down_in, (((0,), (1,)), ((), ())), preferred_element_type=F32
        ).astype(BF16),
        lower,
    )

    incoming = tokens.astype(F32)
    scale_one = inverse_rms(incoming)
    norm1 = (incoming * scale_one * attn_gain).astype(BF16)
    if paired:
        norm1, transfers = tie(norm1, transfers)
        qkv_full, transfers = tie(qkv_full, steps.send(transfers))
        out_full = lax.all_gather(out_weight, "grp", axis=1, tiled=True)
        down_full = lax.all_gather(down_weight, "grp", axis=0)
    latent_qkv = (mm(norm1, qkv_in) * seen_three).astype(BF16)
    latent_q, latent_kv = latent_qkv[:, :slots], latent_qkv[:, slots:]
    half = HEAD_DIM // 2
    freqs = 10000.0 ** (-2.0 * jnp.arange(half).astype(F32) / HEAD_DIM)
    freqs = jnp.tile(freqs, LANES // half)
    angles = position.astype(F32)[:, None] * freqs[None, :]
    cosines, sines = jnp.cos(angles), jnp.sin(angles)

    def widen(table, size):
        return jnp.tile(table, (1, size // LANES))

    qkv = mm(norm1, qkv_full)
    query = qkv[:, :width] + LOWRANK_FACTOR * mm(latent_q, asking)
    own_kv = qkv[:, width:] + LOWRANK_FACTOR * mm(latent_kv, kv_right)
    query = rotate(query, widen(cosines, width), widen(sines, width)).astype(BF16)
    query = query * jnp.asarray(HEAD_DIM**-0.5, BF16)
    key_own = rotate(own_kv[:, :kv_width], widen(cosines, kv_width), widen(sines, kv_width))
    key_value = jnp.concatenate([key_own, own_kv[:, kv_width:]], axis=1).astype(BF16)
    if paired:
        key_value, transfers = tie(gather_key_values(key_value), steps.send(transfers))
    else:
        key_value = lax.all_gather(key_value, "grp", axis=0, tiled=True)
    attended_low, lse = attention_forward(span, query, key_value, bias)
    if paired:
        attended_low, transfers = tie(attended_low, steps.send(transfers))
        try:
            steps.send(transfers)
        except StopIteration as stop:
            far = stop.value

    latent_o = (mm(attended_low, out_in) * seen).astype(BF16)
    stream = incoming + (mm(attended_low, out_full) + LOWRANK_FACTOR * mm(latent_o, final))
    scale_two = inverse_rms(stream)
    norm2 = (stream * scale_two * mlp_gain).astype(BF16)
    if paired:
        response_part, dnorm2, latent_d, dlat_gu, deep = feed_forward_paired(
            norm2, sens, sens_near, own, far, down_full, small, seen, seen_by(member ^ CORE)
        )
    else:
        response_part, dnorm2, latent_d, dlat_gu, deep = feed_forward_alone(
            norm2, sens, gate_up_full, down_full, small, seen
        )
    level_response = (stream + response_part).astype(BF16)
    dhidden = sens.astype(F32) + norm_backward(stream, scale_two, mlp_gain, dnorm2)
    dbranch = dhidden.astype(BF16)
    dlat_o = (LOWRANK_FACTOR * mm_nt(dbranch, final) * seen).astype(BF16)
    dattended = (mm_nt(dbranch, out_full) + mm_nt(dlat_o, out_in)).astype(BF16)

    wide = jnp.concatenate(
        [
            LOWRANK_FACTOR * mm_tn(latent_d, sens),
            mm_tn(dlat_gu, norm2),
            mm_tn(dlat_o, attended_low),
            LOWRANK_FACTOR * mm_tn(latent_o, dbranch),
        ],
        axis=0,
    ).astype(BF16)
    deep_sum = lax.psum_scatter(deep, "grp", scatter_dimension=1, tiled=True)

    dq, dk_all, dv_all = attention_backward(
        span, query, dattended, attended_low, lse, key_value, bias, cosines, sines
    )
    dk_all, (deep_sum,) = tie(dk_all, (deep_sum,))
    dkv_all = jnp.concatenate([dk_all, dv_all], axis=1)
    dkv = exchange_sum(dkv_all.reshape(members, count, 2 * kv_width))
    dlat_q = (LOWRANK_FACTOR * mm_nt(dq, asking) * seen).astype(BF16)
    dnorm_q = mm_nt(dq, qkv_full[:, :width]) + mm_nt(dlat_q, qkv_in[:, :slots])
    late_q = jnp.concatenate(
        [mm_tn(dlat_q, norm1), LOWRANK_FACTOR * mm_tn(latent_q, dq)], axis=0
    ).astype(BF16)
    dk = unrotate(dkv[:, :kv_width], widen(cosines, kv_width), widen(sines, kv_width))
    dkv = jnp.concatenate([dk, dkv[:, kv_width:]], axis=1).astype(BF16)
    dlat_kv = (LOWRANK_FACTOR * mm_nt(dkv, kv_right) * seen_three[:, : 2 * slots]).astype(BF16)
    late_kv = mm_tn(dlat_kv, norm1).astype(BF16)
    thin = (
        LOWRANK_FACTOR
        * jnp.concatenate(
            [
                mm_tn(latent_kv[:, :slots], dkv[:, :kv_width]),
                mm_tn(latent_kv[:, slots:], dkv[:, kv_width:]),
            ],
            axis=0,
        )
    ).astype(BF16)

    def blocks(array):
        rows, size = array.shape
        return array.reshape(rows, members, size // members).transpose(1, 0, 2)

    share, thin_share = width // members, kv_width // members
    thin_rows = 2 * slots * thin_share // share
    late = jnp.concatenate(
        [
            blocks(jnp.concatenate([late_q, late_kv, wide], axis=0)),
            blocks(thin).reshape(members, thin_rows, share),
        ],
        axis=1,
    )
    late, (deep_sum,) = tie(late, (deep_sum,))
    late_sum = round_groups(exchange_sum(late).astype(BF16))
    deep_sum = round_groups(deep_sum)
    dnorm1 = dnorm_q + mm_nt(dkv, qkv_full[:, width:]) + mm_nt(dlat_kv, qkv_in[:, slots:])
    input_grad = (dhidden + norm_backward(incoming, scale_one, attn_gain, dnorm1)).astype(BF16)

    turn = jnp.arange(groups * slots, dtype=jnp.int32)
    source = (group - turn // slots) % groups
    all_column = adapter_ids[2 * source + turn % slots // RANK] * RANK + turn % RANK
    place = (all_column[:, None] == columns[None, :]).astype(BF16)

    def rows_of(arrays, index):
        return jnp.concatenate(
            [array[index * slots : (index + 1) * slots] for array in arrays], axis=0
        )

    def in_grad(arrays, index):
        return mm_tn(rows_of(arrays, index), place)

    def right_grad(arrays, index):
        return mm_tn(place, rows_of(arrays, index))

    thin_sum = [array[9 * slots :].reshape(2 * slots, thin_share) for array in late_sum]
    return (
        level_response,
        input_grad,
        in_grad(late_sum, 0),
        right_grad(late_sum, 1),
        in_grad(late_sum, 2),
        right_grad(thin_sum, 0),
        in_grad(late_sum, 3),
        right_grad(thin_sum, 1),
        in_grad(late_sum, 7),
        right_grad(late_sum, 8),
        in_grad(late_sum, 5),
        right_grad(deep_sum, 1),
        in_grad(late_sum, 6),
        right_grad(deep_sum, 2),
        in_grad(deep_sum, 0),
        right_grad(late_sum, 4),
    )


def solution(mesh):
    rows = P(("rep", "grp"), None)
    split = P(None, "grp")
    in_specs = (rows, rows, *[P()] * 5, *[split] * 4, *[P()] * 14)
    out_specs = (rows, rows, *[P("grp", None), P(None, "grp")] * 7)
    return jax.shard_map(shards, mesh=mesh, in_specs=in_specs, out_specs=out_specs, check_vma=False)
```

time: 847 us -> 560 us (0.66)
  waiting for transfers between devices: 400 us -> 204 us
  matrix products: 185 us -> 74.6 us
  Pallas kernels: 44.9 us -> 109 us
  local copies, waits for them, and re-layouts: 82.1 us -> 42.6 us
  blocking collectives: 33.8 us -> 0 us
  starting transfers between devices: 25.7 us -> 56.1 us
    all_gather x3 -> x1, waiting for transfers between devices: 309 us -> 11.5 us  [shards(): down_full = lax.all_gather(down_weight, 'grp', axis=0)]
    ppermute x0 -> x29, waiting for transfers between devices: none -> 169 us  [the longest x17 110 us: flip(): return lax.ppermute(array, 'grp', [(i, i ^ mask) for i in range(members)])]
    pallas_call x0 -> x1, Pallas kernels: none -> 55.3 us  [feed_forward_paired(): pl.pallas_call(feed_forward_kernel, out_shape=(jax.ShapeDtypeStruct((coun...]
    dot_general x27 -> x15, matrix products: 80.3 us -> 26.4 us  [mm(): return jnp.dot(left, right, preferred_element_type=F32)]
    dot_general x16 -> x11, matrix products: 71.5 us -> 18.2 us  [mm_nt(): lax.dot_general(left, right, (((1,), (1,)), ((), ())), preferred_element_...]
    all_gather x1, waiting for transfers between devices: 52.7 us -> 0.01 us  [shards(): qkv_full = lax.all_gather(qkv_weight, 'grp', axis=1, tiled=True)]
    all_gather x2 -> x0, blocking collectives: 33.8 us -> none  [the longest x1 19.8 us: shards(): early_all = lax.all_gather(early_sum, 'rep', axis=0)]
    ppermute x0 -> x29, starting transfers between devices: none -> 30.3 us  [the longest x17 14 us: flip(): return lax.ppermute(array, 'grp', [(i, i ^ mask) for i in range(members)])]
  transfers between devices with their start and end apart: 8 -> 35, of which waited for: 6 -> 15; matrix products, arithmetic and copies ran while one was open for 19% -> 23% of each run, Pallas kernels for 2% -> 10%
where the time goes in v3:
time: 560 us; the launch traced here: 553 us
  waiting for transfers between devices  204 us (36%)
  Pallas kernels  109 us (19%)
  matrix products  74.6 us (13%)
  starting transfers between devices  56.1 us (10%)
  other arithmetic  49.1 us (9%)
  local copies, waits for them, and re-layouts  42.6 us (8%)
  between operations  18.9 us (3%)
    ppermute x17, waiting for transfers between devices, flip(): return lax.ppermute(array, 'grp', [(i, i ^ mask) for i in range(members)])  110 us
    pallas_call x1, Pallas kernels, feed_forward_paired(): pl.pallas_call(feed_forward_kernel, out_shape=(jax.ShapeDtypeStruct((coun...  55.3 us
    ppermute x6, waiting for transfers between devices, flip_group(): return lax.ppermute(array, 'rep', [(i, i ^ 1) for i in range(groups)])  51.2 us
    pallas_call x1, Pallas kernels, attention_backward(): pl.pallas_call(attention_backward_kernel, out_shape=(jax.ShapeDtypeStruct...  35.8 us
    dot_general x30, matrix products, mm_tn(): lax.dot_general(left, right, (((0,), (0,)), ((), ())), preferred_element_...  27.3 us
    dot_general x15, matrix products, mm(): return jnp.dot(left, right, preferred_element_type=F32)  26.4 us
    all_to_all x2, starting transfers between devices, exchange_sum(): received = lax.all_to_all(parts.astype(BF16), 'grp', 0, 0, tiled=True)  25.6 us
    all_to_all x2, waiting for transfers between devices, exchange_sum(): received = lax.all_to_all(parts.astype(BF16), 'grp', 0, 0, tiled=True)  20.7 us
  transfers between devices with their start and end apart: 35, of which 15 were waited for; matrix products, arithmetic and copies ran while one was open for 23% of the time, Pallas kernels for 10%

profile of v3, /device:TPU:0, one launch (start us, length us, event | category | flops | bytes accessed | tf_op | source)
XLA Modules:
  0.0 553.5 jit_solution(11971170406945339862)
XLA Ops:
  9.5 5.4 constant_dynamic-slice_fusion
  14.9 2.9 collective-permute-start
  25.8 2.0 fusion.249
  28.4 1.9 compare_select_fusion.12
  35.8 1.9 multiply_cosine_fusion
  48.0 21.4 %collective-permute-done.refs_8_ = bf16[512,1408]{1,0:T(8,128)(2,1)} collective-permute-done((bf16[512,1408]{1,0:T(8,128)(2,1)}, bf16[512,1408]{1,0:T(8,128)(2,1)}, u32[]{:S(2)}, u32[]{:S(2)}) %collective-permute-start) | collective-permute-done | bytes 1441824 | tf_op jit(solution)/shard_map/ppermute | solution.py:313
  69.5 3.1 collective-permute-done.1.refs_4_
  72.6 2.5 collective-permute-start.3
  82.1 2.3 constant_dynamic-update-slice_fusion.9
  88.2 34.5 %collective-permute-done.2.refs_9_ = bf16[512,1408]{1,0:T(8,128)(2,1)} collective-permute-done((bf16[512,1408]{1,0:T(8,128)(2,1)}, bf16[512,1408]{1,0:T(8,128)(2,1)}, u32[]{:S(2)}, u32[]{:S(2)}) %collective-permute-start.2) | collective-permute-done | bytes 1441824 | tf_op jit(solution)/shard_map/ppermute | solution.py:313
  124.2 10.5 %collective-permute-done.5.refs_6_ = bf16[512,1408]{1,0:T(8,128)(2,1)} collective-permute-done((bf16[512,1408]{1,0:T(8,128)(2,1)}, bf16[512,1408]{1,0:T(8,128)(2,1)}, u32[]{:S(2)}, u32[]{:S(2)}) %collective-permute-start.5) | collective-permute-done | bytes 1441824 | tf_op jit(solution)/shard_map/ppermute | solution.py:318
  134.8 6.1 %fusion.316 = f32[256,2560]{1,0:T(8,128)S(1)} fusion(bf16[256,2048]{1,0:T(8,128)(2,1)} %fusion.26, bf16[2048,2560]{0,1:T(8,128)(2,1)} %all-gather.5.cloned.1.call-done), kind=kOutput, calls=%fused_computation.477 | convolution fusion | flops 2684354560 | bytes 14155776 | tf_op jit(solution)/shard_map/dot_general | solution.py:23
  143.4 1.7 collective-permute-start.7
  146.2 2.0 maximum_maximum_fusion
  148.2 1.7 collective-permute-start.13
  151.6 6.6 %collective-permute-done.7 = bf16[256,512]{1,0:T(8,128)(2,1)} collective-permute-done((bf16[256,512]{1,0:T(8,128)(2,1)}, bf16[256,512]{1,0:T(8,128)(2,1)}, u32[]{:S(2)}, u32[]{:S(2)}) %collective-permute-start.7) | collective-permute-done | bytes 262176 | tf_op jit(solution)/shard_map/ppermute | solution.py:313
  159.7 5.4 fusion.253
  166.6 2.7 convolution_convert_fusion.refs_20_.refs_21_
  169.3 42.3 %collective-permute-done.11 = bf16[256,512]{1,0:T(8,128)(2,1)S(1)} collective-permute-done((bf16[256,512]{1,0:T(8,128)(2,1)}, bf16[256,512]{1,0:T(8,128)(2,1)S(1)}, u32[]{:S(2)}, u32[]{:S(2)}) %collective-permute-start.11) | collective-permute-done | bytes 262176 | tf_op jit(solution)/shard_map/ppermute | solution.py:313
  211.6 2.1 slice_add_fusion.2
  222.0 2.9 fusion.51.q_ref
  225.0 17.4 %attention_forward.1 = (bf16[256,2048]{1,0:T(8,128)(2,1)S(1)}, f32[16,2,256]{2,1,0:T(2,128)S(1)}) custom-call(s32[4]{0:T(128)S(1)} %pad_add_fusion.span, bf16[256,2048]{1,0:T(8,128)(2,1)S(1)} %fusion.51.q_ref, bf16[2048,512]{1,0:T(8,128)(2,1)S(1)} %constant_dynamic-update-slice_fusion.key_ref.value_ref, ...), custom_call_target="tpu_custom_call" | custom-call | flops 4294967296 | bytes 18874368 | tf_op jit(solution)/shard_map/attention_forward/pallas_call | solution.py:143
  242.4 10.3 %collective-permute-done.17.refs_14_ = bf16[512,1408]{1,0:T(8,128)(2,1)S(1)} collective-permute-done((bf16[512,1408]{1,0:T(8,128)(2,1)}, bf16[512,1408]{1,0:T(8,128)(2,1)S(1)}, u32[]{:S(2)}, u32[]{:S(2)}) %collective-permute-start.17) | collective-permute-done | bytes 1441824 | tf_op jit(solution)/shard_map/ppermute | solution.py:318
  252.8 30.3 %collective-permute-done.18.refs_15_ = bf16[512,1408]{1,0:T(8,128)(2,1)S(1)} collective-permute-done((bf16[512,1408]{1,0:T(8,128)(2,1)}, bf16[512,1408]{1,0:T(8,128)(2,1)S(1)}, u32[]{:S(2)}, u32[]{:S(2)}) %collective-permute-start.18) | collective-permute-done | bytes 1441824 | tf_op jit(solution)/shard_map/ppermute | solution.py:318
  284.8 1.7 convolution_multiply_fusion.1
  286.6 6.6 %multiply_reduce_fusion.1 = (f32[256]{0:T(256)S(1)}, f32[256,2048]{1,0:T(8,128)S(1)}) fusion(f32[256,2048]{1,0:T(8,128)} %convolution_multiply_fusion.1, bf16[256,2048]{1,0:T(8,128)(2,1)S(1)} %copy-done.12, bf16[2048,2048]{1,0:T(8,128)(2,1)} %all-gather.7.cloned.1.call-done, bf16[256,2048]{1,0:T(8,128)(2,1)S(1)} %copy-done.24), kind=kOutput, calls=%fused_computation.80 | convolution fusion | flops 2150104832 | bytes 14681088 | tf_op jit(solution)/shard_map/dot_general | solution.py:23
  303.5 11.5 %all-gather.9.cloned.1.call-done = bf16[45056,256]{1,0:T(8,128)(2,1)} async-done(((bf16[5632,256]{1,0:T(8,128)(2,1)}), bf16[45056,256]{1,0:T(8,128)(2,1)}) %all-gather.9.cloned.1.call-update) | async-done | bytes 23068688 | tf_op jit(solution)/shard_map/all_gather | solution.py:747
  315.0 55.3 %feed_forward.1 = (f32[256,2176]{1,0:T(8,128)}, bf16[256,2176]{1,0:T(8,128)(2,1)}, f32[256,2176]{1,0:T(8,128)}, bf16[256,2176]{1,0:T(8,128)(2,1)}, bf16[2,96,1408]{2,1,0:T(8,128)(2,1)}) custom-call(s32[4]{0:T(128)} %pad_add_fusion.1.meta, bf16[512,2048]{1,0:T(8,128)(2,1)} %pad_maximum_fusion.x_ref, bf16[512,2048]{1,0:T(8,128)(2,1)} %copy-done.50, ...), custom_call_target="tpu_custom_call" | custom-call | flops 35433480192 | bytes 55574528 | tf_op jit(solution)/shard_map/feed_forward/pallas_call | solution.py:558
  372.0 1.9 copy.146
  374.2 2.0 convert_add_fusion.1
  377.2 2.3 subtract_add_fusion
  380.7 2.4 fusion.287
  385.4 35.8 %attention_backward.1 = (bf16[256,2048]{1,0:T(8,128)(2,1)S(1)}, bf16[2048,256]{1,0:T(8,128)(2,1)S(1)}, bf16[2048,256]{1,0:T(8,128)(2,1)S(1)}) custom-call(s32[4]{0:T(128)S(1)} %pad_add_fusion.span, bf16[256,2048]{1,0:T(8,128)(2,1)S(1)} %copy-done.10, bf16[256,2048]{1,0:T(8,128)(2,1)S(1)} %fusion.9.do_ref, bf16[256,2048]{1,0:T(8,128)(2,1)} %copy-done.11, ...), custom_call_target="tpu_custom_call" | custom-call | flops 10737418240 | bytes 30408704 | tf_op jit(solution)/shard_map/attention_backward/pallas_call | solution.py:272
  421.7 1.7 copy.147
  424.9 21.4 %all-to-all-start = ((bf16[8,256,512]{2,1,0:T(8,128)(2,1)}), bf16[8,256,512]{2,1,0:T(8,128)(2,1)}, u32[]{:S(2)}, u32[]{:S(2)}) async-start(bf16[8,256,512]{2,1,0:T(8,128)(2,1)} %bitcast.159), calls=%async_computation | async-start | bytes 4194304 | tf_op jit(solution)/shard_map/all_to_all | solution.py:618
  448.2 1.7 fusion.317
  454.5 18.6 %all-to-all-done = bf16[8,256,512]{2,1,0:T(8,128)(2,1)} async-done(((bf16[8,256,512]{2,1,0:T(8,128)(2,1)}), bf16[8,256,512]{2,1,0:T(8,128)(2,1)}, u32[]{:S(2)}, u32[]{:S(2)}) %all-to-all-start) | async-done | bytes 2097184 | tf_op jit(solution)/shard_map/all_to_all | solution.py:618
  473.1 1.9 convert_reduce_fusion
  478.0 1.8 fusion.15
  488.7 2.4 pad_maximum_fusion.2
  492.5 2.4 collective-permute-start.27
  496.5 3.8 fusion.38
  500.3 4.3 all-to-all-start.1
  504.6 7.1 %fusion.6 = f32[256,2048]{1,0:T(8,128)S(1)} fusion(f32[256,2048]{1,0:T(8,128)} %fusion.38, f32[256,2048]{1,0:T(8,128)} %fusion.317, bf16[256,2048]{1,0:T(8,128)(2,1)S(1)} %get-tuple-element.70, bf16[2048,2560]{0,1:T(8,128)(2,1)} %all-gather.5.cloned.1.call-done), kind=kOutput, calls=%fused_computation.18 | convolution fusion | flops 2148532224 | bytes 15728640 | tf_op jit(solution)/shard_map/dot_general | solution.py:27
  519.7 2.1 all-to-all-done.1
  524.5 2.7 collective-permute-start.25
  527.6 4.5 collective-permute-done.23
  532.3 3.7 collective-permute-done.24
  (444 shorter events, 115.0 us)
Async XLA Ops:
  7.2 287.7 %copy-start = (bf16[128,5632]{1,0:T(8,128)(2,1)S(1)}, bf16[128,5632]{1,0:T(8,128)(2,1)}, u32[]{:S(2)}) copy-start(bf16[128,5632]{1,0:T(8,128)(2,1)} %param.47) | copy-start | bytes 4325380
  7.2 127.6 %all-gather.5.cloned.1.call-start = ((), (), s32[]{:S(2)}) async-start(), calls=%async_computation.3 | async-start | bytes 11796480 | tf_op jit(solution)/shard_map/all_gather | solution.py:671
  7.9 278.6 %all-gather.7.cloned.1.call-start = ((), (), s32[]{:S(2)}) async-start(), calls=%async_computation.4 | async-start | bytes 9437184 | tf_op jit(solution)/shard_map/all_gather | solution.py:746
  8.7 306.3 %all-gather.9.cloned.1.call-start = ((), (), s32[]{:S(2)}) async-start(), calls=%async_computation.5 | async-start | bytes 25952256 | tf_op jit(solution)/shard_map/all_gather | solution.py:747
  9.4 412.3 %reduce-scatter.4.cloned.1.call-start = ((), (), s32[]{:S(2)}) async-start(), calls=%async_computation.6 | async-start | bytes 1622016
  14.9 54.6 %collective-permute-start = (bf16[512,1408]{1,0:T(8,128)(2,1)}, bf16[512,1408]{1,0:T(8,128)(2,1)}, u32[]{:S(2)}, u32[]{:S(2)}) collective-permute-start(bf16[512,1408]{1,0:T(8,128)(2,1)} %get-tuple-element.80.refs_0_), channel_id=1, source_target_pairs={{0,2},{1,3},{2,0},{3,1},{4,6},{5,7},{6,4},{7,5},{8,10},{9,11},{10,... | collective-permute-start | bytes 4325384 | tf_op jit(solution)/shard_map/ppermute | solution.py:313
  17.8 54.8 %collective-permute-start.1 = (bf16[512,1408]{1,0:T(8,128)(2,1)}, bf16[512,1408]{1,0:T(8,128)(2,1)}, u32[]{:S(2)}, u32[]{:S(2)}) collective-permute-start(bf16[512,1408]{1,0:T(8,128)(2,1)} %get-tuple-element.80.refs_0_), channel_id=1, source_target_pairs={{0,4},{1,5},{2,6},{3,7},{4,0},{5,1},{6,2},{7,3},{8,12},{9,13},{10,... | collective-permute-start | bytes 4325384 | tf_op jit(solution)/shard_map/ppermute | solution.py:313
  24.4 258.7 %copy-start.89 = (s32[256]{0:T(256)}, s32[256]{0:T(256)S(1)}, u32[]{:S(2)}) copy-start(s32[256]{0:T(256)S(1)} %fusion.262) | copy-start | bytes 3076
  43.9 38.2 %copy-start.96 = (f32[256]{0:T(256)}, f32[256]{0:T(256)S(1)}, u32[]{:S(2)}) copy-start(f32[256]{0:T(256)S(1)} %get-tuple-element.164) | copy-start | bytes 3076
  48.0 36.3 %copy-start.41 = (bf16[128,5632]{1,0:T(8,128)(2,1)S(1)}, bf16[128,5632]{1,0:T(8,128)(2,1)}, u32[]{:S(2)}) copy-start(bf16[128,5632]{1,0:T(8,128)(2,1)} %param.45) | copy-start | bytes 4325380
  72.6 50.2 %collective-permute-start.2 = (bf16[512,1408]{1,0:T(8,128)(2,1)}, bf16[512,1408]{1,0:T(8,128)(2,1)}, u32[]{:S(2)}, u32[]{:S(2)}) collective-permute-start(bf16[512,1408]{1,0:T(8,128)(2,1)} %get-tuple-element.48.refs_1_), channel_id=1, source_target_pairs={{0,2},{1,3},{2,0},{3,1},{4,6},{5,7},{6,4},{7,5},{8,10},{9,11},{10,... | collective-permute-start | bytes 4325384 | tf_op jit(solution)/shard_map/ppermute | solution.py:313
  72.6 51.6 %collective-permute-start.3 = (bf16[512,1408]{1,0:T(8,128)(2,1)}, bf16[512,1408]{1,0:T(8,128)(2,1)}, u32[]{:S(2)}, u32[]{:S(2)}) collective-permute-start(bf16[512,1408]{1,0:T(8,128)(2,1)} %get-tuple-element.48.refs_1_), channel_id=1, source_target_pairs={{0,4},{1,5},{2,6},{3,7},{4,0},{5,1},{6,2},{7,3},{8,12},{9,13},{10,... | collective-permute-start | bytes 4325384 | tf_op jit(solution)/shard_map/ppermute | solution.py:313
  75.1 49.1 %collective-permute-start.4 = (bf16[512,1408]{1,0:T(8,128)(2,1)}, bf16[512,1408]{1,0:T(8,128)(2,1)}, u32[]{:S(2)}, u32[]{:S(2)}) collective-permute-start(bf16[512,1408]{1,0:T(8,128)(2,1)} %collective-permute-done.refs_8_), channel_id=1, source_target_pairs={{0,8},{8,0},{16,24},{24,16},{1,9},{9,1},{17,25},{25,17},{2,10},{10... | collective-permute-start | bytes 4325384 | tf_op jit(solution)/shard_map/ppermute | solution.py:318
  76.5 58.2 %collective-permute-start.5 = (bf16[512,1408]{1,0:T(8,128)(2,1)}, bf16[512,1408]{1,0:T(8,128)(2,1)}, u32[]{:S(2)}, u32[]{:S(2)}) collective-permute-start(bf16[512,1408]{1,0:T(8,128)(2,1)} %collective-permute-done.1.refs_4_), channel_id=1, source_target_pairs={{0,8},{8,0},{16,24},{24,16},{1,9},{9,1},{17,25},{25,17},{2,10},{10... | collective-permute-start | bytes 4325384 | tf_op jit(solution)/shard_map/ppermute | solution.py:318
  86.9 138.0 %copy-start.2 = (f32[2048,256]{1,0:T(8,128)}, f32[2048,256]{1,0:T(8,128)S(1)}, u32[]{:S(2)}) copy-start(f32[2048,256]{1,0:T(8,128)S(1)} %and_select_fusion.bias_ref) | copy-start | bytes 6291460
  143.4 6.8 %collective-permute-start.6 = (bf16[256,512]{1,0:T(8,128)(2,1)}, bf16[256,512]{1,0:T(8,128)(2,1)}, u32[]{:S(2)}, u32[]{:S(2)}) collective-permute-start(bf16[256,512]{1,0:T(8,128)(2,1)} %get-tuple-element.101), channel_id=1, source_target_pairs={{0,1},{1,0},{2,3},{3,2},{4,5},{5,4},{6,7},{7,6},{8,9},{9,8},{10,11... | collective-permute-start | bytes 786440 | tf_op jit(solution)/shard_map/ppermute | solution.py:313
  143.4 14.8 %collective-permute-start.7 = (bf16[256,512]{1,0:T(8,128)(2,1)}, bf16[256,512]{1,0:T(8,128)(2,1)}, u32[]{:S(2)}, u32[]{:S(2)}) collective-permute-start(bf16[256,512]{1,0:T(8,128)(2,1)} %get-tuple-element.101), channel_id=1, source_target_pairs={{0,2},{1,3},{2,0},{3,1},{4,6},{5,7},{6,4},{7,5},{8,10},{9,11},{10,... | collective-permute-start | bytes 786440 | tf_op jit(solution)/shard_map/ppermute | solution.py:313
  145.2 19.9 %collective-permute-start.9 = (bf16[256,512]{1,0:T(8,128)(2,1)}, bf16[256,512]{1,0:T(8,128)(2,1)}, u32[]{:S(2)}, u32[]{:S(2)}) collective-permute-start(bf16[256,512]{1,0:T(8,128)(2,1)} %get-tuple-element.101), channel_id=1, source_target_pairs={{0,4},{1,5},{2,6},{3,7},{4,0},{5,1},{6,2},{7,3},{8,12},{9,13},{10,... | collective-permute-start | bytes 786440 | tf_op jit(solution)/shard_map/ppermute | solution.py:313
  148.2 69.9 %collective-permute-start.13 = (bf16[512,1408]{1,0:T(8,128)(2,1)}, bf16[512,1408]{1,0:T(8,128)(2,1)}, u32[]{:S(2)}, u32[]{:S(2)}) collective-permute-start(bf16[512,1408]{1,0:T(8,128)(2,1)} %collective-permute-done.refs_8_), channel_id=1, source_target_pairs={{0,4},{1,5},{2,6},{3,7},{4,0},{5,1},{6,2},{7,3},{8,12},{9,13},{10,... | collective-permute-start | bytes 4325384 | tf_op jit(solution)/shard_map/ppermute | solution.py:313
  149.9 68.1 %collective-permute-start.14 = (bf16[512,1408]{1,0:T(8,128)(2,1)}, bf16[512,1408]{1,0:T(8,128)(2,1)}, u32[]{:S(2)}, u32[]{:S(2)}) collective-permute-start(bf16[512,1408]{1,0:T(8,128)(2,1)} %collective-permute-done.3.refs_5_), channel_id=1, source_target_pairs={{0,2},{1,3},{2,0},{3,1},{4,6},{5,7},{6,4},{7,5},{8,10},{9,11},{10,... | collective-permute-start | bytes 4325384 | tf_op jit(solution)/shard_map/ppermute | solution.py:313
  150.2 67.9 %collective-permute-start.16 = (bf16[512,1408]{1,0:T(8,128)(2,1)}, bf16[512,1408]{1,0:T(8,128)(2,1)}, u32[]{:S(2)}, u32[]{:S(2)}) collective-permute-start(bf16[512,1408]{1,0:T(8,128)(2,1)} %collective-permute-done.3.refs_5_), channel_id=1, source_target_pairs={{0,8},{8,0},{16,24},{24,16},{1,9},{9,1},{17,25},{25,17},{2,10},{10... | collective-permute-start | bytes 4325384 | tf_op jit(solution)/shard_map/ppermute | solution.py:318
  158.2 59.8 %collective-permute-start.15 = (bf16[512,1408]{1,0:T(8,128)(2,1)}, bf16[512,1408]{1,0:T(8,128)(2,1)}, u32[]{:S(2)}, u32[]{:S(2)}) collective-permute-start(bf16[512,1408]{1,0:T(8,128)(2,1)} %collective-permute-done.2.refs_9_), channel_id=1, source_target_pairs={{0,8},{8,0},{16,24},{24,16},{1,9},{9,1},{17,25},{25,17},{2,10},{10... | collective-permute-start | bytes 4325384 | tf_op jit(solution)/shard_map/ppermute | solution.py:318
  165.1 46.4 %collective-permute-start.11 = (bf16[256,512]{1,0:T(8,128)(2,1)}, bf16[256,512]{1,0:T(8,128)(2,1)S(1)}, u32[]{:S(2)}, u32[]{:S(2)}) collective-permute-start(bf16[256,512]{1,0:T(8,128)(2,1)} %get-tuple-element.101), channel_id=1, source_target_pairs={{0,6},{1,7},{2,4},{3,5},{4,2},{5,3},{6,0},{7,1},{8,14},{9,15},{10,... | collective-permute-start | bytes 786440 | tf_op jit(solution)/shard_map/ppermute | solution.py:313
  169.3 45.0 %copy-start.14 = (bf16[2048,512]{1,0:T(8,128)(2,1)S(1)}, bf16[2048,512]{1,0:T(8,128)(2,1)}, u32[]{:S(2)}) copy-start(bf16[2048,512]{1,0:T(8,128)(2,1)} %get-tuple-element.102) | copy-start | bytes 6291460
  211.6 2.1 collective-permute-start.8
  213.7 2.5 collective-permute-start.10
  216.3 1.6 collective-permute-start.12
  217.9 78.4 %collective-permute-start.20 = (bf16[256,2048]{1,0:T(8,128)(2,1)}, bf16[256,2048]{1,0:T(8,128)(2,1)}, u32[]{:S(2)}, u32[]{:S(2)}) collective-permute-start(bf16[256,2048]{1,0:T(8,128)(2,1)} %param.26), channel_id=1, source_target_pairs={{0,1},{1,0},{2,3},{3,2},{4,5},{5,4},{6,7},{7,6},{8,9},{9,8},{10,11... | collective-permute-start | bytes 3145736 | tf_op jit(solution)/shard_map/ppermute | solution.py:313
  218.1 34.7 %collective-permute-start.17 = (bf16[512,1408]{1,0:T(8,128)(2,1)}, bf16[512,1408]{1,0:T(8,128)(2,1)S(1)}, u32[]{:S(2)}, u32[]{:S(2)}) collective-permute-start(bf16[512,1408]{1,0:T(8,128)(2,1)} %collective-permute-done.13.refs_12_), channel_id=1, source_target_pairs={{0,8},{8,0},{16,24},{24,16},{1,9},{9,1},{17,25},{25,17},{2,10},{10... | collective-permute-start | bytes 4325384 | tf_op jit(solution)/shard_map/ppermute | solution.py:318
  219.5 63.7 %collective-permute-start.18 = (bf16[512,1408]{1,0:T(8,128)(2,1)}, bf16[512,1408]{1,0:T(8,128)(2,1)S(1)}, u32[]{:S(2)}, u32[]{:S(2)}) collective-permute-start(bf16[512,1408]{1,0:T(8,128)(2,1)} %collective-permute-done.14.refs_13_), channel_id=1, source_target_pairs={{0,8},{8,0},{16,24},{24,16},{1,9},{9,1},{17,25},{25,17},{2,10},{10... | collective-permute-start | bytes 4325384 | tf_op jit(solution)/shard_map/ppermute | solution.py:318
  224.9 58.2 %copy-start.67 = (bf16[32,2048]{1,0:T(8,128)(2,1)S(1)}, bf16[32,2048]{1,0:T(8,128)(2,1)}, u32[]{:S(2)}) copy-start(bf16[32,2048]{1,0:T(8,128)(2,1)} %convolution_convert_fusion.7) | copy-start | bytes 393220
  225.0 58.2 %copy-start.102 = (s32[32]{0:T(128)S(1)}, s32[32]{0:T(128)}, u32[]{:S(2)}) copy-start(s32[32]{0:T(128)} %copy-done.101) | copy-start | bytes 388
  225.0 59.9 %copy-start.42 = (bf16[32,2048]{1,0:T(8,128)(2,1)S(1)}, bf16[32,2048]{1,0:T(8,128)(2,1)}, u32[]{:S(2)}) copy-start(bf16[32,2048]{1,0:T(8,128)(2,1)} %convolution_convert_fusion.14) | copy-start | bytes 393220
  242.4 40.7 %copy-start.11 = (bf16[256,2048]{1,0:T(8,128)(2,1)}, bf16[256,2048]{1,0:T(8,128)(2,1)S(1)}, u32[]{:S(2)}) copy-start(bf16[256,2048]{1,0:T(8,128)(2,1)S(1)} %get-tuple-element.58.o_ref) | copy-start | bytes 3145732
  242.4 41.1 %copy-start.16 = (f32[16,2,256]{2,1,0:T(2,128)}, f32[16,2,256]{2,1,0:T(2,128)S(1)}, u32[]{:S(2)}) copy-start(f32[16,2,256]{2,1,0:T(2,128)S(1)} %get-tuple-element.69.lse_ref) | copy-start | bytes 98308
  242.4 44.1 %copy-start.24 = (bf16[256,2048]{1,0:T(8,128)(2,1)S(1)}, bf16[256,2048]{1,0:T(8,128)(2,1)}, u32[]{:S(2)}) copy-start(bf16[256,2048]{1,0:T(8,128)(2,1)} %param.25) | copy-start | bytes 3145732
  294.6 4.9 collective-permute-start.19
  370.3 3.9 collective-permute-start.22
  373.9 76.0 %collective-permute-start.21 = (bf16[256,2176]{1,0:T(8,128)(2,1)}, bf16[256,2176]{1,0:T(8,128)(2,1)}, u32[]{:S(2)}, u32[]{:S(2)}) collective-permute-start(bf16[256,2176]{1,0:T(8,128)(2,1)} %get-tuple-element.66), channel_id=1, source_target_pairs={{0,1},{1,0},{2,3},{3,2},{4,5},{5,4},{6,7},{7,6},{8,9},{9,8},{10,11... | collective-permute-start | bytes 3342344 | tf_op jit(solution)/shard_map/ppermute | solution.py:313
  385.4 35.8 %copy-start.66 = (bf16[32,2048]{1,0:T(8,128)(2,1)S(1)}, bf16[32,2048]{1,0:T(8,128)(2,1)}, u32[]{:S(2)}) copy-start(bf16[32,2048]{1,0:T(8,128)(2,1)} %convolution_convert_fusion.15) | copy-start | bytes 393220
  424.9 48.2 %all-to-all-start = ((bf16[8,256,512]{2,1,0:T(8,128)(2,1)}), bf16[8,256,512]{2,1,0:T(8,128)(2,1)}, u32[]{:S(2)}, u32[]{:S(2)}) async-start(bf16[8,256,512]{2,1,0:T(8,128)(2,1)} %bitcast.159), calls=%async_computation | async-start | bytes 4194304 | tf_op jit(solution)/shard_map/all_to_all | solution.py:618
  491.0 22.9 %collective-permute-start.26 = (bf16[96,704]{1,0:T(8,128)(2,1)S(1)}, bf16[96,704]{1,0:T(8,128)(2,1)}, u32[]{:S(2)}, u32[]{:S(2)}) collective-permute-start(bf16[96,704]{1,0:T(8,128)(2,1)S(1)} %copy-done.47), channel_id=1, source_target_pairs={{0,8},{8,16},{16,24},{24,0},{1,9},{9,17},{17,25},{25,1},{2,10},{10... | collective-permute-start | bytes 405512 | tf_op jit(solution)/shard_map/ppermute | solution.py:625
  492.5 22.3 %collective-permute-start.27 = (bf16[96,704]{1,0:T(8,128)(2,1)S(1)}, bf16[96,704]{1,0:T(8,128)(2,1)}, u32[]{:S(2)}, u32[]{:S(2)}) collective-permute-start(bf16[96,704]{1,0:T(8,128)(2,1)S(1)} %copy-done.47), channel_id=1, source_target_pairs={{0,16},{8,24},{16,0},{24,8},{1,17},{9,25},{17,1},{25,9},{2,18},{10... | collective-permute-start | bytes 405512 | tf_op jit(solution)/shard_map/ppermute | solution.py:625
  494.9 20.8 %collective-permute-start.28 = (bf16[96,704]{1,0:T(8,128)(2,1)S(1)}, bf16[96,704]{1,0:T(8,128)(2,1)}, u32[]{:S(2)}, u32[]{:S(2)}) collective-permute-start(bf16[96,704]{1,0:T(8,128)(2,1)S(1)} %copy-done.47), channel_id=1, source_target_pairs={{0,24},{8,0},{16,8},{24,16},{1,25},{9,1},{17,9},{25,17},{2,26},{10... | collective-permute-start | bytes 405512 | tf_op jit(solution)/shard_map/ppermute | solution.py:625
  500.3 21.4 %all-to-all-start.1 = ((bf16[8,296,256]{2,1,0:T(8,128)(2,1)}), bf16[8,296,256]{2,1,0:T(8,128)(2,1)}, u32[]{:S(2)}, u32[]{:S(2)}) async-start(bf16[8,296,256]{2,1,0:T(8,128)(2,1)} %pad_maximum_fusion.2), calls=%async_computation.1 | async-start | bytes 2424832 | tf_op jit(solution)/shard_map/all_to_all | solution.py:618
  523.3 8.8 %collective-permute-start.23 = (bf16[296,256]{1,0:T(8,128)(2,1)S(1)}, bf16[296,256]{1,0:T(8,128)(2,1)S(1)}, u32[]{:S(2)}, u32[]{:S(2)}) collective-permute-start(bf16[296,256]{1,0:T(8,128)(2,1)S(1)} %reduce_sum.62), channel_id=1, source_target_pairs={{0,8},{8,16},{16,24},{24,0},{1,9},{9,17},{17,25},{25,1},{2,10},{10... | collective-permute-start | bytes 454664 | tf_op jit(solution)/shard_map/ppermute | solution.py:625
  523.9 12.1 %collective-permute-start.24 = (bf16[296,256]{1,0:T(8,128)(2,1)S(1)}, bf16[296,256]{1,0:T(8,128)(2,1)S(1)}, u32[]{:S(2)}, u32[]{:S(2)}) collective-permute-start(bf16[296,256]{1,0:T(8,128)(2,1)S(1)} %reduce_sum.62), channel_id=1, source_target_pairs={{0,16},{8,24},{16,0},{24,8},{1,17},{9,25},{17,1},{25,9},{2,18},{10... | collective-permute-start | bytes 454664 | tf_op jit(solution)/shard_map/ppermute | solution.py:625
  524.5 11.7 %collective-permute-start.25 = (bf16[296,256]{1,0:T(8,128)(2,1)S(1)}, bf16[296,256]{1,0:T(8,128)(2,1)S(1)}, u32[]{:S(2)}, u32[]{:S(2)}) collective-permute-start(bf16[296,256]{1,0:T(8,128)(2,1)S(1)} %reduce_sum.62), channel_id=1, source_target_pairs={{0,24},{8,0},{16,8},{24,16},{1,25},{9,1},{17,9},{25,17},{2,26},{10... | collective-permute-start | bytes 454664 | tf_op jit(solution)/shard_map/ppermute | solution.py:625
  (105 other events, 569.4 us)
Sparse Core Ops, SparseCore 0:
  9.9 105.3 all-gather.4
  117.2 76.9 all-gather.6
  196.0 118.9 all-gather.8
  374.0 37.9 reduce-scatter.3

commit v4 on v3

v4 whole, which is shorter than its diff:
```python
import functools

import jax
import jax.numpy as jnp
from jax import lax
from jax.experimental import pallas as pl
from jax.experimental.pallas import tpu as pltpu
from jax.sharding import PartitionSpec as P

HEADS = 32
KV_HEADS = 4
HEAD_DIM = 64
RANK = 16
LANES = 128
KEY_BLOCK = 1024
PAIRS = 4

EPS = 1e-05
LOWRANK_FACTOR = 2.0
MASKED = -1e30
F32 = jnp.float32
BF16 = jnp.bfloat16


def mm(left, right):
    return jnp.dot(left, right, preferred_element_type=F32)


def mm_nt(left, right):
    return lax.dot_general(left, right, (((1,), (1,)), ((), ())), preferred_element_type=F32)


def mm_tn(left, right):
    return lax.dot_general(left, right, (((0,), (0,)), ((), ())), preferred_element_type=F32)


def inverse_rms(value):
    return lax.rsqrt(jnp.mean(value * value, axis=-1, keepdims=True) + EPS)


def norm_backward(value, scale, gain, grad):
    scaled = gain * grad
    return scale * scaled - value * (scale * scale * scale) * jnp.mean(
        scaled * value, axis=-1, keepdims=True
    )


def half_turn(value):
    half = HEAD_DIM // 2
    lane = lax.broadcasted_iota(jnp.int32, value.shape, 1) % HEAD_DIM
    return jnp.where(
        lane < half, -jnp.roll(value, -half, axis=1), jnp.roll(value, half, axis=1)
    )


def rotate(value, cosines, sines):
    return value * cosines + half_turn(value) * sines


def unrotate(grad, cosines, sines):
    return grad * cosines - half_turn(grad * sines)


def lane_of(shape):
    return lax.broadcasted_iota(jnp.int32, shape, 1)


def key_rows(span, index):
    return pl.ds(pl.multiple_of((index ^ span[2]) * KEY_BLOCK, KEY_BLOCK), KEY_BLOCK)


def spread_heads(span, odd, source_ref, pair_ref):
    def step(index, carry):
        rows = key_rows(span, index)
        value = source_ref[rows, :].astype(F32)
        turned = pltpu.roll(value, HEAD_DIM, 1)
        low = lane_of(value.shape) < HEAD_DIM
        none = jnp.zeros_like(value)
        pair_ref[0, rows, :] = jnp.where(low, jnp.where(odd, turned, value), none).astype(BF16)
        pair_ref[1, rows, :] = jnp.where(low, none, jnp.where(odd, value, turned)).astype(BF16)
        return carry

    lax.fori_loop(span[0], span[1], step, 0)


def attention_forward_kernel(
    per_kv, span, q_ref, key_ref, value_ref, bias_ref, out_ref, lse_ref, k_ref, v_ref
):
    tokens = q_ref.shape[0]
    odd = lax.rem(pl.program_id(0) // per_kv, LANES // HEAD_DIM) == 1

    @pl.when(lax.rem(pl.program_id(0), per_kv) == 0)
    def _():
        spread_heads(span, odd, key_ref, k_ref)
        spread_heads(span, odd, value_ref, v_ref)

    queries = [q_ref[:, pair * LANES : (pair + 1) * LANES] for pair in range(PAIRS)]

    def step(index, carry):
        rows = key_rows(span, index)
        bias = bias_ref[rows, :]
        new = []
        for pair, (peaks, totals, mixed) in enumerate(carry):
            tops, sums, parts, decays = [], [], [], []
            for side in range(2):
                scores = mm_nt(k_ref[side, rows, :], queries[pair]) + bias
                top = jnp.maximum(peaks[side], jnp.max(scores, axis=0, keepdims=True))
                decay = jnp.exp(peaks[side] - top)
                probs = jnp.exp(scores - top)
                tops.append(top)
                sums.append(totals[side] * decay + jnp.sum(probs, axis=0, keepdims=True))
                decays.append(jnp.broadcast_to(decay, (HEAD_DIM, tokens)))
                parts.append(mm_tn(v_ref[side, rows, :], probs.astype(BF16)))
            mixed = mixed * jnp.concatenate(decays, axis=0) + (parts[0] + parts[1])
            new.append((tuple(tops), tuple(sums), mixed))
        return tuple(new)

    low = jnp.full((1, tokens), MASKED, F32)
    none = jnp.zeros((1, tokens), F32)
    start = ((low, low), (none, none), jnp.zeros((LANES, tokens), F32))
    result = lax.fori_loop(span[0], span[1], step, (start,) * PAIRS)
    for pair, (peaks, totals, mixed) in enumerate(result):
        weight = jnp.concatenate(
            [jnp.broadcast_to(1.0 / total, (HEAD_DIM, tokens)) for total in totals], axis=0
        )
        out_ref[:, pair * LANES : (pair + 1) * LANES] = (mixed * weight).T.astype(BF16)
        lse_ref[pair] = jnp.concatenate(
            [peak + jnp.log(total) for peak, total in zip(peaks, totals)], axis=0
        )


def key_value_specs(keys, per_kv):
    blocks = KV_HEADS * HEAD_DIM // LANES
    heads = LANES // HEAD_DIM
    return [
        pl.BlockSpec((keys, LANES), lambda j, s: (0, j // per_kv // heads)),
        pl.BlockSpec((keys, LANES), lambda j, s: (0, blocks + j // per_kv // heads)),
    ]


def attention_forward(span, query, key_value, bias):
    tokens, width = query.shape
    keys = bias.shape[0]
    pairs = width // LANES
    steps = pairs // PAIRS
    pair_spec = pl.BlockSpec((tokens, PAIRS * LANES), lambda j, s: (0, j))
    return pl.pallas_call(
        functools.partial(attention_forward_kernel, steps // KV_HEADS),
        out_shape=(
            jax.ShapeDtypeStruct((tokens, width), BF16),
            jax.ShapeDtypeStruct((pairs, 2, tokens), F32),
        ),
        grid_spec=pltpu.PrefetchScalarGridSpec(
            num_scalar_prefetch=1,
            grid=(steps,),
            in_specs=[
                pair_spec,
                *key_value_specs(keys, steps // KV_HEADS),
                pl.BlockSpec((keys, tokens), lambda j, s: (0, 0)),
            ],
            out_specs=(pair_spec, pl.BlockSpec((PAIRS, 2, tokens), lambda j, s: (j, 0, 0))),
            scratch_shapes=[pltpu.VMEM((2, keys, LANES), BF16)] * 2,
        ),
        compiler_params=pltpu.CompilerParams(
            dimension_semantics=("arbitrary",), vmem_limit_bytes=40 << 20
        ),
        cost_estimate=pl.CostEstimate(
            flops=4 * tokens * keys * width,
            transcendentals=tokens * keys * HEADS // 2,
            bytes_accessed=4 * tokens * width + 16 * keys * LANES * KV_HEADS,
        ),
        name="attention_forward",
    )(span, query, key_value, key_value, bias)


def attention_backward_kernel(
    per_kv,
    span,
    q_ref,
    do_ref,
    o_ref,
    lse_ref,
    key_ref,
    value_ref,
    bias_ref,
    cos_ref,
    sin_ref,
    dq_ref,
    dkv_ref,
    k_ref,
    v_ref,
    dk_sum,
    dv_sum,
):
    tokens = q_ref.shape[0]
    member = lax.rem(pl.program_id(0), per_kv)
    odd = lax.rem(pl.program_id(0) // per_kv, LANES // HEAD_DIM) == 1

    @pl.when(member == 0)
    def _():
        spread_heads(span, odd, key_ref, k_ref)
        spread_heads(span, odd, value_ref, v_ref)
        dk_sum[...] = jnp.zeros_like(dk_sum)
        dv_sum[...] = jnp.zeros_like(dv_sum)

    low = lane_of((tokens, LANES)) < HEAD_DIM
    row = lax.broadcasted_iota(jnp.int32, (8, LANES), 0)
    column = lax.broadcasted_iota(jnp.int32, (8, LANES), 1)
    chooser = jnp.where(row == column // HEAD_DIM, 1.0, 0.0).astype(F32)
    queries, grads, deltas, query_stack, grad_stack = [], [], [], [], []
    for pair in range(PAIRS):
        lanes = slice(pair * LANES, (pair + 1) * LANES)
        query, grad = q_ref[:, lanes], do_ref[:, lanes]
        none = jnp.zeros_like(query)
        queries.append(query)
        grads.append(grad)
        query_stack += [jnp.where(low, query, none), jnp.where(low, none, query)]
        grad_stack += [jnp.where(low, grad, none), jnp.where(low, none, grad)]
        deltas.append(
            lax.dot_general(
                chooser,
                grad.astype(F32) * o_ref[:, lanes].astype(F32),
                (((1,), (1,)), ((), ())),
                precision=lax.Precision.HIGHEST,
                preferred_element_type=F32,
            )
        )
    query_stack = jnp.concatenate(query_stack, axis=0)
    grad_stack = jnp.concatenate(grad_stack, axis=0)

    def step(index, dqueries):
        rows = key_rows(span, index)
        bias = bias_ref[rows, :]
        all_probs, all_dscores, new = [], [], []
        for pair, dquery in enumerate(dqueries):
            for side in range(2):
                scores = mm_nt(k_ref[side, rows, :], queries[pair]) + bias
                probs = jnp.exp(scores - lse_ref[pair, side : side + 1, :])
                dprobs = mm_nt(v_ref[side, rows, :], grads[pair])
                delta = deltas[pair][side : side + 1, :]
                dscores = (probs * (dprobs - delta)).astype(BF16)
                all_probs.append(probs.astype(BF16))
                all_dscores.append(dscores)
                dquery = dquery + mm_tn(k_ref[side, rows, :], dscores)
            new.append(dquery)
        dk_sum[rows, :] += mm(jnp.concatenate(all_dscores, axis=1), query_stack)
        dv_sum[rows, :] += mm(jnp.concatenate(all_probs, axis=1), grad_stack)
        return tuple(new)

    dqueries = lax.fori_loop(
        span[0], span[1], step, (jnp.zeros((LANES, tokens), F32),) * PAIRS
    )
    half = HEAD_DIM // 2
    for pair, dquery in enumerate(dqueries):
        dquery = dquery.T * (HEAD_DIM**-0.5)
        turned = dquery * sin_ref[...]
        first = lax.rem(lane_of(turned.shape), HEAD_DIM) < half
        turned = jnp.where(
            first, pltpu.roll(turned, LANES - half, 1), -pltpu.roll(turned, half, 1)
        )
        dq_ref[:, pair * LANES : (pair + 1) * LANES] = (dquery * cos_ref[...] + turned).astype(BF16)

    @pl.when(member == per_kv - 1)
    def _():
        block = pl.program_id(0) // per_kv // (LANES // HEAD_DIM)

        def put(index, carry):
            target = index ^ span[3]
            for sum_ref, first in ((dk_sum, 0), (dv_sum, KV_HEADS * HEAD_DIM // LANES)):
                total = sum_ref[pl.ds(pl.multiple_of(index * tokens, tokens), tokens), :]
                total = total + pltpu.roll(total, HEAD_DIM, 1)
                keep = jnp.logical_and(odd, lane_of(total.shape) < HEAD_DIM)
                lanes = pl.ds(pl.multiple_of((first + block) * LANES, LANES), LANES)
                dkv_ref[target, :, lanes] = jnp.where(
                    keep, dkv_ref[target, :, lanes], total.astype(BF16)
                )
            return carry

        lax.fori_loop(0, dkv_ref.shape[0], put, 0)


def attention_backward(span, query, grad, attended, lse, key_value, bias, cosines, sines):
    tokens, width = query.shape
    keys, kv_two = key_value.shape
    pairs = width // LANES
    steps = pairs // PAIRS
    per_kv = steps // KV_HEADS
    pair_spec = pl.BlockSpec((tokens, PAIRS * LANES), lambda j, s: (0, j))
    table_spec = pl.BlockSpec((tokens, LANES), lambda j, s: (0, 0))
    return pl.pallas_call(
        functools.partial(attention_backward_kernel, per_kv),
        out_shape=(
            jax.ShapeDtypeStruct((tokens, width), BF16),
            jax.ShapeDtypeStruct((keys // tokens, tokens, kv_two), BF16),
        ),
        grid_spec=pltpu.PrefetchScalarGridSpec(
            num_scalar_prefetch=1,
            grid=(steps,),
            in_specs=[
                pair_spec,
                pair_spec,
                pair_spec,
                pl.BlockSpec((PAIRS, 2, tokens), lambda j, s: (j, 0, 0)),
                *key_value_specs(keys, per_kv),
                pl.BlockSpec((keys, tokens), lambda j, s: (0, 0)),
                table_spec,
                table_spec,
            ],
            out_specs=(
                pair_spec,
                pl.BlockSpec((keys // tokens, tokens, kv_two), lambda j, s: (0, 0, 0)),
            ),
            scratch_shapes=[pltpu.VMEM((2, keys, LANES), BF16)] * 2
            + [pltpu.VMEM((keys, LANES), F32)] * 2,
        ),
        compiler_params=pltpu.CompilerParams(
            dimension_semantics=("arbitrary",), vmem_limit_bytes=48 << 20
        ),
        cost_estimate=pl.CostEstimate(
            flops=10 * tokens * keys * width,
            transcendentals=tokens * keys * HEADS // 2,
            bytes_accessed=10 * tokens * width + 8 * keys * kv_two,
        ),
        name="attention_backward",
    )(span, query, grad, attended, lse, key_value, key_value, bias, cosines, sines)


CORE, ACROSS_X, ACROSS_Y = 1, 2, 4


def flip(array, mask):
    members = lax.axis_size("grp")
    return lax.ppermute(array, "grp", [(i, i ^ mask) for i in range(members)])


def flip_group(array):
    groups = lax.axis_size("rep")
    return lax.ppermute(array, "rep", [(i, i ^ 1) for i in range(groups)])


def gather_hidden_block(gate_up_weight, down_weight):
    rows = gate_up_weight.shape[0] // 4
    block = gate_up_weight.shape[1]
    member = lax.axis_index("grp")
    parity = lax.axis_index("rep") % 2
    own = [
        lax.dynamic_slice_in_dim(gate_up_weight, ((parity ^ (q // 2)) * 2 + q % 2) * rows, rows, 0)
        for q in range(4)
    ]

    def down_rows(mask):
        start = ((member ^ mask) % ACROSS_Y) * block
        return lax.dynamic_slice_in_dim(down_weight, start, block, 0)

    low, next_quarter, *near = yield (
        flip(own[0], ACROSS_Y),
        own[1],
        flip(down_rows(ACROSS_X), ACROSS_X),
        flip(down_rows(CORE), CORE),
        flip(down_rows(ACROSS_X | CORE), ACROSS_X | CORE),
    )
    down_own = jnp.stack([down_rows(0), near[1], near[0], near[2]])
    high, low_other, down_own = yield flip(next_quarter, ACROSS_Y), flip_group(low), down_own
    mine, second = (
        lax.dynamic_slice_in_dim(down_own, 2 * parity + index, 1, 0) for index in range(2)
    )
    down_mine, high_other, second = yield flip(mine, ACROSS_Y), flip_group(high), second
    down_second, down_other = yield flip(second, ACROSS_Y), flip_group(down_mine)
    (second_other,) = yield (flip_group(down_second),)
    return {
        "own": own,
        "over_y": (low, high, low_other, high_other),
        "down": (down_own, down_mine, down_second, down_other, second_other),
    }


def gather_key_values(own):
    over_y = flip(own, ACROSS_Y)
    pieces = [own, flip(own, ACROSS_X), over_y, flip(over_y, ACROSS_X)]
    return jnp.concatenate(
        [part for piece in pieces for part in (piece, flip(piece, CORE))], axis=0
    )


def tie(value, transfers):
    value, *transfers = lax.optimization_barrier((value, *transfers))
    return value, tuple(transfers)


def feed_forward_alone(norm2, sens, gate_up_full, down_full, small, seen):
    ffn_in, switch, lift, down_in, lower = small
    slots, hidden_width = switch.shape
    seen_two = jnp.concatenate([seen, seen], axis=1)
    latent_gu = (mm(norm2, ffn_in) * seen_two).astype(BF16)
    latent_g, latent_u = latent_gu[:, :slots], latent_gu[:, slots:]
    gate_up = mm(norm2, gate_up_full) + LOWRANK_FACTOR * jnp.concatenate(
        [mm(latent_g, switch), mm(latent_u, lift)], axis=1
    )
    gate = gate_up[:, :hidden_width]
    up = gate_up[:, hidden_width:]
    sigma = jax.nn.sigmoid(gate)
    act = (gate * sigma * up).astype(BF16)
    latent_d = (mm_nt(act, down_in) * seen).astype(BF16)
    response_part = mm(act, down_full) + LOWRANK_FACTOR * mm(latent_d, lower)
    dlat_d = (LOWRANK_FACTOR * mm_nt(sens, lower) * seen).astype(BF16)
    dact = mm_nt(sens, down_full) + mm(dlat_d, down_in)
    dgate = (dact * up * (sigma * (1.0 + gate * (1.0 - sigma)))).astype(BF16)
    dup = (dact * gate * sigma).astype(BF16)
    dlat_gu = (
        LOWRANK_FACTOR
        * jnp.concatenate([mm_nt(dgate, switch), mm_nt(dup, lift)], axis=1)
        * seen_two
    ).astype(BF16)
    dnorm2 = (
        mm_nt(dgate, gate_up_full[:, :hidden_width])
        + mm_nt(dup, gate_up_full[:, hidden_width:])
        + mm_nt(dlat_gu, ffn_in)
    )
    deep = jnp.concatenate(
        [
            mm_tn(dlat_d, act),
            LOWRANK_FACTOR * mm_tn(latent_g, dgate),
            LOWRANK_FACTOR * mm_tn(latent_u, dup),
        ],
        axis=0,
    ).astype(BF16)
    members = lax.axis_size("grp")
    deep = deep.reshape(3 * slots, members, hidden_width // members).transpose(1, 0, 2)
    return response_part, dnorm2, latent_d, dlat_gu, deep


def feed_forward_kernel(
    meta,
    own_x,
    near_x,
    own_g,
    near_g,
    own_seen,
    near_seen,
    lower_ref,
    switch_ref,
    lift_ref,
    in_ref,
    *refs,
):
    whole_refs, whole_down = refs[:8], refs[8:13]
    back_own, back_near, front_own, front_near, deep_ref = refs[13:18]
    x_turned, g_turned, latents, dlats, stack, acts, firsts, seconds, dacts, dlat_sum = refs[18:28]
    kept, kept_down, semaphores = refs[28:]
    count, width = own_g.shape
    tokens = 2 * count
    slots, block = in_ref.shape
    quarter = width // 4
    part = width // kept_down.shape[0]
    parity = meta[0]
    owns_gate = meta[1] == 1
    member = meta[2]
    starts = [
        pl.multiple_of((parity if q < 2 else 1 - parity) * (width // 2) + (q % 2) * quarter, quarter)
        for q in range(4)
    ]
    bases = [0, 1, 2, 3, *(4 + 2 * parity + k for k in (0, 1)), *(6 - 2 * parity + k for k in (0, 1))]
    columns = [pl.ds(pl.multiple_of((member ^ base) * part, part), part) for base in bases]
    down_copies = [
        pltpu.make_async_copy(ref, kept_down.at[pl.ds(start, size)], semaphores.at[8 + index])
        for index, (ref, start, size) in enumerate(zip(whole_down, (0, 4, 5, 6, 7), (4, 1, 1, 1, 1)))
    ]
    copies = [
        pltpu.make_async_copy(ref, kept.at[index], semaphores.at[index])
        for index, ref in enumerate(whole_refs)
    ]
    for copy in down_copies + copies:
        copy.start()
    dlat_sum[...] = jnp.zeros_like(dlat_sum)
    for index, (x_ref, g_ref, seen_ref) in enumerate(
        ((own_x, own_g, own_seen), (near_x, near_g, near_seen))
    ):
        rows = slice(index * count, (index + 1) * count)
        for q in range(4):
            x_turned[rows, q * quarter : (q + 1) * quarter] = x_ref[:, pl.ds(starts[q], quarter)]
        for k, lanes in enumerate(columns):
            g_turned[rows, k * part : (k + 1) * part] = g_ref[:, lanes]
        latents[rows, :] = x_ref[:, width : width + 2 * slots]
        dlat = LOWRANK_FACTOR * mm_nt(g_ref[...], lower_ref[...]) * seen_ref[...]
        dlats[rows, :] = dlat.astype(BF16)
        stack[:slots, rows] = dlat.T.astype(BF16)
        latent = x_ref[:, width : width + LANES].astype(F32).T[: 2 * slots]
        stack[slots:, rows] = latent.astype(BF16)

    def dact_part(start, size):
        here = pl.ds(start, size)
        down = jnp.concatenate([kept_down[k, here, :] for k in range(len(columns))], axis=1)
        dacts[:, here] = mm_nt(g_turned[...], down) + mm(dlats[...], in_ref[:, here])

    def dact_step(index, carry):
        dact_part(pl.multiple_of(index * 2 * LANES, 2 * LANES), 2 * LANES)
        return carry

    for copy in down_copies:
        copy.wait()
    lax.fori_loop(0, block // (2 * LANES), dact_step, 0)
    if block % (2 * LANES):
        dact_part(block // (2 * LANES) * 2 * LANES, block % (2 * LANES))
    for copy in copies:
        copy.wait()

    def hidden_part(start, size):
        here = pl.ds(start, size)
        none = jnp.zeros((slots, size), BF16)
        switch, lift = switch_ref[:, here], lift_ref[:, here]
        pieces = jnp.where(
            owns_gate,
            jnp.concatenate(
                [jnp.concatenate([switch, none], axis=1), jnp.concatenate([none, lift], axis=1)],
                axis=0,
            ),
            jnp.concatenate(
                [jnp.concatenate([none, switch], axis=1), jnp.concatenate([lift, none], axis=1)],
                axis=0,
            ),
        )
        weight = jnp.concatenate(
            [
                jnp.concatenate([kept[q, :, here], kept[4 + q, :, here]], axis=1)
                for q in range(4)
            ],
            axis=0,
        )
        total = mm(x_turned[...], weight)
        total = total + LOWRANK_FACTOR * mm(latents[...], pieces)
        gate = jnp.where(owns_gate, total[:, :size], total[:, size:])
        up = jnp.where(owns_gate, total[:, size:], total[:, :size])
        sigma = jax.nn.sigmoid(gate)
        act = (gate * sigma * up).astype(BF16)
        dact = dacts[:, here]
        dgate = (dact * up * (sigma * (1.0 + gate * (1.0 - sigma)))).astype(BF16)
        dup = (dact * gate * sigma).astype(BF16)
        dfirst, dsecond = jnp.where(owns_gate, dgate, dup), jnp.where(owns_gate, dup, dgate)
        acts[:, here] = act
        firsts[:, here] = dfirst
        seconds[:, here] = dsecond
        both = jnp.concatenate([dfirst, dsecond], axis=1)
        dlat_sum[:, : 2 * slots] += mm_nt(both, pieces)
        piece_grad = LOWRANK_FACTOR * mm(stack[slots:, :], both)
        low, high = piece_grad[:, :size], piece_grad[:, size:]
        deep_ref[:slots, here] = mm(stack[:slots, :], act)
        deep_ref[slots : 2 * slots, here] = jnp.where(owns_gate, low, high)[:slots]
        deep_ref[2 * slots :, here] = jnp.where(owns_gate, high, low)[slots:]

    def hidden_step(index, carry):
        hidden_part(pl.multiple_of(index * 2 * LANES, 2 * LANES), 2 * LANES)
        return carry

    lax.fori_loop(0, block // (2 * LANES), hidden_step, 0)
    if block % (2 * LANES):
        hidden_part(block // (2 * LANES) * 2 * LANES, block % (2 * LANES))

    def back(q, carry):
        value = mm_nt(firsts[...], kept[q]) + mm_nt(seconds[...], kept[4 + q])
        start = ((q // 2) ^ parity) * (width // 2) + lax.rem(q, 2) * quarter
        lanes = pl.ds(pl.multiple_of(start, quarter), quarter)
        back_own[:, lanes] = value[:count]
        back_near[:, lanes] = value[count:].astype(BF16)
        return carry

    def front(index, carry):
        value = mm(acts[...], kept_down[index])
        half = (index - 4) // 2 ^ parity
        base = jnp.where(index < 4, index, 4 + 2 * half + lax.rem(index, 2))
        lanes = pl.ds(pl.multiple_of((member ^ base) * part, part), part)
        front_own[:, lanes] = value[:count].astype(front_own.dtype)
        front_near[:, lanes] = value[count:].astype(BF16)
        return carry

    lax.fori_loop(0, 4, back, 0)
    lax.fori_loop(0, kept_down.shape[0], front, 0)
    back_own[:, width:] = dlat_sum[:count, :]
    back_near[:, width:] = dlat_sum[count:, :].astype(BF16)
    latent = mm_nt(acts[...], in_ref[...])
    latent = jnp.concatenate([latent, jnp.zeros((tokens, LANES - slots), F32)], axis=1)
    front_own[:, width:] = latent[:count, :].astype(front_own.dtype)
    front_near[:, width:] = latent[count:, :].astype(BF16)


def feed_forward_pair(meta, rows, sens, seen, weights, pieces, front_type):
    count, width = sens[0].shape
    slots, block = pieces[-1].shape
    wide, tokens = width + LANES, 2 * count
    operands = (*rows, *sens, *seen, *pieces)
    arrays = (*weights["own"], *weights["over_y"], *weights["down"])
    return pl.pallas_call(
        feed_forward_kernel,
        out_shape=(
            jax.ShapeDtypeStruct((count, wide), F32),
            jax.ShapeDtypeStruct((count, wide), BF16),
            jax.ShapeDtypeStruct((count, wide), front_type),
            jax.ShapeDtypeStruct((count, wide), BF16),
            jax.ShapeDtypeStruct((3 * slots, block), F32),
        ),
        in_specs=[pl.BlockSpec(memory_space=pltpu.SMEM)]
        + [pl.BlockSpec(memory_space=pltpu.VMEM)] * len(operands)
        + [pl.BlockSpec(memory_space=pl.ANY)] * len(arrays),
        scratch_shapes=[
            pltpu.VMEM((tokens, width), BF16),
            pltpu.VMEM((tokens, width), BF16),
            pltpu.VMEM((tokens, 2 * slots), BF16),
            pltpu.VMEM((tokens, slots), BF16),
            pltpu.VMEM((3 * slots, tokens), BF16),
            pltpu.VMEM((tokens, block), BF16),
            pltpu.VMEM((tokens, block), BF16),
            pltpu.VMEM((tokens, block), BF16),
            pltpu.VMEM((tokens, block), F32),
            pltpu.VMEM((tokens, LANES), F32),
            pltpu.VMEM((8, width // 4, block), BF16),
            pltpu.VMEM((8, block, width // 8), BF16),
            pltpu.SemaphoreType.DMA((13,)),
        ],
        compiler_params=pltpu.CompilerParams(vmem_limit_bytes=46 << 20),
        cost_estimate=pl.CostEstimate(
            flops=2 * 6 * tokens * width * block,
            transcendentals=tokens * block,
            bytes_accessed=6 * width * block + 20 * tokens * width,
        ),
        name="feed_forward",
    )(meta, *operands, *arrays)


def feed_forward_shared(norm2, sens_pairs, weights, small, seen_by):
    ffn_in, switch, lift, down_in, lower = small
    width = norm2.shape[1]
    slots, hidden_width = switch.shape
    block = weights["own"][0].shape[1]
    member = lax.axis_index("grp")
    parity = lax.axis_index("rep") % 2
    owns_gate = member < ACROSS_Y
    hidden = member % ACROSS_Y

    meta = jnp.stack([parity, owns_gate.astype(jnp.int32), member]).astype(jnp.int32)
    pieces = (
        lower,
        *(
            lax.dynamic_slice_in_dim(piece, hidden * block, block, 1)
            for piece in (switch, lift, down_in)
        ),
    )
    seen = seen_by(member)
    seen_two = jnp.concatenate([seen, seen], axis=1)
    latent_gu = (mm(norm2, ffn_in) * seen_two).astype(BF16)
    pad = jnp.zeros((norm2.shape[0], LANES - 2 * slots), BF16)
    rows = jnp.concatenate([norm2, latent_gu, pad], axis=1)
    across = flip(rows, ACROSS_X)
    results = []
    for index, sens_pair in enumerate(sens_pairs):
        first = member ^ (index * ACROSS_X)
        if index == 1:
            result, (across,) = tie(results[0][1], (across,))
            results[0][1] = result
            rows = across
        seen_pair = (seen_by(first), seen_by(first ^ CORE))
        row_pair = (rows, flip(rows, CORE))
        results.append(
            list(
                feed_forward_pair(
                    meta, row_pair, sens_pair, seen_pair, weights, pieces, (F32, BF16)[index]
                )
            )
        )

    chips = [result[0] + flip(result[1], CORE).astype(F32) for result in results]
    deep = (results[0][4] + results[1][4]).astype(BF16)
    members = lax.axis_size("grp")
    owners = members * block // hidden_width
    deep = deep.reshape(3 * slots, owners, block // owners).transpose(1, 0, 2)
    placed = jnp.zeros((members, 3 * slots, block // owners), BF16)
    placed = lax.dynamic_update_slice_in_dim(placed, deep, hidden * owners, 0)
    across, (placed,) = tie(flip(chips[1].astype(BF16), ACROSS_X), (placed,))
    backward = chips[0] + across.astype(F32)
    dlat_gu = (LOWRANK_FACTOR * backward[:, width : width + 2 * slots] * seen_two).astype(BF16)
    dnorm2 = backward[:, :width] + mm_nt(dlat_gu, ffn_in)
    forwards = [part for result in results for part in result[2:4]]
    dnorm2, forwards = tie(dnorm2, forwards)
    forward = forwards[0]
    for part, mask in zip(forwards[1:], (CORE, ACROSS_X, ACROSS_X | CORE)):
        forward = forward + flip(part, mask).astype(F32)
    latent_d = (forward[:, width : width + slots] * seen).astype(BF16)
    response_part = forward[:, :width] + LOWRANK_FACTOR * mm(latent_d, lower)
    return response_part, dnorm2, latent_d, dlat_gu, placed


def exchange_sum(parts):
    received = lax.all_to_all(parts.astype(BF16), "grp", 0, 0, tiled=True)
    return jnp.sum(received.astype(F32), axis=0)


def simple_call(kernel, name, out_shape, operands, flops):
    return pl.pallas_call(
        kernel,
        out_shape=out_shape,
        compiler_params=pltpu.CompilerParams(vmem_limit_bytes=32 << 20),
        cost_estimate=pl.CostEstimate(
            flops=flops,
            transcendentals=0,
            bytes_accessed=sum(array.size * array.dtype.itemsize for array in operands),
        ),
        name=name,
    )(*operands)


def early_gradients_kernel(
    dq_ref,
    asking_ref,
    seen_ref,
    latent_q_ref,
    norm1_ref,
    latent_d_ref,
    sens_ref,
    dlat_gu_ref,
    norm2_ref,
    dlat_o_ref,
    attended_ref,
    latent_o_ref,
    dbranch_ref,
    dlat_q_ref,
    early_ref,
):
    dlat_q = (LOWRANK_FACTOR * mm_nt(dq_ref[...], asking_ref[...]) * seen_ref[...]).astype(BF16)
    dlat_q_ref[...] = dlat_q
    two = LOWRANK_FACTOR
    start = 0
    for factor, small, large in (
        (1.0, dlat_q, norm1_ref),
        (two, latent_q_ref[...], dq_ref),
        (two, latent_d_ref[...], sens_ref),
        (1.0, dlat_gu_ref[...], norm2_ref),
        (1.0, dlat_o_ref[...], attended_ref),
        (two, latent_o_ref[...], dbranch_ref),
    ):
        rows = small.shape[1]
        early_ref[start : start + rows, :] = (factor * mm_tn(small, large[...])).astype(BF16)
        start += rows


def early_gradients(*operands):
    count, width = operands[0].shape
    slots = operands[1].shape[0]
    return simple_call(
        early_gradients_kernel,
        "early_gradients",
        (
            jax.ShapeDtypeStruct((count, slots), BF16),
            jax.ShapeDtypeStruct((7 * slots, width), BF16),
        ),
        operands,
        2 * count * width * 8 * slots,
    )


def key_value_gradients_kernel(
    received_ref,
    early_ref,
    cos_ref,
    sin_ref,
    right_ref,
    seen_ref,
    latent_ref,
    norm_ref,
    dkv_ref,
    dlat_ref,
    pack_ref,
):
    half = HEAD_DIM // 2
    total = received_ref[0].astype(F32)
    for source in range(1, received_ref.shape[0]):
        total = total + received_ref[source].astype(F32)
    kv_width = total.shape[1] // 2
    pieces = []
    for start in range(0, kv_width, LANES):
        value = total[:, start : start + LANES]
        turned = value * sin_ref[...]
        first = lax.rem(lane_of(turned.shape), HEAD_DIM) < half
        turned = jnp.where(
            first, pltpu.roll(turned, LANES - half, 1), -pltpu.roll(turned, half, 1)
        )
        pieces.append((value * cos_ref[...] + turned).astype(BF16))
    dkv = jnp.concatenate([*pieces, total[:, kv_width:].astype(BF16)], axis=1)
    dkv_ref[...] = dkv
    dlat = (LOWRANK_FACTOR * mm_nt(dkv, right_ref[...]) * seen_ref[...]).astype(BF16)
    dlat_ref[...] = dlat
    late = mm_tn(dlat, norm_ref[...]).astype(BF16)
    thin = (LOWRANK_FACTOR * mm_tn(latent_ref[...], dkv)).astype(BF16)
    rows, head = late.shape[0], early_ref.shape[0]
    thin = jnp.concatenate([thin[: rows // 2, :kv_width], thin[rows // 2 :, kv_width:]], axis=0)
    share = pack_ref.shape[2]
    for target in range(pack_ref.shape[0]):
        columns = slice(target * share, (target + 1) * share)
        pack_ref[target, :head, :] = early_ref[:, columns]
        pack_ref[target, head : head + rows, :] = late[:, columns]
        for index, start in enumerate(range(0, kv_width, share)):
            place = head + (index + 1) * rows
            pack_ref[target, place : place + rows, :] = thin[:, start : start + share]


def key_value_gradients(received, early, cosines, sines, kv_right, seen_two, latent_kv, norm1):
    members, count, kv_two = received.shape
    rows = kv_right.shape[0]
    share = norm1.shape[1] // members
    packed = early.shape[0] + rows * (1 + kv_two // 2 // share)
    return simple_call(
        key_value_gradients_kernel,
        "key_value_gradients",
        (
            jax.ShapeDtypeStruct((count, kv_two), BF16),
            jax.ShapeDtypeStruct((count, rows), BF16),
            jax.ShapeDtypeStruct((members, packed, share), BF16),
        ),
        (received, early, cosines, sines, kv_right, seen_two, latent_kv, norm1),
        2 * count * rows * (norm1.shape[1] + 2 * kv_two),
    )


def place_kernel(jobs, groups, slots, *refs):
    place_ref, refs = refs[0], refs[1:]
    outs = refs[len(refs) - len(jobs) :]
    for (source, index, is_right), out_ref in zip(jobs, outs):
        value = jnp.concatenate(
            [
                refs[source * groups + g][index * slots : (index + 1) * slots, :]
                for g in range(groups)
            ],
            axis=0,
        )
        if is_right:
            out_ref[...] = mm_tn(place_ref[...], value)
        else:
            out_ref[...] = mm_tn(value, place_ref[...])


def place_gradients(place, sources, slots, jobs):
    groups = len(sources[0])
    narrow = place.shape[1]
    shapes = []
    for source, _, is_right in jobs:
        size = sources[source][0].shape[1]
        shapes.append(
            jax.ShapeDtypeStruct((narrow, size) if is_right else (size, narrow), F32)
        )
    return pl.pallas_call(
        functools.partial(place_kernel, jobs, groups, slots),
        out_shape=tuple(shapes),
        compiler_params=pltpu.CompilerParams(vmem_limit_bytes=32 << 20),
        cost_estimate=pl.CostEstimate(
            flops=2 * sum(shape.size for shape in shapes) * place.shape[0],
            transcendentals=0,
            bytes_accessed=4 * sum(shape.size for shape in shapes),
        ),
        name="place_gradients",
    )(place, *[array for source in sources for array in source])


def round_groups(array):
    groups = lax.axis_size("rep")
    return [array] + [
        lax.ppermute(array, "rep", [(i, (i + shift) % groups) for i in range(groups)])
        for shift in range(1, groups)
    ]


def shards(
    tokens,
    response_sensitivity,
    seq_lengths,
    prefix_lengths,
    adapter_ids,
    attn_gain,
    mlp_gain,
    qkv_weight,
    out_weight,
    gate_up_weight,
    down_weight,
    query_in,
    asking_right_pieces,
    key_in,
    lookup_right_pieces,
    value_in,
    content_right_pieces,
    output_in,
    final_right_pieces,
    gate_in,
    switch_right_pieces,
    up_in,
    lift_right_pieces,
    down_in,
    lower_right_pieces,
):
    count, width = tokens.shape
    members = lax.axis_size("grp")
    groups = lax.axis_size("rep")
    kv_width = lookup_right_pieces.shape[1]
    narrow = query_in.shape[1]
    group = lax.axis_index("rep")
    member = lax.axis_index("grp")
    lengths = lax.dynamic_slice_in_dim(seq_lengths, 2 * group, 2)
    prefixes = lax.dynamic_slice_in_dim(prefix_lengths, 2 * group, 2)
    chosen_ids = lax.dynamic_slice_in_dim(adapter_ids, 2 * group, 2)
    key_count = count * members
    sens = response_sensitivity

    paired = members == 8 and groups % 2 == 0
    qkv_full = lax.all_gather(qkv_weight, "grp", axis=1, tiled=True)
    if paired:
        steps = gather_hidden_block(gate_up_weight, down_weight)
        transfers = next(steps)
    else:
        out_full = lax.all_gather(out_weight, "grp", axis=1, tiled=True)
        down_full = lax.all_gather(down_weight, "grp", axis=1, tiled=True)
        gate_up_full = lax.all_gather(gate_up_weight, "grp", axis=1, tiled=True)

    turn = member if paired else 0
    key_index = jnp.arange(key_count, dtype=jnp.int32)
    key_index = (key_index // count ^ turn) * count + key_index % count
    key_second = (key_index >= lengths[0]).astype(jnp.int32)
    key_position = key_index - key_second * lengths[0]
    own_index = member * count + jnp.arange(count, dtype=jnp.int32)
    own_second = (own_index >= lengths[0]).astype(jnp.int32)
    position = own_index - own_second * lengths[0]
    prefix = jnp.where(own_second == 0, prefixes[0], prefixes[1])
    allowed = (key_second[:, None] == own_second[None, :]) & (
        (key_position[:, None] <= position[None, :]) | (key_position[:, None] < prefix[None, :])
    )
    bias = jnp.where(allowed, 0.0, MASKED).astype(F32)
    first_key = own_second[0] * lengths[0]
    last_key = jnp.max(own_second * lengths[0] + jnp.maximum(position, prefix - 1))
    span = jnp.stack(
        [first_key // KEY_BLOCK, last_key // KEY_BLOCK + 1, turn * count // KEY_BLOCK, turn]
    ).astype(jnp.int32)

    slots = 2 * RANK
    columns = jnp.arange(narrow, dtype=jnp.int32)
    slot = jnp.arange(slots, dtype=jnp.int32)
    slot_column = chosen_ids[slot // RANK] * RANK + slot % RANK
    pick = (columns[:, None] == slot_column[None, :]).astype(BF16)

    def seen_by(device):
        index = device * count + jnp.arange(count, dtype=jnp.int32)
        second = (index >= lengths[0]).astype(jnp.int32)
        return (second[:, None] == slot[None, :] // RANK).astype(F32)

    def pick_in(weight):
        return mm(weight, pick).astype(BF16)

    def pick_right(weight):
        return mm_tn(pick, weight).astype(BF16)

    seen = seen_by(member)
    seen_three = jnp.concatenate([seen, seen, seen], axis=1)
    qkv_in = jnp.concatenate([pick_in(query_in), pick_in(key_in), pick_in(value_in)], axis=1)
    asking = pick_right(asking_right_pieces)
    lookup = pick_right(lookup_right_pieces)
    content = pick_right(content_right_pieces)
    none = jnp.zeros_like(lookup)
    kv_right = jnp.concatenate(
        [jnp.concatenate([lookup, none], axis=1), jnp.concatenate([none, content], axis=1)], axis=0
    )
    out_in = pick_in(output_in)
    final = pick_right(final_right_pieces)
    lower = pick_right(lower_right_pieces)
    small = (
        jnp.concatenate([pick_in(gate_in), pick_in(up_in)], axis=1),
        pick_right(switch_right_pieces),
        pick_right(lift_right_pieces),
        lax.dot_general(
            pick, down_in, (((0,), (1,)), ((), ())), preferred_element_type=F32
        ).astype(BF16),
        lower,
    )

    incoming = tokens.astype(F32)
    scale_one = inverse_rms(incoming)
    norm1 = (incoming * scale_one * attn_gain).astype(BF16)
    if paired:
        norm1, transfers = tie(norm1, transfers)
        transfers = steps.send(transfers)
        out_full = lax.all_gather(out_weight, "grp", axis=1, tiled=True)
    latent_qkv = (mm(norm1, qkv_in) * seen_three).astype(BF16)
    latent_q, latent_kv = latent_qkv[:, :slots], latent_qkv[:, slots:]
    half = HEAD_DIM // 2
    freqs = 10000.0 ** (-2.0 * jnp.arange(half).astype(F32) / HEAD_DIM)
    freqs = jnp.tile(freqs, LANES // half)
    angles = position.astype(F32)[:, None] * freqs[None, :]
    cosines, sines = jnp.cos(angles), jnp.sin(angles)

    def widen(table, size):
        return jnp.tile(table, (1, size // LANES))

    qkv = mm(norm1, qkv_full)
    query = qkv[:, :width] + LOWRANK_FACTOR * mm(latent_q, asking)
    own_kv = qkv[:, width:] + LOWRANK_FACTOR * mm(latent_kv, kv_right)
    query = rotate(query, widen(cosines, width), widen(sines, width)).astype(BF16)
    query = query * jnp.asarray(HEAD_DIM**-0.5, BF16)
    key_own = rotate(own_kv[:, :kv_width], widen(cosines, kv_width), widen(sines, kv_width))
    key_value = jnp.concatenate([key_own, own_kv[:, kv_width:]], axis=1).astype(BF16)
    if paired:
        key_value, transfers = tie(key_value, transfers)
        key_value, (ready, *transfers) = tie(gather_key_values(key_value), (sens, *transfers))
        transfers = steps.send(transfers)
        sens_near, sens_across = flip(ready, CORE), flip(ready, ACROSS_X)
    else:
        key_value = lax.all_gather(key_value, "grp", axis=0, tiled=True)
    attended_low, lse = attention_forward(span, query, key_value, bias)
    if paired:
        attended_low, (sens_near, sens_across, *transfers) = tie(
            attended_low, (sens_near, sens_across, *transfers)
        )
        sens_pairs = [(sens, sens_near), (sens_across, flip(sens_across, CORE))]
        out_full, transfers = tie(out_full, steps.send(transfers))
        transfers = steps.send(transfers)

    latent_o = (mm(attended_low, out_in) * seen).astype(BF16)
    stream = incoming + (mm(attended_low, out_full) + LOWRANK_FACTOR * mm(latent_o, final))
    scale_two = inverse_rms(stream)
    norm2 = (stream * scale_two * mlp_gain).astype(BF16)
    if paired:
        norm2, transfers = tie(norm2, transfers)
        try:
            steps.send(transfers)
        except StopIteration as stop:
            weights = stop.value
        response_part, dnorm2, latent_d, dlat_gu, deep = feed_forward_shared(
            norm2, sens_pairs, weights, small, seen_by
        )
    else:
        response_part, dnorm2, latent_d, dlat_gu, deep = feed_forward_alone(
            norm2, sens, gate_up_full, down_full, small, seen
        )
    level_response = (stream + response_part).astype(BF16)
    dhidden = sens.astype(F32) + norm_backward(stream, scale_two, mlp_gain, dnorm2)
    dbranch = dhidden.astype(BF16)
    dlat_o = (LOWRANK_FACTOR * mm_nt(dbranch, final) * seen).astype(BF16)
    dattended = (mm_nt(dbranch, out_full) + mm_nt(dlat_o, out_in)).astype(BF16)

    dattended, (deep,) = tie(dattended, (deep,))
    deep_sum = lax.psum_scatter(deep, "grp", scatter_dimension=0, tiled=True)[0]

    dq, dkv_all = attention_backward(
        span, query, dattended, attended_low, lse, key_value, bias, cosines, sines
    )
    dkv_all, (deep_sum,) = tie(dkv_all, (deep_sum,))
    received = lax.all_to_all(dkv_all, "grp", 0, 0, tiled=True)
    dlat_q, early = early_gradients(
        dq,
        asking,
        seen,
        latent_q,
        norm1,
        latent_d,
        sens,
        dlat_gu,
        norm2,
        dlat_o,
        attended_low,
        latent_o,
        dbranch,
    )
    dnorm_q = mm_nt(dq, qkv_full[:, :width]) + mm_nt(dlat_q, qkv_in[:, :slots])
    dkv, dlat_kv, late = key_value_gradients(
        received, early, cosines, sines, kv_right, seen_three[:, : 2 * slots], latent_kv, norm1
    )
    deep_sum = round_groups(deep_sum)
    late_sum = round_groups(exchange_sum(late).astype(BF16))
    dnorm1 = dnorm_q + mm_nt(dkv, qkv_full[:, width:]) + mm_nt(dlat_kv, qkv_in[:, slots:])
    input_grad = (dhidden + norm_backward(incoming, scale_one, attn_gain, dnorm1)).astype(BF16)

    cycle = jnp.arange(groups * slots, dtype=jnp.int32)
    source = (group - cycle // slots) % groups
    all_column = adapter_ids[2 * source + cycle % slots // RANK] * RANK + cycle % RANK
    place = (all_column[:, None] == columns[None, :]).astype(BF16)
    share = width // members
    pieces = kv_width // share
    thin_start = 9 * slots
    thin_sum = [
        jnp.concatenate(
            [
                array[thin_start + 2 * slots * i : thin_start + 2 * slots * (i + 1)]
                for i in range(pieces)
            ],
            axis=1,
        )
        for array in late_sum
    ]
    jobs = (
        (0, 0, False),
        (0, 1, True),
        (0, 7, False),
        (2, 0, True),
        (0, 8, False),
        (2, 1, True),
        (0, 5, False),
        (0, 6, True),
        (0, 3, False),
        (1, 1, True),
        (0, 4, False),
        (1, 2, True),
        (1, 0, False),
        (0, 2, True),
    )
    grads = list(place_gradients(place, (late_sum, deep_sum, thin_sum), slots, jobs))
    own = kv_width // members
    for index in (3, 5):
        grads[index] = lax.dynamic_slice_in_dim(grads[index], member * own, own, 1)
    return (level_response, input_grad, *grads)


def solution(mesh):
    rows = P(("rep", "grp"), None)
    split = P(None, "grp")
    in_specs = (rows, rows, *[P()] * 5, *[split] * 4, *[P()] * 14)
    out_specs = (rows, rows, *[P("grp", None), P(None, "grp")] * 7)
    return jax.shard_map(shards, mesh=mesh, in_specs=in_specs, out_specs=out_specs, check_vma=False)
```

time: 560 us -> 517 us (0.923)
  waiting for transfers between devices: 204 us -> 158 us
  Pallas kernels: 109 us -> 133 us
  matrix products: 74.6 us -> 50.8 us
  local copies, waits for them, and re-layouts: 42.6 us -> 53.3 us
  starting transfers between devices: 56.1 us -> 49.3 us
    ppermute x6 -> x4, waiting for transfers between devices: 51.2 us -> 9.21 us  [flip_group(): return lax.ppermute(array, 'rep', [(i, i ^ 1) for i in range(groups)])]
    pallas_call x3 -> x7, Pallas kernels: 109 us -> 133 us  [the longest x2 68.1 us: feed_forward_pair(): pl.pallas_call(feed_forward_kernel, out_shape=(jax.ShapeDtypeStruct((coun...]
    all_gather x1, waiting for transfers between devices: 0.01 us -> 23.9 us  [shards(): qkv_full = lax.all_gather(qkv_weight, 'grp', axis=1, tiled=True)]
    dot_general x30 -> x7, matrix products: 27.3 us -> 6 us  [mm_tn(): lax.dot_general(left, right, (((0,), (0,)), ((), ())), preferred_element_...]
    all_to_all x2 -> x1, starting transfers between devices: 25.6 us -> 4.68 us  [exchange_sum(): received = lax.all_to_all(parts.astype(BF16), 'grp', 0, 0, tiled=True)]
    all_to_all x2 -> x1, waiting for transfers between devices: 20.7 us -> 4.92 us  [exchange_sum(): received = lax.all_to_all(parts.astype(BF16), 'grp', 0, 0, tiled=True)]
    all_to_all x0 -> x1, waiting for transfers between devices: none -> 12.3 us  [shards(): received = lax.all_to_all(dkv_all, 'grp', 0, 0, tiled=True)]
    unnamed x244 -> x255, local copies, waits for them, and re-layouts: 16.2 us -> 27.9 us
  transfers between devices with their start and end apart: 35 -> 41, of which waited for: 15 -> 20; matrix products, arithmetic and copies ran while one was open for 23% -> 20% of each run, Pallas kernels for 10% -> 19%
where the time goes in v4:
time: 517 us; the launch traced here: 509 us
  waiting for transfers between devices  158 us (31%)
  Pallas kernels  133 us (26%)
  local copies, waits for them, and re-layouts  53.3 us (10%)
  matrix products  50.8 us (10%)
  starting transfers between devices  49.3 us (10%)
  other arithmetic  45.6 us (9%)
  between operations  18.9 us (4%)
    ppermute x26, waiting for transfers between devices, flip(): return lax.ppermute(array, 'grp', [(i, i ^ mask) for i in range(members)])  102 us
    pallas_call x2, Pallas kernels, feed_forward_pair(): pl.pallas_call(feed_forward_kernel, out_shape=(jax.ShapeDtypeStruct((coun...  68.1 us
    pallas_call x1, Pallas kernels, attention_backward(): pl.pallas_call(functools.partial(attention_backward_kernel, per_kv), out_...  38.8 us
    unnamed x255, local copies, waits for them, and re-layouts  27.9 us
    dot_general x15, matrix products, mm(): return jnp.dot(left, right, preferred_element_type=F32)  25.8 us
    all_gather x1, waiting for transfers between devices, shards(): qkv_full = lax.all_gather(qkv_weight, 'grp', axis=1, tiled=True)  23.9 us
    ppermute x26, starting transfers between devices, flip(): return lax.ppermute(array, 'grp', [(i, i ^ mask) for i in range(members)])  22.5 us
    pallas_call x1, Pallas kernels, attention_forward(): pl.pallas_call(functools.partial(attention_forward_kernel, steps // KV_HE...  20 us
  transfers between devices with their start and end apart: 41, of which 20 were waited for; matrix products, arithmetic and copies ran while one was open for 20% of the time, Pallas kernels for 19%

profile of v4, /device:TPU:0, one launch (start us, length us, event | category | flops | bytes accessed | tf_op | source)
XLA Modules:
  0.0 508.9 jit_solution(17086206173104946407)
XLA Ops:
  8.8 5.3 %constant_dynamic-slice_fusion.2 = (bf16[512,1408]{1,0:T(8,128)(2,1)}, bf16[512,1408]{1,0:T(8,128)(2,1)}, bf16[512,1408]{1,0:T(8,128)(2,1)}, bf16[512,1408]{1,0:T(8,128)(2,1)}) fusion(bf16[2048,1408]{1,0:T(8,128)(2,1)} %param.34, s32[]{:T(128)S(6)} %select_n.286, s32[]{:T(128)S(6)} %select_n.263, s32[]{:T(128)S(6)} %select_n.262, s32[]{:T(128)S(6)} %select_n.285), kind=kLoop, calls=%fused_computation.175 | loop fusion | bytes 11534352 | tf_op jit(solution)/shard_map/dynamic_slice | solution.py:347
  14.0 3.0 collective-permute-start
  17.0 3.5 dynamic-slice_bitcast_fusion
  48.4 2.9 and_select_fusion.bias_ref
  53.1 22.2 %collective-permute-done.3 = bf16[1408,256]{1,0:T(8,128)(2,1)} collective-permute-done((bf16[1408,256]{1,0:T(8,128)(2,1)}, bf16[1408,256]{1,0:T(8,128)(2,1)}, u32[]{:S(2)}, u32[]{:S(2)}) %collective-permute-start.3) | collective-permute-done | bytes 720928 | tf_op jit(solution)/shard_map/ppermute | solution.py:333
  78.0 3.0 pad_maximum_fusion.refs_8_
  81.0 23.9 %all-gather.3.cloned.1.call-done = bf16[2048,2560]{0,1:T(8,128)(2,1)} async-done(((bf16[2048,320]{0,1:T(8,128)(2,1)}), bf16[2048,2560]{0,1:T(8,128)(2,1)}) %all-gather.3.cloned.1.call-update) | async-done | bytes 10485776 | tf_op jit(solution)/shard_map/all_gather | solution.py:909
  104.9 5.6 %fusion.116 = f32[256,2560]{1,0:T(8,128)S(1)} fusion(bf16[256,2048]{1,0:T(8,128)(2,1)S(1)} %fusion.10.norm1_ref.norm_ref, bf16[2048,2560]{0,1:T(8,128)(2,1)} %all-gather.3.cloned.1.call-done), kind=kOutput, calls=%fused_computation.263 | convolution fusion | flops 2684354560 | bytes 14155776 | tf_op jit(solution)/shard_map/dot_general | solution.py:26
  111.6 12.0 %collective-permute-done.4.refs_5_ = bf16[512,1408]{1,0:T(8,128)(2,1)} collective-permute-done((bf16[512,1408]{1,0:T(8,128)(2,1)}, bf16[512,1408]{1,0:T(8,128)(2,1)}, u32[]{:S(2)}, u32[]{:S(2)}) %collective-permute-start.4) | collective-permute-done | bytes 1441824 | tf_op jit(solution)/shard_map/ppermute | solution.py:333
  125.4 2.5 collective-permute-start.9
  129.0 8.0 %collective-permute-done.7 = bf16[256,512]{1,0:T(8,128)(2,1)S(1)} collective-permute-done((bf16[256,512]{1,0:T(8,128)(2,1)S(1)}, bf16[256,512]{1,0:T(8,128)(2,1)S(1)}, u32[]{:S(2)}, u32[]{:S(2)}) %collective-permute-start.7) | collective-permute-done | bytes 262176 | tf_op jit(solution)/shard_map/ppermute | solution.py:333
  140.6 7.5 %collective-permute-done.11 = bf16[256,512]{1,0:T(8,128)(2,1)S(1)} collective-permute-done((bf16[256,512]{1,0:T(8,128)(2,1)S(1)}, bf16[256,512]{1,0:T(8,128)(2,1)S(1)}, u32[]{:S(2)}, u32[]{:S(2)}) %collective-permute-start.11) | collective-permute-done | bytes 262176 | tf_op jit(solution)/shard_map/ppermute | solution.py:333
  150.9 2.5 collective-permute-start.14
  156.9 2.7 fusion.27.q_ref
  159.7 20.0 %attention_forward.1 = (bf16[256,2048]{1,0:T(8,128)(2,1)S(1)}, f32[16,2,256]{2,1,0:T(2,128)S(1)}) custom-call(s32[4]{0:T(128)S(1)} %pad_add_fusion.span, bf16[256,2048]{1,0:T(8,128)(2,1)S(1)} %fusion.27.q_ref, bf16[2048,512]{1,0:T(8,128)(2,1)S(1)} %constant_dynamic-update-slice_fusion.key_ref.value_ref, ...), custom_call_target="tpu_custom_call" | custom-call | flops 4294967296 | bytes 18874368 | tf_op jit(solution)/shard_map/attention_forward/pallas_call | solution.py:147
  180.3 4.9 collective-permute-done.15.refs_9_
  186.2 6.0 %collective-permute-done.14.own_g = bf16[256,2048]{1,0:T(8,128)(2,1)S(1)} collective-permute-done((bf16[256,2048]{1,0:T(8,128)(2,1)S(1)}, bf16[256,2048]{1,0:T(8,128)(2,1)S(1)}, u32[]{:S(2)}, u32[]{:S(2)}) %collective-permute-start.14) | collective-permute-done | bytes 1048608 | tf_op jit(solution)/shard_map/ppermute | solution.py:333
  199.5 11.1 %collective-permute-done.17.refs_10_ = bf16[1,1408,256]{2,1,0:T(8,128)(2,1)} collective-permute-done((bf16[1,1408,256]{2,1,0:T(8,128)(2,1)}, bf16[1,1408,256]{2,1,0:T(8,128)(2,1)}, u32[]{:S(2)}, u32[]{:S(2)}) %collective-permute-start.17) | collective-permute-done | bytes 720928 | tf_op jit(solution)/shard_map/ppermute | solution.py:333
  213.3 6.7 %multiply_reduce_fusion.1 = (f32[256]{0:T(256)S(1)}, f32[256,2048]{1,0:T(8,128)S(1)}) fusion(f32[256,2048]{1,0:T(8,128)} %convolution_multiply_fusion.1, bf16[256,2048]{1,0:T(8,128)(2,1)S(1)} %get-tuple-element.103.o_ref.attended_ref, bf16[2048,2048]{1,0:T(8,128)(2,1)} %all-gather.5.cloned.1.call-done, bf16[256,2048]{1,0:T(8,128)(2,1)} %param.25), kind=kOutput, calls=%fused_computation.57 | convolution fusion | flops 2150104832 | bytes 14681088 | tf_op jit(solution)/shard_map/dot_general | solution.py:26
  220.9 8.0 %collective-permute-done.19.refs_12_ = bf16[1,1408,256]{2,1,0:T(8,128)(2,1)S(1)} collective-permute-done((bf16[1,1408,256]{2,1,0:T(8,128)(2,1)}, bf16[1,1408,256]{2,1,0:T(8,128)(2,1)S(1)}, u32[]{:S(2)}, u32[]{:S(2)}) %collective-permute-start.19) | collective-permute-done | bytes 720928 | tf_op jit(solution)/shard_map/ppermute | solution.py:338
  231.6 2.6 concatenate.64.own_x
  234.2 2.1 fusion.45
  240.3 34.6 %feed_forward.2 = (f32[256,2176]{1,0:T(8,128)}, bf16[256,2176]{1,0:T(8,128)(2,1)}, f32[256,2176]{1,0:T(8,128)}, bf16[256,2176]{1,0:T(8,128)(2,1)}, f32[96,1408]{1,0:T(8,128)S(1)}) custom-call(s32[3]{0:T(128)S(1)} %pad_add_fusion.1.meta, bf16[256,2176]{1,0:T(8,128)(2,1)} %concatenate.64.own_x, bf16[256,2176]{1,0:T(8,128)(2,1)} %copy-done.117, ...), custom_call_target="tpu_custom_call" | custom-call | flops 17716740096 | bytes 38273024 | tf_op jit(solution)/shard_map/feed_forward/pallas_call | solution.py:591
  276.3 3.7 collective-permute-done.24.near_g
  281.0 33.6 %feed_forward.3 = (f32[256,2176]{1,0:T(8,128)}, bf16[256,2176]{1,0:T(8,128)(2,1)S(1)}, bf16[256,2176]{1,0:T(8,128)(2,1)}, bf16[256,2176]{1,0:T(8,128)(2,1)}, f32[96,1408]{1,0:T(8,128)S(1)}) custom-call(s32[3]{0:T(128)S(1)} %pad_add_fusion.1.meta, bf16[256,2176]{1,0:T(8,128)(2,1)} %copy-done.115, bf16[256,2176]{1,0:T(8,128)(2,1)} %copy-done.116, ...), custom_call_target="tpu_custom_call" | custom-call | flops 17716740096 | bytes 38273024 | tf_op jit(solution)/shard_map/feed_forward/pallas_call | solution.py:591
  314.9 2.5 collective-permute-done.25
  317.4 2.9 add_convert_fusion
  323.2 2.0 reshape.472
  328.0 19.3 %collective-permute-done.26 = bf16[256,2176]{1,0:T(8,128)(2,1)} collective-permute-done((bf16[256,2176]{1,0:T(8,128)(2,1)}, bf16[256,2176]{1,0:T(8,128)(2,1)}, u32[]{:S(2)}, u32[]{:S(2)}) %collective-permute-start.26) | collective-permute-done | bytes 1114144 | tf_op jit(solution)/shard_map/ppermute | solution.py:333
  347.3 2.6 convert_add_fusion.2
  353.0 2.1 fusion.108
  357.2 3.3 fusion.3.do_ref
  361.2 5.1 %fusion.90 = s32[128]{0:T(128)S(1)} fusion(s32[]{:T(128)} %bitcast.26, s32[]{:T(128)} %bitcast.27, s32[]{:T(128)} %bitcast.28, s32[]{:T(128)} %bitcast.29, s32[]{:T(128)} %bitcast.30, s32[]{:T(128)} %bitcast.32, s32[]{:T(128)} %bitcast.31, s32[]{:T(128)} %bitcast.25, s32[]{:T(128)S(6)} %axis_index.17), kind=kLoop, calls=%fused_computation.232 | loop fusion | flops 8448 | bytes 548 | tf_op jit(solution)/shard_map/add | solution.py:1075
  376.3 38.8 %attention_backward.1 = (bf16[256,2048]{1,0:T(8,128)(2,1)S(1)}, bf16[8,256,512]{2,1,0:T(8,128)(2,1)}) custom-call(s32[4]{0:T(128)S(1)} %pad_add_fusion.span, bf16[256,2048]{1,0:T(8,128)(2,1)S(1)} %copy-done.12, bf16[256,2048]{1,0:T(8,128)(2,1)S(1)} %copy-done.50, bf16[256,2048]{1,0:T(8,128)(2,1)S(1)} %copy-done.14, f32[16,2,256]{2,1,0:T(2,128)S(1)} %copy-done.52, ...), custom_call_target="tpu_custom_call" | custom-call | flops 10737418240 | bytes 13631488 | tf_op jit(solution)/shard_map/attention_backward/pallas_call | solution.py:290
  416.1 4.4 all-to-all-start
  420.5 7.5 %fusion = f32[256,2048]{1,0:T(8,128)} fusion(bf16[256,2048]{1,0:T(8,128)(2,1)} %copy-done.16, bf16[2048,2560]{0,1:T(8,128)(2,1)} %all-gather.3.cloned.1.call-done), kind=kOutput, calls=%fused_computation | convolution fusion | flops 2147483648 | bytes 11534336 | tf_op jit(solution)/shard_map/dot_general | solution.py:30
  428.1 2.6 convert_add_fusion.1
  436.3 12.3 %all-to-all-done.received_ref = bf16[8,256,512]{2,1,0:T(8,128)(2,1)} async-done(((bf16[8,256,512]{2,1,0:T(8,128)(2,1)}), bf16[8,256,512]{2,1,0:T(8,128)(2,1)}, u32[]{:S(2)}, u32[]{:S(2)}) %all-to-all-start) | async-done | bytes 2097184 | tf_op jit(solution)/shard_map/all_to_all | solution.py:1048
  452.3 2.5 key_value_gradients.1
  456.0 4.7 all-to-all-start.1
  462.4 3.1 fusion.20
  467.0 2.6 collective-permute-start.34
  471.0 2.5 convolution_add_fusion.1
  475.4 4.9 all-to-all-done.1
  483.5 2.6 collective-permute-start.31
  486.1 4.3 collective-permute-done.30.refs_2_
  490.5 2.3 collective-permute-start.32
  492.8 4.1 fusion.14
  (410 shorter events, 113.2 us)
Async XLA Ops:
  7.2 97.7 %all-gather.3.cloned.1.call-start = ((), (), s32[]{:S(2)}) async-start(), calls=%async_computation.3 | async-start | bytes 11796480 | tf_op jit(solution)/shard_map/all_gather | solution.py:909
  7.9 191.6 %all-gather.5.cloned.1.call-start = ((), (), s32[]{:S(2)}) async-start(), calls=%async_computation.4 | async-start | bytes 9437184 | tf_op jit(solution)/shard_map/all_gather | solution.py:983
  8.7 407.4 %reduce-scatter.2.cloned.1.call-start = ((), (), s32[]{:S(2)}) async-start(), calls=%async_computation.5 | async-start | bytes 1327104 | tf_op jit(solution)/shard_map/reduce_scatter | solution.py:1042
  14.0 61.3 %collective-permute-start = (bf16[512,1408]{1,0:T(8,128)(2,1)}, bf16[512,1408]{1,0:T(8,128)(2,1)}, u32[]{:S(2)}, u32[]{:S(2)}) collective-permute-start(bf16[512,1408]{1,0:T(8,128)(2,1)} %get-tuple-element.212.refs_0_), channel_id=1, source_target_pairs={{0,4},{1,5},{2,6},{3,7},{4,0},{5,1},{6,2},{7,3},{8,12},{9,13},{10,... | collective-permute-start | bytes 4325384 | tf_op jit(solution)/shard_map/ppermute | solution.py:333
  20.5 32.6 %collective-permute-start.1 = (bf16[1408,256]{1,0:T(8,128)(2,1)}, bf16[1408,256]{1,0:T(8,128)(2,1)}, u32[]{:S(2)}, u32[]{:S(2)}) collective-permute-start(bf16[1408,256]{1,0:T(8,128)(2,1)} %get-tuple-element.218), channel_id=1, source_target_pairs={{0,2},{1,3},{2,0},{3,1},{4,6},{5,7},{6,4},{7,5},{8,10},{9,11},{10,... | collective-permute-start | bytes 2162696 | tf_op jit(solution)/shard_map/ppermute | solution.py:333
  22.0 31.1 %collective-permute-start.2 = (bf16[1408,256]{1,0:T(8,128)(2,1)}, bf16[1408,256]{1,0:T(8,128)(2,1)}, u32[]{:S(2)}, u32[]{:S(2)}) collective-permute-start(bf16[1408,256]{1,0:T(8,128)(2,1)} %get-tuple-element.217), channel_id=1, source_target_pairs={{0,1},{1,0},{2,3},{3,2},{4,5},{5,4},{6,7},{7,6},{8,9},{9,8},{10,11... | collective-permute-start | bytes 2162696 | tf_op jit(solution)/shard_map/ppermute | solution.py:333
  22.0 53.3 %collective-permute-start.3 = (bf16[1408,256]{1,0:T(8,128)(2,1)}, bf16[1408,256]{1,0:T(8,128)(2,1)}, u32[]{:S(2)}, u32[]{:S(2)}) collective-permute-start(bf16[1408,256]{1,0:T(8,128)(2,1)} %get-tuple-element.219), channel_id=1, source_target_pairs={{0,3},{1,2},{2,1},{3,0},{4,7},{5,6},{6,5},{7,4},{8,11},{9,10},{10,... | collective-permute-start | bytes 2162696 | tf_op jit(solution)/shard_map/ppermute | solution.py:333
  42.3 85.6 %copy-start.7 = (bf16[32,2048]{1,0:T(8,128)(2,1)}, bf16[32,2048]{1,0:T(8,128)(2,1)S(1)}, u32[]{:S(2)}) copy-start(bf16[32,2048]{1,0:T(8,128)(2,1)S(1)} %convolution_convert_fusion.8.asking_ref) | copy-start | bytes 393220
  48.3 62.2 %copy-start.86 = (bf16[32,256]{1,0:T(8,128)(2,1)}, bf16[32,256]{1,0:T(8,128)(2,1)S(1)}, u32[]{:S(2)}) copy-start(bf16[32,256]{1,0:T(8,128)(2,1)S(1)} %convolution_convert_fusion.9) | copy-start | bytes 49156
  75.3 48.3 %collective-permute-start.4 = (bf16[512,1408]{1,0:T(8,128)(2,1)}, bf16[512,1408]{1,0:T(8,128)(2,1)}, u32[]{:S(2)}, u32[]{:S(2)}) collective-permute-start(bf16[512,1408]{1,0:T(8,128)(2,1)} %get-tuple-element.89.refs_1_), channel_id=1, source_target_pairs={{0,4},{1,5},{2,6},{3,7},{4,0},{5,1},{6,2},{7,3},{8,12},{9,13},{10,... | collective-permute-start | bytes 4325384 | tf_op jit(solution)/shard_map/ppermute | solution.py:333
  75.9 47.7 %collective-permute-start.5 = (bf16[512,1408]{1,0:T(8,128)(2,1)}, bf16[512,1408]{1,0:T(8,128)(2,1)}, u32[]{:S(2)}, u32[]{:S(2)}) collective-permute-start(bf16[512,1408]{1,0:T(8,128)(2,1)} %collective-permute-done.refs_4_), channel_id=1, source_target_pairs={{0,8},{8,0},{16,24},{24,16},{1,9},{9,1},{17,25},{25,17},{2,10},{10... | collective-permute-start | bytes 4325384 | tf_op jit(solution)/shard_map/ppermute | solution.py:338
  78.0 49.9 %copy-start.9 = (bf16[256,96]{1,0:T(8,128)(2,1)}, bf16[256,96]{1,0:T(8,128)(2,1)S(1)}, u32[]{:S(2)}) copy-start(bf16[256,96]{1,0:T(8,128)(2,1)S(1)} %fusion.23) | copy-start | bytes 147460
  123.6 16.9 %collective-permute-start.6 = (bf16[256,512]{1,0:T(8,128)(2,1)S(1)}, bf16[256,512]{1,0:T(8,128)(2,1)S(1)}, u32[]{:S(2)}, u32[]{:S(2)}) collective-permute-start(bf16[256,512]{1,0:T(8,128)(2,1)S(1)} %pad_maximum_fusion.1), channel_id=1, source_target_pairs={{0,1},{1,0},{2,3},{3,2},{4,5},{5,4},{6,7},{7,6},{8,9},{9,8},{10,11... | collective-permute-start | bytes 786440 | tf_op jit(solution)/shard_map/ppermute | solution.py:333
  123.7 13.3 %collective-permute-start.7 = (bf16[256,512]{1,0:T(8,128)(2,1)S(1)}, bf16[256,512]{1,0:T(8,128)(2,1)S(1)}, u32[]{:S(2)}, u32[]{:S(2)}) collective-permute-start(bf16[256,512]{1,0:T(8,128)(2,1)S(1)} %pad_maximum_fusion.1), channel_id=1, source_target_pairs={{0,2},{1,3},{2,0},{3,1},{4,6},{5,7},{6,4},{7,5},{8,10},{9,11},{10,... | collective-permute-start | bytes 786440 | tf_op jit(solution)/shard_map/ppermute | solution.py:333
  125.4 13.3 %collective-permute-start.9 = (bf16[256,512]{1,0:T(8,128)(2,1)S(1)}, bf16[256,512]{1,0:T(8,128)(2,1)S(1)}, u32[]{:S(2)}, u32[]{:S(2)}) collective-permute-start(bf16[256,512]{1,0:T(8,128)(2,1)S(1)} %pad_maximum_fusion.1), channel_id=1, source_target_pairs={{0,4},{1,5},{2,6},{3,7},{4,0},{5,1},{6,2},{7,3},{8,12},{9,13},{10,... | collective-permute-start | bytes 786440 | tf_op jit(solution)/shard_map/ppermute | solution.py:333
  137.0 11.1 %collective-permute-start.8 = (bf16[256,512]{1,0:T(8,128)(2,1)S(1)}, bf16[256,512]{1,0:T(8,128)(2,1)S(1)}, u32[]{:S(2)}, u32[]{:S(2)}) collective-permute-start(bf16[256,512]{1,0:T(8,128)(2,1)S(1)} %collective-permute-done.7), channel_id=1, source_target_pairs={{0,1},{1,0},{2,3},{3,2},{4,5},{5,4},{6,7},{7,6},{8,9},{9,8},{10,11... | collective-permute-start | bytes 786440 | tf_op jit(solution)/shard_map/ppermute | solution.py:333
  138.7 9.4 %collective-permute-start.11 = (bf16[256,512]{1,0:T(8,128)(2,1)S(1)}, bf16[256,512]{1,0:T(8,128)(2,1)S(1)}, u32[]{:S(2)}, u32[]{:S(2)}) collective-permute-start(bf16[256,512]{1,0:T(8,128)(2,1)S(1)} %collective-permute-done.9), channel_id=1, source_target_pairs={{0,2},{1,3},{2,0},{3,1},{4,6},{5,7},{6,4},{7,5},{8,10},{9,11},{10,... | collective-permute-start | bytes 786440 | tf_op jit(solution)/shard_map/ppermute | solution.py:333
  140.5 7.7 %collective-permute-start.10 = (bf16[256,512]{1,0:T(8,128)(2,1)S(1)}, bf16[256,512]{1,0:T(8,128)(2,1)S(1)}, u32[]{:S(2)}, u32[]{:S(2)}) collective-permute-start(bf16[256,512]{1,0:T(8,128)(2,1)S(1)} %collective-permute-done.9), channel_id=1, source_target_pairs={{0,1},{1,0},{2,3},{3,2},{4,5},{5,4},{6,7},{7,6},{8,9},{9,8},{10,11... | collective-permute-start | bytes 786440 | tf_op jit(solution)/shard_map/ppermute | solution.py:333
  148.1 1.5 collective-permute-start.12
  149.7 42.5 %collective-permute-start.16 = (bf16[512,1408]{1,0:T(8,128)(2,1)}, bf16[512,1408]{1,0:T(8,128)(2,1)S(1)}, u32[]{:S(2)}, u32[]{:S(2)}) collective-permute-start(bf16[512,1408]{1,0:T(8,128)(2,1)} %collective-permute-done.4.refs_5_), channel_id=1, source_target_pairs={{0,8},{8,0},{16,24},{24,16},{1,9},{9,1},{17,25},{25,17},{2,10},{10... | collective-permute-start | bytes 4325384 | tf_op jit(solution)/shard_map/ppermute | solution.py:338
  150.8 34.4 %collective-permute-start.13 = (bf16[256,2048]{1,0:T(8,128)(2,1)S(1)}, bf16[256,2048]{1,0:T(8,128)(2,1)S(1)}, u32[]{:S(2)}, u32[]{:S(2)}) collective-permute-start(bf16[256,2048]{1,0:T(8,128)(2,1)S(1)} %copy-done.2), channel_id=1, source_target_pairs={{0,1},{1,0},{2,3},{3,2},{4,5},{5,4},{6,7},{7,6},{8,9},{9,8},{10,11... | collective-permute-start | bytes 3145736 | tf_op jit(solution)/shard_map/ppermute | solution.py:333
  150.9 41.3 %collective-permute-start.14 = (bf16[256,2048]{1,0:T(8,128)(2,1)S(1)}, bf16[256,2048]{1,0:T(8,128)(2,1)S(1)}, u32[]{:S(2)}, u32[]{:S(2)}) collective-permute-start(bf16[256,2048]{1,0:T(8,128)(2,1)S(1)} %copy-done.2), channel_id=1, source_target_pairs={{0,2},{1,3},{2,0},{3,1},{4,6},{5,7},{6,4},{7,5},{8,10},{9,11},{10,... | collective-permute-start | bytes 3145736 | tf_op jit(solution)/shard_map/ppermute | solution.py:333
  154.4 30.8 %collective-permute-start.15 = (bf16[1,1408,256]{2,1,0:T(8,128)(2,1)S(1)}, bf16[1,1408,256]{2,1,0:T(8,128)(2,1)}, u32[]{:S(2)}, u32[]{:S(2)}) collective-permute-start(bf16[1,1408,256]{2,1,0:T(8,128)(2,1)S(1)} %get-tuple-element.215), channel_id=1, source_target_pairs={{0,4},{1,5},{2,6},{3,7},{4,0},{5,1},{6,2},{7,3},{8,12},{9,13},{10,... | collective-permute-start | bytes 2162696 | tf_op jit(solution)/shard_map/ppermute | solution.py:333
  180.3 39.7 %copy-start.13 = (bf16[256,2048]{1,0:T(8,128)(2,1)}, bf16[256,2048]{1,0:T(8,128)(2,1)S(1)}, u32[]{:S(2)}) copy-start(bf16[256,2048]{1,0:T(8,128)(2,1)S(1)} %get-tuple-element.103.o_ref.attended_ref) | copy-start | bytes 3145732
  192.1 18.4 %collective-permute-start.17 = (bf16[1,1408,256]{2,1,0:T(8,128)(2,1)}, bf16[1,1408,256]{2,1,0:T(8,128)(2,1)}, u32[]{:S(2)}, u32[]{:S(2)}) collective-permute-start(bf16[1,1408,256]{2,1,0:T(8,128)(2,1)} %get-tuple-element.104), channel_id=1, source_target_pairs={{0,4},{1,5},{2,6},{3,7},{4,0},{5,1},{6,2},{7,3},{8,12},{9,13},{10,... | collective-permute-start | bytes 2162696 | tf_op jit(solution)/shard_map/ppermute | solution.py:333
  193.7 18.1 %collective-permute-start.18 = (bf16[1,1408,256]{2,1,0:T(8,128)(2,1)}, bf16[1,1408,256]{2,1,0:T(8,128)(2,1)}, u32[]{:S(2)}, u32[]{:S(2)}) collective-permute-start(bf16[1,1408,256]{2,1,0:T(8,128)(2,1)} %collective-permute-done.15.refs_9_), channel_id=1, source_target_pairs={{0,8},{8,0},{16,24},{24,16},{1,9},{9,1},{17,25},{25,17},{2,10},{10... | collective-permute-start | bytes 2162696 | tf_op jit(solution)/shard_map/ppermute | solution.py:338
  211.8 17.1 %collective-permute-start.19 = (bf16[1,1408,256]{2,1,0:T(8,128)(2,1)}, bf16[1,1408,256]{2,1,0:T(8,128)(2,1)S(1)}, u32[]{:S(2)}, u32[]{:S(2)}) collective-permute-start(bf16[1,1408,256]{2,1,0:T(8,128)(2,1)} %collective-permute-done.17.refs_10_), channel_id=1, source_target_pairs={{0,8},{8,0},{16,24},{24,16},{1,9},{9,1},{17,25},{25,17},{2,10},{10... | collective-permute-start | bytes 2162696 | tf_op jit(solution)/shard_map/ppermute | solution.py:338
  234.1 5.2 %collective-permute-start.20 = (bf16[256,2176]{1,0:T(8,128)(2,1)}, bf16[256,2176]{1,0:T(8,128)(2,1)S(1)}, u32[]{:S(2)}, u32[]{:S(2)}) collective-permute-start(bf16[256,2176]{1,0:T(8,128)(2,1)} %concatenate.64.own_x), channel_id=1, source_target_pairs={{0,1},{1,0},{2,3},{3,2},{4,5},{5,4},{6,7},{7,6},{8,9},{9,8},{10,11... | collective-permute-start | bytes 3342344 | tf_op jit(solution)/shard_map/ppermute | solution.py:333
  238.1 41.9 %copy-start.27 = (bf16[32,2048]{1,0:T(8,128)(2,1)}, bf16[32,2048]{1,0:T(8,128)(2,1)S(1)}, u32[]{:S(2)}) copy-start(bf16[32,2048]{1,0:T(8,128)(2,1)S(1)} %convolution_convert_fusion.6.lower_ref) | copy-start | bytes 393220
  238.1 37.6 %collective-permute-start.21 = (bf16[256,2176]{1,0:T(8,128)(2,1)S(1)}, bf16[256,2176]{1,0:T(8,128)(2,1)S(1)}, u32[]{:S(2)}, u32[]{:S(2)}) collective-permute-start(bf16[256,2176]{1,0:T(8,128)(2,1)S(1)} %copy-done.65), channel_id=1, source_target_pairs={{0,2},{1,3},{2,0},{3,1},{4,6},{5,7},{6,4},{7,5},{8,10},{9,11},{10,... | collective-permute-start | bytes 3342344 | tf_op jit(solution)/shard_map/ppermute | solution.py:333
  240.3 40.7 %copy-start.36 = (f32[256,32]{1,0:T(8,128)S(1)}, f32[256,32]{1,0:T(8,128)}, u32[]{:S(2)}) copy-start(f32[256,32]{1,0:T(8,128)} %get-tuple-element.244.near_seen) | copy-start | bytes 98308
  240.3 40.7 %copy-start.37 = (f32[256,32]{1,0:T(8,128)S(1)}, f32[256,32]{1,0:T(8,128)}, u32[]{:S(2)}) copy-start(f32[256,32]{1,0:T(8,128)} %get-tuple-element.246.own_seen) | copy-start | bytes 98308
  275.7 4.3 collective-permute-start.23
  276.0 4.0 collective-permute-start.24
  314.6 2.8 collective-permute-start.25
  320.3 27.0 %collective-permute-start.26 = (bf16[256,2176]{1,0:T(8,128)(2,1)}, bf16[256,2176]{1,0:T(8,128)(2,1)}, u32[]{:S(2)}, u32[]{:S(2)}) collective-permute-start(bf16[256,2176]{1,0:T(8,128)(2,1)} %add_convert_fusion), channel_id=1, source_target_pairs={{0,2},{1,3},{2,0},{3,1},{4,6},{5,7},{6,4},{7,5},{8,10},{9,11},{10,... | collective-permute-start | bytes 3342344 | tf_op jit(solution)/shard_map/ppermute | solution.py:333
  321.2 26.1 %collective-permute-start.22 = (bf16[256,2176]{1,0:T(8,128)(2,1)}, bf16[256,2176]{1,0:T(8,128)(2,1)}, u32[]{:S(2)}, u32[]{:S(2)}) collective-permute-start(bf16[256,2176]{1,0:T(8,128)(2,1)} %get-tuple-element.116), channel_id=1, source_target_pairs={{0,1},{1,0},{2,3},{3,2},{4,5},{5,4},{6,7},{7,6},{8,9},{9,8},{10,11... | collective-permute-start | bytes 3342344 | tf_op jit(solution)/shard_map/ppermute | solution.py:333
  370.0 58.1 %collective-permute-start.27 = (bf16[256,2176]{1,0:T(8,128)(2,1)}, bf16[256,2176]{1,0:T(8,128)(2,1)}, u32[]{:S(2)}, u32[]{:S(2)}) collective-permute-start(bf16[256,2176]{1,0:T(8,128)(2,1)} %get-tuple-element.129), channel_id=1, source_target_pairs={{0,1},{1,0},{2,3},{3,2},{4,5},{5,4},{6,7},{7,6},{8,9},{9,8},{10,11... | collective-permute-start | bytes 3342344 | tf_op jit(solution)/shard_map/ppermute | solution.py:333
  370.0 58.1 %collective-permute-start.28 = (bf16[256,2176]{1,0:T(8,128)(2,1)}, bf16[256,2176]{1,0:T(8,128)(2,1)}, u32[]{:S(2)}, u32[]{:S(2)}) collective-permute-start(bf16[256,2176]{1,0:T(8,128)(2,1)} %get-tuple-element.130), channel_id=1, source_target_pairs={{0,2},{1,3},{2,0},{3,1},{4,6},{5,7},{6,4},{7,5},{8,10},{9,11},{10,... | collective-permute-start | bytes 3342344 | tf_op jit(solution)/shard_map/ppermute | solution.py:333
  370.9 57.2 %collective-permute-start.29 = (bf16[256,2176]{1,0:T(8,128)(2,1)}, bf16[256,2176]{1,0:T(8,128)(2,1)}, u32[]{:S(2)}, u32[]{:S(2)}) collective-permute-start(bf16[256,2176]{1,0:T(8,128)(2,1)} %get-tuple-element.131), channel_id=1, source_target_pairs={{0,3},{1,2},{2,1},{3,0},{4,7},{5,6},{6,5},{7,4},{8,11},{9,10},{10,... | collective-permute-start | bytes 3342344 | tf_op jit(solution)/shard_map/ppermute | solution.py:333
  416.1 32.5 %all-to-all-start = ((bf16[8,256,512]{2,1,0:T(8,128)(2,1)}), bf16[8,256,512]{2,1,0:T(8,128)(2,1)}, u32[]{:S(2)}, u32[]{:S(2)}) async-start(bf16[8,256,512]{2,1,0:T(8,128)(2,1)} %get-tuple-element.140), calls=%async_computation.1 | async-start | bytes 4194304 | tf_op jit(solution)/shard_map/all_to_all | solution.py:1048
  456.0 24.3 %all-to-all-start.1 = ((bf16[8,352,256]{2,1,0:T(8,128)(2,1)}), bf16[8,352,256]{2,1,0:T(8,128)(2,1)}, u32[]{:S(2)}, u32[]{:S(2)}) async-start(bf16[8,352,256]{2,1,0:T(8,128)(2,1)} %copy-done.6), calls=%async_computation.2 | async-start | bytes 2883584 | tf_op jit(solution)/shard_map/all_to_all | solution.py:691
  465.5 31.6 %collective-permute-start.33 = (bf16[96,704]{1,0:T(8,128)(2,1)S(1)}, bf16[96,704]{1,0:T(8,128)(2,1)S(1)}, u32[]{:S(2)}, u32[]{:S(2)}) collective-permute-start(bf16[96,704]{1,0:T(8,128)(2,1)S(1)} %bitcast.125), channel_id=1, source_target_pairs={{0,8},{8,16},{16,24},{24,0},{1,9},{9,17},{17,25},{25,1},{2,10},{10... | collective-permute-start | bytes 405512 | tf_op jit(solution)/shard_map/ppermute | solution.py:863
  467.0 30.0 %collective-permute-start.34 = (bf16[96,704]{1,0:T(8,128)(2,1)S(1)}, bf16[96,704]{1,0:T(8,128)(2,1)S(1)}, u32[]{:S(2)}, u32[]{:S(2)}) collective-permute-start(bf16[96,704]{1,0:T(8,128)(2,1)S(1)} %bitcast.126), channel_id=1, source_target_pairs={{0,16},{8,24},{16,0},{24,8},{1,17},{9,25},{17,1},{25,9},{2,18},{10... | collective-permute-start | bytes 405512 | tf_op jit(solution)/shard_map/ppermute | solution.py:863
  469.7 27.4 %collective-permute-start.35 = (bf16[96,704]{1,0:T(8,128)(2,1)S(1)}, bf16[96,704]{1,0:T(8,128)(2,1)S(1)}, u32[]{:S(2)}, u32[]{:S(2)}) collective-permute-start(bf16[96,704]{1,0:T(8,128)(2,1)S(1)} %bitcast.127), channel_id=1, source_target_pairs={{0,24},{8,0},{16,8},{24,16},{1,25},{9,1},{17,9},{25,17},{2,26},{10... | collective-permute-start | bytes 405512 | tf_op jit(solution)/shard_map/ppermute | solution.py:863
  481.9 8.6 %collective-permute-start.30 = (bf16[352,256]{1,0:T(8,128)(2,1)S(1)}, bf16[352,256]{1,0:T(8,128)(2,1)S(1)}, u32[]{:S(2)}, u32[]{:S(2)}) collective-permute-start(bf16[352,256]{1,0:T(8,128)(2,1)S(1)} %reduce_sum.52.refs_1_), channel_id=1, source_target_pairs={{0,8},{8,16},{16,24},{24,0},{1,9},{9,17},{17,25},{25,1},{2,10},{10... | collective-permute-start | bytes 540680 | tf_op jit(solution)/shard_map/ppermute | solution.py:863
  483.5 13.5 %collective-permute-start.31 = (bf16[352,256]{1,0:T(8,128)(2,1)S(1)}, bf16[352,256]{1,0:T(8,128)(2,1)S(1)}, u32[]{:S(2)}, u32[]{:S(2)}) collective-permute-start(bf16[352,256]{1,0:T(8,128)(2,1)S(1)} %reduce_sum.52.refs_1_), channel_id=1, source_target_pairs={{0,16},{8,24},{16,0},{24,8},{1,17},{9,25},{17,1},{25,9},{2,18},{10... | collective-permute-start | bytes 540680 | tf_op jit(solution)/shard_map/ppermute | solution.py:863
  490.5 6.6 %collective-permute-start.32 = (bf16[352,256]{1,0:T(8,128)(2,1)S(1)}, bf16[352,256]{1,0:T(8,128)(2,1)S(1)}, u32[]{:S(2)}, u32[]{:S(2)}) collective-permute-start(bf16[352,256]{1,0:T(8,128)(2,1)S(1)} %reduce_sum.52.refs_1_), channel_id=1, source_target_pairs={{0,24},{8,0},{16,8},{24,16},{1,25},{9,1},{17,9},{25,17},{2,26},{10... | collective-permute-start | bytes 540680 | tf_op jit(solution)/shard_map/ppermute | solution.py:863
  (115 other events, 898.0 us)
Sparse Core Ops, SparseCore 0:
  9.9 94.9 all-gather.2
  106.8 80.2 all-gather.4
  360.7 42.3 reduce-scatter.1

commit v5 on v4

--- a/solution.py
+++ b/solution.py
@@ -162,7 +162,7 @@
             scratch_shapes=[pltpu.VMEM((2, keys, LANES), BF16)] * 2,
         ),
         compiler_params=pltpu.CompilerParams(
-            dimension_semantics=("arbitrary",), vmem_limit_bytes=40 << 20
+            dimension_semantics=("arbitrary",), vmem_limit_bytes=30 << 20
         ),
         cost_estimate=pl.CostEstimate(
             flops=4 * tokens * keys * width,
@@ -314,7 +314,7 @@
             + [pltpu.VMEM((keys, LANES), F32)] * 2,
         ),
         compiler_params=pltpu.CompilerParams(
-            dimension_semantics=("arbitrary",), vmem_limit_bytes=48 << 20
+            dimension_semantics=("arbitrary",), vmem_limit_bytes=46 << 20
         ),
         cost_estimate=pl.CostEstimate(
             flops=10 * tokens * keys * width,
@@ -444,9 +444,9 @@
     *refs,
 ):
     whole_refs, whole_down = refs[:8], refs[8:13]
-    back_own, back_near, front_own, front_near, deep_ref = refs[13:18]
-    x_turned, g_turned, latents, dlats, stack, acts, firsts, seconds, dacts, dlat_sum = refs[18:28]
-    kept, kept_down, semaphores = refs[28:]
+    back_own, back_near, acts, deep_ref = refs[13:17]
+    x_turned, g_turned, latents, dlats, stack, firsts, seconds, dacts, dlat_sum = refs[17:26]
+    kept, kept_down, semaphores = refs[26:]
     count, width = own_g.shape
     tokens = 2 * count
     slots, block = in_ref.shape
@@ -563,26 +563,77 @@
         back_near[:, lanes] = value[count:].astype(BF16)
         return carry
 
-    def front(index, carry):
-        value = mm(acts[...], kept_down[index])
+    lax.fori_loop(0, 4, back, 0)
+    back_own[:, width:] = dlat_sum[:count, :]
+    back_near[:, width:] = dlat_sum[count:, :].astype(BF16)
+
+
+def down_kernel(meta, in_ref, *refs):
+    acts_refs, whole_down = refs[:2], refs[2:7]
+    results = (refs[7:9], refs[9:11])
+    kept_down, semaphores = refs[11:]
+    slots = in_ref.shape[0]
+    parts, _, part = kept_down.shape
+    width = parts * part
+    parity, member = meta[0], meta[2]
+    copies = [
+        pltpu.make_async_copy(ref, kept_down.at[pl.ds(start, size)], semaphores.at[index])
+        for index, (ref, start, size) in enumerate(zip(whole_down, (0, 4, 5, 6, 7), (4, 1, 1, 1, 1)))
+    ]
+    for copy in copies:
+        copy.start()
+    for acts, outs in zip(acts_refs, results):
+        latent = mm_nt(acts[...], in_ref[...])
+        pad = jnp.zeros((latent.shape[0], LANES - slots), F32)
+        latent = jnp.concatenate([latent, pad], axis=1)
+        for index, out in enumerate(outs):
+            rows = slice(index * out.shape[0], (index + 1) * out.shape[0])
+            out[:, width:] = latent[rows].astype(out.dtype)
+    for copy in copies:
+        copy.wait()
+
+    def columns(index, carry):
         half = (index - 4) // 2 ^ parity
         base = jnp.where(index < 4, index, 4 + 2 * half + lax.rem(index, 2))
         lanes = pl.ds(pl.multiple_of((member ^ base) * part, part), part)
-        front_own[:, lanes] = value[:count].astype(front_own.dtype)
-        front_near[:, lanes] = value[count:].astype(BF16)
+        for acts, outs in zip(acts_refs, results):
+            value = mm(acts[...], kept_down[index])
+            for side, out in enumerate(outs):
+                rows = slice(side * out.shape[0], (side + 1) * out.shape[0])
+                out[:, lanes] = value[rows].astype(out.dtype)
         return carry
 
-    lax.fori_loop(0, 4, back, 0)
-    lax.fori_loop(0, kept_down.shape[0], front, 0)
-    back_own[:, width:] = dlat_sum[:count, :]
-    back_near[:, width:] = dlat_sum[count:, :].astype(BF16)
-    latent = mm_nt(acts[...], in_ref[...])
-    latent = jnp.concatenate([latent, jnp.zeros((tokens, LANES - slots), F32)], axis=1)
-    front_own[:, width:] = latent[:count, :].astype(front_own.dtype)
-    front_near[:, width:] = latent[count:, :].astype(BF16)
-
-
-def feed_forward_pair(meta, rows, sens, seen, weights, pieces, front_type):
+    lax.fori_loop(0, parts, columns, 0)
+
+
+def down_projection(meta, acts, down_in, weights):
+    tokens, block = acts[0].shape
+    slots = down_in.shape[0]
+    width = 8 * weights["down"][0].shape[2]
+    wide, count = width + LANES, tokens // 2
+    kept = jax.ShapeDtypeStruct((count, wide), F32)
+    sent = jax.ShapeDtypeStruct((count, wide), BF16)
+    return pl.pallas_call(
+        down_kernel,
+        out_shape=(kept, sent, sent, sent),
+        in_specs=[pl.BlockSpec(memory_space=pltpu.SMEM)]
+        + [pl.BlockSpec(memory_space=pltpu.VMEM)] * 3
+        + [pl.BlockSpec(memory_space=pl.ANY)] * 5,
+        scratch_shapes=[
+            pltpu.VMEM((8, block, width // 8), BF16),
+            pltpu.SemaphoreType.DMA((5,)),
+        ],
+        compiler_params=pltpu.CompilerParams(vmem_limit_bytes=24 << 20),
+        cost_estimate=pl.CostEstimate(
+            flops=4 * tokens * width * block,
+            transcendentals=0,
+            bytes_accessed=2 * width * block + 8 * tokens * width,
+        ),
+        name="down_projection",
+    )(meta, down_in, *acts, *weights["down"])
+
+
+def feed_forward_pair(meta, rows, sens, seen, weights, pieces):
     count, width = sens[0].shape
     slots, block = pieces[-1].shape
     wide, tokens = width + LANES, 2 * count
@@ -593,8 +644,7 @@
         out_shape=(
             jax.ShapeDtypeStruct((count, wide), F32),
             jax.ShapeDtypeStruct((count, wide), BF16),
-            jax.ShapeDtypeStruct((count, wide), front_type),
-            jax.ShapeDtypeStruct((count, wide), BF16),
+            jax.ShapeDtypeStruct((tokens, block), BF16),
             jax.ShapeDtypeStruct((3 * slots, block), F32),
         ),
         in_specs=[pl.BlockSpec(memory_space=pltpu.SMEM)]
@@ -608,16 +658,15 @@
             pltpu.VMEM((3 * slots, tokens), BF16),
             pltpu.VMEM((tokens, block), BF16),
             pltpu.VMEM((tokens, block), BF16),
-            pltpu.VMEM((tokens, block), BF16),
             pltpu.VMEM((tokens, block), F32),
             pltpu.VMEM((tokens, LANES), F32),
             pltpu.VMEM((8, width // 4, block), BF16),
             pltpu.VMEM((8, block, width // 8), BF16),
             pltpu.SemaphoreType.DMA((13,)),
         ],
-        compiler_params=pltpu.CompilerParams(vmem_limit_bytes=46 << 20),
+        compiler_params=pltpu.CompilerParams(vmem_limit_bytes=50 << 20),
         cost_estimate=pl.CostEstimate(
-            flops=2 * 6 * tokens * width * block,
+            flops=2 * 5 * tokens * width * block,
             transcendentals=tokens * block,
             bytes_accessed=6 * width * block + 20 * tokens * width,
         ),
@@ -625,25 +674,18 @@
     )(meta, *operands, *arrays)
 
 
-def feed_forward_shared(norm2, sens_pairs, weights, small, seen_by):
-    ffn_in, switch, lift, down_in, lower = small
+def feed_forward_shared(norm2, sens_pairs, weights, small, all_seen):
+    ffn_in, *pieces = small
+    lower = pieces[0]
     width = norm2.shape[1]
-    slots, hidden_width = switch.shape
-    block = weights["own"][0].shape[1]
+    slots, block = pieces[-1].shape
+    hidden_width = block * ACROSS_Y
     member = lax.axis_index("grp")
     parity = lax.axis_index("rep") % 2
     owns_gate = member < ACROSS_Y
     hidden = member % ACROSS_Y
-
     meta = jnp.stack([parity, owns_gate.astype(jnp.int32), member]).astype(jnp.int32)
-    pieces = (
-        lower,
-        *(
-            lax.dynamic_slice_in_dim(piece, hidden * block, block, 1)
-            for piece in (switch, lift, down_in)
-        ),
-    )
-    seen = seen_by(member)
+    seen = all_seen[0]
     seen_two = jnp.concatenate([seen, seen], axis=1)
     latent_gu = (mm(norm2, ffn_in) * seen_two).astype(BF16)
     pad = jnp.zeros((norm2.shape[0], LANES - 2 * slots), BF16)
@@ -651,33 +693,29 @@
     across = flip(rows, ACROSS_X)
     results = []
     for index, sens_pair in enumerate(sens_pairs):
-        first = member ^ (index * ACROSS_X)
         if index == 1:
             result, (across,) = tie(results[0][1], (across,))
             results[0][1] = result
             rows = across
-        seen_pair = (seen_by(first), seen_by(first ^ CORE))
+        seen_pair = all_seen[2 * index : 2 * index + 2]
         row_pair = (rows, flip(rows, CORE))
         results.append(
-            list(
-                feed_forward_pair(
-                    meta, row_pair, sens_pair, seen_pair, weights, pieces, (F32, BF16)[index]
-                )
-            )
+            list(feed_forward_pair(meta, row_pair, sens_pair, seen_pair, weights, pieces))
         )
 
     chips = [result[0] + flip(result[1], CORE).astype(F32) for result in results]
-    deep = (results[0][4] + results[1][4]).astype(BF16)
+    deep = (results[0][3] + results[1][3]).astype(BF16)
     members = lax.axis_size("grp")
     owners = members * block // hidden_width
     deep = deep.reshape(3 * slots, owners, block // owners).transpose(1, 0, 2)
     placed = jnp.zeros((members, 3 * slots, block // owners), BF16)
     placed = lax.dynamic_update_slice_in_dim(placed, deep, hidden * owners, 0)
-    across, (placed,) = tie(flip(chips[1].astype(BF16), ACROSS_X), (placed,))
+    forwards = down_projection(meta, [result[2] for result in results], pieces[-1], weights)
+    across = flip(chips[1].astype(BF16), ACROSS_X)
+    across, (placed, *forwards) = tie(across, (placed, *forwards))
     backward = chips[0] + across.astype(F32)
     dlat_gu = (LOWRANK_FACTOR * backward[:, width : width + 2 * slots] * seen_two).astype(BF16)
     dnorm2 = backward[:, :width] + mm_nt(dlat_gu, ffn_in)
-    forwards = [part for result in results for part in result[2:4]]
     dnorm2, forwards = tie(dnorm2, forwards)
     forward = forwards[0]
     for part, mask in zip(forwards[1:], (CORE, ACROSS_X, ACROSS_X | CORE)):
@@ -937,7 +975,7 @@
     slots = 2 * RANK
     columns = jnp.arange(narrow, dtype=jnp.int32)
     slot = jnp.arange(slots, dtype=jnp.int32)
-    slot_column = chosen_ids[slot // RANK] * RANK + slot % RANK
+    slot_column = jnp.where(slot < RANK, chosen_ids[0], chosen_ids[1]) * RANK + slot % RANK
     pick = (columns[:, None] == slot_column[None, :]).astype(BF16)
 
     def seen_by(device):
@@ -974,11 +1012,27 @@
         lower,
     )
 
+    cycle = jnp.arange(groups * slots, dtype=jnp.int32)
+    source = (group - cycle // slots) % groups
+    sequence = 2 * source + cycle % slots // RANK
+    sequences = jnp.arange(adapter_ids.shape[0], dtype=jnp.int32)
+    theirs = jnp.where(sequence[:, None] == sequences[None, :], adapter_ids[None, :], 0)
+    all_column = jnp.sum(theirs, axis=1) * RANK + cycle % RANK
+    place = (all_column[:, None] == columns[None, :]).astype(BF16)
     incoming = tokens.astype(F32)
     scale_one = inverse_rms(incoming)
     norm1 = (incoming * scale_one * attn_gain).astype(BF16)
     if paired:
-        norm1, transfers = tie(norm1, transfers)
+        block = down_weight.shape[0] // ACROSS_Y
+        start = member % ACROSS_Y * block
+        pieces = [lax.dynamic_slice_in_dim(piece, start, block, 1) for piece in small[1:4]]
+        others = (seen_by(member ^ mask) for mask in (CORE, ACROSS_X, ACROSS_X | CORE))
+        ready = (*transfers, asking, kv_right, out_in, final, lower, place, small[0], *pieces)
+        norm1, ready = tie(norm1, (*ready, *others))
+        transfers = ready[: len(transfers)]
+        asking, kv_right, out_in, final, lower, place, ffn_in, *ready = ready[len(transfers) :]
+        small = (ffn_in, lower, *ready[:3])
+        all_seen = (seen, *ready[3:])
         transfers = steps.send(transfers)
         out_full = lax.all_gather(out_weight, "grp", axis=1, tiled=True)
     latent_qkv = (mm(norm1, qkv_in) * seen_three).astype(BF16)
@@ -1011,8 +1065,10 @@
         attended_low, (sens_near, sens_across, *transfers) = tie(
             attended_low, (sens_near, sens_across, *transfers)
         )
-        sens_pairs = [(sens, sens_near), (sens_across, flip(sens_across, CORE))]
-        out_full, transfers = tie(out_full, steps.send(transfers))
+        out_full, (sens_last, *transfers) = tie(
+            out_full, (flip(sens_across, CORE), *steps.send(transfers))
+        )
+        sens_pairs = [(sens, sens_near), (sens_across, sens_last)]
         transfers = steps.send(transfers)
 
     latent_o = (mm(attended_low, out_in) * seen).astype(BF16)
@@ -1026,7 +1082,7 @@
         except StopIteration as stop:
             weights = stop.value
         response_part, dnorm2, latent_d, dlat_gu, deep = feed_forward_shared(
-            norm2, sens_pairs, weights, small, seen_by
+            norm2, sens_pairs, weights, small, all_seen
         )
     else:
         response_part, dnorm2, latent_d, dlat_gu, deep = feed_forward_alone(
@@ -1070,10 +1126,6 @@
     dnorm1 = dnorm_q + mm_nt(dkv, qkv_full[:, width:]) + mm_nt(dlat_kv, qkv_in[:, slots:])
     input_grad = (dhidden + norm_backward(incoming, scale_one, attn_gain, dnorm1)).astype(BF16)
 
-    cycle = jnp.arange(groups * slots, dtype=jnp.int32)
-    source = (group - cycle // slots) % groups
-    all_column = adapter_ids[2 * source + cycle % slots // RANK] * RANK + cycle % RANK
-    place = (all_column[:, None] == columns[None, :]).astype(BF16)
     share = width // members
     pieces = kv_width // share
     thin_start = 9 * slots

time: 517 us -> 507 us (0.981)
  Pallas kernels: 133 us -> 143 us
  other arithmetic: 45.6 us -> 37.1 us
  matrix products: 50.8 us -> 43.2 us
    pallas_call x0 -> x1, Pallas kernels: none -> 10.2 us  [down_projection(): pl.pallas_call(down_kernel, out_shape=(kept, sent, sent, sent), in_specs=...]
    unnamed x255 -> x279, local copies, waits for them, and re-layouts: 27.9 us -> 33.6 us
  transfers between devices with their start and end apart: 41 -> 41, of which waited for: 20 -> 21; matrix products, arithmetic and copies ran while one was open for 20% -> 18% of each run, Pallas kernels for 19% -> 22%
where the time goes in v5:
time: 507 us; the launch traced here: 499 us
  waiting for transfers between devices  157 us (31%)
  Pallas kernels  143 us (28%)
  local copies, waits for them, and re-layouts  52.8 us (10%)
  starting transfers between devices  46.7 us (9%)
  matrix products  43.2 us (9%)
  other arithmetic  37.1 us (7%)
  between operations  19.2 us (4%)
    ppermute x26, waiting for transfers between devices, flip(): return lax.ppermute(array, 'grp', [(i, i ^ mask) for i in range(members)])  100 us
    pallas_call x2, Pallas kernels, feed_forward_pair(): pl.pallas_call(feed_forward_kernel, out_shape=(jax.ShapeDtypeStruct((coun...  68.8 us
    pallas_call x1, Pallas kernels, attention_backward(): pl.pallas_call(functools.partial(attention_backward_kernel, per_kv), out_...  37.6 us
    unnamed x279, local copies, waits for them, and re-layouts  33.6 us
    all_gather x1, waiting for transfers between devices, shards(): qkv_full = lax.all_gather(qkv_weight, 'grp', axis=1, tiled=True)  24.7 us
    dot_general x15, matrix products, mm(): return jnp.dot(left, right, preferred_element_type=F32)  21.5 us
    pallas_call x1, Pallas kernels, attention_forward(): pl.pallas_call(functools.partial(attention_forward_kernel, steps // KV_HE...  19.9 us
    ppermute x26, starting transfers between devices, flip(): return lax.ppermute(array, 'grp', [(i, i ^ mask) for i in range(members)])  18.7 us
  transfers between devices with their start and end apart: 41, of which 21 were waited for; matrix products, arithmetic and copies ran while one was open for 18% of the time, Pallas kernels for 22%

profile of v5, /device:TPU:0, one launch (start us, length us, event | category | flops | bytes accessed | tf_op | source)
XLA Modules:
  0.0 498.8 jit_solution(14621715432354387520)
XLA Ops:
  8.0 5.2 %constant_dynamic-slice_fusion.2 = (bf16[512,1408]{1,0:T(8,128)(2,1)}, bf16[512,1408]{1,0:T(8,128)(2,1)}, bf16[512,1408]{1,0:T(8,128)(2,1)}, bf16[512,1408]{1,0:T(8,128)(2,1)}) fusion(bf16[2048,1408]{1,0:T(8,128)(2,1)} %param.34, s32[]{:T(128)S(6)} %select_n.259, s32[]{:T(128)S(6)} %select_n.231, s32[]{:T(128)S(6)} %select_n.230, s32[]{:T(128)S(6)} %select_n.258), kind=kLoop, calls=%fused_computation.177 | loop fusion | bytes 11534352 | tf_op jit(solution)/shard_map/dynamic_slice | solution.py:347
  13.2 3.0 collective-permute-start
  16.2 3.2 dynamic-slice_bitcast_fusion
  24.2 2.0 fusion.86
  45.0 2.9 and_select_fusion.bias_ref
  47.9 5.0 %collective-permute-done.1 = bf16[1408,256]{1,0:T(8,128)(2,1)} collective-permute-done((bf16[1408,256]{1,0:T(8,128)(2,1)}, bf16[1408,256]{1,0:T(8,128)(2,1)}, u32[]{:S(2)}, u32[]{:S(2)}) %collective-permute-start.1) | collective-permute-done | bytes 720928 | tf_op jit(solution)/shard_map/ppermute | solution.py:333
  52.9 21.5 %collective-permute-done.3 = bf16[1408,256]{1,0:T(8,128)(2,1)} collective-permute-done((bf16[1408,256]{1,0:T(8,128)(2,1)}, bf16[1408,256]{1,0:T(8,128)(2,1)}, u32[]{:S(2)}, u32[]{:S(2)}) %collective-permute-start.3) | collective-permute-done | bytes 720928 | tf_op jit(solution)/shard_map/ppermute | solution.py:333
  76.6 3.0 pad_maximum_fusion.refs_8_.refs_2_
  79.6 24.7 %all-gather.3.cloned.1.call-done = bf16[2048,2560]{0,1:T(8,128)(2,1)} async-done(((bf16[2048,320]{0,1:T(8,128)(2,1)}), bf16[2048,2560]{0,1:T(8,128)(2,1)}) %all-gather.3.cloned.1.call-update) | async-done | bytes 10485776 | tf_op jit(solution)/shard_map/all_gather | solution.py:947
  104.3 5.6 %fusion.109 = f32[256,2560]{1,0:T(8,128)S(1)} fusion(bf16[256,2048]{1,0:T(8,128)(2,1)S(1)} %fusion.11.norm1_ref.norm_ref, bf16[2048,2560]{0,1:T(8,128)(2,1)} %all-gather.3.cloned.1.call-done), kind=kOutput, calls=%fused_computation.246 | convolution fusion | flops 2684354560 | bytes 14155776 | tf_op jit(solution)/shard_map/dot_general | solution.py:26
  111.0 10.9 %collective-permute-done.4.refs_5_ = bf16[512,1408]{1,0:T(8,128)(2,1)} collective-permute-done((bf16[512,1408]{1,0:T(8,128)(2,1)}, bf16[512,1408]{1,0:T(8,128)(2,1)}, u32[]{:S(2)}, u32[]{:S(2)}) %collective-permute-start.4) | collective-permute-done | bytes 1441824 | tf_op jit(solution)/shard_map/ppermute | solution.py:333
  123.8 2.5 collective-permute-start.9
  127.4 9.2 %collective-permute-done.7 = bf16[256,512]{1,0:T(8,128)(2,1)S(1)} collective-permute-done((bf16[256,512]{1,0:T(8,128)(2,1)S(1)}, bf16[256,512]{1,0:T(8,128)(2,1)S(1)}, u32[]{:S(2)}, u32[]{:S(2)}) %collective-permute-start.7) | collective-permute-done | bytes 262176 | tf_op jit(solution)/shard_map/ppermute | solution.py:333
  139.3 6.5 %collective-permute-done.11 = bf16[256,512]{1,0:T(8,128)(2,1)S(1)} collective-permute-done((bf16[256,512]{1,0:T(8,128)(2,1)S(1)}, bf16[256,512]{1,0:T(8,128)(2,1)S(1)}, u32[]{:S(2)}, u32[]{:S(2)}) %collective-permute-start.11) | collective-permute-done | bytes 262176 | tf_op jit(solution)/shard_map/ppermute | solution.py:333
  154.1 2.7 fusion.28.q_ref
  156.8 19.9 %attention_forward.1 = (bf16[256,2048]{1,0:T(8,128)(2,1)S(1)}, f32[16,2,256]{2,1,0:T(2,128)S(1)}) custom-call(s32[4]{0:T(128)S(1)} %pad_add_fusion.span, bf16[256,2048]{1,0:T(8,128)(2,1)S(1)} %fusion.28.q_ref, bf16[2048,512]{1,0:T(8,128)(2,1)S(1)} %constant_dynamic-update-slice_fusion.key_ref.value_ref, ...), custom_call_target="tpu_custom_call" | custom-call | flops 4294967296 | bytes 18874368 | tf_op jit(solution)/shard_map/attention_forward/pallas_call | solution.py:147
  177.3 7.6 %collective-permute-done.15.refs_9_.refs_3_ = bf16[1,1408,256]{2,1,0:T(8,128)(2,1)} collective-permute-done((bf16[1,1408,256]{2,1,0:T(8,128)(2,1)S(1)}, bf16[1,1408,256]{2,1,0:T(8,128)(2,1)}, u32[]{:S(2)}, u32[]{:S(2)}) %collective-permute-start.15) | collective-permute-done | bytes 720928 | tf_op jit(solution)/shard_map/ppermute | solution.py:333
  184.9 7.0 %collective-permute-done.14.own_g = bf16[256,2048]{1,0:T(8,128)(2,1)} collective-permute-done((bf16[256,2048]{1,0:T(8,128)(2,1)S(1)}, bf16[256,2048]{1,0:T(8,128)(2,1)}, u32[]{:S(2)}, u32[]{:S(2)}) %collective-permute-start.14) | collective-permute-done | bytes 1048608 | tf_op jit(solution)/shard_map/ppermute | solution.py:333
  197.2 13.6 %collective-permute-done.18.refs_10_.refs_4_ = bf16[1,1408,256]{2,1,0:T(8,128)(2,1)} collective-permute-done((bf16[1,1408,256]{2,1,0:T(8,128)(2,1)}, bf16[1,1408,256]{2,1,0:T(8,128)(2,1)}, u32[]{:S(2)}, u32[]{:S(2)}) %collective-permute-start.18) | collective-permute-done | bytes 720928 | tf_op jit(solution)/shard_map/ppermute | solution.py:333
  213.5 6.7 %multiply_reduce_fusion.1 = (f32[256]{0:T(256)S(1)}, f32[256,2048]{1,0:T(8,128)S(1)}) fusion(f32[256,2048]{1,0:T(8,128)} %convolution_multiply_fusion.1, bf16[256,2048]{1,0:T(8,128)(2,1)S(1)} %get-tuple-element.125.o_ref.attended_ref, bf16[2048,2048]{1,0:T(8,128)(2,1)} %all-gather.5.cloned.1.call-done, bf16[256,2048]{1,0:T(8,128)(2,1)} %param.25), kind=kOutput, calls=%fused_computation.58 | convolution fusion | flops 2150104832 | bytes 14681088 | tf_op jit(solution)/shard_map/dot_general | solution.py:26
  221.5 8.1 %collective-permute-done.20.refs_12_.refs_6_ = bf16[1,1408,256]{2,1,0:T(8,128)(2,1)S(1)} collective-permute-done((bf16[1,1408,256]{2,1,0:T(8,128)(2,1)}, bf16[1,1408,256]{2,1,0:T(8,128)(2,1)S(1)}, u32[]{:S(2)}, u32[]{:S(2)}) %collective-permute-start.20) | collective-permute-done | bytes 720928 | tf_op jit(solution)/shard_map/ppermute | solution.py:338
  233.5 2.4 collective-permute-done.21.near_x
  239.7 39.6 %feed_forward.2 = (f32[256,2176]{1,0:T(8,128)}, bf16[256,2176]{1,0:T(8,128)(2,1)}, bf16[512,1408]{1,0:T(8,128)(2,1)}, f32[96,1408]{1,0:T(8,128)S(1)}) custom-call(s32[3]{0:T(128)S(1)} %pad_add_fusion.1.meta, bf16[256,2176]{1,0:T(8,128)(2,1)} %concatenate.64.own_x, bf16[256,2176]{1,0:T(8,128)(2,1)} %collective-permute-done.21.near_x, ...), custom_call_target="tpu_custom_call" | custom-call | flops 14763950080 | bytes 38273024 | tf_op jit(solution)/shard_map/feed_forward/pallas_call | solution.py:642
  279.6 2.6 collective-permute-done.24.near_x
  283.2 29.2 %feed_forward.3 = (f32[256,2176]{1,0:T(8,128)}, bf16[256,2176]{1,0:T(8,128)(2,1)}, bf16[512,1408]{1,0:T(8,128)(2,1)}, f32[96,1408]{1,0:T(8,128)S(1)}) custom-call(s32[3]{0:T(128)S(1)} %pad_add_fusion.1.meta, bf16[256,2176]{1,0:T(8,128)(2,1)} %copy-done.126, bf16[256,2176]{1,0:T(8,128)(2,1)} %copy-done.127, bf16[256,2048]{1,0:T(8,128)(2,1)} %collective-permute-done.14.own_g, ...), custom_call_target="tpu_custom_call" | custom-call | flops 14763950080 | bytes 38273024 | tf_op jit(solution)/shard_map/feed_forward/pallas_call | solution.py:642
  313.8 2.6 collective-permute-done.25
  316.4 3.1 add_convert_fusion
  328.0 10.2 %down_projection.1 = (f32[256,2176]{1,0:T(8,128)S(1)}, bf16[256,2176]{1,0:T(8,128)(2,1)S(1)}, bf16[256,2176]{1,0:T(8,128)(2,1)S(1)}, bf16[256,2176]{1,0:T(8,128)(2,1)S(1)}) custom-call(s32[3]{0:T(128)S(1)} %copy-done.58, bf16[32,1408]{1,0:T(8,128)(2,1)S(1)} %copy-done.50, bf16[512,1408]{1,0:T(8,128)(2,1)S(1)} %copy-done.66, ...), custom_call_target="tpu_custom_call" | custom-call | flops 5905580032 | bytes 14155776 | tf_op jit(solution)/shard_map/down_projection/pallas_call | solution.py:616
  338.2 8.3 %collective-permute-done.26 = bf16[256,2176]{1,0:T(8,128)(2,1)} collective-permute-done((bf16[256,2176]{1,0:T(8,128)(2,1)}, bf16[256,2176]{1,0:T(8,128)(2,1)}, u32[]{:S(2)}, u32[]{:S(2)}) %collective-permute-start.26) | collective-permute-done | bytes 1114144 | tf_op jit(solution)/shard_map/ppermute | solution.py:333
  346.5 2.0 convert_add_fusion.2
  352.2 2.1 fusion.102
  355.9 3.3 fusion.3.do_ref
  365.6 37.6 %attention_backward.1 = (bf16[256,2048]{1,0:T(8,128)(2,1)S(1)}, bf16[8,256,512]{2,1,0:T(8,128)(2,1)S(1)}) custom-call(s32[4]{0:T(128)S(1)} %copy-done.56, bf16[256,2048]{1,0:T(8,128)(2,1)S(1)} %copy-done.20, bf16[256,2048]{1,0:T(8,128)(2,1)S(1)} %copy-done.65, bf16[256,2048]{1,0:T(8,128)(2,1)S(1)} %copy-done.22, f32[16,2,256]{2,1,0:T(2,128)S(1)} %copy-done.69, ...), custom_call_target="tpu_custom_call" | custom-call | flops 10737418240 | bytes 13631488 | tf_op jit(solution)/shard_map/attention_backward/pallas_call | solution.py:290
  405.5 4.3 all-to-all-start
  409.8 7.5 %fusion = f32[256,2048]{1,0:T(8,128)} fusion(bf16[256,2048]{1,0:T(8,128)(2,1)} %copy-done.24, bf16[2048,2560]{0,1:T(8,128)(2,1)} %all-gather.3.cloned.1.call-done), kind=kOutput, calls=%fused_computation | convolution fusion | flops 2147483648 | bytes 11534336 | tf_op jit(solution)/shard_map/dot_general | solution.py:30
  417.4 2.6 convert_add_fusion.1
  425.6 12.8 %all-to-all-done.received_ref = bf16[8,256,512]{2,1,0:T(8,128)(2,1)} async-done(((bf16[8,256,512]{2,1,0:T(8,128)(2,1)}), bf16[8,256,512]{2,1,0:T(8,128)(2,1)}, u32[]{:S(2)}, u32[]{:S(2)}) %all-to-all-start) | async-done | bytes 2097184 | tf_op jit(solution)/shard_map/all_to_all | solution.py:1104
  442.2 3.5 key_value_gradients.1
  445.7 4.6 all-to-all-start.1
  450.4 2.1 convolution_add_fusion.2
  452.7 3.1 fusion.21
  457.3 2.4 collective-permute-start.34
  461.2 2.5 convolution_add_fusion.1
  465.6 4.4 all-to-all-done.1
  473.2 2.4 collective-permute-start.31
  475.6 3.5 collective-permute-done.30.refs_2_
  479.1 3.1 collective-permute-start.32
  482.2 4.2 fusion.15
  (437 shorter events, 102.6 us)
Async XLA Ops:
  7.2 97.1 %all-gather.3.cloned.1.call-start = ((), (), s32[]{:S(2)}) async-start(), calls=%async_computation.3 | async-start | bytes 11796480 | tf_op jit(solution)/shard_map/all_gather | solution.py:947
  7.9 189.2 %all-gather.5.cloned.1.call-start = ((), (), s32[]{:S(2)}) async-start(), calls=%async_computation.4 | async-start | bytes 9437184 | tf_op jit(solution)/shard_map/all_gather | solution.py:1037
  13.2 61.2 %collective-permute-start = (bf16[512,1408]{1,0:T(8,128)(2,1)}, bf16[512,1408]{1,0:T(8,128)(2,1)}, u32[]{:S(2)}, u32[]{:S(2)}) collective-permute-start(bf16[512,1408]{1,0:T(8,128)(2,1)} %get-tuple-element.252.refs_0_), channel_id=1, source_target_pairs={{0,4},{1,5},{2,6},{3,7},{4,0},{5,1},{6,2},{7,3},{8,12},{9,13},{10,... | collective-permute-start | bytes 4325384 | tf_op jit(solution)/shard_map/ppermute | solution.py:333
  19.4 33.4 %collective-permute-start.1 = (bf16[1408,256]{1,0:T(8,128)(2,1)}, bf16[1408,256]{1,0:T(8,128)(2,1)}, u32[]{:S(2)}, u32[]{:S(2)}) collective-permute-start(bf16[1408,256]{1,0:T(8,128)(2,1)} %get-tuple-element.258), channel_id=1, source_target_pairs={{0,2},{1,3},{2,0},{3,1},{4,6},{5,7},{6,4},{7,5},{8,10},{9,11},{10,... | collective-permute-start | bytes 2162696 | tf_op jit(solution)/shard_map/ppermute | solution.py:333
  20.9 31.9 %collective-permute-start.2 = (bf16[1408,256]{1,0:T(8,128)(2,1)}, bf16[1408,256]{1,0:T(8,128)(2,1)}, u32[]{:S(2)}, u32[]{:S(2)}) collective-permute-start(bf16[1408,256]{1,0:T(8,128)(2,1)} %get-tuple-element.257), channel_id=1, source_target_pairs={{0,1},{1,0},{2,3},{3,2},{4,5},{5,4},{6,7},{7,6},{8,9},{9,8},{10,11... | collective-permute-start | bytes 2162696 | tf_op jit(solution)/shard_map/ppermute | solution.py:333
  20.9 53.4 %collective-permute-start.3 = (bf16[1408,256]{1,0:T(8,128)(2,1)}, bf16[1408,256]{1,0:T(8,128)(2,1)}, u32[]{:S(2)}, u32[]{:S(2)}) collective-permute-start(bf16[1408,256]{1,0:T(8,128)(2,1)} %get-tuple-element.259), channel_id=1, source_target_pairs={{0,3},{1,2},{2,1},{3,0},{4,7},{5,6},{6,5},{7,4},{8,11},{9,10},{10,... | collective-permute-start | bytes 2162696 | tf_op jit(solution)/shard_map/ppermute | solution.py:333
  21.6 383.9 %reduce-scatter.2.cloned.1.call-start = ((), (), s32[]{:S(2)}) async-start(), calls=%async_computation.5 | async-start | bytes 1327104 | tf_op jit(solution)/shard_map/reduce_scatter | solution.py:1098
  31.0 125.7 %copy-start.55 = (s32[4]{0:T(128)}, s32[4]{0:T(128)S(1)}, u32[]{:S(2)}) copy-start(s32[4]{0:T(128)S(1)} %pad_add_fusion.span) | copy-start | bytes 52
  34.8 75.2 %copy-start.32 = (bf16[64,512]{1,0:T(8,128)(2,1)}, bf16[64,512]{1,0:T(8,128)(2,1)S(1)}, u32[]{:S(2)}) copy-start(bf16[64,512]{1,0:T(8,128)(2,1)S(1)} %fusion.53.right_ref) | copy-start | bytes 196612
  40.5 308.0 %copy-start.12 = (f32[256,32]{1,0:T(8,128)}, f32[256,32]{1,0:T(8,128)S(1)}, u32[]{:S(2)}) copy-start(f32[256,32]{1,0:T(8,128)S(1)} %get-tuple-element.276.own_seen.seen_ref) | copy-start | bytes 98308
  40.8 241.4 %copy-start.37 = (bf16[32,2048]{1,0:T(8,128)(2,1)}, bf16[32,2048]{1,0:T(8,128)(2,1)S(1)}, u32[]{:S(2)}) copy-start(bf16[32,2048]{1,0:T(8,128)(2,1)S(1)} %convolution_convert_fusion.6.lower_ref) | copy-start | bytes 393220
  42.0 84.2 %copy-start.14 = (bf16[32,2048]{1,0:T(8,128)(2,1)}, bf16[32,2048]{1,0:T(8,128)(2,1)S(1)}, u32[]{:S(2)}) copy-start(bf16[32,2048]{1,0:T(8,128)(2,1)S(1)} %convolution_convert_fusion.8.asking_ref) | copy-start | bytes 393220
  74.3 47.6 %collective-permute-start.4 = (bf16[512,1408]{1,0:T(8,128)(2,1)}, bf16[512,1408]{1,0:T(8,128)(2,1)}, u32[]{:S(2)}, u32[]{:S(2)}) collective-permute-start(bf16[512,1408]{1,0:T(8,128)(2,1)} %get-tuple-element.111.refs_1_), channel_id=1, source_target_pairs={{0,4},{1,5},{2,6},{3,7},{4,0},{5,1},{6,2},{7,3},{8,12},{9,13},{10,... | collective-permute-start | bytes 4325384 | tf_op jit(solution)/shard_map/ppermute | solution.py:333
  74.5 47.5 %collective-permute-start.5 = (bf16[512,1408]{1,0:T(8,128)(2,1)}, bf16[512,1408]{1,0:T(8,128)(2,1)}, u32[]{:S(2)}, u32[]{:S(2)}) collective-permute-start(bf16[512,1408]{1,0:T(8,128)(2,1)} %collective-permute-done.refs_4_), channel_id=1, source_target_pairs={{0,8},{8,0},{16,24},{24,16},{1,9},{9,1},{17,25},{25,17},{2,10},{10... | collective-permute-start | bytes 4325384 | tf_op jit(solution)/shard_map/ppermute | solution.py:338
  76.6 49.6 %copy-start.16 = (bf16[256,96]{1,0:T(8,128)(2,1)}, bf16[256,96]{1,0:T(8,128)(2,1)S(1)}, u32[]{:S(2)}) copy-start(bf16[256,96]{1,0:T(8,128)(2,1)S(1)} %fusion.24) | copy-start | bytes 147460
  122.0 17.3 %collective-permute-start.6 = (bf16[256,512]{1,0:T(8,128)(2,1)S(1)}, bf16[256,512]{1,0:T(8,128)(2,1)S(1)}, u32[]{:S(2)}, u32[]{:S(2)}) collective-permute-start(bf16[256,512]{1,0:T(8,128)(2,1)S(1)} %pad_maximum_fusion.2), channel_id=1, source_target_pairs={{0,1},{1,0},{2,3},{3,2},{4,5},{5,4},{6,7},{7,6},{8,9},{9,8},{10,11... | collective-permute-start | bytes 786440 | tf_op jit(solution)/shard_map/ppermute | solution.py:333
  122.1 14.6 %collective-permute-start.7 = (bf16[256,512]{1,0:T(8,128)(2,1)S(1)}, bf16[256,512]{1,0:T(8,128)(2,1)S(1)}, u32[]{:S(2)}, u32[]{:S(2)}) collective-permute-start(bf16[256,512]{1,0:T(8,128)(2,1)S(1)} %pad_maximum_fusion.2), channel_id=1, source_target_pairs={{0,2},{1,3},{2,0},{3,1},{4,6},{5,7},{6,4},{7,5},{8,10},{9,11},{10,... | collective-permute-start | bytes 786440 | tf_op jit(solution)/shard_map/ppermute | solution.py:333
  123.8 14.1 %collective-permute-start.9 = (bf16[256,512]{1,0:T(8,128)(2,1)S(1)}, bf16[256,512]{1,0:T(8,128)(2,1)S(1)}, u32[]{:S(2)}, u32[]{:S(2)}) collective-permute-start(bf16[256,512]{1,0:T(8,128)(2,1)S(1)} %pad_maximum_fusion.2), channel_id=1, source_target_pairs={{0,4},{1,5},{2,6},{3,7},{4,0},{5,1},{6,2},{7,3},{8,12},{9,13},{10,... | collective-permute-start | bytes 786440 | tf_op jit(solution)/shard_map/ppermute | solution.py:333
  136.7 9.2 %collective-permute-start.8 = (bf16[256,512]{1,0:T(8,128)(2,1)S(1)}, bf16[256,512]{1,0:T(8,128)(2,1)S(1)}, u32[]{:S(2)}, u32[]{:S(2)}) collective-permute-start(bf16[256,512]{1,0:T(8,128)(2,1)S(1)} %collective-permute-done.7), channel_id=1, source_target_pairs={{0,1},{1,0},{2,3},{3,2},{4,5},{5,4},{6,7},{7,6},{8,9},{9,8},{10,11... | collective-permute-start | bytes 786440 | tf_op jit(solution)/shard_map/ppermute | solution.py:333
  137.8 8.0 %collective-permute-start.11 = (bf16[256,512]{1,0:T(8,128)(2,1)S(1)}, bf16[256,512]{1,0:T(8,128)(2,1)S(1)}, u32[]{:S(2)}, u32[]{:S(2)}) collective-permute-start(bf16[256,512]{1,0:T(8,128)(2,1)S(1)} %collective-permute-done.9), channel_id=1, source_target_pairs={{0,2},{1,3},{2,0},{3,1},{4,6},{5,7},{6,4},{7,5},{8,10},{9,11},{10,... | collective-permute-start | bytes 786440 | tf_op jit(solution)/shard_map/ppermute | solution.py:333
  139.2 6.7 %collective-permute-start.10 = (bf16[256,512]{1,0:T(8,128)(2,1)S(1)}, bf16[256,512]{1,0:T(8,128)(2,1)S(1)}, u32[]{:S(2)}, u32[]{:S(2)}) collective-permute-start(bf16[256,512]{1,0:T(8,128)(2,1)S(1)} %collective-permute-done.9), channel_id=1, source_target_pairs={{0,1},{1,0},{2,3},{3,2},{4,5},{5,4},{6,7},{7,6},{8,9},{9,8},{10,11... | collective-permute-start | bytes 786440 | tf_op jit(solution)/shard_map/ppermute | solution.py:333
  145.9 1.9 collective-permute-start.12
  147.8 44.1 %collective-permute-start.16 = (bf16[512,1408]{1,0:T(8,128)(2,1)}, bf16[512,1408]{1,0:T(8,128)(2,1)S(1)}, u32[]{:S(2)}, u32[]{:S(2)}) collective-permute-start(bf16[512,1408]{1,0:T(8,128)(2,1)} %collective-permute-done.4.refs_5_), channel_id=1, source_target_pairs={{0,8},{8,0},{16,24},{24,16},{1,9},{9,1},{17,25},{25,17},{2,10},{10... | collective-permute-start | bytes 4325384 | tf_op jit(solution)/shard_map/ppermute | solution.py:338
  149.8 35.1 %collective-permute-start.13 = (bf16[256,2048]{1,0:T(8,128)(2,1)S(1)}, bf16[256,2048]{1,0:T(8,128)(2,1)S(1)}, u32[]{:S(2)}, u32[]{:S(2)}) collective-permute-start(bf16[256,2048]{1,0:T(8,128)(2,1)S(1)} %copy-done.4), channel_id=1, source_target_pairs={{0,1},{1,0},{2,3},{3,2},{4,5},{5,4},{6,7},{7,6},{8,9},{9,8},{10,11... | collective-permute-start | bytes 3145736 | tf_op jit(solution)/shard_map/ppermute | solution.py:333
  149.9 42.1 %collective-permute-start.14 = (bf16[256,2048]{1,0:T(8,128)(2,1)S(1)}, bf16[256,2048]{1,0:T(8,128)(2,1)}, u32[]{:S(2)}, u32[]{:S(2)}) collective-permute-start(bf16[256,2048]{1,0:T(8,128)(2,1)S(1)} %copy-done.4), channel_id=1, source_target_pairs={{0,2},{1,3},{2,0},{3,1},{4,6},{5,7},{6,4},{7,5},{8,10},{9,11},{10,... | collective-permute-start | bytes 3145736 | tf_op jit(solution)/shard_map/ppermute | solution.py:333
  151.7 33.2 %collective-permute-start.15 = (bf16[1,1408,256]{2,1,0:T(8,128)(2,1)S(1)}, bf16[1,1408,256]{2,1,0:T(8,128)(2,1)}, u32[]{:S(2)}, u32[]{:S(2)}) collective-permute-start(bf16[1,1408,256]{2,1,0:T(8,128)(2,1)S(1)} %get-tuple-element.255), channel_id=1, source_target_pairs={{0,4},{1,5},{2,6},{3,7},{4,0},{5,1},{6,2},{7,3},{8,12},{9,13},{10,... | collective-permute-start | bytes 2162696 | tf_op jit(solution)/shard_map/ppermute | solution.py:333
  191.9 20.1 %collective-permute-start.17 = (bf16[256,2048]{1,0:T(8,128)(2,1)}, bf16[256,2048]{1,0:T(8,128)(2,1)}, u32[]{:S(2)}, u32[]{:S(2)}) collective-permute-start(bf16[256,2048]{1,0:T(8,128)(2,1)} %collective-permute-done.14.own_g), channel_id=1, source_target_pairs={{0,1},{1,0},{2,3},{3,2},{4,5},{5,4},{6,7},{7,6},{8,9},{9,8},{10,11... | collective-permute-start | bytes 3145736 | tf_op jit(solution)/shard_map/ppermute | solution.py:333
  191.9 18.9 %collective-permute-start.18 = (bf16[1,1408,256]{2,1,0:T(8,128)(2,1)}, bf16[1,1408,256]{2,1,0:T(8,128)(2,1)}, u32[]{:S(2)}, u32[]{:S(2)}) collective-permute-start(bf16[1,1408,256]{2,1,0:T(8,128)(2,1)} %get-tuple-element.127), channel_id=1, source_target_pairs={{0,4},{1,5},{2,6},{3,7},{4,0},{5,1},{6,2},{7,3},{8,12},{9,13},{10,... | collective-permute-start | bytes 2162696 | tf_op jit(solution)/shard_map/ppermute | solution.py:333
  193.5 18.5 %collective-permute-start.19 = (bf16[1,1408,256]{2,1,0:T(8,128)(2,1)}, bf16[1,1408,256]{2,1,0:T(8,128)(2,1)}, u32[]{:S(2)}, u32[]{:S(2)}) collective-permute-start(bf16[1,1408,256]{2,1,0:T(8,128)(2,1)} %collective-permute-done.15.refs_9_.refs_3_), channel_id=1, source_target_pairs={{0,8},{8,0},{16,24},{24,16},{1,9},{9,1},{17,25},{25,17},{2,10},{10... | collective-permute-start | bytes 2162696 | tf_op jit(solution)/shard_map/ppermute | solution.py:338
  212.0 17.6 %collective-permute-start.20 = (bf16[1,1408,256]{2,1,0:T(8,128)(2,1)}, bf16[1,1408,256]{2,1,0:T(8,128)(2,1)S(1)}, u32[]{:S(2)}, u32[]{:S(2)}) collective-permute-start(bf16[1,1408,256]{2,1,0:T(8,128)(2,1)} %collective-permute-done.18.refs_10_.refs_4_), channel_id=1, source_target_pairs={{0,8},{8,0},{16,24},{24,16},{1,9},{9,1},{17,25},{25,17},{2,10},{10... | collective-permute-start | bytes 2162696 | tf_op jit(solution)/shard_map/ppermute | solution.py:338
  232.8 3.1 collective-permute-start.21
  232.9 49.3 %copy-start.57 = (s32[3]{0:T(128)}, s32[3]{0:T(128)S(1)}, u32[]{:S(2)}) copy-start(s32[3]{0:T(128)S(1)} %pad_add_fusion.1.meta) | copy-start | bytes 40
  232.9 46.4 %collective-permute-start.22 = (bf16[256,2176]{1,0:T(8,128)(2,1)}, bf16[256,2176]{1,0:T(8,128)(2,1)S(1)}, u32[]{:S(2)}, u32[]{:S(2)}) collective-permute-start(bf16[256,2176]{1,0:T(8,128)(2,1)} %concatenate.64.own_x), channel_id=1, source_target_pairs={{0,2},{1,3},{2,0},{3,1},{4,6},{5,7},{6,4},{7,5},{8,10},{9,11},{10,... | collective-permute-start | bytes 3342344 | tf_op jit(solution)/shard_map/ppermute | solution.py:333
  279.4 2.8 collective-permute-start.24
  313.3 3.1 collective-permute-start.25
  313.4 33.0 %collective-permute-start.23 = (bf16[256,2176]{1,0:T(8,128)(2,1)}, bf16[256,2176]{1,0:T(8,128)(2,1)}, u32[]{:S(2)}, u32[]{:S(2)}) collective-permute-start(bf16[256,2176]{1,0:T(8,128)(2,1)} %get-tuple-element.147), channel_id=1, source_target_pairs={{0,1},{1,0},{2,3},{3,2},{4,5},{5,4},{6,7},{7,6},{8,9},{9,8},{10,11... | collective-permute-start | bytes 3342344 | tf_op jit(solution)/shard_map/ppermute | solution.py:333
  319.5 26.9 %collective-permute-start.26 = (bf16[256,2176]{1,0:T(8,128)(2,1)}, bf16[256,2176]{1,0:T(8,128)(2,1)}, u32[]{:S(2)}, u32[]{:S(2)}) collective-permute-start(bf16[256,2176]{1,0:T(8,128)(2,1)} %add_convert_fusion), channel_id=1, source_target_pairs={{0,2},{1,3},{2,0},{3,1},{4,6},{5,7},{6,4},{7,5},{8,10},{9,11},{10,... | collective-permute-start | bytes 3342344 | tf_op jit(solution)/shard_map/ppermute | solution.py:333
  360.0 57.4 %collective-permute-start.27 = (bf16[256,2176]{1,0:T(8,128)(2,1)}, bf16[256,2176]{1,0:T(8,128)(2,1)}, u32[]{:S(2)}, u32[]{:S(2)}) collective-permute-start(bf16[256,2176]{1,0:T(8,128)(2,1)} %copy-done.61), channel_id=1, source_target_pairs={{0,1},{1,0},{2,3},{3,2},{4,5},{5,4},{6,7},{7,6},{8,9},{9,8},{10,11... | collective-permute-start | bytes 3342344 | tf_op jit(solution)/shard_map/ppermute | solution.py:333
  360.0 57.4 %collective-permute-start.28 = (bf16[256,2176]{1,0:T(8,128)(2,1)}, bf16[256,2176]{1,0:T(8,128)(2,1)}, u32[]{:S(2)}, u32[]{:S(2)}) collective-permute-start(bf16[256,2176]{1,0:T(8,128)(2,1)} %copy-done.60), channel_id=1, source_target_pairs={{0,2},{1,3},{2,0},{3,1},{4,6},{5,7},{6,4},{7,5},{8,10},{9,11},{10,... | collective-permute-start | bytes 3342344 | tf_op jit(solution)/shard_map/ppermute | solution.py:333
  360.5 56.9 %collective-permute-start.29 = (bf16[256,2176]{1,0:T(8,128)(2,1)}, bf16[256,2176]{1,0:T(8,128)(2,1)}, u32[]{:S(2)}, u32[]{:S(2)}) collective-permute-start(bf16[256,2176]{1,0:T(8,128)(2,1)} %copy-done.59), channel_id=1, source_target_pairs={{0,3},{1,2},{2,1},{3,0},{4,7},{5,6},{6,5},{7,4},{8,11},{9,10},{10,... | collective-permute-start | bytes 3342344 | tf_op jit(solution)/shard_map/ppermute | solution.py:333
  405.5 32.9 %all-to-all-start = ((bf16[8,256,512]{2,1,0:T(8,128)(2,1)}), bf16[8,256,512]{2,1,0:T(8,128)(2,1)}, u32[]{:S(2)}, u32[]{:S(2)}) async-start(bf16[8,256,512]{2,1,0:T(8,128)(2,1)} %copy-done.11), calls=%async_computation.1 | async-start | bytes 4194304 | tf_op jit(solution)/shard_map/all_to_all | solution.py:1104
  445.7 24.3 %all-to-all-start.1 = ((bf16[8,352,256]{2,1,0:T(8,128)(2,1)}), bf16[8,352,256]{2,1,0:T(8,128)(2,1)}, u32[]{:S(2)}, u32[]{:S(2)}) async-start(bf16[8,352,256]{2,1,0:T(8,128)(2,1)} %get-tuple-element.184), calls=%async_computation.2 | async-start | bytes 2883584 | tf_op jit(solution)/shard_map/all_to_all | solution.py:729
  455.9 31.2 %collective-permute-start.33 = (bf16[96,704]{1,0:T(8,128)(2,1)S(1)}, bf16[96,704]{1,0:T(8,128)(2,1)S(1)}, u32[]{:S(2)}, u32[]{:S(2)}) collective-permute-start(bf16[96,704]{1,0:T(8,128)(2,1)S(1)} %bitcast.104), channel_id=1, source_target_pairs={{0,8},{8,16},{16,24},{24,0},{1,9},{9,17},{17,25},{25,1},{2,10},{10... | collective-permute-start | bytes 405512 | tf_op jit(solution)/shard_map/ppermute | solution.py:901
  457.3 29.7 %collective-permute-start.34 = (bf16[96,704]{1,0:T(8,128)(2,1)S(1)}, bf16[96,704]{1,0:T(8,128)(2,1)S(1)}, u32[]{:S(2)}, u32[]{:S(2)}) collective-permute-start(bf16[96,704]{1,0:T(8,128)(2,1)S(1)} %bitcast.105), channel_id=1, source_target_pairs={{0,16},{8,24},{16,0},{24,8},{1,17},{9,25},{17,1},{25,9},{2,18},{10... | collective-permute-start | bytes 405512 | tf_op jit(solution)/shard_map/ppermute | solution.py:901
  459.8 27.3 %collective-permute-start.35 = (bf16[96,704]{1,0:T(8,128)(2,1)S(1)}, bf16[96,704]{1,0:T(8,128)(2,1)S(1)}, u32[]{:S(2)}, u32[]{:S(2)}) collective-permute-start(bf16[96,704]{1,0:T(8,128)(2,1)S(1)} %bitcast.106), channel_id=1, source_target_pairs={{0,24},{8,0},{16,8},{24,16},{1,25},{9,1},{17,9},{25,17},{2,26},{10... | collective-permute-start | bytes 405512 | tf_op jit(solution)/shard_map/ppermute | solution.py:901
  471.6 7.5 %collective-permute-start.30 = (bf16[352,256]{1,0:T(8,128)(2,1)S(1)}, bf16[352,256]{1,0:T(8,128)(2,1)S(1)}, u32[]{:S(2)}, u32[]{:S(2)}) collective-permute-start(bf16[352,256]{1,0:T(8,128)(2,1)S(1)} %reduce_sum.62.refs_1_), channel_id=1, source_target_pairs={{0,8},{8,16},{16,24},{24,0},{1,9},{9,17},{17,25},{25,1},{2,10},{10... | collective-permute-start | bytes 540680 | tf_op jit(solution)/shard_map/ppermute | solution.py:901
  473.2 13.2 %collective-permute-start.31 = (bf16[352,256]{1,0:T(8,128)(2,1)S(1)}, bf16[352,256]{1,0:T(8,128)(2,1)S(1)}, u32[]{:S(2)}, u32[]{:S(2)}) collective-permute-start(bf16[352,256]{1,0:T(8,128)(2,1)S(1)} %reduce_sum.62.refs_1_), channel_id=1, source_target_pairs={{0,16},{8,24},{16,0},{24,8},{1,17},{9,25},{17,1},{25,9},{2,18},{10... | collective-permute-start | bytes 540680 | tf_op jit(solution)/shard_map/ppermute | solution.py:901
  479.1 7.9 %collective-permute-start.32 = (bf16[352,256]{1,0:T(8,128)(2,1)S(1)}, bf16[352,256]{1,0:T(8,128)(2,1)S(1)}, u32[]{:S(2)}, u32[]{:S(2)}) collective-permute-start(bf16[352,256]{1,0:T(8,128)(2,1)S(1)} %reduce_sum.62.refs_1_), channel_id=1, source_target_pairs={{0,24},{8,0},{16,8},{24,16},{1,25},{9,1},{17,9},{25,17},{2,26},{10... | collective-permute-start | bytes 540680 | tf_op jit(solution)/shard_map/ppermute | solution.py:901
  (127 other events, 959.8 us)
Sparse Core Ops, SparseCore 0:
  9.9 94.3 all-gather.2
  106.2 81.7 all-gather.4
  359.4 40.7 reduce-scatter.1

commit v6 on v5

--- a/solution.py
+++ b/solution.py
@@ -100,6 +100,7 @@
         rows = key_rows(span, index)
         bias = bias_ref[rows, :]
         new = []
+        flat = jnp.concatenate([v_ref[0, rows, :], v_ref[1, rows, :]], axis=0).T
         for pair, (peaks, totals, mixed) in enumerate(carry):
             tops, sums, parts, decays = [], [], [], []
             for side in range(2):
@@ -110,8 +111,9 @@
                 tops.append(top)
                 sums.append(totals[side] * decay + jnp.sum(probs, axis=0, keepdims=True))
                 decays.append(jnp.broadcast_to(decay, (HEAD_DIM, tokens)))
-                parts.append(mm_tn(v_ref[side, rows, :], probs.astype(BF16)))
-            mixed = mixed * jnp.concatenate(decays, axis=0) + (parts[0] + parts[1])
+                parts.append(probs.astype(BF16))
+            mixed = mixed * jnp.concatenate(decays, axis=0)
+            mixed = mixed + mm(flat, jnp.concatenate(parts, axis=0))
             new.append((tuple(tops), tuple(sums), mixed))
         return tuple(new)
 
@@ -232,6 +234,7 @@
         rows = key_rows(span, index)
         bias = bias_ref[rows, :]
         all_probs, all_dscores, new = [], [], []
+        flat = jnp.concatenate([k_ref[0, rows, :], k_ref[1, rows, :]], axis=0).T
         for pair, dquery in enumerate(dqueries):
             for side in range(2):
                 scores = mm_nt(k_ref[side, rows, :], queries[pair]) + bias
@@ -241,8 +244,7 @@
                 dscores = (probs * (dprobs - delta)).astype(BF16)
                 all_probs.append(probs.astype(BF16))
                 all_dscores.append(dscores)
-                dquery = dquery + mm_tn(k_ref[side, rows, :], dscores)
-            new.append(dquery)
+            new.append(dquery + mm(flat, jnp.concatenate(all_dscores[-2:], axis=0)))
         dk_sum[rows, :] += mm(jnp.concatenate(all_dscores, axis=1), query_stack)
         dv_sum[rows, :] += mm(jnp.concatenate(all_probs, axis=1), grad_stack)
         return tuple(new)

time: 507 us -> 497 us (0.980)
  Pallas kernels: 143 us -> 130 us
    pallas_call x2, Pallas kernels: 68.8 us -> 58.9 us  [feed_forward_pair(): pl.pallas_call(feed_forward_kernel, out_shape=(jax.ShapeDtypeStruct((coun...]
  transfers between devices with their start and end apart: 41 -> 41, of which waited for: 21 -> 22; matrix products, arithmetic and copies ran while one was open for 18% -> 18% of each run, Pallas kernels for 22% -> 20%
where the time goes in v6:
time: 497 us; the launch traced here: 489 us
  waiting for transfers between devices  160 us (32%)
  Pallas kernels  130 us (26%)
  local copies, waits for them, and re-layouts  52.8 us (11%)
  starting transfers between devices  46.7 us (9%)
  matrix products  43.2 us (9%)
  other arithmetic  37.4 us (8%)
  between operations  18.9 us (4%)
    ppermute x26, waiting for transfers between devices, flip(): return lax.ppermute(array, 'grp', [(i, i ^ mask) for i in range(members)])  102 us
    pallas_call x2, Pallas kernels, feed_forward_pair(): pl.pallas_call(feed_forward_kernel, out_shape=(jax.ShapeDtypeStruct((coun...  58.9 us
    pallas_call x1, Pallas kernels, attention_backward(): pl.pallas_call(functools.partial(attention_backward_kernel, per_kv), out_...  35.5 us
    unnamed x279, local copies, waits for them, and re-layouts  33.6 us
    all_gather x1, waiting for transfers between devices, shards(): qkv_full = lax.all_gather(qkv_weight, 'grp', axis=1, tiled=True)  24.7 us
    dot_general x15, matrix products, mm(): return jnp.dot(left, right, preferred_element_type=F32)  21.5 us
    ppermute x26, starting transfers between devices, flip(): return lax.ppermute(array, 'grp', [(i, i ^ mask) for i in range(members)])  18.7 us
    dot_general x8, matrix products, mm_nt(): lax.dot_general(left, right, (((1,), (1,)), ((), ())), preferred_element_...  18.6 us
  transfers between devices with their start and end apart: 41, of which 22 were waited for; matrix products, arithmetic and copies ran while one was open for 18% of the time, Pallas kernels for 20%

profile of v6, /device:TPU:0, one launch (start us, length us, event | category | flops | bytes accessed | tf_op | source)
XLA Modules:
  0.0 488.7 jit_solution(1326857024499315076)
XLA Ops:
  8.0 5.2 %constant_dynamic-slice_fusion.2 = (bf16[512,1408]{1,0:T(8,128)(2,1)}, bf16[512,1408]{1,0:T(8,128)(2,1)}, bf16[512,1408]{1,0:T(8,128)(2,1)}, bf16[512,1408]{1,0:T(8,128)(2,1)}) fusion(bf16[2048,1408]{1,0:T(8,128)(2,1)} %param.34, s32[]{:T(128)S(6)} %select_n.259, s32[]{:T(128)S(6)} %select_n.231, s32[]{:T(128)S(6)} %select_n.230, s32[]{:T(128)S(6)} %select_n.258), kind=kLoop, calls=%fused_computation.177 | loop fusion | bytes 11534352 | tf_op jit(solution)/shard_map/dynamic_slice | solution.py:349
  13.2 3.0 collective-permute-start
  16.2 3.2 dynamic-slice_bitcast_fusion
  24.2 2.0 fusion.86
  45.0 3.2 and_select_fusion.bias_ref
  48.2 4.7 collective-permute-done.1
  52.9 21.5 %collective-permute-done.3 = bf16[1408,256]{1,0:T(8,128)(2,1)} collective-permute-done((bf16[1408,256]{1,0:T(8,128)(2,1)}, bf16[1408,256]{1,0:T(8,128)(2,1)}, u32[]{:S(2)}, u32[]{:S(2)}) %collective-permute-start.3) | collective-permute-done | bytes 720928 | tf_op jit(solution)/shard_map/ppermute | solution.py:335
  76.6 3.0 pad_maximum_fusion.refs_8_.refs_2_
  79.6 24.7 %all-gather.3.cloned.1.call-done = bf16[2048,2560]{0,1:T(8,128)(2,1)} async-done(((bf16[2048,320]{0,1:T(8,128)(2,1)}), bf16[2048,2560]{0,1:T(8,128)(2,1)}) %all-gather.3.cloned.1.call-update) | async-done | bytes 10485776 | tf_op jit(solution)/shard_map/all_gather | solution.py:949
  104.3 5.6 %fusion.109 = f32[256,2560]{1,0:T(8,128)S(1)} fusion(bf16[256,2048]{1,0:T(8,128)(2,1)S(1)} %fusion.11.norm1_ref.norm_ref, bf16[2048,2560]{0,1:T(8,128)(2,1)} %all-gather.3.cloned.1.call-done), kind=kOutput, calls=%fused_computation.246 | convolution fusion | flops 2684354560 | bytes 14155776 | tf_op jit(solution)/shard_map/dot_general | solution.py:26
  111.0 10.9 %collective-permute-done.4.refs_5_ = bf16[512,1408]{1,0:T(8,128)(2,1)} collective-permute-done((bf16[512,1408]{1,0:T(8,128)(2,1)}, bf16[512,1408]{1,0:T(8,128)(2,1)}, u32[]{:S(2)}, u32[]{:S(2)}) %collective-permute-start.4) | collective-permute-done | bytes 1441824 | tf_op jit(solution)/shard_map/ppermute | solution.py:335
  123.8 2.5 collective-permute-start.9
  127.4 9.2 %collective-permute-done.7 = bf16[256,512]{1,0:T(8,128)(2,1)S(1)} collective-permute-done((bf16[256,512]{1,0:T(8,128)(2,1)S(1)}, bf16[256,512]{1,0:T(8,128)(2,1)S(1)}, u32[]{:S(2)}, u32[]{:S(2)}) %collective-permute-start.7) | collective-permute-done | bytes 262176 | tf_op jit(solution)/shard_map/ppermute | solution.py:335
  139.3 6.5 %collective-permute-done.11 = bf16[256,512]{1,0:T(8,128)(2,1)S(1)} collective-permute-done((bf16[256,512]{1,0:T(8,128)(2,1)S(1)}, bf16[256,512]{1,0:T(8,128)(2,1)S(1)}, u32[]{:S(2)}, u32[]{:S(2)}) %collective-permute-start.11) | collective-permute-done | bytes 262176 | tf_op jit(solution)/shard_map/ppermute | solution.py:335
  154.1 2.7 fusion.28.q_ref
  156.8 18.5 %attention_forward.1 = (bf16[256,2048]{1,0:T(8,128)(2,1)S(1)}, f32[16,2,256]{2,1,0:T(2,128)S(1)}) custom-call(s32[4]{0:T(128)S(1)} %pad_add_fusion.span, bf16[256,2048]{1,0:T(8,128)(2,1)S(1)} %fusion.28.q_ref, bf16[2048,512]{1,0:T(8,128)(2,1)S(1)} %constant_dynamic-update-slice_fusion.key_ref.value_ref, ...), custom_call_target="tpu_custom_call" | custom-call | flops 4294967296 | bytes 18874368 | tf_op jit(solution)/shard_map/attention_forward/pallas_call | solution.py:149
  176.0 8.9 %collective-permute-done.15.refs_9_.refs_3_ = bf16[1,1408,256]{2,1,0:T(8,128)(2,1)} collective-permute-done((bf16[1,1408,256]{2,1,0:T(8,128)(2,1)S(1)}, bf16[1,1408,256]{2,1,0:T(8,128)(2,1)}, u32[]{:S(2)}, u32[]{:S(2)}) %collective-permute-start.15) | collective-permute-done | bytes 720928 | tf_op jit(solution)/shard_map/ppermute | solution.py:335
  184.9 7.0 %collective-permute-done.14.own_g = bf16[256,2048]{1,0:T(8,128)(2,1)} collective-permute-done((bf16[256,2048]{1,0:T(8,128)(2,1)S(1)}, bf16[256,2048]{1,0:T(8,128)(2,1)}, u32[]{:S(2)}, u32[]{:S(2)}) %collective-permute-start.14) | collective-permute-done | bytes 1048608 | tf_op jit(solution)/shard_map/ppermute | solution.py:335
  197.2 13.6 %collective-permute-done.18.refs_10_.refs_4_ = bf16[1,1408,256]{2,1,0:T(8,128)(2,1)} collective-permute-done((bf16[1,1408,256]{2,1,0:T(8,128)(2,1)}, bf16[1,1408,256]{2,1,0:T(8,128)(2,1)}, u32[]{:S(2)}, u32[]{:S(2)}) %collective-permute-start.18) | collective-permute-done | bytes 720928 | tf_op jit(solution)/shard_map/ppermute | solution.py:335
  213.5 6.7 %multiply_reduce_fusion.1 = (f32[256]{0:T(256)S(1)}, f32[256,2048]{1,0:T(8,128)S(1)}) fusion(f32[256,2048]{1,0:T(8,128)} %convolution_multiply_fusion.1, bf16[256,2048]{1,0:T(8,128)(2,1)S(1)} %get-tuple-element.125.o_ref.attended_ref, bf16[2048,2048]{1,0:T(8,128)(2,1)} %all-gather.5.cloned.1.call-done, bf16[256,2048]{1,0:T(8,128)(2,1)} %param.25), kind=kOutput, calls=%fused_computation.58 | convolution fusion | flops 2150104832 | bytes 14681088 | tf_op jit(solution)/shard_map/dot_general | solution.py:26
  221.5 8.1 %collective-permute-done.20.refs_12_.refs_6_ = bf16[1,1408,256]{2,1,0:T(8,128)(2,1)S(1)} collective-permute-done((bf16[1,1408,256]{2,1,0:T(8,128)(2,1)}, bf16[1,1408,256]{2,1,0:T(8,128)(2,1)S(1)}, u32[]{:S(2)}, u32[]{:S(2)}) %collective-permute-start.20) | collective-permute-done | bytes 720928 | tf_op jit(solution)/shard_map/ppermute | solution.py:340
  233.5 2.5 collective-permute-done.21.near_x
  239.7 29.7 %feed_forward.2 = (f32[256,2176]{1,0:T(8,128)}, bf16[256,2176]{1,0:T(8,128)(2,1)}, bf16[512,1408]{1,0:T(8,128)(2,1)}, f32[96,1408]{1,0:T(8,128)S(1)}) custom-call(s32[3]{0:T(128)S(1)} %pad_add_fusion.1.meta, bf16[256,2176]{1,0:T(8,128)(2,1)} %concatenate.64.own_x, bf16[256,2176]{1,0:T(8,128)(2,1)} %collective-permute-done.21.near_x, ...), custom_call_target="tpu_custom_call" | custom-call | flops 14763950080 | bytes 38273024 | tf_op jit(solution)/shard_map/feed_forward/pallas_call | solution.py:644
  269.7 2.6 collective-permute-done.24.near_x
  273.4 29.2 %feed_forward.3 = (f32[256,2176]{1,0:T(8,128)}, bf16[256,2176]{1,0:T(8,128)(2,1)}, bf16[512,1408]{1,0:T(8,128)(2,1)}, f32[96,1408]{1,0:T(8,128)S(1)}) custom-call(s32[3]{0:T(128)S(1)} %pad_add_fusion.1.meta, bf16[256,2176]{1,0:T(8,128)(2,1)} %copy-done.126, bf16[256,2176]{1,0:T(8,128)(2,1)} %copy-done.127, bf16[256,2048]{1,0:T(8,128)(2,1)} %collective-permute-done.14.own_g, ...), custom_call_target="tpu_custom_call" | custom-call | flops 14763950080 | bytes 38273024 | tf_op jit(solution)/shard_map/feed_forward/pallas_call | solution.py:644
  303.9 2.6 collective-permute-done.25
  306.5 3.1 add_convert_fusion
  318.1 10.2 %down_projection.1 = (f32[256,2176]{1,0:T(8,128)S(1)}, bf16[256,2176]{1,0:T(8,128)(2,1)S(1)}, bf16[256,2176]{1,0:T(8,128)(2,1)S(1)}, bf16[256,2176]{1,0:T(8,128)(2,1)S(1)}) custom-call(s32[3]{0:T(128)S(1)} %copy-done.58, bf16[32,1408]{1,0:T(8,128)(2,1)S(1)} %copy-done.50, bf16[512,1408]{1,0:T(8,128)(2,1)S(1)} %copy-done.66, ...), custom_call_target="tpu_custom_call" | custom-call | flops 5905580032 | bytes 14155776 | tf_op jit(solution)/shard_map/down_projection/pallas_call | solution.py:618
  328.3 8.3 %collective-permute-done.26 = bf16[256,2176]{1,0:T(8,128)(2,1)} collective-permute-done((bf16[256,2176]{1,0:T(8,128)(2,1)}, bf16[256,2176]{1,0:T(8,128)(2,1)}, u32[]{:S(2)}, u32[]{:S(2)}) %collective-permute-start.26) | collective-permute-done | bytes 1114144 | tf_op jit(solution)/shard_map/ppermute | solution.py:335
  336.6 2.0 convert_add_fusion.2
  342.3 2.1 fusion.102
  346.0 3.3 fusion.3.do_ref
  355.7 35.5 %attention_backward.1 = (bf16[256,2048]{1,0:T(8,128)(2,1)S(1)}, bf16[8,256,512]{2,1,0:T(8,128)(2,1)S(1)}) custom-call(s32[4]{0:T(128)S(1)} %copy-done.56, bf16[256,2048]{1,0:T(8,128)(2,1)S(1)} %copy-done.20, bf16[256,2048]{1,0:T(8,128)(2,1)S(1)} %copy-done.65, bf16[256,2048]{1,0:T(8,128)(2,1)S(1)} %copy-done.22, f32[16,2,256]{2,1,0:T(2,128)S(1)} %copy-done.69, ...), custom_call_target="tpu_custom_call" | custom-call | flops 10737418240 | bytes 13631488 | tf_op jit(solution)/shard_map/attention_backward/pallas_call | solution.py:292
  393.4 4.3 all-to-all-start
  397.8 7.5 %fusion = f32[256,2048]{1,0:T(8,128)} fusion(bf16[256,2048]{1,0:T(8,128)(2,1)} %copy-done.24, bf16[2048,2560]{0,1:T(8,128)(2,1)} %all-gather.3.cloned.1.call-done), kind=kOutput, calls=%fused_computation | convolution fusion | flops 2147483648 | bytes 11534336 | tf_op jit(solution)/shard_map/dot_general | solution.py:30
  405.6 2.6 convert_add_fusion.1
  413.7 14.8 %all-to-all-done.received_ref = bf16[8,256,512]{2,1,0:T(8,128)(2,1)} async-done(((bf16[8,256,512]{2,1,0:T(8,128)(2,1)}), bf16[8,256,512]{2,1,0:T(8,128)(2,1)}, u32[]{:S(2)}, u32[]{:S(2)}) %all-to-all-start) | async-done | bytes 2097184 | tf_op jit(solution)/shard_map/all_to_all | solution.py:1106
  432.3 3.5 key_value_gradients.1
  435.9 4.6 all-to-all-start.1
  440.5 2.1 convolution_add_fusion.2
  442.8 3.1 fusion.21
  447.4 2.4 collective-permute-start.34
  451.3 2.5 convolution_add_fusion.1
  455.7 4.4 all-to-all-done.1
  463.2 2.4 collective-permute-start.31
  465.6 3.5 collective-permute-done.30.refs_2_
  469.2 3.1 collective-permute-start.32
  472.3 4.2 fusion.15
  (437 shorter events, 102.8 us)
Async XLA Ops:
  7.2 97.1 %all-gather.3.cloned.1.call-start = ((), (), s32[]{:S(2)}) async-start(), calls=%async_computation.3 | async-start | bytes 11796480 | tf_op jit(solution)/shard_map/all_gather | solution.py:949
  7.9 189.2 %all-gather.5.cloned.1.call-start = ((), (), s32[]{:S(2)}) async-start(), calls=%async_computation.4 | async-start | bytes 9437184 | tf_op jit(solution)/shard_map/all_gather | solution.py:1039
  13.2 61.2 %collective-permute-start = (bf16[512,1408]{1,0:T(8,128)(2,1)}, bf16[512,1408]{1,0:T(8,128)(2,1)}, u32[]{:S(2)}, u32[]{:S(2)}) collective-permute-start(bf16[512,1408]{1,0:T(8,128)(2,1)} %get-tuple-element.252.refs_0_), channel_id=1, source_target_pairs={{0,4},{1,5},{2,6},{3,7},{4,0},{5,1},{6,2},{7,3},{8,12},{9,13},{10,... | collective-permute-start | bytes 4325384 | tf_op jit(solution)/shard_map/ppermute | solution.py:335
  19.4 33.4 %collective-permute-start.1 = (bf16[1408,256]{1,0:T(8,128)(2,1)}, bf16[1408,256]{1,0:T(8,128)(2,1)}, u32[]{:S(2)}, u32[]{:S(2)}) collective-permute-start(bf16[1408,256]{1,0:T(8,128)(2,1)} %get-tuple-element.258), channel_id=1, source_target_pairs={{0,2},{1,3},{2,0},{3,1},{4,6},{5,7},{6,4},{7,5},{8,10},{9,11},{10,... | collective-permute-start | bytes 2162696 | tf_op jit(solution)/shard_map/ppermute | solution.py:335
  20.9 31.9 %collective-permute-start.2 = (bf16[1408,256]{1,0:T(8,128)(2,1)}, bf16[1408,256]{1,0:T(8,128)(2,1)}, u32[]{:S(2)}, u32[]{:S(2)}) collective-permute-start(bf16[1408,256]{1,0:T(8,128)(2,1)} %get-tuple-element.257), channel_id=1, source_target_pairs={{0,1},{1,0},{2,3},{3,2},{4,5},{5,4},{6,7},{7,6},{8,9},{9,8},{10,11... | collective-permute-start | bytes 2162696 | tf_op jit(solution)/shard_map/ppermute | solution.py:335
  20.9 53.4 %collective-permute-start.3 = (bf16[1408,256]{1,0:T(8,128)(2,1)}, bf16[1408,256]{1,0:T(8,128)(2,1)}, u32[]{:S(2)}, u32[]{:S(2)}) collective-permute-start(bf16[1408,256]{1,0:T(8,128)(2,1)} %get-tuple-element.259), channel_id=1, source_target_pairs={{0,3},{1,2},{2,1},{3,0},{4,7},{5,6},{6,5},{7,4},{8,11},{9,10},{10,... | collective-permute-start | bytes 2162696 | tf_op jit(solution)/shard_map/ppermute | solution.py:335
  21.6 371.9 %reduce-scatter.2.cloned.1.call-start = ((), (), s32[]{:S(2)}) async-start(), calls=%async_computation.5 | async-start | bytes 1327104 | tf_op jit(solution)/shard_map/reduce_scatter | solution.py:1100
  31.0 125.7 %copy-start.55 = (s32[4]{0:T(128)}, s32[4]{0:T(128)S(1)}, u32[]{:S(2)}) copy-start(s32[4]{0:T(128)S(1)} %pad_add_fusion.span) | copy-start | bytes 52
  34.8 75.2 %copy-start.32 = (bf16[64,512]{1,0:T(8,128)(2,1)}, bf16[64,512]{1,0:T(8,128)(2,1)S(1)}, u32[]{:S(2)}) copy-start(bf16[64,512]{1,0:T(8,128)(2,1)S(1)} %fusion.53.right_ref) | copy-start | bytes 196612
  40.5 298.1 %copy-start.12 = (f32[256,32]{1,0:T(8,128)}, f32[256,32]{1,0:T(8,128)S(1)}, u32[]{:S(2)}) copy-start(f32[256,32]{1,0:T(8,128)S(1)} %get-tuple-element.276.own_seen.seen_ref) | copy-start | bytes 98308
  40.8 231.5 %copy-start.37 = (bf16[32,2048]{1,0:T(8,128)(2,1)}, bf16[32,2048]{1,0:T(8,128)(2,1)S(1)}, u32[]{:S(2)}) copy-start(bf16[32,2048]{1,0:T(8,128)(2,1)S(1)} %convolution_convert_fusion.6.lower_ref) | copy-start | bytes 393220
  42.0 84.2 %copy-start.14 = (bf16[32,2048]{1,0:T(8,128)(2,1)}, bf16[32,2048]{1,0:T(8,128)(2,1)S(1)}, u32[]{:S(2)}) copy-start(bf16[32,2048]{1,0:T(8,128)(2,1)S(1)} %convolution_convert_fusion.8.asking_ref) | copy-start | bytes 393220
  74.3 47.6 %collective-permute-start.4 = (bf16[512,1408]{1,0:T(8,128)(2,1)}, bf16[512,1408]{1,0:T(8,128)(2,1)}, u32[]{:S(2)}, u32[]{:S(2)}) collective-permute-start(bf16[512,1408]{1,0:T(8,128)(2,1)} %get-tuple-element.111.refs_1_), channel_id=1, source_target_pairs={{0,4},{1,5},{2,6},{3,7},{4,0},{5,1},{6,2},{7,3},{8,12},{9,13},{10,... | collective-permute-start | bytes 4325384 | tf_op jit(solution)/shard_map/ppermute | solution.py:335
  74.5 47.5 %collective-permute-start.5 = (bf16[512,1408]{1,0:T(8,128)(2,1)}, bf16[512,1408]{1,0:T(8,128)(2,1)}, u32[]{:S(2)}, u32[]{:S(2)}) collective-permute-start(bf16[512,1408]{1,0:T(8,128)(2,1)} %collective-permute-done.refs_4_), channel_id=1, source_target_pairs={{0,8},{8,0},{16,24},{24,16},{1,9},{9,1},{17,25},{25,17},{2,10},{10... | collective-permute-start | bytes 4325384 | tf_op jit(solution)/shard_map/ppermute | solution.py:340
  76.6 49.6 %copy-start.16 = (bf16[256,96]{1,0:T(8,128)(2,1)}, bf16[256,96]{1,0:T(8,128)(2,1)S(1)}, u32[]{:S(2)}) copy-start(bf16[256,96]{1,0:T(8,128)(2,1)S(1)} %fusion.24) | copy-start | bytes 147460
  122.0 17.3 %collective-permute-start.6 = (bf16[256,512]{1,0:T(8,128)(2,1)S(1)}, bf16[256,512]{1,0:T(8,128)(2,1)S(1)}, u32[]{:S(2)}, u32[]{:S(2)}) collective-permute-start(bf16[256,512]{1,0:T(8,128)(2,1)S(1)} %pad_maximum_fusion.2), channel_id=1, source_target_pairs={{0,1},{1,0},{2,3},{3,2},{4,5},{5,4},{6,7},{7,6},{8,9},{9,8},{10,11... | collective-permute-start | bytes 786440 | tf_op jit(solution)/shard_map/ppermute | solution.py:335
  122.1 14.6 %collective-permute-start.7 = (bf16[256,512]{1,0:T(8,128)(2,1)S(1)}, bf16[256,512]{1,0:T(8,128)(2,1)S(1)}, u32[]{:S(2)}, u32[]{:S(2)}) collective-permute-start(bf16[256,512]{1,0:T(8,128)(2,1)S(1)} %pad_maximum_fusion.2), channel_id=1, source_target_pairs={{0,2},{1,3},{2,0},{3,1},{4,6},{5,7},{6,4},{7,5},{8,10},{9,11},{10,... | collective-permute-start | bytes 786440 | tf_op jit(solution)/shard_map/ppermute | solution.py:335
  123.8 14.1 %collective-permute-start.9 = (bf16[256,512]{1,0:T(8,128)(2,1)S(1)}, bf16[256,512]{1,0:T(8,128)(2,1)S(1)}, u32[]{:S(2)}, u32[]{:S(2)}) collective-permute-start(bf16[256,512]{1,0:T(8,128)(2,1)S(1)} %pad_maximum_fusion.2), channel_id=1, source_target_pairs={{0,4},{1,5},{2,6},{3,7},{4,0},{5,1},{6,2},{7,3},{8,12},{9,13},{10,... | collective-permute-start | bytes 786440 | tf_op jit(solution)/shard_map/ppermute | solution.py:335
  136.7 9.2 %collective-permute-start.8 = (bf16[256,512]{1,0:T(8,128)(2,1)S(1)}, bf16[256,512]{1,0:T(8,128)(2,1)S(1)}, u32[]{:S(2)}, u32[]{:S(2)}) collective-permute-start(bf16[256,512]{1,0:T(8,128)(2,1)S(1)} %collective-permute-done.7), channel_id=1, source_target_pairs={{0,1},{1,0},{2,3},{3,2},{4,5},{5,4},{6,7},{7,6},{8,9},{9,8},{10,11... | collective-permute-start | bytes 786440 | tf_op jit(solution)/shard_map/ppermute | solution.py:335
  137.8 8.0 %collective-permute-start.11 = (bf16[256,512]{1,0:T(8,128)(2,1)S(1)}, bf16[256,512]{1,0:T(8,128)(2,1)S(1)}, u32[]{:S(2)}, u32[]{:S(2)}) collective-permute-start(bf16[256,512]{1,0:T(8,128)(2,1)S(1)} %collective-permute-done.9), channel_id=1, source_target_pairs={{0,2},{1,3},{2,0},{3,1},{4,6},{5,7},{6,4},{7,5},{8,10},{9,11},{10,... | collective-permute-start | bytes 786440 | tf_op jit(solution)/shard_map/ppermute | solution.py:335
  139.2 6.7 %collective-permute-start.10 = (bf16[256,512]{1,0:T(8,128)(2,1)S(1)}, bf16[256,512]{1,0:T(8,128)(2,1)S(1)}, u32[]{:S(2)}, u32[]{:S(2)}) collective-permute-start(bf16[256,512]{1,0:T(8,128)(2,1)S(1)} %collective-permute-done.9), channel_id=1, source_target_pairs={{0,1},{1,0},{2,3},{3,2},{4,5},{5,4},{6,7},{7,6},{8,9},{9,8},{10,11... | collective-permute-start | bytes 786440 | tf_op jit(solution)/shard_map/ppermute | solution.py:335
  145.9 1.9 collective-permute-start.12
  147.8 44.1 %collective-permute-start.16 = (bf16[512,1408]{1,0:T(8,128)(2,1)}, bf16[512,1408]{1,0:T(8,128)(2,1)S(1)}, u32[]{:S(2)}, u32[]{:S(2)}) collective-permute-start(bf16[512,1408]{1,0:T(8,128)(2,1)} %collective-permute-done.4.refs_5_), channel_id=1, source_target_pairs={{0,8},{8,0},{16,24},{24,16},{1,9},{9,1},{17,25},{25,17},{2,10},{10... | collective-permute-start | bytes 4325384 | tf_op jit(solution)/shard_map/ppermute | solution.py:340
  149.8 35.1 %collective-permute-start.13 = (bf16[256,2048]{1,0:T(8,128)(2,1)S(1)}, bf16[256,2048]{1,0:T(8,128)(2,1)S(1)}, u32[]{:S(2)}, u32[]{:S(2)}) collective-permute-start(bf16[256,2048]{1,0:T(8,128)(2,1)S(1)} %copy-done.4), channel_id=1, source_target_pairs={{0,1},{1,0},{2,3},{3,2},{4,5},{5,4},{6,7},{7,6},{8,9},{9,8},{10,11... | collective-permute-start | bytes 3145736 | tf_op jit(solution)/shard_map/ppermute | solution.py:335
  149.9 42.1 %collective-permute-start.14 = (bf16[256,2048]{1,0:T(8,128)(2,1)S(1)}, bf16[256,2048]{1,0:T(8,128)(2,1)}, u32[]{:S(2)}, u32[]{:S(2)}) collective-permute-start(bf16[256,2048]{1,0:T(8,128)(2,1)S(1)} %copy-done.4), channel_id=1, source_target_pairs={{0,2},{1,3},{2,0},{3,1},{4,6},{5,7},{6,4},{7,5},{8,10},{9,11},{10,... | collective-permute-start | bytes 3145736 | tf_op jit(solution)/shard_map/ppermute | solution.py:335
  151.7 33.2 %collective-permute-start.15 = (bf16[1,1408,256]{2,1,0:T(8,128)(2,1)S(1)}, bf16[1,1408,256]{2,1,0:T(8,128)(2,1)}, u32[]{:S(2)}, u32[]{:S(2)}) collective-permute-start(bf16[1,1408,256]{2,1,0:T(8,128)(2,1)S(1)} %get-tuple-element.255), channel_id=1, source_target_pairs={{0,4},{1,5},{2,6},{3,7},{4,0},{5,1},{6,2},{7,3},{8,12},{9,13},{10,... | collective-permute-start | bytes 2162696 | tf_op jit(solution)/shard_map/ppermute | solution.py:335
  176.0 44.3 %copy-start.21 = (bf16[256,2048]{1,0:T(8,128)(2,1)}, bf16[256,2048]{1,0:T(8,128)(2,1)S(1)}, u32[]{:S(2)}) copy-start(bf16[256,2048]{1,0:T(8,128)(2,1)S(1)} %get-tuple-element.125.o_ref.attended_ref) | copy-start | bytes 3145732
  191.9 20.1 %collective-permute-start.17 = (bf16[256,2048]{1,0:T(8,128)(2,1)}, bf16[256,2048]{1,0:T(8,128)(2,1)}, u32[]{:S(2)}, u32[]{:S(2)}) collective-permute-start(bf16[256,2048]{1,0:T(8,128)(2,1)} %collective-permute-done.14.own_g), channel_id=1, source_target_pairs={{0,1},{1,0},{2,3},{3,2},{4,5},{5,4},{6,7},{7,6},{8,9},{9,8},{10,11... | collective-permute-start | bytes 3145736 | tf_op jit(solution)/shard_map/ppermute | solution.py:335
  191.9 18.9 %collective-permute-start.18 = (bf16[1,1408,256]{2,1,0:T(8,128)(2,1)}, bf16[1,1408,256]{2,1,0:T(8,128)(2,1)}, u32[]{:S(2)}, u32[]{:S(2)}) collective-permute-start(bf16[1,1408,256]{2,1,0:T(8,128)(2,1)} %get-tuple-element.127), channel_id=1, source_target_pairs={{0,4},{1,5},{2,6},{3,7},{4,0},{5,1},{6,2},{7,3},{8,12},{9,13},{10,... | collective-permute-start | bytes 2162696 | tf_op jit(solution)/shard_map/ppermute | solution.py:335
  193.5 18.5 %collective-permute-start.19 = (bf16[1,1408,256]{2,1,0:T(8,128)(2,1)}, bf16[1,1408,256]{2,1,0:T(8,128)(2,1)}, u32[]{:S(2)}, u32[]{:S(2)}) collective-permute-start(bf16[1,1408,256]{2,1,0:T(8,128)(2,1)} %collective-permute-done.15.refs_9_.refs_3_), channel_id=1, source_target_pairs={{0,8},{8,0},{16,24},{24,16},{1,9},{9,1},{17,25},{25,17},{2,10},{10... | collective-permute-start | bytes 2162696 | tf_op jit(solution)/shard_map/ppermute | solution.py:340
  212.0 17.6 %collective-permute-start.20 = (bf16[1,1408,256]{2,1,0:T(8,128)(2,1)}, bf16[1,1408,256]{2,1,0:T(8,128)(2,1)S(1)}, u32[]{:S(2)}, u32[]{:S(2)}) collective-permute-start(bf16[1,1408,256]{2,1,0:T(8,128)(2,1)} %collective-permute-done.18.refs_10_.refs_4_), channel_id=1, source_target_pairs={{0,8},{8,0},{16,24},{24,16},{1,9},{9,1},{17,25},{25,17},{2,10},{10... | collective-permute-start | bytes 2162696 | tf_op jit(solution)/shard_map/ppermute | solution.py:340
  232.8 3.1 collective-permute-start.21
  232.9 36.6 %collective-permute-start.22 = (bf16[256,2176]{1,0:T(8,128)(2,1)}, bf16[256,2176]{1,0:T(8,128)(2,1)S(1)}, u32[]{:S(2)}, u32[]{:S(2)}) collective-permute-start(bf16[256,2176]{1,0:T(8,128)(2,1)} %concatenate.64.own_x), channel_id=1, source_target_pairs={{0,2},{1,3},{2,0},{3,1},{4,6},{5,7},{6,4},{7,5},{8,10},{9,11},{10,... | collective-permute-start | bytes 3342344 | tf_op jit(solution)/shard_map/ppermute | solution.py:335
  269.5 2.8 collective-permute-start.24
  303.4 3.1 collective-permute-start.25
  303.5 33.0 %collective-permute-start.23 = (bf16[256,2176]{1,0:T(8,128)(2,1)}, bf16[256,2176]{1,0:T(8,128)(2,1)}, u32[]{:S(2)}, u32[]{:S(2)}) collective-permute-start(bf16[256,2176]{1,0:T(8,128)(2,1)} %get-tuple-element.147), channel_id=1, source_target_pairs={{0,1},{1,0},{2,3},{3,2},{4,5},{5,4},{6,7},{7,6},{8,9},{9,8},{10,11... | collective-permute-start | bytes 3342344 | tf_op jit(solution)/shard_map/ppermute | solution.py:335
  309.6 26.9 %collective-permute-start.26 = (bf16[256,2176]{1,0:T(8,128)(2,1)}, bf16[256,2176]{1,0:T(8,128)(2,1)}, u32[]{:S(2)}, u32[]{:S(2)}) collective-permute-start(bf16[256,2176]{1,0:T(8,128)(2,1)} %add_convert_fusion), channel_id=1, source_target_pairs={{0,2},{1,3},{2,0},{3,1},{4,6},{5,7},{6,4},{7,5},{8,10},{9,11},{10,... | collective-permute-start | bytes 3342344 | tf_op jit(solution)/shard_map/ppermute | solution.py:335
  350.1 55.3 %collective-permute-start.27 = (bf16[256,2176]{1,0:T(8,128)(2,1)}, bf16[256,2176]{1,0:T(8,128)(2,1)}, u32[]{:S(2)}, u32[]{:S(2)}) collective-permute-start(bf16[256,2176]{1,0:T(8,128)(2,1)} %copy-done.61), channel_id=1, source_target_pairs={{0,1},{1,0},{2,3},{3,2},{4,5},{5,4},{6,7},{7,6},{8,9},{9,8},{10,11... | collective-permute-start | bytes 3342344 | tf_op jit(solution)/shard_map/ppermute | solution.py:335
  350.1 55.3 %collective-permute-start.28 = (bf16[256,2176]{1,0:T(8,128)(2,1)}, bf16[256,2176]{1,0:T(8,128)(2,1)}, u32[]{:S(2)}, u32[]{:S(2)}) collective-permute-start(bf16[256,2176]{1,0:T(8,128)(2,1)} %copy-done.60), channel_id=1, source_target_pairs={{0,2},{1,3},{2,0},{3,1},{4,6},{5,7},{6,4},{7,5},{8,10},{9,11},{10,... | collective-permute-start | bytes 3342344 | tf_op jit(solution)/shard_map/ppermute | solution.py:335
  350.6 55.0 %collective-permute-start.29 = (bf16[256,2176]{1,0:T(8,128)(2,1)}, bf16[256,2176]{1,0:T(8,128)(2,1)}, u32[]{:S(2)}, u32[]{:S(2)}) collective-permute-start(bf16[256,2176]{1,0:T(8,128)(2,1)} %copy-done.59), channel_id=1, source_target_pairs={{0,3},{1,2},{2,1},{3,0},{4,7},{5,6},{6,5},{7,4},{8,11},{9,10},{10,... | collective-permute-start | bytes 3342344 | tf_op jit(solution)/shard_map/ppermute | solution.py:335
  393.4 35.1 %all-to-all-start = ((bf16[8,256,512]{2,1,0:T(8,128)(2,1)}), bf16[8,256,512]{2,1,0:T(8,128)(2,1)}, u32[]{:S(2)}, u32[]{:S(2)}) async-start(bf16[8,256,512]{2,1,0:T(8,128)(2,1)} %copy-done.11), calls=%async_computation.1 | async-start | bytes 4194304 | tf_op jit(solution)/shard_map/all_to_all | solution.py:1106
  435.9 24.3 %all-to-all-start.1 = ((bf16[8,352,256]{2,1,0:T(8,128)(2,1)}), bf16[8,352,256]{2,1,0:T(8,128)(2,1)}, u32[]{:S(2)}, u32[]{:S(2)}) async-start(bf16[8,352,256]{2,1,0:T(8,128)(2,1)} %get-tuple-element.184), calls=%async_computation.2 | async-start | bytes 2883584 | tf_op jit(solution)/shard_map/all_to_all | solution.py:731
  445.9 31.2 %collective-permute-start.33 = (bf16[96,704]{1,0:T(8,128)(2,1)S(1)}, bf16[96,704]{1,0:T(8,128)(2,1)S(1)}, u32[]{:S(2)}, u32[]{:S(2)}) collective-permute-start(bf16[96,704]{1,0:T(8,128)(2,1)S(1)} %bitcast.104), channel_id=1, source_target_pairs={{0,8},{8,16},{16,24},{24,0},{1,9},{9,17},{17,25},{25,1},{2,10},{10... | collective-permute-start | bytes 405512 | tf_op jit(solution)/shard_map/ppermute | solution.py:903
  447.4 29.7 %collective-permute-start.34 = (bf16[96,704]{1,0:T(8,128)(2,1)S(1)}, bf16[96,704]{1,0:T(8,128)(2,1)S(1)}, u32[]{:S(2)}, u32[]{:S(2)}) collective-permute-start(bf16[96,704]{1,0:T(8,128)(2,1)S(1)} %bitcast.105), channel_id=1, source_target_pairs={{0,16},{8,24},{16,0},{24,8},{1,17},{9,25},{17,1},{25,9},{2,18},{10... | collective-permute-start | bytes 405512 | tf_op jit(solution)/shard_map/ppermute | solution.py:903
  449.8 27.3 %collective-permute-start.35 = (bf16[96,704]{1,0:T(8,128)(2,1)S(1)}, bf16[96,704]{1,0:T(8,128)(2,1)S(1)}, u32[]{:S(2)}, u32[]{:S(2)}) collective-permute-start(bf16[96,704]{1,0:T(8,128)(2,1)S(1)} %bitcast.106), channel_id=1, source_target_pairs={{0,24},{8,0},{16,8},{24,16},{1,25},{9,1},{17,9},{25,17},{2,26},{10... | collective-permute-start | bytes 405512 | tf_op jit(solution)/shard_map/ppermute | solution.py:903
  461.7 7.5 %collective-permute-start.30 = (bf16[352,256]{1,0:T(8,128)(2,1)S(1)}, bf16[352,256]{1,0:T(8,128)(2,1)S(1)}, u32[]{:S(2)}, u32[]{:S(2)}) collective-permute-start(bf16[352,256]{1,0:T(8,128)(2,1)S(1)} %reduce_sum.62.refs_1_), channel_id=1, source_target_pairs={{0,8},{8,16},{16,24},{24,0},{1,9},{9,17},{17,25},{25,1},{2,10},{10... | collective-permute-start | bytes 540680 | tf_op jit(solution)/shard_map/ppermute | solution.py:903
  463.2 13.2 %collective-permute-start.31 = (bf16[352,256]{1,0:T(8,128)(2,1)S(1)}, bf16[352,256]{1,0:T(8,128)(2,1)S(1)}, u32[]{:S(2)}, u32[]{:S(2)}) collective-permute-start(bf16[352,256]{1,0:T(8,128)(2,1)S(1)} %reduce_sum.62.refs_1_), channel_id=1, source_target_pairs={{0,16},{8,24},{16,0},{24,8},{1,17},{9,25},{17,1},{25,9},{2,18},{10... | collective-permute-start | bytes 540680 | tf_op jit(solution)/shard_map/ppermute | solution.py:903
  469.2 7.9 %collective-permute-start.32 = (bf16[352,256]{1,0:T(8,128)(2,1)S(1)}, bf16[352,256]{1,0:T(8,128)(2,1)S(1)}, u32[]{:S(2)}, u32[]{:S(2)}) collective-permute-start(bf16[352,256]{1,0:T(8,128)(2,1)S(1)} %reduce_sum.62.refs_1_), channel_id=1, source_target_pairs={{0,24},{8,0},{16,8},{24,16},{1,25},{9,1},{17,9},{25,17},{2,26},{10... | collective-permute-start | bytes 540680 | tf_op jit(solution)/shard_map/ppermute | solution.py:903
  (127 other events, 937.0 us)
Sparse Core Ops, SparseCore 0:
  9.9 94.3 all-gather.2
  106.2 81.7 all-gather.4
  349.5 40.7 reduce-scatter.1

commit v7 on v6

--- a/solution.py
+++ b/solution.py
@@ -188,7 +188,8 @@
     cos_ref,
     sin_ref,
     dq_ref,
-    dkv_ref,
+    even_ref,
+    odd_ref,
     k_ref,
     v_ref,
     dk_sum,
@@ -267,18 +268,19 @@
         block = pl.program_id(0) // per_kv // (LANES // HEAD_DIM)
 
         def put(index, carry):
-            target = index ^ span[3]
-            for sum_ref, first in ((dk_sum, 0), (dv_sum, KV_HEADS * HEAD_DIM // LANES)):
-                total = sum_ref[pl.ds(pl.multiple_of(index * tokens, tokens), tokens), :]
-                total = total + pltpu.roll(total, HEAD_DIM, 1)
-                keep = jnp.logical_and(odd, lane_of(total.shape) < HEAD_DIM)
-                lanes = pl.ds(pl.multiple_of((first + block) * LANES, LANES), LANES)
-                dkv_ref[target, :, lanes] = jnp.where(
-                    keep, dkv_ref[target, :, lanes], total.astype(BF16)
-                )
+            for side, out_ref in enumerate((even_ref, odd_ref)):
+                rows = pl.ds(pl.multiple_of((2 * index + side) * tokens, tokens), tokens)
+                for sum_ref, first in ((dk_sum, 0), (dv_sum, KV_HEADS * HEAD_DIM // LANES)):
+                    total = sum_ref[rows, :]
+                    total = total + pltpu.roll(total, HEAD_DIM, 1)
+                    keep = jnp.logical_and(odd, lane_of(total.shape) < HEAD_DIM)
+                    lanes = pl.ds(pl.multiple_of((first + block) * LANES, LANES), LANES)
+                    out_ref[index, :, lanes] = jnp.where(
+                        keep, out_ref[index, :, lanes], total.astype(BF16)
+                    )
             return carry
 
-        lax.fori_loop(0, dkv_ref.shape[0], put, 0)
+        lax.fori_loop(0, even_ref.shape[0], put, 0)
 
 
 def attention_backward(span, query, grad, attended, lse, key_value, bias, cosines, sines):
@@ -293,7 +295,7 @@
         functools.partial(attention_backward_kernel, per_kv),
         out_shape=(
             jax.ShapeDtypeStruct((tokens, width), BF16),
-            jax.ShapeDtypeStruct((keys // tokens, tokens, kv_two), BF16),
+            *[jax.ShapeDtypeStruct((keys // tokens // 2, tokens, kv_two), BF16)] * 2,
         ),
         grid_spec=pltpu.PrefetchScalarGridSpec(
             num_scalar_prefetch=1,
@@ -310,7 +312,7 @@
             ],
             out_specs=(
                 pair_spec,
-                pl.BlockSpec((keys // tokens, tokens, kv_two), lambda j, s: (0, 0, 0)),
+                *[pl.BlockSpec((keys // tokens // 2, tokens, kv_two), lambda j, s: (0, 0, 0))] * 2,
             ),
             scratch_shapes=[pltpu.VMEM((2, keys, LANES), BF16)] * 2
             + [pltpu.VMEM((keys, LANES), F32)] * 2,
@@ -428,7 +430,7 @@
     ).astype(BF16)
     members = lax.axis_size("grp")
     deep = deep.reshape(3 * slots, members, hidden_width // members).transpose(1, 0, 2)
-    return response_part, dnorm2, latent_d, dlat_gu, deep
+    return (lambda shares: shares[0], (response_part,)), dnorm2, latent_d, dlat_gu, deep
 
 
 def feed_forward_kernel(
@@ -566,17 +568,16 @@
         return carry
 
     lax.fori_loop(0, 4, back, 0)
+    dlat_sum[:, 2 * slots : 3 * slots] = mm_nt(acts[...], in_ref[...])
     back_own[:, width:] = dlat_sum[:count, :]
     back_near[:, width:] = dlat_sum[count:, :].astype(BF16)
 
 
-def down_kernel(meta, in_ref, *refs):
+def down_kernel(meta, *refs):
     acts_refs, whole_down = refs[:2], refs[2:7]
     results = (refs[7:9], refs[9:11])
     kept_down, semaphores = refs[11:]
-    slots = in_ref.shape[0]
     parts, _, part = kept_down.shape
-    width = parts * part
     parity, member = meta[0], meta[2]
     copies = [
         pltpu.make_async_copy(ref, kept_down.at[pl.ds(start, size)], semaphores.at[index])
@@ -584,13 +585,6 @@
     ]
     for copy in copies:
         copy.start()
-    for acts, outs in zip(acts_refs, results):
-        latent = mm_nt(acts[...], in_ref[...])
-        pad = jnp.zeros((latent.shape[0], LANES - slots), F32)
-        latent = jnp.concatenate([latent, pad], axis=1)
-        for index, out in enumerate(outs):
-            rows = slice(index * out.shape[0], (index + 1) * out.shape[0])
-            out[:, width:] = latent[rows].astype(out.dtype)
     for copy in copies:
         copy.wait()
 
@@ -608,18 +602,17 @@
     lax.fori_loop(0, parts, columns, 0)
 
 
-def down_projection(meta, acts, down_in, weights):
+def down_projection(meta, acts, weights):
     tokens, block = acts[0].shape
-    slots = down_in.shape[0]
     width = 8 * weights["down"][0].shape[2]
-    wide, count = width + LANES, tokens // 2
-    kept = jax.ShapeDtypeStruct((count, wide), F32)
-    sent = jax.ShapeDtypeStruct((count, wide), BF16)
+    count = tokens // 2
+    kept = jax.ShapeDtypeStruct((count, width), F32)
+    sent = jax.ShapeDtypeStruct((count, width), BF16)
     return pl.pallas_call(
         down_kernel,
         out_shape=(kept, sent, sent, sent),
         in_specs=[pl.BlockSpec(memory_space=pltpu.SMEM)]
-        + [pl.BlockSpec(memory_space=pltpu.VMEM)] * 3
+        + [pl.BlockSpec(memory_space=pltpu.VMEM)] * 2
         + [pl.BlockSpec(memory_space=pl.ANY)] * 5,
         scratch_shapes=[
             pltpu.VMEM((8, block, width // 8), BF16),
@@ -632,7 +625,7 @@
             bytes_accessed=2 * width * block + 8 * tokens * width,
         ),
         name="down_projection",
-    )(meta, down_in, *acts, *weights["down"])
+    )(meta, *acts, *weights["down"])
 
 
 def feed_forward_pair(meta, rows, sens, seen, weights, pieces):
@@ -712,24 +705,36 @@
     deep = deep.reshape(3 * slots, owners, block // owners).transpose(1, 0, 2)
     placed = jnp.zeros((members, 3 * slots, block // owners), BF16)
     placed = lax.dynamic_update_slice_in_dim(placed, deep, hidden * owners, 0)
-    forwards = down_projection(meta, [result[2] for result in results], pieces[-1], weights)
+    forwards = down_projection(meta, [result[2] for result in results], weights)
     across = flip(chips[1].astype(BF16), ACROSS_X)
     across, (placed, *forwards) = tie(across, (placed, *forwards))
     backward = chips[0] + across.astype(F32)
     dlat_gu = (LOWRANK_FACTOR * backward[:, width : width + 2 * slots] * seen_two).astype(BF16)
     dnorm2 = backward[:, :width] + mm_nt(dlat_gu, ffn_in)
-    dnorm2, forwards = tie(dnorm2, forwards)
-    forward = forwards[0]
-    for part, mask in zip(forwards[1:], (CORE, ACROSS_X, ACROSS_X | CORE)):
-        forward = forward + flip(part, mask).astype(F32)
-    latent_d = (forward[:, width : width + slots] * seen).astype(BF16)
-    response_part = forward[:, :width] + LOWRANK_FACTOR * mm(latent_d, lower)
-    return response_part, dnorm2, latent_d, dlat_gu, placed
-
-
-def exchange_sum(parts):
-    received = lax.all_to_all(parts.astype(BF16), "grp", 0, 0, tiled=True)
-    return jnp.sum(received.astype(F32), axis=0)
+    latent_d = (backward[:, width + 2 * slots : width + 3 * slots] * seen).astype(BF16)
+
+    dnorm2, (mine, near, other, other_near) = tie(dnorm2, forwards)
+    other = (other.astype(F32) + flip(other_near, CORE).astype(F32)).astype(BF16)
+    shares = (mine, flip(near, CORE), flip(other, ACROSS_X))
+
+    def finish(shares):
+        mine, near, other = shares
+        response_part = mine + near.astype(F32) + other.astype(F32)
+        return response_part + LOWRANK_FACTOR * mm(latent_d, lower)
+
+    return (finish, shares), dnorm2, latent_d, dlat_gu, placed
+
+
+def exchange(evens, odds, by_permutes, later=None):
+    if by_permutes:
+        total = (evens.astype(F32) + flip(odds, CORE).astype(F32)).astype(BF16)
+        if later is not None:
+            total, (later,) = tie(total, (later,))
+        masks = (ACROSS_X, ACROSS_Y, ACROSS_X | ACROSS_Y)
+        return [total[0], *(flip(total[i], mask) for i, mask in enumerate(masks, start=1))], later
+    parts = jnp.stack([evens, odds], axis=1).reshape(-1, *evens.shape[1:])
+    received = lax.all_to_all(parts, "grp", 0, 0, tiled=True)
+    return [received[i] for i in range(received.shape[0])], later
 
 
 def simple_call(kernel, name, out_shape, operands, flops):
@@ -795,23 +800,14 @@
     )
 
 
-def key_value_gradients_kernel(
-    received_ref,
-    early_ref,
-    cos_ref,
-    sin_ref,
-    right_ref,
-    seen_ref,
-    latent_ref,
-    norm_ref,
-    dkv_ref,
-    dlat_ref,
-    pack_ref,
-):
+def key_value_gradients_kernel(turn_ref, *refs):
+    received, refs = refs[:-12], refs[-12:]
+    early_ref, cos_ref, sin_ref, right_ref, seen_ref, latent_ref, norm_ref = refs[:7]
+    dkv_ref, dlat_ref, even_ref, odd_ref, late_ref = refs[7:12]
     half = HEAD_DIM // 2
-    total = received_ref[0].astype(F32)
-    for source in range(1, received_ref.shape[0]):
-        total = total + received_ref[source].astype(F32)
+    total = received[0][...].astype(F32)
+    for source in received[1:]:
+        total = total + source[...].astype(F32)
     kv_width = total.shape[1] // 2
     pieces = []
     for start in range(0, kv_width, LANES):
@@ -826,36 +822,48 @@
     dkv_ref[...] = dkv
     dlat = (LOWRANK_FACTOR * mm_nt(dkv, right_ref[...]) * seen_ref[...]).astype(BF16)
     dlat_ref[...] = dlat
-    late = mm_tn(dlat, norm_ref[...]).astype(BF16)
+    late_ref[...] = mm_tn(dlat, norm_ref[...]).astype(BF16)
     thin = (LOWRANK_FACTOR * mm_tn(latent_ref[...], dkv)).astype(BF16)
-    rows, head = late.shape[0], early_ref.shape[0]
+    rows, head = late_ref.shape[0], early_ref.shape[0]
     thin = jnp.concatenate([thin[: rows // 2, :kv_width], thin[rows // 2 :, kv_width:]], axis=0)
-    share = pack_ref.shape[2]
-    for target in range(pack_ref.shape[0]):
-        columns = slice(target * share, (target + 1) * share)
-        pack_ref[target, :head, :] = early_ref[:, columns]
-        pack_ref[target, head : head + rows, :] = late[:, columns]
+    share = even_ref.shape[2]
+    for place in range(2 * even_ref.shape[0]):
+        pack_ref = (even_ref, odd_ref)[place % 2]
+        columns = pl.ds(pl.multiple_of((place ^ turn_ref[0]) * share, share), share)
+        pack_ref[place // 2, :head, :] = early_ref[:, columns]
+        pack_ref[place // 2, head : head + rows, :] = late_ref[:, columns]
         for index, start in enumerate(range(0, kv_width, share)):
-            place = head + (index + 1) * rows
-            pack_ref[target, place : place + rows, :] = thin[:, start : start + share]
-
-
-def key_value_gradients(received, early, cosines, sines, kv_right, seen_two, latent_kv, norm1):
-    members, count, kv_two = received.shape
-    rows = kv_right.shape[0]
-    share = norm1.shape[1] // members
+            first = head + (index + 1) * rows
+            pack_ref[place // 2, first : first + rows, :] = thin[:, start : start + share]
+
+
+def key_value_gradients(turn, received, early, cosines, sines, kv_right, seen_two, latent_kv, norm1):
+    members = lax.axis_size("grp")
+    count, kv_two = received[0].shape
+    rows, width = kv_right.shape[0], norm1.shape[1]
+    share = width // members
     packed = early.shape[0] + rows * (1 + kv_two // 2 // share)
-    return simple_call(
+    operands = (*received, early, cosines, sines, kv_right, seen_two, latent_kv, norm1)
+    pack = jax.ShapeDtypeStruct((members // 2, packed, share), BF16)
+    return pl.pallas_call(
         key_value_gradients_kernel,
-        "key_value_gradients",
-        (
+        out_shape=(
             jax.ShapeDtypeStruct((count, kv_two), BF16),
             jax.ShapeDtypeStruct((count, rows), BF16),
-            jax.ShapeDtypeStruct((members, packed, share), BF16),
-        ),
-        (received, early, cosines, sines, kv_right, seen_two, latent_kv, norm1),
-        2 * count * rows * (norm1.shape[1] + 2 * kv_two),
-    )
+            pack,
+            pack,
+        ),
+        in_specs=[pl.BlockSpec(memory_space=pltpu.SMEM)]
+        + [pl.BlockSpec(memory_space=pltpu.VMEM)] * len(operands),
+        scratch_shapes=[pltpu.VMEM((rows, width), BF16)],
+        compiler_params=pltpu.CompilerParams(vmem_limit_bytes=32 << 20),
+        cost_estimate=pl.CostEstimate(
+            flops=2 * count * rows * (width + 2 * kv_two),
+            transcendentals=0,
+            bytes_accessed=sum(array.size * array.dtype.itemsize for array in operands),
+        ),
+        name="key_value_gradients",
+    )(turn, *operands)
 
 
 def place_kernel(jobs, groups, slots, *refs):
@@ -971,7 +979,7 @@
     first_key = own_second[0] * lengths[0]
     last_key = jnp.max(own_second * lengths[0] + jnp.maximum(position, prefix - 1))
     span = jnp.stack(
-        [first_key // KEY_BLOCK, last_key // KEY_BLOCK + 1, turn * count // KEY_BLOCK, turn]
+        [first_key // KEY_BLOCK, last_key // KEY_BLOCK + 1, turn * count // KEY_BLOCK]
     ).astype(jnp.int32)
 
     slots = 2 * RANK
@@ -1083,14 +1091,13 @@
             steps.send(transfers)
         except StopIteration as stop:
             weights = stop.value
-        response_part, dnorm2, latent_d, dlat_gu, deep = feed_forward_shared(
+        (finish, shares), dnorm2, latent_d, dlat_gu, deep = feed_forward_shared(
             norm2, sens_pairs, weights, small, all_seen
         )
     else:
-        response_part, dnorm2, latent_d, dlat_gu, deep = feed_forward_alone(
+        (finish, shares), dnorm2, latent_d, dlat_gu, deep = feed_forward_alone(
             norm2, sens, gate_up_full, down_full, small, seen
         )
-    level_response = (stream + response_part).astype(BF16)
     dhidden = sens.astype(F32) + norm_backward(stream, scale_two, mlp_gain, dnorm2)
     dbranch = dhidden.astype(BF16)
     dlat_o = (LOWRANK_FACTOR * mm_nt(dbranch, final) * seen).astype(BF16)
@@ -1099,11 +1106,11 @@
     dattended, (deep,) = tie(dattended, (deep,))
     deep_sum = lax.psum_scatter(deep, "grp", scatter_dimension=0, tiled=True)[0]
 
-    dq, dkv_all = attention_backward(
+    dq, dkv_even, dkv_odd = attention_backward(
         span, query, dattended, attended_low, lse, key_value, bias, cosines, sines
     )
-    dkv_all, (deep_sum,) = tie(dkv_all, (deep_sum,))
-    received = lax.all_to_all(dkv_all, "grp", 0, 0, tiled=True)
+    dkv_odd, (deep_sum, *shares) = tie(dkv_odd, (deep_sum, *shares))
+    received, dq = exchange(dkv_even, dkv_odd, paired, dq)
     dlat_q, early = early_gradients(
         dq,
         asking,
@@ -1120,11 +1127,14 @@
         dbranch,
     )
     dnorm_q = mm_nt(dq, qkv_full[:, :width]) + mm_nt(dlat_q, qkv_in[:, :slots])
-    dkv, dlat_kv, late = key_value_gradients(
-        received, early, cosines, sines, kv_right, seen_three[:, : 2 * slots], latent_kv, norm1
+    turns = jnp.full((1,), turn, jnp.int32)
+    dkv, dlat_kv, late_even, late_odd = key_value_gradients(
+        turns, received, early, cosines, sines, kv_right, seen_three[:, : 2 * slots], latent_kv, norm1
     )
     deep_sum = round_groups(deep_sum)
-    late_sum = round_groups(exchange_sum(late).astype(BF16))
+    late_parts = [part.astype(F32) for part in exchange(late_even, late_odd, paired)[0]]
+    late_sum = round_groups(sum(late_parts[1:], late_parts[0]).astype(BF16))
+    level_response = (stream + finish(shares)).astype(BF16)
     dnorm1 = dnorm_q + mm_nt(dkv, qkv_full[:, width:]) + mm_nt(dlat_kv, qkv_in[:, slots:])
     input_grad = (dhidden + norm_backward(incoming, scale_one, attn_gain, dnorm1)).astype(BF16)
 

time: 497 us -> 468 us (0.942)
  local copies, waits for them, and re-layouts: 52.8 us -> 43.2 us
  starting transfers between devices: 46.7 us -> 39.3 us
    all_to_all x2 -> x0, waiting for transfers between devices: 19.2 us -> none  [the longest x1 14.8 us: shards(): received = lax.all_to_all(dkv_all, 'grp', 0, 0, tiled=True)]
    unnamed x279 -> x259, local copies, waits for them, and re-layouts: 33.6 us -> 23.7 us
    all_to_all x2 -> x0, starting transfers between devices: 8.96 us -> none  [the longest x1 4.61 us: exchange_sum(): received = lax.all_to_all(parts.astype(BF16), 'grp', 0, 0, tiled=True)]
    ppermute x6, waiting for transfers between devices: 4.17 us -> 13.1 us  [round_groups(): lax.ppermute(array, 'rep', [(i, (i + shift) % groups) for i in range(grou...]
    ppermute x26 -> x34, waiting for transfers between devices: 102 us -> 110 us  [flip(): return lax.ppermute(array, 'grp', [(i, i ^ mask) for i in range(members)])]
    ppermute x26 -> x34, starting transfers between devices: 18.7 us -> 25 us  [flip(): return lax.ppermute(array, 'grp', [(i, i ^ mask) for i in range(members)])]
    convert_element_type x1 -> x5, other arithmetic: 0.1 us -> 6.35 us  [the longest x1 3.06 us: feed_forward_shared(): (other.astype(F32) + flip(other_near, CORE).astype(F32)).astype(BF16)]
  transfers between devices with their start and end apart: 41 -> 47, of which waited for: 22 -> 24; matrix products, arithmetic and copies ran while one was open for 18% -> 19% of each run, Pallas kernels for 20% -> 21%
where the time goes in v7:
time: 468 us; the launch traced here: 463 us
  waiting for transfers between devices  157 us (34%)
  Pallas kernels  129 us (28%)
  local copies, waits for them, and re-layouts  43.2 us (9%)
  starting transfers between devices  39.3 us (8%)
  matrix products  38.8 us (8%)
  other arithmetic  36.9 us (8%)
  between operations  18.9 us (4%)
    ppermute x34, waiting for transfers between devices, flip(): return lax.ppermute(array, 'grp', [(i, i ^ mask) for i in range(members)])  110 us
    pallas_call x2, Pallas kernels, feed_forward_pair(): pl.pallas_call(feed_forward_kernel, out_shape=(jax.ShapeDtypeStruct((coun...  59.9 us
    pallas_call x1, Pallas kernels, attention_backward(): pl.pallas_call(functools.partial(attention_backward_kernel, per_kv), out_...  34.7 us
    ppermute x34, starting transfers between devices, flip(): return lax.ppermute(array, 'grp', [(i, i ^ mask) for i in range(members)])  25 us
    all_gather x1, waiting for transfers between devices, shards(): qkv_full = lax.all_gather(qkv_weight, 'grp', axis=1, tiled=True)  24.7 us
    unnamed x259, local copies, waits for them, and re-layouts  23.7 us
    dot_general x15, matrix products, mm(): return jnp.dot(left, right, preferred_element_type=F32)  21.7 us
    pallas_call x1, Pallas kernels, attention_forward(): pl.pallas_call(functools.partial(attention_forward_kernel, steps // KV_HE...  18.5 us
  transfers between devices with their start and end apart: 47, of which 24 were waited for; matrix products, arithmetic and copies ran while one was open for 19% of the time, Pallas kernels for 21%

profile of v7, /device:TPU:0, one launch (start us, length us, event | category | flops | bytes accessed | tf_op | source)
XLA Modules:
  0.0 463.1 jit_solution(15739506746631516534)
XLA Ops:
  8.0 5.2 %constant_dynamic-slice_fusion.2 = (bf16[512,1408]{1,0:T(8,128)(2,1)}, bf16[512,1408]{1,0:T(8,128)(2,1)}, bf16[512,1408]{1,0:T(8,128)(2,1)}, bf16[512,1408]{1,0:T(8,128)(2,1)}) fusion(bf16[2048,1408]{1,0:T(8,128)(2,1)} %param.34, s32[]{:T(128)S(6)} %select_n.259, s32[]{:T(128)S(6)} %select_n.231, s32[]{:T(128)S(6)} %select_n.230, s32[]{:T(128)S(6)} %select_n.258), kind=kLoop, calls=%fused_computation.190 | loop fusion | bytes 11534352 | tf_op jit(solution)/shard_map/dynamic_slice | solution.py:351
  13.2 3.0 collective-permute-start
  16.2 3.2 dynamic-slice_bitcast_fusion
  24.2 2.0 fusion.89
  44.9 3.2 and_select_fusion.bias_ref
  48.1 4.8 %collective-permute-done.1 = bf16[1408,256]{1,0:T(8,128)(2,1)} collective-permute-done((bf16[1408,256]{1,0:T(8,128)(2,1)}, bf16[1408,256]{1,0:T(8,128)(2,1)}, u32[]{:S(2)}, u32[]{:S(2)}) %collective-permute-start.1) | collective-permute-done | bytes 720928 | tf_op jit(solution)/shard_map/ppermute | solution.py:337
  52.9 21.5 %collective-permute-done.3 = bf16[1408,256]{1,0:T(8,128)(2,1)} collective-permute-done((bf16[1408,256]{1,0:T(8,128)(2,1)}, bf16[1408,256]{1,0:T(8,128)(2,1)}, u32[]{:S(2)}, u32[]{:S(2)}) %collective-permute-start.3) | collective-permute-done | bytes 720928 | tf_op jit(solution)/shard_map/ppermute | solution.py:337
  76.7 3.0 pad_maximum_fusion.refs_8_.refs_2_
  79.6 24.7 %all-gather.3.cloned.1.call-done = bf16[2048,2560]{0,1:T(8,128)(2,1)} async-done(((bf16[2048,320]{0,1:T(8,128)(2,1)}), bf16[2048,2560]{0,1:T(8,128)(2,1)}) %all-gather.3.cloned.1.call-update) | async-done | bytes 10485776 | tf_op jit(solution)/shard_map/all_gather | solution.py:957
  104.3 5.6 %fusion.112 = f32[256,2560]{1,0:T(8,128)S(1)} fusion(bf16[256,2048]{1,0:T(8,128)(2,1)S(1)} %fusion.12.norm1_ref.refs_10_, bf16[2048,2560]{0,1:T(8,128)(2,1)} %all-gather.3.cloned.1.call-done), kind=kOutput, calls=%fused_computation.259 | convolution fusion | flops 2684354560 | bytes 14155776 | tf_op jit(solution)/shard_map/dot_general | solution.py:26
  111.0 11.0 %collective-permute-done.4.refs_5_ = bf16[512,1408]{1,0:T(8,128)(2,1)} collective-permute-done((bf16[512,1408]{1,0:T(8,128)(2,1)}, bf16[512,1408]{1,0:T(8,128)(2,1)}, u32[]{:S(2)}, u32[]{:S(2)}) %collective-permute-start.4) | collective-permute-done | bytes 1441824 | tf_op jit(solution)/shard_map/ppermute | solution.py:337
  123.8 2.5 collective-permute-start.9
  127.4 9.2 %collective-permute-done.7 = bf16[256,512]{1,0:T(8,128)(2,1)S(1)} collective-permute-done((bf16[256,512]{1,0:T(8,128)(2,1)S(1)}, bf16[256,512]{1,0:T(8,128)(2,1)S(1)}, u32[]{:S(2)}, u32[]{:S(2)}) %collective-permute-start.7) | collective-permute-done | bytes 262176 | tf_op jit(solution)/shard_map/ppermute | solution.py:337
  139.3 6.5 %collective-permute-done.11 = bf16[256,512]{1,0:T(8,128)(2,1)S(1)} collective-permute-done((bf16[256,512]{1,0:T(8,128)(2,1)S(1)}, bf16[256,512]{1,0:T(8,128)(2,1)S(1)}, u32[]{:S(2)}, u32[]{:S(2)}) %collective-permute-start.11) | collective-permute-done | bytes 262176 | tf_op jit(solution)/shard_map/ppermute | solution.py:337
  147.8 1.9 collective-permute-start.16
  154.1 2.7 fusion.27.q_ref
  156.9 18.5 %attention_forward.1 = (bf16[256,2048]{1,0:T(8,128)(2,1)S(1)}, f32[16,2,256]{2,1,0:T(2,128)S(1)}) custom-call(s32[3]{0:T(128)S(1)} %pad_add_fusion.span, bf16[256,2048]{1,0:T(8,128)(2,1)S(1)} %fusion.27.q_ref, bf16[2048,512]{1,0:T(8,128)(2,1)S(1)} %constant_dynamic-update-slice_fusion.key_ref.value_ref, ...), custom_call_target="tpu_custom_call" | custom-call | flops 4294967296 | bytes 18874368 | tf_op jit(solution)/shard_map/attention_forward/pallas_call | solution.py:149
  176.0 8.9 %collective-permute-done.15.refs_9_.refs_3_ = bf16[1,1408,256]{2,1,0:T(8,128)(2,1)} collective-permute-done((bf16[1,1408,256]{2,1,0:T(8,128)(2,1)S(1)}, bf16[1,1408,256]{2,1,0:T(8,128)(2,1)}, u32[]{:S(2)}, u32[]{:S(2)}) %collective-permute-start.15) | collective-permute-done | bytes 720928 | tf_op jit(solution)/shard_map/ppermute | solution.py:337
  184.9 7.0 %collective-permute-done.14.own_g = bf16[256,2048]{1,0:T(8,128)(2,1)} collective-permute-done((bf16[256,2048]{1,0:T(8,128)(2,1)S(1)}, bf16[256,2048]{1,0:T(8,128)(2,1)}, u32[]{:S(2)}, u32[]{:S(2)}) %collective-permute-start.14) | collective-permute-done | bytes 1048608 | tf_op jit(solution)/shard_map/ppermute | solution.py:337
  195.4 1.8 convolution_multiply_fusion.1
  197.2 13.6 %collective-permute-done.18.refs_10_.refs_4_ = bf16[1,1408,256]{2,1,0:T(8,128)(2,1)} collective-permute-done((bf16[1,1408,256]{2,1,0:T(8,128)(2,1)}, bf16[1,1408,256]{2,1,0:T(8,128)(2,1)}, u32[]{:S(2)}, u32[]{:S(2)}) %collective-permute-start.18) | collective-permute-done | bytes 720928 | tf_op jit(solution)/shard_map/ppermute | solution.py:337
  213.5 6.8 %multiply_reduce_fusion.1 = (f32[256]{0:T(256)S(1)}, f32[256,2048]{1,0:T(8,128)S(1)}) fusion(f32[256,2048]{1,0:T(8,128)} %convolution_multiply_fusion.1, bf16[256,2048]{1,0:T(8,128)(2,1)S(1)} %get-tuple-element.132.o_ref.attended_ref, bf16[2048,2048]{1,0:T(8,128)(2,1)} %all-gather.5.cloned.1.call-done, bf16[256,2048]{1,0:T(8,128)(2,1)} %param.25), kind=kOutput, calls=%fused_computation.57 | convolution fusion | flops 2150104832 | bytes 14681088 | tf_op jit(solution)/shard_map/dot_general | solution.py:26
  221.6 8.0 %collective-permute-done.20.refs_12_.refs_6_ = bf16[1,1408,256]{2,1,0:T(8,128)(2,1)S(1)} collective-permute-done((bf16[1,1408,256]{2,1,0:T(8,128)(2,1)}, bf16[1,1408,256]{2,1,0:T(8,128)(2,1)S(1)}, u32[]{:S(2)}, u32[]{:S(2)}) %collective-permute-start.20) | collective-permute-done | bytes 720928 | tf_op jit(solution)/shard_map/ppermute | solution.py:342
  230.9 1.9 concatenate.64.own_x
  233.4 2.4 collective-permute-done.21.near_x
  239.6 30.1 %feed_forward.2 = (f32[256,2176]{1,0:T(8,128)}, bf16[256,2176]{1,0:T(8,128)(2,1)}, bf16[512,1408]{1,0:T(8,128)(2,1)}, f32[96,1408]{1,0:T(8,128)S(1)}) custom-call(s32[3]{0:T(128)S(1)} %pad_add_fusion.1.meta, bf16[256,2176]{1,0:T(8,128)(2,1)} %concatenate.64.own_x, bf16[256,2176]{1,0:T(8,128)(2,1)} %collective-permute-done.21.near_x, ...), custom_call_target="tpu_custom_call" | custom-call | flops 14763950080 | bytes 38273024 | tf_op jit(solution)/shard_map/feed_forward/pallas_call | solution.py:637
  270.0 2.6 collective-permute-done.24.near_x
  273.7 29.8 %feed_forward.3 = (f32[256,2176]{1,0:T(8,128)}, bf16[256,2176]{1,0:T(8,128)(2,1)}, bf16[512,1408]{1,0:T(8,128)(2,1)}, f32[96,1408]{1,0:T(8,128)S(1)}) custom-call(s32[3]{0:T(128)S(1)} %pad_add_fusion.1.meta, bf16[256,2176]{1,0:T(8,128)(2,1)} %copy-done.116, bf16[256,2176]{1,0:T(8,128)(2,1)} %copy-done.117, bf16[256,2048]{1,0:T(8,128)(2,1)} %collective-permute-done.14.own_g, ...), custom_call_target="tpu_custom_call" | custom-call | flops 14763950080 | bytes 38273024 | tf_op jit(solution)/shard_map/feed_forward/pallas_call | solution.py:637
  304.8 2.6 collective-permute-done.25
  307.4 3.2 add_convert_fusion
  313.4 1.8 copy-done.3
  319.0 11.4 %down_projection.1 = (f32[256,2048]{1,0:T(8,128)S(1)}, bf16[256,2048]{1,0:T(8,128)(2,1)S(1)}, bf16[256,2048]{1,0:T(8,128)(2,1)S(1)}, bf16[256,2048]{1,0:T(8,128)(2,1)}) custom-call(s32[3]{0:T(128)S(1)} %copy-done.48, bf16[512,1408]{1,0:T(8,128)(2,1)S(1)} %copy-done.55, bf16[512,1408]{1,0:T(8,128)(2,1)S(1)} %copy-done.56, ...), custom_call_target="tpu_custom_call" | custom-call | flops 5905580032 | bytes 14155776 | tf_op jit(solution)/shard_map/down_projection/pallas_call | solution.py:611
  330.4 7.0 %collective-permute-done.26 = bf16[256,2176]{1,0:T(8,128)(2,1)} collective-permute-done((bf16[256,2176]{1,0:T(8,128)(2,1)}, bf16[256,2176]{1,0:T(8,128)(2,1)}, u32[]{:S(2)}, u32[]{:S(2)}) %collective-permute-start.26) | collective-permute-done | bytes 1114144 | tf_op jit(solution)/shard_map/ppermute | solution.py:337
  337.5 2.0 convert_add_fusion.1
  342.5 2.1 fusion.105
  346.2 3.4 fusion.4.do_ref
  349.8 3.1 add_convert_fusion.3
  354.1 34.7 %attention_backward.1 = (bf16[256,2048]{1,0:T(8,128)(2,1)S(1)}, bf16[4,256,512]{2,1,0:T(8,128)(2,1)S(1)}, bf16[4,256,512]{2,1,0:T(8,128)(2,1)S(1)}) custom-call(s32[3]{0:T(128)S(1)} %copy-done.46, bf16[256,2048]{1,0:T(8,128)(2,1)S(1)} %copy-done.16, bf16[256,2048]{1,0:T(8,128)(2,1)S(1)} %copy-done.54, bf16[256,2048]{1,0:T(8,128)(2,1)S(1)} %copy-done.20, ...), custom_call_target="tpu_custom_call" | custom-call | flops 10737418240 | bytes 13631488 | tf_op jit(solution)/shard_map/attention_backward/pallas_call | solution.py:294
  395.6 2.5 collective-permute-start.42
  398.2 2.0 add_convert_fusion.1
  403.9 3.2 add_convert_fusion.2
  407.2 2.0 early_gradients.1
  409.5 5.6 %collective-permute-done.32.refs_2_ = bf16[256,512]{1,0:T(8,128)(2,1)S(1)} collective-permute-done((bf16[256,512]{1,0:T(8,128)(2,1)S(1)}, bf16[256,512]{1,0:T(8,128)(2,1)S(1)}, u32[]{:S(2)}, u32[]{:S(2)}) %collective-permute-start.32) | collective-permute-done | bytes 262176 | tf_op jit(solution)/shard_map/ppermute | solution.py:337
  416.1 5.8 %fusion = f32[256,2048]{1,0:T(8,128)S(1)} fusion(bf16[256,2048]{1,0:T(8,128)(2,1)S(1)} %copy-done.23, bf16[2048,2560]{0,1:T(8,128)(2,1)} %all-gather.3.cloned.1.call-done), kind=kOutput, calls=%fused_computation | convolution fusion | flops 2147483648 | bytes 11534336 | tf_op jit(solution)/shard_map/dot_general | solution.py:30
  427.1 2.8 fusion.17
  432.4 2.4 collective-permute-done.36
  436.9 7.5 %collective-permute-done.38.refs_2_ = bf16[352,256]{1,0:T(8,128)(2,1)S(1)} collective-permute-done((bf16[352,256]{1,0:T(8,128)(2,1)S(1)}, bf16[352,256]{1,0:T(8,128)(2,1)S(1)}, u32[]{:S(2)}, u32[]{:S(2)}) %collective-permute-start.38) | collective-permute-done | bytes 180256 | tf_op jit(solution)/shard_map/ppermute | solution.py:911
  445.9 4.5 collective-permute-done.39.refs_3_
  (433 shorter events, 93.5 us)
Async XLA Ops:
  7.2 97.1 %all-gather.3.cloned.1.call-start = ((), (), s32[]{:S(2)}) async-start(), calls=%async_computation.1 | async-start | bytes 11796480 | tf_op jit(solution)/shard_map/all_gather | solution.py:957
  7.9 189.3 %all-gather.5.cloned.1.call-start = ((), (), s32[]{:S(2)}) async-start(), calls=%async_computation.2 | async-start | bytes 9437184 | tf_op jit(solution)/shard_map/all_gather | solution.py:1047
  13.2 61.2 %collective-permute-start = (bf16[512,1408]{1,0:T(8,128)(2,1)}, bf16[512,1408]{1,0:T(8,128)(2,1)}, u32[]{:S(2)}, u32[]{:S(2)}) collective-permute-start(bf16[512,1408]{1,0:T(8,128)(2,1)} %get-tuple-element.266.refs_0_), channel_id=1, source_target_pairs={{0,4},{1,5},{2,6},{3,7},{4,0},{5,1},{6,2},{7,3},{8,12},{9,13},{10,... | collective-permute-start | bytes 4325384 | tf_op jit(solution)/shard_map/ppermute | solution.py:337
  19.4 33.4 %collective-permute-start.1 = (bf16[1408,256]{1,0:T(8,128)(2,1)}, bf16[1408,256]{1,0:T(8,128)(2,1)}, u32[]{:S(2)}, u32[]{:S(2)}) collective-permute-start(bf16[1408,256]{1,0:T(8,128)(2,1)} %get-tuple-element.272), channel_id=1, source_target_pairs={{0,2},{1,3},{2,0},{3,1},{4,6},{5,7},{6,4},{7,5},{8,10},{9,11},{10,... | collective-permute-start | bytes 2162696 | tf_op jit(solution)/shard_map/ppermute | solution.py:337
  20.9 31.9 %collective-permute-start.2 = (bf16[1408,256]{1,0:T(8,128)(2,1)}, bf16[1408,256]{1,0:T(8,128)(2,1)}, u32[]{:S(2)}, u32[]{:S(2)}) collective-permute-start(bf16[1408,256]{1,0:T(8,128)(2,1)} %get-tuple-element.271), channel_id=1, source_target_pairs={{0,1},{1,0},{2,3},{3,2},{4,5},{5,4},{6,7},{7,6},{8,9},{9,8},{10,11... | collective-permute-start | bytes 2162696 | tf_op jit(solution)/shard_map/ppermute | solution.py:337
  20.9 53.4 %collective-permute-start.3 = (bf16[1408,256]{1,0:T(8,128)(2,1)}, bf16[1408,256]{1,0:T(8,128)(2,1)}, u32[]{:S(2)}, u32[]{:S(2)}) collective-permute-start(bf16[1408,256]{1,0:T(8,128)(2,1)} %get-tuple-element.273), channel_id=1, source_target_pairs={{0,3},{1,2},{2,1},{3,0},{4,7},{5,6},{6,5},{7,4},{8,11},{9,10},{10,... | collective-permute-start | bytes 2162696 | tf_op jit(solution)/shard_map/ppermute | solution.py:337
  21.6 370.3 %reduce-scatter.2.cloned.1.call-start = ((), (), s32[]{:S(2)}) async-start(), calls=%async_computation.3 | async-start | bytes 1327104 | tf_op jit(solution)/shard_map/reduce_scatter | solution.py:1107
  40.8 231.8 %copy-start.30 = (bf16[32,2048]{1,0:T(8,128)(2,1)}, bf16[32,2048]{1,0:T(8,128)(2,1)S(1)}, u32[]{:S(2)}) copy-start(bf16[32,2048]{1,0:T(8,128)(2,1)S(1)} %convolution_convert_fusion.6.lower_ref) | copy-start | bytes 393220
  74.4 47.6 %collective-permute-start.4 = (bf16[512,1408]{1,0:T(8,128)(2,1)}, bf16[512,1408]{1,0:T(8,128)(2,1)}, u32[]{:S(2)}, u32[]{:S(2)}) collective-permute-start(bf16[512,1408]{1,0:T(8,128)(2,1)} %get-tuple-element.118.refs_1_), channel_id=1, source_target_pairs={{0,4},{1,5},{2,6},{3,7},{4,0},{5,1},{6,2},{7,3},{8,12},{9,13},{10,... | collective-permute-start | bytes 4325384 | tf_op jit(solution)/shard_map/ppermute | solution.py:337
  74.5 47.5 %collective-permute-start.5 = (bf16[512,1408]{1,0:T(8,128)(2,1)}, bf16[512,1408]{1,0:T(8,128)(2,1)}, u32[]{:S(2)}, u32[]{:S(2)}) collective-permute-start(bf16[512,1408]{1,0:T(8,128)(2,1)} %collective-permute-done.refs_4_), channel_id=1, source_target_pairs={{0,8},{8,0},{16,24},{24,16},{1,9},{9,1},{17,25},{25,17},{2,10},{10... | collective-permute-start | bytes 4325384 | tf_op jit(solution)/shard_map/ppermute | solution.py:342
  122.0 17.3 %collective-permute-start.6 = (bf16[256,512]{1,0:T(8,128)(2,1)S(1)}, bf16[256,512]{1,0:T(8,128)(2,1)S(1)}, u32[]{:S(2)}, u32[]{:S(2)}) collective-permute-start(bf16[256,512]{1,0:T(8,128)(2,1)S(1)} %pad_maximum_fusion.2), channel_id=1, source_target_pairs={{0,1},{1,0},{2,3},{3,2},{4,5},{5,4},{6,7},{7,6},{8,9},{9,8},{10,11... | collective-permute-start | bytes 786440 | tf_op jit(solution)/shard_map/ppermute | solution.py:337
  122.1 14.6 %collective-permute-start.7 = (bf16[256,512]{1,0:T(8,128)(2,1)S(1)}, bf16[256,512]{1,0:T(8,128)(2,1)S(1)}, u32[]{:S(2)}, u32[]{:S(2)}) collective-permute-start(bf16[256,512]{1,0:T(8,128)(2,1)S(1)} %pad_maximum_fusion.2), channel_id=1, source_target_pairs={{0,2},{1,3},{2,0},{3,1},{4,6},{5,7},{6,4},{7,5},{8,10},{9,11},{10,... | collective-permute-start | bytes 786440 | tf_op jit(solution)/shard_map/ppermute | solution.py:337
  123.8 14.1 %collective-permute-start.9 = (bf16[256,512]{1,0:T(8,128)(2,1)S(1)}, bf16[256,512]{1,0:T(8,128)(2,1)S(1)}, u32[]{:S(2)}, u32[]{:S(2)}) collective-permute-start(bf16[256,512]{1,0:T(8,128)(2,1)S(1)} %pad_maximum_fusion.2), channel_id=1, source_target_pairs={{0,4},{1,5},{2,6},{3,7},{4,0},{5,1},{6,2},{7,3},{8,12},{9,13},{10,... | collective-permute-start | bytes 786440 | tf_op jit(solution)/shard_map/ppermute | solution.py:337
  136.7 9.2 %collective-permute-start.8 = (bf16[256,512]{1,0:T(8,128)(2,1)S(1)}, bf16[256,512]{1,0:T(8,128)(2,1)S(1)}, u32[]{:S(2)}, u32[]{:S(2)}) collective-permute-start(bf16[256,512]{1,0:T(8,128)(2,1)S(1)} %collective-permute-done.7), channel_id=1, source_target_pairs={{0,1},{1,0},{2,3},{3,2},{4,5},{5,4},{6,7},{7,6},{8,9},{9,8},{10,11... | collective-permute-start | bytes 786440 | tf_op jit(solution)/shard_map/ppermute | solution.py:337
  137.8 8.0 %collective-permute-start.11 = (bf16[256,512]{1,0:T(8,128)(2,1)S(1)}, bf16[256,512]{1,0:T(8,128)(2,1)S(1)}, u32[]{:S(2)}, u32[]{:S(2)}) collective-permute-start(bf16[256,512]{1,0:T(8,128)(2,1)S(1)} %collective-permute-done.9), channel_id=1, source_target_pairs={{0,2},{1,3},{2,0},{3,1},{4,6},{5,7},{6,4},{7,5},{8,10},{9,11},{10,... | collective-permute-start | bytes 786440 | tf_op jit(solution)/shard_map/ppermute | solution.py:337
  139.2 6.7 %collective-permute-start.10 = (bf16[256,512]{1,0:T(8,128)(2,1)S(1)}, bf16[256,512]{1,0:T(8,128)(2,1)S(1)}, u32[]{:S(2)}, u32[]{:S(2)}) collective-permute-start(bf16[256,512]{1,0:T(8,128)(2,1)S(1)} %collective-permute-done.9), channel_id=1, source_target_pairs={{0,1},{1,0},{2,3},{3,2},{4,5},{5,4},{6,7},{7,6},{8,9},{9,8},{10,11... | collective-permute-start | bytes 786440 | tf_op jit(solution)/shard_map/ppermute | solution.py:337
  145.8 1.9 collective-permute-start.12
  147.8 44.2 %collective-permute-start.16 = (bf16[512,1408]{1,0:T(8,128)(2,1)}, bf16[512,1408]{1,0:T(8,128)(2,1)S(1)}, u32[]{:S(2)}, u32[]{:S(2)}) collective-permute-start(bf16[512,1408]{1,0:T(8,128)(2,1)} %collective-permute-done.4.refs_5_), channel_id=1, source_target_pairs={{0,8},{8,0},{16,24},{24,16},{1,9},{9,1},{17,25},{25,17},{2,10},{10... | collective-permute-start | bytes 4325384 | tf_op jit(solution)/shard_map/ppermute | solution.py:342
  149.8 35.1 %collective-permute-start.13 = (bf16[256,2048]{1,0:T(8,128)(2,1)S(1)}, bf16[256,2048]{1,0:T(8,128)(2,1)S(1)}, u32[]{:S(2)}, u32[]{:S(2)}) collective-permute-start(bf16[256,2048]{1,0:T(8,128)(2,1)S(1)} %copy-done.4), channel_id=1, source_target_pairs={{0,1},{1,0},{2,3},{3,2},{4,5},{5,4},{6,7},{7,6},{8,9},{9,8},{10,11... | collective-permute-start | bytes 3145736 | tf_op jit(solution)/shard_map/ppermute | solution.py:337
  149.9 42.1 %collective-permute-start.14 = (bf16[256,2048]{1,0:T(8,128)(2,1)S(1)}, bf16[256,2048]{1,0:T(8,128)(2,1)}, u32[]{:S(2)}, u32[]{:S(2)}) collective-permute-start(bf16[256,2048]{1,0:T(8,128)(2,1)S(1)} %copy-done.4), channel_id=1, source_target_pairs={{0,2},{1,3},{2,0},{3,1},{4,6},{5,7},{6,4},{7,5},{8,10},{9,11},{10,... | collective-permute-start | bytes 3145736 | tf_op jit(solution)/shard_map/ppermute | solution.py:337
  151.7 33.2 %collective-permute-start.15 = (bf16[1,1408,256]{2,1,0:T(8,128)(2,1)S(1)}, bf16[1,1408,256]{2,1,0:T(8,128)(2,1)}, u32[]{:S(2)}, u32[]{:S(2)}) collective-permute-start(bf16[1,1408,256]{2,1,0:T(8,128)(2,1)S(1)} %get-tuple-element.269), channel_id=1, source_target_pairs={{0,4},{1,5},{2,6},{3,7},{4,0},{5,1},{6,2},{7,3},{8,12},{9,13},{10,... | collective-permute-start | bytes 2162696 | tf_op jit(solution)/shard_map/ppermute | solution.py:337
  191.9 20.1 %collective-permute-start.17 = (bf16[256,2048]{1,0:T(8,128)(2,1)}, bf16[256,2048]{1,0:T(8,128)(2,1)}, u32[]{:S(2)}, u32[]{:S(2)}) collective-permute-start(bf16[256,2048]{1,0:T(8,128)(2,1)} %collective-permute-done.14.own_g), channel_id=1, source_target_pairs={{0,1},{1,0},{2,3},{3,2},{4,5},{5,4},{6,7},{7,6},{8,9},{9,8},{10,11... | collective-permute-start | bytes 3145736 | tf_op jit(solution)/shard_map/ppermute | solution.py:337
  191.9 18.9 %collective-permute-start.18 = (bf16[1,1408,256]{2,1,0:T(8,128)(2,1)}, bf16[1,1408,256]{2,1,0:T(8,128)(2,1)}, u32[]{:S(2)}, u32[]{:S(2)}) collective-permute-start(bf16[1,1408,256]{2,1,0:T(8,128)(2,1)} %get-tuple-element.134), channel_id=1, source_target_pairs={{0,4},{1,5},{2,6},{3,7},{4,0},{5,1},{6,2},{7,3},{8,12},{9,13},{10,... | collective-permute-start | bytes 2162696 | tf_op jit(solution)/shard_map/ppermute | solution.py:337
  193.5 18.5 %collective-permute-start.19 = (bf16[1,1408,256]{2,1,0:T(8,128)(2,1)}, bf16[1,1408,256]{2,1,0:T(8,128)(2,1)}, u32[]{:S(2)}, u32[]{:S(2)}) collective-permute-start(bf16[1,1408,256]{2,1,0:T(8,128)(2,1)} %collective-permute-done.15.refs_9_.refs_3_), channel_id=1, source_target_pairs={{0,8},{8,0},{16,24},{24,16},{1,9},{9,1},{17,25},{25,17},{2,10},{10... | collective-permute-start | bytes 2162696 | tf_op jit(solution)/shard_map/ppermute | solution.py:342
  212.0 17.6 %collective-permute-start.20 = (bf16[1,1408,256]{2,1,0:T(8,128)(2,1)}, bf16[1,1408,256]{2,1,0:T(8,128)(2,1)S(1)}, u32[]{:S(2)}, u32[]{:S(2)}) collective-permute-start(bf16[1,1408,256]{2,1,0:T(8,128)(2,1)} %collective-permute-done.18.refs_10_.refs_4_), channel_id=1, source_target_pairs={{0,8},{8,0},{16,24},{24,16},{1,9},{9,1},{17,25},{25,17},{2,10},{10... | collective-permute-start | bytes 2162696 | tf_op jit(solution)/shard_map/ppermute | solution.py:342
  232.8 3.1 collective-permute-start.21
  232.8 36.9 %collective-permute-start.22 = (bf16[256,2176]{1,0:T(8,128)(2,1)}, bf16[256,2176]{1,0:T(8,128)(2,1)S(1)}, u32[]{:S(2)}, u32[]{:S(2)}) collective-permute-start(bf16[256,2176]{1,0:T(8,128)(2,1)} %concatenate.64.own_x), channel_id=1, source_target_pairs={{0,2},{1,3},{2,0},{3,1},{4,6},{5,7},{6,4},{7,5},{8,10},{9,11},{10,... | collective-permute-start | bytes 3342344 | tf_op jit(solution)/shard_map/ppermute | solution.py:337
  269.8 2.8 collective-permute-start.24
  304.3 3.1 collective-permute-start.25
  304.4 33.0 %collective-permute-start.23 = (bf16[256,2176]{1,0:T(8,128)(2,1)}, bf16[256,2176]{1,0:T(8,128)(2,1)}, u32[]{:S(2)}, u32[]{:S(2)}) collective-permute-start(bf16[256,2176]{1,0:T(8,128)(2,1)} %get-tuple-element.154), channel_id=1, source_target_pairs={{0,1},{1,0},{2,3},{3,2},{4,5},{5,4},{6,7},{7,6},{8,9},{9,8},{10,11... | collective-permute-start | bytes 3342344 | tf_op jit(solution)/shard_map/ppermute | solution.py:337
  310.5 26.9 %collective-permute-start.26 = (bf16[256,2176]{1,0:T(8,128)(2,1)}, bf16[256,2176]{1,0:T(8,128)(2,1)}, u32[]{:S(2)}, u32[]{:S(2)}) collective-permute-start(bf16[256,2176]{1,0:T(8,128)(2,1)} %add_convert_fusion), channel_id=1, source_target_pairs={{0,2},{1,3},{2,0},{3,1},{4,6},{5,7},{6,4},{7,5},{8,10},{9,11},{10,... | collective-permute-start | bytes 3342344 | tf_op jit(solution)/shard_map/ppermute | solution.py:337
  341.1 8.6 %collective-permute-start.28 = (bf16[256,2048]{1,0:T(8,128)(2,1)}, bf16[256,2048]{1,0:T(8,128)(2,1)}, u32[]{:S(2)}, u32[]{:S(2)}) collective-permute-start(bf16[256,2048]{1,0:T(8,128)(2,1)} %get-tuple-element.183), channel_id=1, source_target_pairs={{0,1},{1,0},{2,3},{3,2},{4,5},{5,4},{6,7},{7,6},{8,9},{9,8},{10,11... | collective-permute-start | bytes 3145736 | tf_op jit(solution)/shard_map/ppermute | solution.py:337
  349.7 42.2 %collective-permute-start.27 = (bf16[256,2048]{1,0:T(8,128)(2,1)}, bf16[256,2048]{1,0:T(8,128)(2,1)}, u32[]{:S(2)}, u32[]{:S(2)}) collective-permute-start(bf16[256,2048]{1,0:T(8,128)(2,1)} %copy-done.49), channel_id=1, source_target_pairs={{0,1},{1,0},{2,3},{3,2},{4,5},{5,4},{6,7},{7,6},{8,9},{9,8},{10,11... | collective-permute-start | bytes 3145736 | tf_op jit(solution)/shard_map/ppermute | solution.py:337
  352.8 39.0 %collective-permute-start.29 = (bf16[256,2048]{1,0:T(8,128)(2,1)}, bf16[256,2048]{1,0:T(8,128)(2,1)}, u32[]{:S(2)}, u32[]{:S(2)}) collective-permute-start(bf16[256,2048]{1,0:T(8,128)(2,1)} %add_convert_fusion.3), channel_id=1, source_target_pairs={{0,2},{1,3},{2,0},{3,1},{4,6},{5,7},{6,4},{7,5},{8,10},{9,11},{10,... | collective-permute-start | bytes 3145736 | tf_op jit(solution)/shard_map/ppermute | solution.py:337
  391.9 6.3 %collective-permute-start.30 = (bf16[4,256,512]{2,1,0:T(8,128)(2,1)}, bf16[4,256,512]{2,1,0:T(8,128)(2,1)}, u32[]{:S(2)}, u32[]{:S(2)}) collective-permute-start(bf16[4,256,512]{2,1,0:T(8,128)(2,1)} %copy-done.50), channel_id=1, source_target_pairs={{0,1},{1,0},{2,3},{3,2},{4,5},{5,4},{6,7},{7,6},{8,9},{9,8},{10,11... | collective-permute-start | bytes 3145736 | tf_op jit(solution)/shard_map/ppermute | solution.py:337
  393.9 57.6 %collective-permute-start.41 = (bf16[96,704]{1,0:T(8,128)(2,1)}, bf16[96,704]{1,0:T(8,128)(2,1)S(1)}, u32[]{:S(2)}, u32[]{:S(2)}) collective-permute-start(bf16[96,704]{1,0:T(8,128)(2,1)} %bitcast.123), channel_id=1, source_target_pairs={{0,8},{8,16},{16,24},{24,0},{1,9},{9,17},{17,25},{25,1},{2,10},{10... | collective-permute-start | bytes 405512 | tf_op jit(solution)/shard_map/ppermute | solution.py:911
  395.6 55.9 %collective-permute-start.42 = (bf16[96,704]{1,0:T(8,128)(2,1)}, bf16[96,704]{1,0:T(8,128)(2,1)S(1)}, u32[]{:S(2)}, u32[]{:S(2)}) collective-permute-start(bf16[96,704]{1,0:T(8,128)(2,1)} %bitcast.124), channel_id=1, source_target_pairs={{0,16},{8,24},{16,0},{24,8},{1,17},{9,25},{17,1},{25,9},{2,18},{10... | collective-permute-start | bytes 405512 | tf_op jit(solution)/shard_map/ppermute | solution.py:911
  400.2 9.2 %collective-permute-start.31 = (bf16[256,512]{1,0:T(8,128)(2,1)S(1)}, bf16[256,512]{1,0:T(8,128)(2,1)S(1)}, u32[]{:S(2)}, u32[]{:S(2)}) collective-permute-start(bf16[256,512]{1,0:T(8,128)(2,1)S(1)} %get-tuple-element.280), channel_id=1, source_target_pairs={{0,2},{1,3},{2,0},{3,1},{4,6},{5,7},{6,4},{7,5},{8,10},{9,11},{10,... | collective-permute-start | bytes 786440 | tf_op jit(solution)/shard_map/ppermute | solution.py:337
  401.6 13.5 %collective-permute-start.32 = (bf16[256,512]{1,0:T(8,128)(2,1)S(1)}, bf16[256,512]{1,0:T(8,128)(2,1)S(1)}, u32[]{:S(2)}, u32[]{:S(2)}) collective-permute-start(bf16[256,512]{1,0:T(8,128)(2,1)S(1)} %get-tuple-element.279), channel_id=1, source_target_pairs={{0,4},{1,5},{2,6},{3,7},{4,0},{5,1},{6,2},{7,3},{8,12},{9,13},{10,... | collective-permute-start | bytes 786440 | tf_op jit(solution)/shard_map/ppermute | solution.py:337
  402.2 12.9 %collective-permute-start.33 = (bf16[256,512]{1,0:T(8,128)(2,1)S(1)}, bf16[256,512]{1,0:T(8,128)(2,1)S(1)}, u32[]{:S(2)}, u32[]{:S(2)}) collective-permute-start(bf16[256,512]{1,0:T(8,128)(2,1)S(1)} %get-tuple-element.278), channel_id=1, source_target_pairs={{0,6},{1,7},{2,4},{3,5},{4,2},{5,3},{6,0},{7,1},{8,14},{9,15},{10,... | collective-permute-start | bytes 786440 | tf_op jit(solution)/shard_map/ppermute | solution.py:337
  416.0 7.3 %collective-permute-start.34 = (bf16[4,352,256]{2,1,0:T(8,128)(2,1)S(1)}, bf16[4,352,256]{2,1,0:T(8,128)(2,1)S(1)}, u32[]{:S(2)}, u32[]{:S(2)}) collective-permute-start(bf16[4,352,256]{2,1,0:T(8,128)(2,1)S(1)} %get-tuple-element.198), channel_id=1, source_target_pairs={{0,1},{1,0},{2,3},{3,2},{4,5},{5,4},{6,7},{7,6},{8,9},{9,8},{10,11... | collective-permute-start | bytes 2162696 | tf_op jit(solution)/shard_map/ppermute | solution.py:337
  423.5 7.4 %collective-permute-start.35 = (bf16[352,256]{1,0:T(8,128)(2,1)S(1)}, bf16[352,256]{1,0:T(8,128)(2,1)S(1)}, u32[]{:S(2)}, u32[]{:S(2)}) collective-permute-start(bf16[352,256]{1,0:T(8,128)(2,1)S(1)} %get-tuple-element.282), channel_id=1, source_target_pairs={{0,2},{1,3},{2,0},{3,1},{4,6},{5,7},{6,4},{7,5},{8,10},{9,11},{10,... | collective-permute-start | bytes 540680 | tf_op jit(solution)/shard_map/ppermute | solution.py:337
  424.3 10.5 %collective-permute-start.36 = (bf16[352,256]{1,0:T(8,128)(2,1)S(1)}, bf16[352,256]{1,0:T(8,128)(2,1)S(1)}, u32[]{:S(2)}, u32[]{:S(2)}) collective-permute-start(bf16[352,256]{1,0:T(8,128)(2,1)S(1)} %get-tuple-element.284), channel_id=1, source_target_pairs={{0,4},{1,5},{2,6},{3,7},{4,0},{5,1},{6,2},{7,3},{8,12},{9,13},{10,... | collective-permute-start | bytes 540680 | tf_op jit(solution)/shard_map/ppermute | solution.py:337
  425.3 9.5 %collective-permute-start.37 = (bf16[352,256]{1,0:T(8,128)(2,1)S(1)}, bf16[352,256]{1,0:T(8,128)(2,1)S(1)}, u32[]{:S(2)}, u32[]{:S(2)}) collective-permute-start(bf16[352,256]{1,0:T(8,128)(2,1)S(1)} %get-tuple-element.283), channel_id=1, source_target_pairs={{0,6},{1,7},{2,4},{3,5},{4,2},{5,3},{6,0},{7,1},{8,14},{9,15},{10,... | collective-permute-start | bytes 540680 | tf_op jit(solution)/shard_map/ppermute | solution.py:337
  430.9 20.6 %collective-permute-start.43 = (bf16[96,704]{1,0:T(8,128)(2,1)S(1)}, bf16[96,704]{1,0:T(8,128)(2,1)S(1)}, u32[]{:S(2)}, u32[]{:S(2)}) collective-permute-start(bf16[96,704]{1,0:T(8,128)(2,1)S(1)} %bitcast.125), channel_id=1, source_target_pairs={{0,24},{8,0},{16,8},{24,16},{1,25},{9,1},{17,9},{25,17},{2,26},{10... | collective-permute-start | bytes 405512 | tf_op jit(solution)/shard_map/ppermute | solution.py:911
  434.9 9.4 %collective-permute-start.38 = (bf16[352,256]{1,0:T(8,128)(2,1)S(1)}, bf16[352,256]{1,0:T(8,128)(2,1)S(1)}, u32[]{:S(2)}, u32[]{:S(2)}) collective-permute-start(bf16[352,256]{1,0:T(8,128)(2,1)S(1)} %fusion.35.refs_1_), channel_id=1, source_target_pairs={{0,8},{8,16},{16,24},{24,0},{1,9},{9,17},{17,25},{25,1},{2,10},{10... | collective-permute-start | bytes 540680 | tf_op jit(solution)/shard_map/ppermute | solution.py:911
  435.4 15.1 %collective-permute-start.39 = (bf16[352,256]{1,0:T(8,128)(2,1)S(1)}, bf16[352,256]{1,0:T(8,128)(2,1)S(1)}, u32[]{:S(2)}, u32[]{:S(2)}) collective-permute-start(bf16[352,256]{1,0:T(8,128)(2,1)S(1)} %fusion.35.refs_1_), channel_id=1, source_target_pairs={{0,16},{8,24},{16,0},{24,8},{1,17},{9,25},{17,1},{25,9},{2,18},{10... | collective-permute-start | bytes 540680 | tf_op jit(solution)/shard_map/ppermute | solution.py:911
  444.3 7.2 %collective-permute-start.40 = (bf16[352,256]{1,0:T(8,128)(2,1)S(1)}, bf16[352,256]{1,0:T(8,128)(2,1)S(1)}, u32[]{:S(2)}, u32[]{:S(2)}) collective-permute-start(bf16[352,256]{1,0:T(8,128)(2,1)S(1)} %fusion.35.refs_1_), channel_id=1, source_target_pairs={{0,24},{8,0},{16,8},{24,16},{1,25},{9,1},{17,9},{25,17},{2,26},{10... | collective-permute-start | bytes 540680 | tf_op jit(solution)/shard_map/ppermute | solution.py:911
  (123 other events, 1322.9 us)
Sparse Core Ops, SparseCore 0:
  9.9 94.3 all-gather.2
  106.2 81.7 all-gather.4
  349.8 39.2 reduce-scatter.1

commit v8 on v7

--- a/solution.py
+++ b/solution.py
@@ -1072,21 +1072,17 @@
         key_value = lax.all_gather(key_value, "grp", axis=0, tiled=True)
     attended_low, lse = attention_forward(span, query, key_value, bias)
     if paired:
-        attended_low, (sens_near, sens_across, *transfers) = tie(
-            attended_low, (sens_near, sens_across, *transfers)
-        )
-        out_full, (sens_last, *transfers) = tie(
-            out_full, (flip(sens_across, CORE), *steps.send(transfers))
-        )
-        sens_pairs = [(sens, sens_near), (sens_across, sens_last)]
-        transfers = steps.send(transfers)
+        attended_low, (sens_near, *transfers) = tie(attended_low, (sens_near, *transfers))
+        transfers = (sens_across, *steps.send(transfers))
 
     latent_o = (mm(attended_low, out_in) * seen).astype(BF16)
     stream = incoming + (mm(attended_low, out_full) + LOWRANK_FACTOR * mm(latent_o, final))
     scale_two = inverse_rms(stream)
     norm2 = (stream * scale_two * mlp_gain).astype(BF16)
     if paired:
-        norm2, transfers = tie(norm2, transfers)
+        norm2, (sens_across, *transfers) = tie(norm2, transfers)
+        sens_pairs = [(sens, sens_near), (sens_across, flip(sens_across, CORE))]
+        transfers = steps.send(transfers)
         try:
             steps.send(transfers)
         except StopIteration as stop:

time: 468 us -> 458 us (0.979)
  waiting for transfers between devices: 157 us -> 146 us
    ppermute x34, waiting for transfers between devices: 110 us -> 91.6 us  [flip(): return lax.ppermute(array, 'grp', [(i, i ^ mask) for i in range(members)])]
    ppermute x4, waiting for transfers between devices: 9.22 us -> 16.1 us  [flip_group(): return lax.ppermute(array, 'rep', [(i, i ^ 1) for i in range(groups)])]
    unnamed x259 -> x241, local copies, waits for them, and re-layouts: 23.7 us -> 19.1 us
  transfers between devices with their start and end apart: 47 -> 47, of which waited for: 24 -> 22; matrix products, arithmetic and copies ran while one was open for 19% -> 20% of each run, Pallas kernels for 21% -> 22%
where the time goes in v8:
time: 458 us; the launch traced here: 454 us
  waiting for transfers between devices  146 us (32%)
  Pallas kernels  131 us (29%)
  starting transfers between devices  42.2 us (9%)
  matrix products  39.4 us (9%)
  local copies, waits for them, and re-layouts  38.7 us (8%)
  other arithmetic  37.6 us (8%)
  between operations  18.8 us (4%)
    ppermute x34, waiting for transfers between devices, flip(): return lax.ppermute(array, 'grp', [(i, i ^ mask) for i in range(members)])  91.6 us
    pallas_call x2, Pallas kernels, feed_forward_pair(): pl.pallas_call(feed_forward_kernel, out_shape=(jax.ShapeDtypeStruct((coun...  61.9 us
    pallas_call x1, Pallas kernels, attention_backward(): pl.pallas_call(functools.partial(attention_backward_kernel, per_kv), out_...  34.7 us
    ppermute x34, starting transfers between devices, flip(): return lax.ppermute(array, 'grp', [(i, i ^ mask) for i in range(members)])  27.2 us
    all_gather x1, waiting for transfers between devices, shards(): qkv_full = lax.all_gather(qkv_weight, 'grp', axis=1, tiled=True)  24.6 us
    dot_general x15, matrix products, mm(): return jnp.dot(left, right, preferred_element_type=F32)  21.7 us
    unnamed x241, local copies, waits for them, and re-layouts  19.1 us
    pallas_call x1, Pallas kernels, attention_forward(): pl.pallas_call(functools.partial(attention_forward_kernel, steps // KV_HE...  18.5 us
  transfers between devices with their start and end apart: 47, of which 22 were waited for; matrix products, arithmetic and copies ran while one was open for 20% of the time, Pallas kernels for 22%

profile of v8, /device:TPU:0, one launch (start us, length us, event | category | flops | bytes accessed | tf_op | source)
XLA Modules:
  0.0 453.6 jit_solution(18446665745506760160)
XLA Ops:
  8.0 5.2 %constant_dynamic-slice_fusion.2 = (bf16[512,1408]{1,0:T(8,128)(2,1)}, bf16[512,1408]{1,0:T(8,128)(2,1)}, bf16[512,1408]{1,0:T(8,128)(2,1)}, bf16[512,1408]{1,0:T(8,128)(2,1)}) fusion(bf16[2048,1408]{1,0:T(8,128)(2,1)} %param.34, s32[]{:T(128)S(6)} %select_n.259, s32[]{:T(128)S(6)} %select_n.231, s32[]{:T(128)S(6)} %select_n.230, s32[]{:T(128)S(6)} %select_n.258), kind=kLoop, calls=%fused_computation.190 | loop fusion | bytes 11534352 | tf_op jit(solution)/shard_map/dynamic_slice | solution.py:351
  13.2 3.0 collective-permute-start
  16.2 3.3 dynamic-slice_bitcast_fusion
  22.5 2.0 fusion.89
  46.2 3.2 and_select_fusion.bias_ref
  49.3 3.5 collective-permute-done.1
  52.9 21.5 %collective-permute-done.3 = bf16[1408,256]{1,0:T(8,128)(2,1)} collective-permute-done((bf16[1408,256]{1,0:T(8,128)(2,1)}, bf16[1408,256]{1,0:T(8,128)(2,1)}, u32[]{:S(2)}, u32[]{:S(2)}) %collective-permute-start.3) | collective-permute-done | bytes 720928 | tf_op jit(solution)/shard_map/ppermute | solution.py:337
  76.7 3.0 pad_maximum_fusion.refs_8_.refs_2_
  79.7 24.6 %all-gather.3.cloned.1.call-done = bf16[2048,2560]{0,1:T(8,128)(2,1)} async-done(((bf16[2048,320]{0,1:T(8,128)(2,1)}), bf16[2048,2560]{0,1:T(8,128)(2,1)}) %all-gather.3.cloned.1.call-update) | async-done | bytes 10485776 | tf_op jit(solution)/shard_map/all_gather | solution.py:957
  104.3 5.6 %fusion.112 = f32[256,2560]{1,0:T(8,128)S(1)} fusion(bf16[256,2048]{1,0:T(8,128)(2,1)S(1)} %fusion.12.norm1_ref.refs_10_, bf16[2048,2560]{0,1:T(8,128)(2,1)} %all-gather.3.cloned.1.call-done), kind=kOutput, calls=%fused_computation.259 | convolution fusion | flops 2684354560 | bytes 14155776 | tf_op jit(solution)/shard_map/dot_general | solution.py:26
  111.0 11.1 %collective-permute-done.4.refs_5_ = bf16[512,1408]{1,0:T(8,128)(2,1)} collective-permute-done((bf16[512,1408]{1,0:T(8,128)(2,1)}, bf16[512,1408]{1,0:T(8,128)(2,1)}, u32[]{:S(2)}, u32[]{:S(2)}) %collective-permute-start.4) | collective-permute-done | bytes 1441824 | tf_op jit(solution)/shard_map/ppermute | solution.py:337
  123.8 2.5 collective-permute-start.9
  127.5 9.2 %collective-permute-done.7 = bf16[256,512]{1,0:T(8,128)(2,1)S(1)} collective-permute-done((bf16[256,512]{1,0:T(8,128)(2,1)S(1)}, bf16[256,512]{1,0:T(8,128)(2,1)S(1)}, u32[]{:S(2)}, u32[]{:S(2)}) %collective-permute-start.7) | collective-permute-done | bytes 262176 | tf_op jit(solution)/shard_map/ppermute | solution.py:337
  139.4 6.5 %collective-permute-done.11 = bf16[256,512]{1,0:T(8,128)(2,1)S(1)} collective-permute-done((bf16[256,512]{1,0:T(8,128)(2,1)S(1)}, bf16[256,512]{1,0:T(8,128)(2,1)S(1)}, u32[]{:S(2)}, u32[]{:S(2)}) %collective-permute-start.11) | collective-permute-done | bytes 262176 | tf_op jit(solution)/shard_map/ppermute | solution.py:337
  147.8 1.9 collective-permute-start.15
  152.9 2.7 fusion.27.q_ref
  156.8 18.5 %attention_forward.1 = (bf16[256,2048]{1,0:T(8,128)(2,1)S(1)}, f32[16,2,256]{2,1,0:T(2,128)S(1)}) custom-call(s32[3]{0:T(128)S(1)} %pad_add_fusion.span, bf16[256,2048]{1,0:T(8,128)(2,1)S(1)} %fusion.27.q_ref, bf16[2048,512]{1,0:T(8,128)(2,1)S(1)} %constant_dynamic-update-slice_fusion.key_ref.value_ref, ...), custom_call_target="tpu_custom_call" | custom-call | flops 4294967296 | bytes 18874368 | tf_op jit(solution)/shard_map/attention_forward/pallas_call | solution.py:149
  176.0 8.9 %collective-permute-done.14.refs_9_.refs_3_ = bf16[1,1408,256]{2,1,0:T(8,128)(2,1)} collective-permute-done((bf16[1,1408,256]{2,1,0:T(8,128)(2,1)S(1)}, bf16[1,1408,256]{2,1,0:T(8,128)(2,1)}, u32[]{:S(2)}, u32[]{:S(2)}) %collective-permute-start.14) | collective-permute-done | bytes 720928 | tf_op jit(solution)/shard_map/ppermute | solution.py:337
  187.4 1.8 convolution_multiply_fusion.1
  189.9 6.8 %multiply_reduce_fusion.1 = (f32[256]{0:T(256)S(1)}, f32[256,2048]{1,0:T(8,128)S(1)}) fusion(f32[256,2048]{1,0:T(8,128)} %convolution_multiply_fusion.1, bf16[256,2048]{1,0:T(8,128)(2,1)S(1)} %get-tuple-element.129.o_ref.attended_ref, bf16[2048,2048]{1,0:T(8,128)(2,1)} %all-gather.5.cloned.1.call-done, bf16[256,2048]{1,0:T(8,128)(2,1)} %param.25), kind=kOutput, calls=%fused_computation.57 | convolution fusion | flops 2150104832 | bytes 14681088 | tf_op jit(solution)/shard_map/dot_general | solution.py:26
  197.5 5.6 %collective-permute-done.17.refs_10_.refs_4_ = bf16[1,1408,256]{2,1,0:T(8,128)(2,1)} collective-permute-done((bf16[1,1408,256]{2,1,0:T(8,128)(2,1)}, bf16[1,1408,256]{2,1,0:T(8,128)(2,1)}, u32[]{:S(2)}, u32[]{:S(2)}) %collective-permute-start.17) | collective-permute-done | bytes 720928 | tf_op jit(solution)/shard_map/ppermute | solution.py:337
  203.8 1.9 concatenate.64.own_x
  208.5 16.0 %collective-permute-done.20.refs_12_.refs_6_ = bf16[1,1408,256]{2,1,0:T(8,128)(2,1)} collective-permute-done((bf16[1,1408,256]{2,1,0:T(8,128)(2,1)}, bf16[1,1408,256]{2,1,0:T(8,128)(2,1)}, u32[]{:S(2)}, u32[]{:S(2)}) %collective-permute-start.20) | collective-permute-done | bytes 720928 | tf_op jit(solution)/shard_map/ppermute | solution.py:342
  225.4 31.1 %feed_forward.2 = (f32[256,2176]{1,0:T(8,128)}, bf16[256,2176]{1,0:T(8,128)(2,1)}, bf16[512,1408]{1,0:T(8,128)(2,1)}, f32[96,1408]{1,0:T(8,128)S(1)}) custom-call(s32[3]{0:T(128)S(1)} %pad_add_fusion.1.meta, bf16[256,2176]{1,0:T(8,128)(2,1)} %concatenate.64.own_x, bf16[256,2176]{1,0:T(8,128)(2,1)} %collective-permute-done.19.near_x, ...), custom_call_target="tpu_custom_call" | custom-call | flops 14763950080 | bytes 38273024 | tf_op jit(solution)/shard_map/feed_forward/pallas_call | solution.py:637
  257.2 4.0 collective-permute-done.24.near_g
  263.1 30.8 %feed_forward.3 = (f32[256,2176]{1,0:T(8,128)}, bf16[256,2176]{1,0:T(8,128)(2,1)}, bf16[512,1408]{1,0:T(8,128)(2,1)}, f32[96,1408]{1,0:T(8,128)S(1)}) custom-call(s32[3]{0:T(128)S(1)} %pad_add_fusion.1.meta, bf16[256,2176]{1,0:T(8,128)(2,1)} %copy-done.106, bf16[256,2176]{1,0:T(8,128)(2,1)} %copy-done.107, bf16[256,2048]{1,0:T(8,128)(2,1)} %collective-permute-done.16.own_g, ...), custom_call_target="tpu_custom_call" | custom-call | flops 14763950080 | bytes 38273024 | tf_op jit(solution)/shard_map/feed_forward/pallas_call | solution.py:637
  295.2 2.6 collective-permute-done.25
  297.8 3.2 add_convert_fusion
  304.9 1.8 copy-done.3
  309.5 11.6 %down_projection.1 = (f32[256,2048]{1,0:T(8,128)S(1)}, bf16[256,2048]{1,0:T(8,128)(2,1)S(1)}, bf16[256,2048]{1,0:T(8,128)(2,1)S(1)}, bf16[256,2048]{1,0:T(8,128)(2,1)}) custom-call(s32[3]{0:T(128)S(1)} %pad_add_fusion.1.meta, bf16[512,1408]{1,0:T(8,128)(2,1)S(1)} %copy-done.50, bf16[512,1408]{1,0:T(8,128)(2,1)S(1)} %copy-done.51, ...), custom_call_target="tpu_custom_call" | custom-call | flops 5905580032 | bytes 14155776 | tf_op jit(solution)/shard_map/down_projection/pallas_call | solution.py:611
  321.1 6.8 %collective-permute-done.26 = bf16[256,2176]{1,0:T(8,128)(2,1)} collective-permute-done((bf16[256,2176]{1,0:T(8,128)(2,1)}, bf16[256,2176]{1,0:T(8,128)(2,1)}, u32[]{:S(2)}, u32[]{:S(2)}) %collective-permute-start.26) | collective-permute-done | bytes 1114144 | tf_op jit(solution)/shard_map/ppermute | solution.py:337
  327.9 2.0 convert_add_fusion.1
  332.9 2.1 fusion.105
  335.5 2.4 fusion.113
  339.4 3.1 add_convert_fusion.3
  344.9 34.7 %attention_backward.1 = (bf16[256,2048]{1,0:T(8,128)(2,1)S(1)}, bf16[4,256,512]{2,1,0:T(8,128)(2,1)S(1)}, bf16[4,256,512]{2,1,0:T(8,128)(2,1)S(1)}) custom-call(s32[3]{0:T(128)S(1)} %pad_add_fusion.span, bf16[256,2048]{1,0:T(8,128)(2,1)S(1)} %copy-done.16, bf16[256,2048]{1,0:T(8,128)(2,1)S(1)} %copy-done.19, bf16[256,2048]{1,0:T(8,128)(2,1)S(1)} %copy-done.21, ...), custom_call_target="tpu_custom_call" | custom-call | flops 10737418240 | bytes 13631488 | tf_op jit(solution)/shard_map/attention_backward/pallas_call | solution.py:294
  386.0 2.5 collective-permute-start.42
  388.5 2.0 add_convert_fusion.1
  392.1 2.1 collective-permute-start.33
  394.2 3.2 add_convert_fusion.2
  397.5 2.0 early_gradients.1
  399.8 5.0 %collective-permute-done.32.refs_2_ = bf16[256,512]{1,0:T(8,128)(2,1)S(1)} collective-permute-done((bf16[256,512]{1,0:T(8,128)(2,1)S(1)}, bf16[256,512]{1,0:T(8,128)(2,1)S(1)}, u32[]{:S(2)}, u32[]{:S(2)}) %collective-permute-start.32) | collective-permute-done | bytes 262176 | tf_op jit(solution)/shard_map/ppermute | solution.py:337
  405.8 5.8 %fusion = f32[256,2048]{1,0:T(8,128)S(1)} fusion(bf16[256,2048]{1,0:T(8,128)(2,1)S(1)} %copy-done.24, bf16[2048,2560]{0,1:T(8,128)(2,1)} %all-gather.3.cloned.1.call-done), kind=kOutput, calls=%fused_computation | convolution fusion | flops 2147483648 | bytes 11534336 | tf_op jit(solution)/shard_map/dot_general | solution.py:30
  416.8 2.8 fusion.17
  420.6 2.0 collective-permute-start.43
  422.6 2.5 collective-permute-done.36
  427.6 7.1 %collective-permute-done.38.refs_2_ = bf16[352,256]{1,0:T(8,128)(2,1)S(1)} collective-permute-done((bf16[352,256]{1,0:T(8,128)(2,1)S(1)}, bf16[352,256]{1,0:T(8,128)(2,1)S(1)}, u32[]{:S(2)}, u32[]{:S(2)}) %collective-permute-start.38) | collective-permute-done | bytes 180256 | tf_op jit(solution)/shard_map/ppermute | solution.py:911
  436.2 4.4 collective-permute-done.39.refs_3_
  (415 shorter events, 89.6 us)
Async XLA Ops:
  7.2 97.1 %all-gather.3.cloned.1.call-start = ((), (), s32[]{:S(2)}) async-start(), calls=%async_computation.1 | async-start | bytes 11796480 | tf_op jit(solution)/shard_map/all_gather | solution.py:957
  7.9 181.9 %all-gather.5.cloned.1.call-start = ((), (), s32[]{:S(2)}) async-start(), calls=%async_computation.2 | async-start | bytes 9437184 | tf_op jit(solution)/shard_map/all_gather | solution.py:1047
  13.2 61.2 %collective-permute-start = (bf16[512,1408]{1,0:T(8,128)(2,1)}, bf16[512,1408]{1,0:T(8,128)(2,1)}, u32[]{:S(2)}, u32[]{:S(2)}) collective-permute-start(bf16[512,1408]{1,0:T(8,128)(2,1)} %get-tuple-element.260.refs_0_), channel_id=1, source_target_pairs={{0,4},{1,5},{2,6},{3,7},{4,0},{5,1},{6,2},{7,3},{8,12},{9,13},{10,... | collective-permute-start | bytes 4325384 | tf_op jit(solution)/shard_map/ppermute | solution.py:337
  19.4 33.4 %collective-permute-start.1 = (bf16[1408,256]{1,0:T(8,128)(2,1)}, bf16[1408,256]{1,0:T(8,128)(2,1)}, u32[]{:S(2)}, u32[]{:S(2)}) collective-permute-start(bf16[1408,256]{1,0:T(8,128)(2,1)} %get-tuple-element.266), channel_id=1, source_target_pairs={{0,2},{1,3},{2,0},{3,1},{4,6},{5,7},{6,4},{7,5},{8,10},{9,11},{10,... | collective-permute-start | bytes 2162696 | tf_op jit(solution)/shard_map/ppermute | solution.py:337
  20.9 31.9 %collective-permute-start.2 = (bf16[1408,256]{1,0:T(8,128)(2,1)}, bf16[1408,256]{1,0:T(8,128)(2,1)}, u32[]{:S(2)}, u32[]{:S(2)}) collective-permute-start(bf16[1408,256]{1,0:T(8,128)(2,1)} %get-tuple-element.265), channel_id=1, source_target_pairs={{0,1},{1,0},{2,3},{3,2},{4,5},{5,4},{6,7},{7,6},{8,9},{9,8},{10,11... | collective-permute-start | bytes 2162696 | tf_op jit(solution)/shard_map/ppermute | solution.py:337
  20.9 53.4 %collective-permute-start.3 = (bf16[1408,256]{1,0:T(8,128)(2,1)}, bf16[1408,256]{1,0:T(8,128)(2,1)}, u32[]{:S(2)}, u32[]{:S(2)}) collective-permute-start(bf16[1408,256]{1,0:T(8,128)(2,1)} %get-tuple-element.267), channel_id=1, source_target_pairs={{0,3},{1,2},{2,1},{3,0},{4,7},{5,6},{6,5},{7,4},{8,11},{9,10},{10,... | collective-permute-start | bytes 2162696 | tf_op jit(solution)/shard_map/ppermute | solution.py:337
  21.6 360.9 %reduce-scatter.2.cloned.1.call-start = ((), (), s32[]{:S(2)}) async-start(), calls=%async_computation.3 | async-start | bytes 1327104 | tf_op jit(solution)/shard_map/reduce_scatter | solution.py:1103
  43.2 83.1 %copy-start.11 = (bf16[32,2048]{1,0:T(8,128)(2,1)}, bf16[32,2048]{1,0:T(8,128)(2,1)S(1)}, u32[]{:S(2)}) copy-start(bf16[32,2048]{1,0:T(8,128)(2,1)S(1)} %convolution_convert_fusion.8.asking_ref) | copy-start | bytes 393220
  74.4 47.7 %collective-permute-start.4 = (bf16[512,1408]{1,0:T(8,128)(2,1)}, bf16[512,1408]{1,0:T(8,128)(2,1)}, u32[]{:S(2)}, u32[]{:S(2)}) collective-permute-start(bf16[512,1408]{1,0:T(8,128)(2,1)} %get-tuple-element.115.refs_1_), channel_id=1, source_target_pairs={{0,4},{1,5},{2,6},{3,7},{4,0},{5,1},{6,2},{7,3},{8,12},{9,13},{10,... | collective-permute-start | bytes 4325384 | tf_op jit(solution)/shard_map/ppermute | solution.py:337
  74.6 47.5 %collective-permute-start.5 = (bf16[512,1408]{1,0:T(8,128)(2,1)}, bf16[512,1408]{1,0:T(8,128)(2,1)}, u32[]{:S(2)}, u32[]{:S(2)}) collective-permute-start(bf16[512,1408]{1,0:T(8,128)(2,1)} %collective-permute-done.refs_4_), channel_id=1, source_target_pairs={{0,8},{8,0},{16,24},{24,16},{1,9},{9,1},{17,25},{25,17},{2,10},{10... | collective-permute-start | bytes 4325384 | tf_op jit(solution)/shard_map/ppermute | solution.py:342
  122.1 17.3 %collective-permute-start.6 = (bf16[256,512]{1,0:T(8,128)(2,1)S(1)}, bf16[256,512]{1,0:T(8,128)(2,1)S(1)}, u32[]{:S(2)}, u32[]{:S(2)}) collective-permute-start(bf16[256,512]{1,0:T(8,128)(2,1)S(1)} %pad_maximum_fusion.2), channel_id=1, source_target_pairs={{0,1},{1,0},{2,3},{3,2},{4,5},{5,4},{6,7},{7,6},{8,9},{9,8},{10,11... | collective-permute-start | bytes 786440 | tf_op jit(solution)/shard_map/ppermute | solution.py:337
  122.1 14.6 %collective-permute-start.7 = (bf16[256,512]{1,0:T(8,128)(2,1)S(1)}, bf16[256,512]{1,0:T(8,128)(2,1)S(1)}, u32[]{:S(2)}, u32[]{:S(2)}) collective-permute-start(bf16[256,512]{1,0:T(8,128)(2,1)S(1)} %pad_maximum_fusion.2), channel_id=1, source_target_pairs={{0,2},{1,3},{2,0},{3,1},{4,6},{5,7},{6,4},{7,5},{8,10},{9,11},{10,... | collective-permute-start | bytes 786440 | tf_op jit(solution)/shard_map/ppermute | solution.py:337
  123.8 14.0 %collective-permute-start.9 = (bf16[256,512]{1,0:T(8,128)(2,1)S(1)}, bf16[256,512]{1,0:T(8,128)(2,1)S(1)}, u32[]{:S(2)}, u32[]{:S(2)}) collective-permute-start(bf16[256,512]{1,0:T(8,128)(2,1)S(1)} %pad_maximum_fusion.2), channel_id=1, source_target_pairs={{0,4},{1,5},{2,6},{3,7},{4,0},{5,1},{6,2},{7,3},{8,12},{9,13},{10,... | collective-permute-start | bytes 786440 | tf_op jit(solution)/shard_map/ppermute | solution.py:337
  136.7 9.2 %collective-permute-start.8 = (bf16[256,512]{1,0:T(8,128)(2,1)S(1)}, bf16[256,512]{1,0:T(8,128)(2,1)S(1)}, u32[]{:S(2)}, u32[]{:S(2)}) collective-permute-start(bf16[256,512]{1,0:T(8,128)(2,1)S(1)} %collective-permute-done.7), channel_id=1, source_target_pairs={{0,1},{1,0},{2,3},{3,2},{4,5},{5,4},{6,7},{7,6},{8,9},{9,8},{10,11... | collective-permute-start | bytes 786440 | tf_op jit(solution)/shard_map/ppermute | solution.py:337
  137.8 8.0 %collective-permute-start.11 = (bf16[256,512]{1,0:T(8,128)(2,1)S(1)}, bf16[256,512]{1,0:T(8,128)(2,1)S(1)}, u32[]{:S(2)}, u32[]{:S(2)}) collective-permute-start(bf16[256,512]{1,0:T(8,128)(2,1)S(1)} %collective-permute-done.9), channel_id=1, source_target_pairs={{0,2},{1,3},{2,0},{3,1},{4,6},{5,7},{6,4},{7,5},{8,10},{9,11},{10,... | collective-permute-start | bytes 786440 | tf_op jit(solution)/shard_map/ppermute | solution.py:337
  139.2 6.7 %collective-permute-start.10 = (bf16[256,512]{1,0:T(8,128)(2,1)S(1)}, bf16[256,512]{1,0:T(8,128)(2,1)S(1)}, u32[]{:S(2)}, u32[]{:S(2)}) collective-permute-start(bf16[256,512]{1,0:T(8,128)(2,1)S(1)} %collective-permute-done.9), channel_id=1, source_target_pairs={{0,1},{1,0},{2,3},{3,2},{4,5},{5,4},{6,7},{7,6},{8,9},{9,8},{10,11... | collective-permute-start | bytes 786440 | tf_op jit(solution)/shard_map/ppermute | solution.py:337
  145.9 1.9 collective-permute-start.12
  147.8 37.1 %collective-permute-start.15 = (bf16[512,1408]{1,0:T(8,128)(2,1)}, bf16[512,1408]{1,0:T(8,128)(2,1)S(1)}, u32[]{:S(2)}, u32[]{:S(2)}) collective-permute-start(bf16[512,1408]{1,0:T(8,128)(2,1)} %collective-permute-done.4.refs_5_), channel_id=1, source_target_pairs={{0,8},{8,0},{16,24},{24,16},{1,9},{9,1},{17,25},{25,17},{2,10},{10... | collective-permute-start | bytes 4325384 | tf_op jit(solution)/shard_map/ppermute | solution.py:342
  149.8 35.1 %collective-permute-start.13 = (bf16[256,2048]{1,0:T(8,128)(2,1)S(1)}, bf16[256,2048]{1,0:T(8,128)(2,1)S(1)}, u32[]{:S(2)}, u32[]{:S(2)}) collective-permute-start(bf16[256,2048]{1,0:T(8,128)(2,1)S(1)} %copy-done.4), channel_id=1, source_target_pairs={{0,1},{1,0},{2,3},{3,2},{4,5},{5,4},{6,7},{7,6},{8,9},{9,8},{10,11... | collective-permute-start | bytes 3145736 | tf_op jit(solution)/shard_map/ppermute | solution.py:337
  150.8 34.1 %collective-permute-start.14 = (bf16[1,1408,256]{2,1,0:T(8,128)(2,1)S(1)}, bf16[1,1408,256]{2,1,0:T(8,128)(2,1)}, u32[]{:S(2)}, u32[]{:S(2)}) collective-permute-start(bf16[1,1408,256]{2,1,0:T(8,128)(2,1)S(1)} %get-tuple-element.263), channel_id=1, source_target_pairs={{0,4},{1,5},{2,6},{3,7},{4,0},{5,1},{6,2},{7,3},{8,12},{9,13},{10,... | collective-permute-start | bytes 2162696 | tf_op jit(solution)/shard_map/ppermute | solution.py:337
  155.7 41.8 %collective-permute-start.16 = (bf16[256,2048]{1,0:T(8,128)(2,1)S(1)}, bf16[256,2048]{1,0:T(8,128)(2,1)}, u32[]{:S(2)}, u32[]{:S(2)}) collective-permute-start(bf16[256,2048]{1,0:T(8,128)(2,1)S(1)} %copy-done.4), channel_id=1, source_target_pairs={{0,2},{1,3},{2,0},{3,1},{4,6},{5,7},{6,4},{7,5},{8,10},{9,11},{10,... | collective-permute-start | bytes 3145736 | tf_op jit(solution)/shard_map/ppermute | solution.py:337
  184.9 18.3 %collective-permute-start.17 = (bf16[1,1408,256]{2,1,0:T(8,128)(2,1)}, bf16[1,1408,256]{2,1,0:T(8,128)(2,1)}, u32[]{:S(2)}, u32[]{:S(2)}) collective-permute-start(bf16[1,1408,256]{2,1,0:T(8,128)(2,1)} %get-tuple-element.132), channel_id=1, source_target_pairs={{0,4},{1,5},{2,6},{3,7},{4,0},{5,1},{6,2},{7,3},{8,12},{9,13},{10,... | collective-permute-start | bytes 2162696 | tf_op jit(solution)/shard_map/ppermute | solution.py:337
  185.3 18.0 %collective-permute-start.18 = (bf16[1,1408,256]{2,1,0:T(8,128)(2,1)}, bf16[1,1408,256]{2,1,0:T(8,128)(2,1)}, u32[]{:S(2)}, u32[]{:S(2)}) collective-permute-start(bf16[1,1408,256]{2,1,0:T(8,128)(2,1)} %collective-permute-done.14.refs_9_.refs_3_), channel_id=1, source_target_pairs={{0,8},{8,0},{16,24},{24,16},{1,9},{9,1},{17,25},{25,17},{2,10},{10... | collective-permute-start | bytes 2162696 | tf_op jit(solution)/shard_map/ppermute | solution.py:342
  205.7 18.9 %collective-permute-start.19 = (bf16[256,2176]{1,0:T(8,128)(2,1)}, bf16[256,2176]{1,0:T(8,128)(2,1)}, u32[]{:S(2)}, u32[]{:S(2)}) collective-permute-start(bf16[256,2176]{1,0:T(8,128)(2,1)} %concatenate.64.own_x), channel_id=1, source_target_pairs={{0,1},{1,0},{2,3},{3,2},{4,5},{5,4},{6,7},{7,6},{8,9},{9,8},{10,11... | collective-permute-start | bytes 3342344 | tf_op jit(solution)/shard_map/ppermute | solution.py:337
  205.7 18.9 %collective-permute-start.20 = (bf16[1,1408,256]{2,1,0:T(8,128)(2,1)}, bf16[1,1408,256]{2,1,0:T(8,128)(2,1)}, u32[]{:S(2)}, u32[]{:S(2)}) collective-permute-start(bf16[1,1408,256]{2,1,0:T(8,128)(2,1)} %collective-permute-done.17.refs_10_.refs_4_), channel_id=1, source_target_pairs={{0,8},{8,0},{16,24},{24,16},{1,9},{9,1},{17,25},{25,17},{2,10},{10... | collective-permute-start | bytes 2162696 | tf_op jit(solution)/shard_map/ppermute | solution.py:342
  207.3 49.3 %collective-permute-start.21 = (bf16[256,2176]{1,0:T(8,128)(2,1)}, bf16[256,2176]{1,0:T(8,128)(2,1)S(1)}, u32[]{:S(2)}, u32[]{:S(2)}) collective-permute-start(bf16[256,2176]{1,0:T(8,128)(2,1)} %concatenate.64.own_x), channel_id=1, source_target_pairs={{0,2},{1,3},{2,0},{3,1},{4,6},{5,7},{6,4},{7,5},{8,10},{9,11},{10,... | collective-permute-start | bytes 3342344 | tf_op jit(solution)/shard_map/ppermute | solution.py:337
  256.6 4.5 collective-permute-start.23
  256.7 4.5 collective-permute-start.24
  294.7 3.1 collective-permute-start.25
  294.8 33.1 %collective-permute-start.22 = (bf16[256,2176]{1,0:T(8,128)(2,1)}, bf16[256,2176]{1,0:T(8,128)(2,1)}, u32[]{:S(2)}, u32[]{:S(2)}) collective-permute-start(bf16[256,2176]{1,0:T(8,128)(2,1)} %get-tuple-element.148), channel_id=1, source_target_pairs={{0,1},{1,0},{2,3},{3,2},{4,5},{5,4},{6,7},{7,6},{8,9},{9,8},{10,11... | collective-permute-start | bytes 3342344 | tf_op jit(solution)/shard_map/ppermute | solution.py:337
  301.0 26.9 %collective-permute-start.26 = (bf16[256,2176]{1,0:T(8,128)(2,1)}, bf16[256,2176]{1,0:T(8,128)(2,1)}, u32[]{:S(2)}, u32[]{:S(2)}) collective-permute-start(bf16[256,2176]{1,0:T(8,128)(2,1)} %add_convert_fusion), channel_id=1, source_target_pairs={{0,2},{1,3},{2,0},{3,1},{4,6},{5,7},{6,4},{7,5},{8,10},{9,11},{10,... | collective-permute-start | bytes 3342344 | tf_op jit(solution)/shard_map/ppermute | solution.py:337
  331.5 7.9 %collective-permute-start.28 = (bf16[256,2048]{1,0:T(8,128)(2,1)}, bf16[256,2048]{1,0:T(8,128)(2,1)}, u32[]{:S(2)}, u32[]{:S(2)}) collective-permute-start(bf16[256,2048]{1,0:T(8,128)(2,1)} %get-tuple-element.177), channel_id=1, source_target_pairs={{0,1},{1,0},{2,3},{3,2},{4,5},{5,4},{6,7},{7,6},{8,9},{9,8},{10,11... | collective-permute-start | bytes 3145736 | tf_op jit(solution)/shard_map/ppermute | solution.py:337
  339.3 43.2 %collective-permute-start.27 = (bf16[256,2048]{1,0:T(8,128)(2,1)}, bf16[256,2048]{1,0:T(8,128)(2,1)}, u32[]{:S(2)}, u32[]{:S(2)}) collective-permute-start(bf16[256,2048]{1,0:T(8,128)(2,1)} %copy-done.48), channel_id=1, source_target_pairs={{0,1},{1,0},{2,3},{3,2},{4,5},{5,4},{6,7},{7,6},{8,9},{9,8},{10,11... | collective-permute-start | bytes 3145736 | tf_op jit(solution)/shard_map/ppermute | solution.py:337
  342.5 40.1 %collective-permute-start.29 = (bf16[256,2048]{1,0:T(8,128)(2,1)}, bf16[256,2048]{1,0:T(8,128)(2,1)}, u32[]{:S(2)}, u32[]{:S(2)}) collective-permute-start(bf16[256,2048]{1,0:T(8,128)(2,1)} %add_convert_fusion.3), channel_id=1, source_target_pairs={{0,2},{1,3},{2,0},{3,1},{4,6},{5,7},{6,4},{7,5},{8,10},{9,11},{10,... | collective-permute-start | bytes 3145736 | tf_op jit(solution)/shard_map/ppermute | solution.py:337
  382.6 5.9 %collective-permute-start.30 = (bf16[4,256,512]{2,1,0:T(8,128)(2,1)}, bf16[4,256,512]{2,1,0:T(8,128)(2,1)}, u32[]{:S(2)}, u32[]{:S(2)}) collective-permute-start(bf16[4,256,512]{2,1,0:T(8,128)(2,1)} %copy-done.49), channel_id=1, source_target_pairs={{0,1},{1,0},{2,3},{3,2},{4,5},{5,4},{6,7},{7,6},{8,9},{9,8},{10,11... | collective-permute-start | bytes 3145736 | tf_op jit(solution)/shard_map/ppermute | solution.py:337
  384.6 57.4 %collective-permute-start.41 = (bf16[96,704]{1,0:T(8,128)(2,1)}, bf16[96,704]{1,0:T(8,128)(2,1)S(1)}, u32[]{:S(2)}, u32[]{:S(2)}) collective-permute-start(bf16[96,704]{1,0:T(8,128)(2,1)} %bitcast.123), channel_id=1, source_target_pairs={{0,8},{8,16},{16,24},{24,0},{1,9},{9,17},{17,25},{25,1},{2,10},{10... | collective-permute-start | bytes 405512 | tf_op jit(solution)/shard_map/ppermute | solution.py:911
  386.0 56.1 %collective-permute-start.42 = (bf16[96,704]{1,0:T(8,128)(2,1)}, bf16[96,704]{1,0:T(8,128)(2,1)S(1)}, u32[]{:S(2)}, u32[]{:S(2)}) collective-permute-start(bf16[96,704]{1,0:T(8,128)(2,1)} %bitcast.124), channel_id=1, source_target_pairs={{0,16},{8,24},{16,0},{24,8},{1,17},{9,25},{17,1},{25,9},{2,18},{10... | collective-permute-start | bytes 405512 | tf_op jit(solution)/shard_map/ppermute | solution.py:911
  390.6 9.3 %collective-permute-start.31 = (bf16[256,512]{1,0:T(8,128)(2,1)S(1)}, bf16[256,512]{1,0:T(8,128)(2,1)S(1)}, u32[]{:S(2)}, u32[]{:S(2)}) collective-permute-start(bf16[256,512]{1,0:T(8,128)(2,1)S(1)} %get-tuple-element.274), channel_id=1, source_target_pairs={{0,2},{1,3},{2,0},{3,1},{4,6},{5,7},{6,4},{7,5},{8,10},{9,11},{10,... | collective-permute-start | bytes 786440 | tf_op jit(solution)/shard_map/ppermute | solution.py:337
  391.3 13.5 %collective-permute-start.32 = (bf16[256,512]{1,0:T(8,128)(2,1)S(1)}, bf16[256,512]{1,0:T(8,128)(2,1)S(1)}, u32[]{:S(2)}, u32[]{:S(2)}) collective-permute-start(bf16[256,512]{1,0:T(8,128)(2,1)S(1)} %get-tuple-element.273), channel_id=1, source_target_pairs={{0,4},{1,5},{2,6},{3,7},{4,0},{5,1},{6,2},{7,3},{8,12},{9,13},{10,... | collective-permute-start | bytes 786440 | tf_op jit(solution)/shard_map/ppermute | solution.py:337
  392.1 12.7 %collective-permute-start.33 = (bf16[256,512]{1,0:T(8,128)(2,1)S(1)}, bf16[256,512]{1,0:T(8,128)(2,1)S(1)}, u32[]{:S(2)}, u32[]{:S(2)}) collective-permute-start(bf16[256,512]{1,0:T(8,128)(2,1)S(1)} %get-tuple-element.272), channel_id=1, source_target_pairs={{0,6},{1,7},{2,4},{3,5},{4,2},{5,3},{6,0},{7,1},{8,14},{9,15},{10,... | collective-permute-start | bytes 786440 | tf_op jit(solution)/shard_map/ppermute | solution.py:337
  405.7 7.3 %collective-permute-start.34 = (bf16[4,352,256]{2,1,0:T(8,128)(2,1)S(1)}, bf16[4,352,256]{2,1,0:T(8,128)(2,1)S(1)}, u32[]{:S(2)}, u32[]{:S(2)}) collective-permute-start(bf16[4,352,256]{2,1,0:T(8,128)(2,1)S(1)} %get-tuple-element.192), channel_id=1, source_target_pairs={{0,1},{1,0},{2,3},{3,2},{4,5},{5,4},{6,7},{7,6},{8,9},{9,8},{10,11... | collective-permute-start | bytes 2162696 | tf_op jit(solution)/shard_map/ppermute | solution.py:337
  413.2 7.4 %collective-permute-start.35 = (bf16[352,256]{1,0:T(8,128)(2,1)S(1)}, bf16[352,256]{1,0:T(8,128)(2,1)S(1)}, u32[]{:S(2)}, u32[]{:S(2)}) collective-permute-start(bf16[352,256]{1,0:T(8,128)(2,1)S(1)} %get-tuple-element.276), channel_id=1, source_target_pairs={{0,2},{1,3},{2,0},{3,1},{4,6},{5,7},{6,4},{7,5},{8,10},{9,11},{10,... | collective-permute-start | bytes 540680 | tf_op jit(solution)/shard_map/ppermute | solution.py:337
  414.6 10.5 %collective-permute-start.36 = (bf16[352,256]{1,0:T(8,128)(2,1)S(1)}, bf16[352,256]{1,0:T(8,128)(2,1)S(1)}, u32[]{:S(2)}, u32[]{:S(2)}) collective-permute-start(bf16[352,256]{1,0:T(8,128)(2,1)S(1)} %get-tuple-element.278), channel_id=1, source_target_pairs={{0,4},{1,5},{2,6},{3,7},{4,0},{5,1},{6,2},{7,3},{8,12},{9,13},{10,... | collective-permute-start | bytes 540680 | tf_op jit(solution)/shard_map/ppermute | solution.py:337
  415.0 10.1 %collective-permute-start.37 = (bf16[352,256]{1,0:T(8,128)(2,1)S(1)}, bf16[352,256]{1,0:T(8,128)(2,1)S(1)}, u32[]{:S(2)}, u32[]{:S(2)}) collective-permute-start(bf16[352,256]{1,0:T(8,128)(2,1)S(1)} %get-tuple-element.277), channel_id=1, source_target_pairs={{0,6},{1,7},{2,4},{3,5},{4,2},{5,3},{6,0},{7,1},{8,14},{9,15},{10,... | collective-permute-start | bytes 540680 | tf_op jit(solution)/shard_map/ppermute | solution.py:337
  420.6 21.5 %collective-permute-start.43 = (bf16[96,704]{1,0:T(8,128)(2,1)S(1)}, bf16[96,704]{1,0:T(8,128)(2,1)S(1)}, u32[]{:S(2)}, u32[]{:S(2)}) collective-permute-start(bf16[96,704]{1,0:T(8,128)(2,1)S(1)} %bitcast.125), channel_id=1, source_target_pairs={{0,24},{8,0},{16,8},{24,16},{1,25},{9,1},{17,9},{25,17},{2,26},{10... | collective-permute-start | bytes 405512 | tf_op jit(solution)/shard_map/ppermute | solution.py:911
  425.2 9.4 %collective-permute-start.38 = (bf16[352,256]{1,0:T(8,128)(2,1)S(1)}, bf16[352,256]{1,0:T(8,128)(2,1)S(1)}, u32[]{:S(2)}, u32[]{:S(2)}) collective-permute-start(bf16[352,256]{1,0:T(8,128)(2,1)S(1)} %fusion.35.refs_1_), channel_id=1, source_target_pairs={{0,8},{8,16},{16,24},{24,0},{1,9},{9,17},{17,25},{25,1},{2,10},{10... | collective-permute-start | bytes 540680 | tf_op jit(solution)/shard_map/ppermute | solution.py:911
  426.0 14.6 %collective-permute-start.39 = (bf16[352,256]{1,0:T(8,128)(2,1)S(1)}, bf16[352,256]{1,0:T(8,128)(2,1)S(1)}, u32[]{:S(2)}, u32[]{:S(2)}) collective-permute-start(bf16[352,256]{1,0:T(8,128)(2,1)S(1)} %fusion.35.refs_1_), channel_id=1, source_target_pairs={{0,16},{8,24},{16,0},{24,8},{1,17},{9,25},{17,1},{25,9},{2,18},{10... | collective-permute-start | bytes 540680 | tf_op jit(solution)/shard_map/ppermute | solution.py:911
  434.6 7.5 %collective-permute-start.40 = (bf16[352,256]{1,0:T(8,128)(2,1)S(1)}, bf16[352,256]{1,0:T(8,128)(2,1)S(1)}, u32[]{:S(2)}, u32[]{:S(2)}) collective-permute-start(bf16[352,256]{1,0:T(8,128)(2,1)S(1)} %fusion.35.refs_1_), channel_id=1, source_target_pairs={{0,24},{8,0},{16,8},{24,16},{1,25},{9,1},{17,9},{25,17},{2,26},{10... | collective-permute-start | bytes 540680 | tf_op jit(solution)/shard_map/ppermute | solution.py:911
  (114 other events, 1149.6 us)
Sparse Core Ops, SparseCore 0:
  9.9 94.3 all-gather.2
  106.2 82.1 all-gather.4
  339.4 40.0 reduce-scatter.1

commit v9 on v8

--- a/solution.py
+++ b/solution.py
@@ -685,6 +685,8 @@
     latent_gu = (mm(norm2, ffn_in) * seen_two).astype(BF16)
     pad = jnp.zeros((norm2.shape[0], LANES - 2 * slots), BF16)
     rows = jnp.concatenate([norm2, latent_gu, pad], axis=1)
+    rows, (last,) = tie(rows, (sens_pairs[1][1],))
+    sens_pairs = [sens_pairs[0], (sens_pairs[1][0], last)]
     across = flip(rows, ACROSS_X)
     results = []
     for index, sens_pair in enumerate(sens_pairs):

time: 458 us -> 456 us (level)
    unnamed x241 -> x239, local copies, waits for them, and re-layouts: 19.1 us -> 18.1 us
  transfers between devices with their start and end apart: 47 -> 47, of which waited for: 22 -> 23; matrix products, arithmetic and copies ran while one was open for 20% -> 21% of each run, Pallas kernels for 22% -> 22%
where the time goes in v9:
time: 456 us; the launch traced here: 452 us
  waiting for transfers between devices  145 us (32%)
  Pallas kernels  131 us (29%)
  starting transfers between devices  42 us (9%)
  matrix products  39.4 us (9%)
  local copies, waits for them, and re-layouts  37.7 us (8%)
  other arithmetic  37.7 us (8%)
  between operations  18.8 us (4%)
    ppermute x34, waiting for transfers between devices, flip(): return lax.ppermute(array, 'grp', [(i, i ^ mask) for i in range(members)])  90.8 us
    pallas_call x2, Pallas kernels, feed_forward_pair(): pl.pallas_call(feed_forward_kernel, out_shape=(jax.ShapeDtypeStruct((coun...  61.9 us
    pallas_call x1, Pallas kernels, attention_backward(): pl.pallas_call(functools.partial(attention_backward_kernel, per_kv), out_...  34.7 us
    ppermute x34, starting transfers between devices, flip(): return lax.ppermute(array, 'grp', [(i, i ^ mask) for i in range(members)])  26.9 us
    all_gather x1, waiting for transfers between devices, shards(): qkv_full = lax.all_gather(qkv_weight, 'grp', axis=1, tiled=True)  24.6 us
    dot_general x15, matrix products, mm(): return jnp.dot(left, right, preferred_element_type=F32)  21.7 us
    pallas_call x1, Pallas kernels, attention_forward(): pl.pallas_call(functools.partial(attention_forward_kernel, steps // KV_HE...  18.5 us
    unnamed x239, local copies, waits for them, and re-layouts  18.1 us
  transfers between devices with their start and end apart: 47, of which 23 were waited for; matrix products, arithmetic and copies ran while one was open for 21% of the time, Pallas kernels for 22%

profile of v9, /device:TPU:0, one launch (start us, length us, event | category | flops | bytes accessed | tf_op | source)
XLA Modules:
  0.0 451.6 jit_solution(2597494614678560854)
XLA Ops:
  8.0 5.2 %constant_dynamic-slice_fusion.2 = (bf16[512,1408]{1,0:T(8,128)(2,1)}, bf16[512,1408]{1,0:T(8,128)(2,1)}, bf16[512,1408]{1,0:T(8,128)(2,1)}, bf16[512,1408]{1,0:T(8,128)(2,1)}) fusion(bf16[2048,1408]{1,0:T(8,128)(2,1)} %param.34, s32[]{:T(128)S(6)} %select_n.259, s32[]{:T(128)S(6)} %select_n.231, s32[]{:T(128)S(6)} %select_n.230, s32[]{:T(128)S(6)} %select_n.258), kind=kLoop, calls=%fused_computation.190 | loop fusion | bytes 11534352 | tf_op jit(solution)/shard_map/dynamic_slice | solution.py:351
  13.2 3.0 collective-permute-start
  16.2 3.3 dynamic-slice_bitcast_fusion
  22.5 2.0 fusion.89
  46.3 3.2 and_select_fusion.bias_ref
  49.4 3.4 collective-permute-done.1
  52.9 21.5 %collective-permute-done.3 = bf16[1408,256]{1,0:T(8,128)(2,1)} collective-permute-done((bf16[1408,256]{1,0:T(8,128)(2,1)}, bf16[1408,256]{1,0:T(8,128)(2,1)}, u32[]{:S(2)}, u32[]{:S(2)}) %collective-permute-start.3) | collective-permute-done | bytes 720928 | tf_op jit(solution)/shard_map/ppermute | solution.py:337
  76.7 3.0 pad_maximum_fusion.refs_8_.refs_2_
  79.7 24.6 %all-gather.3.cloned.1.call-done = bf16[2048,2560]{0,1:T(8,128)(2,1)} async-done(((bf16[2048,320]{0,1:T(8,128)(2,1)}), bf16[2048,2560]{0,1:T(8,128)(2,1)}) %all-gather.3.cloned.1.call-update) | async-done | bytes 10485776 | tf_op jit(solution)/shard_map/all_gather | solution.py:959
  104.3 5.6 %fusion.112 = f32[256,2560]{1,0:T(8,128)S(1)} fusion(bf16[256,2048]{1,0:T(8,128)(2,1)S(1)} %fusion.12.norm1_ref.refs_10_, bf16[2048,2560]{0,1:T(8,128)(2,1)} %all-gather.3.cloned.1.call-done), kind=kOutput, calls=%fused_computation.259 | convolution fusion | flops 2684354560 | bytes 14155776 | tf_op jit(solution)/shard_map/dot_general | solution.py:26
  111.0 11.1 %collective-permute-done.4.refs_5_ = bf16[512,1408]{1,0:T(8,128)(2,1)} collective-permute-done((bf16[512,1408]{1,0:T(8,128)(2,1)}, bf16[512,1408]{1,0:T(8,128)(2,1)}, u32[]{:S(2)}, u32[]{:S(2)}) %collective-permute-start.4) | collective-permute-done | bytes 1441824 | tf_op jit(solution)/shard_map/ppermute | solution.py:337
  123.8 2.5 collective-permute-start.9
  127.5 9.2 %collective-permute-done.7 = bf16[256,512]{1,0:T(8,128)(2,1)S(1)} collective-permute-done((bf16[256,512]{1,0:T(8,128)(2,1)S(1)}, bf16[256,512]{1,0:T(8,128)(2,1)S(1)}, u32[]{:S(2)}, u32[]{:S(2)}) %collective-permute-start.7) | collective-permute-done | bytes 262176 | tf_op jit(solution)/shard_map/ppermute | solution.py:337
  139.4 6.5 %collective-permute-done.11 = bf16[256,512]{1,0:T(8,128)(2,1)S(1)} collective-permute-done((bf16[256,512]{1,0:T(8,128)(2,1)S(1)}, bf16[256,512]{1,0:T(8,128)(2,1)S(1)}, u32[]{:S(2)}, u32[]{:S(2)}) %collective-permute-start.11) | collective-permute-done | bytes 262176 | tf_op jit(solution)/shard_map/ppermute | solution.py:337
  147.8 1.9 collective-permute-start.15
  152.9 2.7 fusion.27.q_ref
  156.8 18.5 %attention_forward.1 = (bf16[256,2048]{1,0:T(8,128)(2,1)S(1)}, f32[16,2,256]{2,1,0:T(2,128)S(1)}) custom-call(s32[3]{0:T(128)S(1)} %pad_add_fusion.span, bf16[256,2048]{1,0:T(8,128)(2,1)S(1)} %fusion.27.q_ref, bf16[2048,512]{1,0:T(8,128)(2,1)S(1)} %constant_dynamic-update-slice_fusion.key_ref.value_ref, ...), custom_call_target="tpu_custom_call" | custom-call | flops 4294967296 | bytes 18874368 | tf_op jit(solution)/shard_map/attention_forward/pallas_call | solution.py:149
  176.0 8.9 %collective-permute-done.14.refs_9_.refs_3_ = bf16[1,1408,256]{2,1,0:T(8,128)(2,1)} collective-permute-done((bf16[1,1408,256]{2,1,0:T(8,128)(2,1)S(1)}, bf16[1,1408,256]{2,1,0:T(8,128)(2,1)}, u32[]{:S(2)}, u32[]{:S(2)}) %collective-permute-start.14) | collective-permute-done | bytes 720928 | tf_op jit(solution)/shard_map/ppermute | solution.py:337
  187.4 1.8 convolution_multiply_fusion.1
  189.9 6.8 %multiply_reduce_fusion.1 = (f32[256]{0:T(256)S(1)}, f32[256,2048]{1,0:T(8,128)S(1)}) fusion(f32[256,2048]{1,0:T(8,128)} %convolution_multiply_fusion.1, bf16[256,2048]{1,0:T(8,128)(2,1)S(1)} %get-tuple-element.131.o_ref.attended_ref, bf16[2048,2048]{1,0:T(8,128)(2,1)} %all-gather.5.cloned.1.call-done, bf16[256,2048]{1,0:T(8,128)(2,1)} %param.25), kind=kOutput, calls=%fused_computation.57 | convolution fusion | flops 2150104832 | bytes 14681088 | tf_op jit(solution)/shard_map/dot_general | solution.py:26
  197.5 5.6 %collective-permute-done.17.refs_10_.refs_4_ = bf16[1,1408,256]{2,1,0:T(8,128)(2,1)} collective-permute-done((bf16[1,1408,256]{2,1,0:T(8,128)(2,1)}, bf16[1,1408,256]{2,1,0:T(8,128)(2,1)}, u32[]{:S(2)}, u32[]{:S(2)}) %collective-permute-start.17) | collective-permute-done | bytes 720928 | tf_op jit(solution)/shard_map/ppermute | solution.py:337
  203.8 1.8 concatenate.64.own_x
  209.4 15.8 %collective-permute-done.21.refs_12_.refs_6_ = bf16[1,1408,256]{2,1,0:T(8,128)(2,1)} collective-permute-done((bf16[1,1408,256]{2,1,0:T(8,128)(2,1)}, bf16[1,1408,256]{2,1,0:T(8,128)(2,1)}, u32[]{:S(2)}, u32[]{:S(2)}) %collective-permute-start.21) | collective-permute-done | bytes 720928 | tf_op jit(solution)/shard_map/ppermute | solution.py:342
  226.1 31.1 %feed_forward.2 = (f32[256,2176]{1,0:T(8,128)}, bf16[256,2176]{1,0:T(8,128)(2,1)}, bf16[512,1408]{1,0:T(8,128)(2,1)}, f32[96,1408]{1,0:T(8,128)S(1)}) custom-call(s32[3]{0:T(128)S(1)} %pad_add_fusion.1.meta, bf16[256,2176]{1,0:T(8,128)(2,1)} %concatenate.64.own_x, bf16[256,2176]{1,0:T(8,128)(2,1)} %collective-permute-done.20.near_x, ...), custom_call_target="tpu_custom_call" | custom-call | flops 14763950080 | bytes 38273024 | tf_op jit(solution)/shard_map/feed_forward/pallas_call | solution.py:637
  257.3 2.7 collective-permute-done.24.near_x
  261.1 30.8 %feed_forward.3 = (f32[256,2176]{1,0:T(8,128)}, bf16[256,2176]{1,0:T(8,128)(2,1)}, bf16[512,1408]{1,0:T(8,128)(2,1)}, f32[96,1408]{1,0:T(8,128)S(1)}) custom-call(s32[3]{0:T(128)S(1)} %pad_add_fusion.1.meta, bf16[256,2176]{1,0:T(8,128)(2,1)} %copy-done.106, bf16[256,2176]{1,0:T(8,128)(2,1)} %copy-done.107, bf16[256,2048]{1,0:T(8,128)(2,1)} %collective-permute-done.16.own_g, ...), custom_call_target="tpu_custom_call" | custom-call | flops 14763950080 | bytes 38273024 | tf_op jit(solution)/shard_map/feed_forward/pallas_call | solution.py:637
  293.2 2.6 collective-permute-done.25
  295.8 3.2 add_convert_fusion
  302.9 1.8 copy-done.3
  307.4 11.6 %down_projection.1 = (f32[256,2048]{1,0:T(8,128)S(1)}, bf16[256,2048]{1,0:T(8,128)(2,1)S(1)}, bf16[256,2048]{1,0:T(8,128)(2,1)S(1)}, bf16[256,2048]{1,0:T(8,128)(2,1)}) custom-call(s32[3]{0:T(128)S(1)} %pad_add_fusion.1.meta, bf16[512,1408]{1,0:T(8,128)(2,1)S(1)} %copy-done.50, bf16[512,1408]{1,0:T(8,128)(2,1)S(1)} %copy-done.51, ...), custom_call_target="tpu_custom_call" | custom-call | flops 5905580032 | bytes 14155776 | tf_op jit(solution)/shard_map/down_projection/pallas_call | solution.py:611
  319.0 6.8 %collective-permute-done.26 = bf16[256,2176]{1,0:T(8,128)(2,1)} collective-permute-done((bf16[256,2176]{1,0:T(8,128)(2,1)}, bf16[256,2176]{1,0:T(8,128)(2,1)}, u32[]{:S(2)}, u32[]{:S(2)}) %collective-permute-start.26) | collective-permute-done | bytes 1114144 | tf_op jit(solution)/shard_map/ppermute | solution.py:337
  325.9 2.0 convert_add_fusion.1
  330.8 2.1 fusion.105
  333.4 2.4 fusion.113
  337.3 3.1 add_convert_fusion.3
  342.8 34.7 %attention_backward.1 = (bf16[256,2048]{1,0:T(8,128)(2,1)S(1)}, bf16[4,256,512]{2,1,0:T(8,128)(2,1)S(1)}, bf16[4,256,512]{2,1,0:T(8,128)(2,1)S(1)}) custom-call(s32[3]{0:T(128)S(1)} %pad_add_fusion.span, bf16[256,2048]{1,0:T(8,128)(2,1)S(1)} %copy-done.16, bf16[256,2048]{1,0:T(8,128)(2,1)S(1)} %copy-done.19, bf16[256,2048]{1,0:T(8,128)(2,1)S(1)} %copy-done.21, ...), custom_call_target="tpu_custom_call" | custom-call | flops 10737418240 | bytes 13631488 | tf_op jit(solution)/shard_map/attention_backward/pallas_call | solution.py:294
  383.9 2.5 collective-permute-start.42
  386.4 2.0 add_convert_fusion.1
  390.0 2.1 collective-permute-start.33
  392.1 3.2 add_convert_fusion.2
  395.4 2.0 early_gradients.1
  397.7 5.0 %collective-permute-done.32.refs_2_ = bf16[256,512]{1,0:T(8,128)(2,1)S(1)} collective-permute-done((bf16[256,512]{1,0:T(8,128)(2,1)S(1)}, bf16[256,512]{1,0:T(8,128)(2,1)S(1)}, u32[]{:S(2)}, u32[]{:S(2)}) %collective-permute-start.32) | collective-permute-done | bytes 262176 | tf_op jit(solution)/shard_map/ppermute | solution.py:337
  403.6 5.8 %fusion = f32[256,2048]{1,0:T(8,128)S(1)} fusion(bf16[256,2048]{1,0:T(8,128)(2,1)S(1)} %copy-done.24, bf16[2048,2560]{0,1:T(8,128)(2,1)} %all-gather.3.cloned.1.call-done), kind=kOutput, calls=%fused_computation | convolution fusion | flops 2147483648 | bytes 11534336 | tf_op jit(solution)/shard_map/dot_general | solution.py:30
  414.7 2.8 fusion.17
  418.5 2.1 collective-permute-start.43
  420.6 2.4 collective-permute-done.36
  425.5 7.0 %collective-permute-done.38.refs_2_ = bf16[352,256]{1,0:T(8,128)(2,1)S(1)} collective-permute-done((bf16[352,256]{1,0:T(8,128)(2,1)S(1)}, bf16[352,256]{1,0:T(8,128)(2,1)S(1)}, u32[]{:S(2)}, u32[]{:S(2)}) %collective-permute-start.38) | collective-permute-done | bytes 180256 | tf_op jit(solution)/shard_map/ppermute | solution.py:913
  434.1 4.4 collective-permute-done.39.refs_3_
  (413 shorter events, 89.1 us)
Async XLA Ops:
  7.2 97.1 %all-gather.3.cloned.1.call-start = ((), (), s32[]{:S(2)}) async-start(), calls=%async_computation.1 | async-start | bytes 11796480 | tf_op jit(solution)/shard_map/all_gather | solution.py:959
  7.9 181.9 %all-gather.5.cloned.1.call-start = ((), (), s32[]{:S(2)}) async-start(), calls=%async_computation.2 | async-start | bytes 9437184 | tf_op jit(solution)/shard_map/all_gather | solution.py:1049
  13.2 61.2 %collective-permute-start = (bf16[512,1408]{1,0:T(8,128)(2,1)}, bf16[512,1408]{1,0:T(8,128)(2,1)}, u32[]{:S(2)}, u32[]{:S(2)}) collective-permute-start(bf16[512,1408]{1,0:T(8,128)(2,1)} %get-tuple-element.264.refs_0_), channel_id=1, source_target_pairs={{0,4},{1,5},{2,6},{3,7},{4,0},{5,1},{6,2},{7,3},{8,12},{9,13},{10,... | collective-permute-start | bytes 4325384 | tf_op jit(solution)/shard_map/ppermute | solution.py:337
  19.4 33.4 %collective-permute-start.1 = (bf16[1408,256]{1,0:T(8,128)(2,1)}, bf16[1408,256]{1,0:T(8,128)(2,1)}, u32[]{:S(2)}, u32[]{:S(2)}) collective-permute-start(bf16[1408,256]{1,0:T(8,128)(2,1)} %get-tuple-element.270), channel_id=1, source_target_pairs={{0,2},{1,3},{2,0},{3,1},{4,6},{5,7},{6,4},{7,5},{8,10},{9,11},{10,... | collective-permute-start | bytes 2162696 | tf_op jit(solution)/shard_map/ppermute | solution.py:337
  20.9 31.9 %collective-permute-start.2 = (bf16[1408,256]{1,0:T(8,128)(2,1)}, bf16[1408,256]{1,0:T(8,128)(2,1)}, u32[]{:S(2)}, u32[]{:S(2)}) collective-permute-start(bf16[1408,256]{1,0:T(8,128)(2,1)} %get-tuple-element.269), channel_id=1, source_target_pairs={{0,1},{1,0},{2,3},{3,2},{4,5},{5,4},{6,7},{7,6},{8,9},{9,8},{10,11... | collective-permute-start | bytes 2162696 | tf_op jit(solution)/shard_map/ppermute | solution.py:337
  20.9 53.4 %collective-permute-start.3 = (bf16[1408,256]{1,0:T(8,128)(2,1)}, bf16[1408,256]{1,0:T(8,128)(2,1)}, u32[]{:S(2)}, u32[]{:S(2)}) collective-permute-start(bf16[1408,256]{1,0:T(8,128)(2,1)} %get-tuple-element.271), channel_id=1, source_target_pairs={{0,3},{1,2},{2,1},{3,0},{4,7},{5,6},{6,5},{7,4},{8,11},{9,10},{10,... | collective-permute-start | bytes 2162696 | tf_op jit(solution)/shard_map/ppermute | solution.py:337
  21.6 358.9 %reduce-scatter.2.cloned.1.call-start = ((), (), s32[]{:S(2)}) async-start(), calls=%async_computation.3 | async-start | bytes 1327104 | tf_op jit(solution)/shard_map/reduce_scatter | solution.py:1105
  43.3 83.0 %copy-start.11 = (bf16[32,2048]{1,0:T(8,128)(2,1)}, bf16[32,2048]{1,0:T(8,128)(2,1)S(1)}, u32[]{:S(2)}) copy-start(bf16[32,2048]{1,0:T(8,128)(2,1)S(1)} %convolution_convert_fusion.8.asking_ref) | copy-start | bytes 393220
  74.4 47.7 %collective-permute-start.4 = (bf16[512,1408]{1,0:T(8,128)(2,1)}, bf16[512,1408]{1,0:T(8,128)(2,1)}, u32[]{:S(2)}, u32[]{:S(2)}) collective-permute-start(bf16[512,1408]{1,0:T(8,128)(2,1)} %get-tuple-element.117.refs_1_), channel_id=1, source_target_pairs={{0,4},{1,5},{2,6},{3,7},{4,0},{5,1},{6,2},{7,3},{8,12},{9,13},{10,... | collective-permute-start | bytes 4325384 | tf_op jit(solution)/shard_map/ppermute | solution.py:337
  74.6 47.5 %collective-permute-start.5 = (bf16[512,1408]{1,0:T(8,128)(2,1)}, bf16[512,1408]{1,0:T(8,128)(2,1)}, u32[]{:S(2)}, u32[]{:S(2)}) collective-permute-start(bf16[512,1408]{1,0:T(8,128)(2,1)} %collective-permute-done.refs_4_), channel_id=1, source_target_pairs={{0,8},{8,0},{16,24},{24,16},{1,9},{9,1},{17,25},{25,17},{2,10},{10... | collective-permute-start | bytes 4325384 | tf_op jit(solution)/shard_map/ppermute | solution.py:342
  122.1 17.3 %collective-permute-start.6 = (bf16[256,512]{1,0:T(8,128)(2,1)S(1)}, bf16[256,512]{1,0:T(8,128)(2,1)S(1)}, u32[]{:S(2)}, u32[]{:S(2)}) collective-permute-start(bf16[256,512]{1,0:T(8,128)(2,1)S(1)} %pad_maximum_fusion.2), channel_id=1, source_target_pairs={{0,1},{1,0},{2,3},{3,2},{4,5},{5,4},{6,7},{7,6},{8,9},{9,8},{10,11... | collective-permute-start | bytes 786440 | tf_op jit(solution)/shard_map/ppermute | solution.py:337
  122.1 14.6 %collective-permute-start.7 = (bf16[256,512]{1,0:T(8,128)(2,1)S(1)}, bf16[256,512]{1,0:T(8,128)(2,1)S(1)}, u32[]{:S(2)}, u32[]{:S(2)}) collective-permute-start(bf16[256,512]{1,0:T(8,128)(2,1)S(1)} %pad_maximum_fusion.2), channel_id=1, source_target_pairs={{0,2},{1,3},{2,0},{3,1},{4,6},{5,7},{6,4},{7,5},{8,10},{9,11},{10,... | collective-permute-start | bytes 786440 | tf_op jit(solution)/shard_map/ppermute | solution.py:337
  123.8 14.0 %collective-permute-start.9 = (bf16[256,512]{1,0:T(8,128)(2,1)S(1)}, bf16[256,512]{1,0:T(8,128)(2,1)S(1)}, u32[]{:S(2)}, u32[]{:S(2)}) collective-permute-start(bf16[256,512]{1,0:T(8,128)(2,1)S(1)} %pad_maximum_fusion.2), channel_id=1, source_target_pairs={{0,4},{1,5},{2,6},{3,7},{4,0},{5,1},{6,2},{7,3},{8,12},{9,13},{10,... | collective-permute-start | bytes 786440 | tf_op jit(solution)/shard_map/ppermute | solution.py:337
  136.7 9.2 %collective-permute-start.8 = (bf16[256,512]{1,0:T(8,128)(2,1)S(1)}, bf16[256,512]{1,0:T(8,128)(2,1)S(1)}, u32[]{:S(2)}, u32[]{:S(2)}) collective-permute-start(bf16[256,512]{1,0:T(8,128)(2,1)S(1)} %collective-permute-done.7), channel_id=1, source_target_pairs={{0,1},{1,0},{2,3},{3,2},{4,5},{5,4},{6,7},{7,6},{8,9},{9,8},{10,11... | collective-permute-start | bytes 786440 | tf_op jit(solution)/shard_map/ppermute | solution.py:337
  137.8 8.0 %collective-permute-start.11 = (bf16[256,512]{1,0:T(8,128)(2,1)S(1)}, bf16[256,512]{1,0:T(8,128)(2,1)S(1)}, u32[]{:S(2)}, u32[]{:S(2)}) collective-permute-start(bf16[256,512]{1,0:T(8,128)(2,1)S(1)} %collective-permute-done.9), channel_id=1, source_target_pairs={{0,2},{1,3},{2,0},{3,1},{4,6},{5,7},{6,4},{7,5},{8,10},{9,11},{10,... | collective-permute-start | bytes 786440 | tf_op jit(solution)/shard_map/ppermute | solution.py:337
  139.2 6.7 %collective-permute-start.10 = (bf16[256,512]{1,0:T(8,128)(2,1)S(1)}, bf16[256,512]{1,0:T(8,128)(2,1)S(1)}, u32[]{:S(2)}, u32[]{:S(2)}) collective-permute-start(bf16[256,512]{1,0:T(8,128)(2,1)S(1)} %collective-permute-done.9), channel_id=1, source_target_pairs={{0,1},{1,0},{2,3},{3,2},{4,5},{5,4},{6,7},{7,6},{8,9},{9,8},{10,11... | collective-permute-start | bytes 786440 | tf_op jit(solution)/shard_map/ppermute | solution.py:337
  145.8 1.9 collective-permute-start.12
  147.8 37.1 %collective-permute-start.15 = (bf16[512,1408]{1,0:T(8,128)(2,1)}, bf16[512,1408]{1,0:T(8,128)(2,1)S(1)}, u32[]{:S(2)}, u32[]{:S(2)}) collective-permute-start(bf16[512,1408]{1,0:T(8,128)(2,1)} %collective-permute-done.4.refs_5_), channel_id=1, source_target_pairs={{0,8},{8,0},{16,24},{24,16},{1,9},{9,1},{17,25},{25,17},{2,10},{10... | collective-permute-start | bytes 4325384 | tf_op jit(solution)/shard_map/ppermute | solution.py:342
  149.8 35.1 %collective-permute-start.13 = (bf16[256,2048]{1,0:T(8,128)(2,1)S(1)}, bf16[256,2048]{1,0:T(8,128)(2,1)S(1)}, u32[]{:S(2)}, u32[]{:S(2)}) collective-permute-start(bf16[256,2048]{1,0:T(8,128)(2,1)S(1)} %copy-done.4), channel_id=1, source_target_pairs={{0,1},{1,0},{2,3},{3,2},{4,5},{5,4},{6,7},{7,6},{8,9},{9,8},{10,11... | collective-permute-start | bytes 3145736 | tf_op jit(solution)/shard_map/ppermute | solution.py:337
  150.8 34.1 %collective-permute-start.14 = (bf16[1,1408,256]{2,1,0:T(8,128)(2,1)S(1)}, bf16[1,1408,256]{2,1,0:T(8,128)(2,1)}, u32[]{:S(2)}, u32[]{:S(2)}) collective-permute-start(bf16[1,1408,256]{2,1,0:T(8,128)(2,1)S(1)} %get-tuple-element.267), channel_id=1, source_target_pairs={{0,4},{1,5},{2,6},{3,7},{4,0},{5,1},{6,2},{7,3},{8,12},{9,13},{10,... | collective-permute-start | bytes 2162696 | tf_op jit(solution)/shard_map/ppermute | solution.py:337
  155.7 41.8 %collective-permute-start.16 = (bf16[256,2048]{1,0:T(8,128)(2,1)S(1)}, bf16[256,2048]{1,0:T(8,128)(2,1)}, u32[]{:S(2)}, u32[]{:S(2)}) collective-permute-start(bf16[256,2048]{1,0:T(8,128)(2,1)S(1)} %copy-done.4), channel_id=1, source_target_pairs={{0,2},{1,3},{2,0},{3,1},{4,6},{5,7},{6,4},{7,5},{8,10},{9,11},{10,... | collective-permute-start | bytes 3145736 | tf_op jit(solution)/shard_map/ppermute | solution.py:337
  184.9 18.3 %collective-permute-start.17 = (bf16[1,1408,256]{2,1,0:T(8,128)(2,1)}, bf16[1,1408,256]{2,1,0:T(8,128)(2,1)}, u32[]{:S(2)}, u32[]{:S(2)}) collective-permute-start(bf16[1,1408,256]{2,1,0:T(8,128)(2,1)} %get-tuple-element.134), channel_id=1, source_target_pairs={{0,4},{1,5},{2,6},{3,7},{4,0},{5,1},{6,2},{7,3},{8,12},{9,13},{10,... | collective-permute-start | bytes 2162696 | tf_op jit(solution)/shard_map/ppermute | solution.py:337
  185.3 18.0 %collective-permute-start.18 = (bf16[1,1408,256]{2,1,0:T(8,128)(2,1)}, bf16[1,1408,256]{2,1,0:T(8,128)(2,1)}, u32[]{:S(2)}, u32[]{:S(2)}) collective-permute-start(bf16[1,1408,256]{2,1,0:T(8,128)(2,1)} %collective-permute-done.14.refs_9_.refs_3_), channel_id=1, source_target_pairs={{0,8},{8,0},{16,24},{24,16},{1,9},{9,1},{17,25},{25,17},{2,10},{10... | collective-permute-start | bytes 2162696 | tf_op jit(solution)/shard_map/ppermute | solution.py:342
  203.3 3.0 collective-permute-start.19
  206.3 18.9 %collective-permute-start.20 = (bf16[256,2176]{1,0:T(8,128)(2,1)}, bf16[256,2176]{1,0:T(8,128)(2,1)}, u32[]{:S(2)}, u32[]{:S(2)}) collective-permute-start(bf16[256,2176]{1,0:T(8,128)(2,1)} %concatenate.64.own_x), channel_id=1, source_target_pairs={{0,1},{1,0},{2,3},{3,2},{4,5},{5,4},{6,7},{7,6},{8,9},{9,8},{10,11... | collective-permute-start | bytes 3342344 | tf_op jit(solution)/shard_map/ppermute | solution.py:337
  206.4 18.7 %collective-permute-start.21 = (bf16[1,1408,256]{2,1,0:T(8,128)(2,1)}, bf16[1,1408,256]{2,1,0:T(8,128)(2,1)}, u32[]{:S(2)}, u32[]{:S(2)}) collective-permute-start(bf16[1,1408,256]{2,1,0:T(8,128)(2,1)} %collective-permute-done.17.refs_10_.refs_4_), channel_id=1, source_target_pairs={{0,8},{8,0},{16,24},{24,16},{1,9},{9,1},{17,25},{25,17},{2,10},{10... | collective-permute-start | bytes 2162696 | tf_op jit(solution)/shard_map/ppermute | solution.py:342
  208.1 49.2 %collective-permute-start.22 = (bf16[256,2176]{1,0:T(8,128)(2,1)}, bf16[256,2176]{1,0:T(8,128)(2,1)S(1)}, u32[]{:S(2)}, u32[]{:S(2)}) collective-permute-start(bf16[256,2176]{1,0:T(8,128)(2,1)} %concatenate.64.own_x), channel_id=1, source_target_pairs={{0,2},{1,3},{2,0},{3,1},{4,6},{5,7},{6,4},{7,5},{8,10},{9,11},{10,... | collective-permute-start | bytes 3342344 | tf_op jit(solution)/shard_map/ppermute | solution.py:337
  257.2 2.8 collective-permute-start.24
  292.7 3.1 collective-permute-start.25
  292.8 33.1 %collective-permute-start.23 = (bf16[256,2176]{1,0:T(8,128)(2,1)}, bf16[256,2176]{1,0:T(8,128)(2,1)}, u32[]{:S(2)}, u32[]{:S(2)}) collective-permute-start(bf16[256,2176]{1,0:T(8,128)(2,1)} %get-tuple-element.152), channel_id=1, source_target_pairs={{0,1},{1,0},{2,3},{3,2},{4,5},{5,4},{6,7},{7,6},{8,9},{9,8},{10,11... | collective-permute-start | bytes 3342344 | tf_op jit(solution)/shard_map/ppermute | solution.py:337
  298.9 26.9 %collective-permute-start.26 = (bf16[256,2176]{1,0:T(8,128)(2,1)}, bf16[256,2176]{1,0:T(8,128)(2,1)}, u32[]{:S(2)}, u32[]{:S(2)}) collective-permute-start(bf16[256,2176]{1,0:T(8,128)(2,1)} %add_convert_fusion), channel_id=1, source_target_pairs={{0,2},{1,3},{2,0},{3,1},{4,6},{5,7},{6,4},{7,5},{8,10},{9,11},{10,... | collective-permute-start | bytes 3342344 | tf_op jit(solution)/shard_map/ppermute | solution.py:337
  329.5 7.8 %collective-permute-start.28 = (bf16[256,2048]{1,0:T(8,128)(2,1)}, bf16[256,2048]{1,0:T(8,128)(2,1)}, u32[]{:S(2)}, u32[]{:S(2)}) collective-permute-start(bf16[256,2048]{1,0:T(8,128)(2,1)} %get-tuple-element.181), channel_id=1, source_target_pairs={{0,1},{1,0},{2,3},{3,2},{4,5},{5,4},{6,7},{7,6},{8,9},{9,8},{10,11... | collective-permute-start | bytes 3145736 | tf_op jit(solution)/shard_map/ppermute | solution.py:337
  337.2 43.3 %collective-permute-start.27 = (bf16[256,2048]{1,0:T(8,128)(2,1)}, bf16[256,2048]{1,0:T(8,128)(2,1)}, u32[]{:S(2)}, u32[]{:S(2)}) collective-permute-start(bf16[256,2048]{1,0:T(8,128)(2,1)} %copy-done.48), channel_id=1, source_target_pairs={{0,1},{1,0},{2,3},{3,2},{4,5},{5,4},{6,7},{7,6},{8,9},{9,8},{10,11... | collective-permute-start | bytes 3145736 | tf_op jit(solution)/shard_map/ppermute | solution.py:337
  340.4 40.1 %collective-permute-start.29 = (bf16[256,2048]{1,0:T(8,128)(2,1)}, bf16[256,2048]{1,0:T(8,128)(2,1)}, u32[]{:S(2)}, u32[]{:S(2)}) collective-permute-start(bf16[256,2048]{1,0:T(8,128)(2,1)} %add_convert_fusion.3), channel_id=1, source_target_pairs={{0,2},{1,3},{2,0},{3,1},{4,6},{5,7},{6,4},{7,5},{8,10},{9,11},{10,... | collective-permute-start | bytes 3145736 | tf_op jit(solution)/shard_map/ppermute | solution.py:337
  380.5 5.9 %collective-permute-start.30 = (bf16[4,256,512]{2,1,0:T(8,128)(2,1)}, bf16[4,256,512]{2,1,0:T(8,128)(2,1)}, u32[]{:S(2)}, u32[]{:S(2)}) collective-permute-start(bf16[4,256,512]{2,1,0:T(8,128)(2,1)} %copy-done.49), channel_id=1, source_target_pairs={{0,1},{1,0},{2,3},{3,2},{4,5},{5,4},{6,7},{7,6},{8,9},{9,8},{10,11... | collective-permute-start | bytes 3145736 | tf_op jit(solution)/shard_map/ppermute | solution.py:337
  382.6 57.4 %collective-permute-start.41 = (bf16[96,704]{1,0:T(8,128)(2,1)}, bf16[96,704]{1,0:T(8,128)(2,1)S(1)}, u32[]{:S(2)}, u32[]{:S(2)}) collective-permute-start(bf16[96,704]{1,0:T(8,128)(2,1)} %bitcast.123), channel_id=1, source_target_pairs={{0,8},{8,16},{16,24},{24,0},{1,9},{9,17},{17,25},{25,1},{2,10},{10... | collective-permute-start | bytes 405512 | tf_op jit(solution)/shard_map/ppermute | solution.py:913
  383.9 56.1 %collective-permute-start.42 = (bf16[96,704]{1,0:T(8,128)(2,1)}, bf16[96,704]{1,0:T(8,128)(2,1)S(1)}, u32[]{:S(2)}, u32[]{:S(2)}) collective-permute-start(bf16[96,704]{1,0:T(8,128)(2,1)} %bitcast.124), channel_id=1, source_target_pairs={{0,16},{8,24},{16,0},{24,8},{1,17},{9,25},{17,1},{25,9},{2,18},{10... | collective-permute-start | bytes 405512 | tf_op jit(solution)/shard_map/ppermute | solution.py:913
  388.4 9.2 %collective-permute-start.31 = (bf16[256,512]{1,0:T(8,128)(2,1)S(1)}, bf16[256,512]{1,0:T(8,128)(2,1)S(1)}, u32[]{:S(2)}, u32[]{:S(2)}) collective-permute-start(bf16[256,512]{1,0:T(8,128)(2,1)S(1)} %get-tuple-element.278), channel_id=1, source_target_pairs={{0,2},{1,3},{2,0},{3,1},{4,6},{5,7},{6,4},{7,5},{8,10},{9,11},{10,... | collective-permute-start | bytes 786440 | tf_op jit(solution)/shard_map/ppermute | solution.py:337
  389.2 13.5 %collective-permute-start.32 = (bf16[256,512]{1,0:T(8,128)(2,1)S(1)}, bf16[256,512]{1,0:T(8,128)(2,1)S(1)}, u32[]{:S(2)}, u32[]{:S(2)}) collective-permute-start(bf16[256,512]{1,0:T(8,128)(2,1)S(1)} %get-tuple-element.277), channel_id=1, source_target_pairs={{0,4},{1,5},{2,6},{3,7},{4,0},{5,1},{6,2},{7,3},{8,12},{9,13},{10,... | collective-permute-start | bytes 786440 | tf_op jit(solution)/shard_map/ppermute | solution.py:337
  390.0 12.6 %collective-permute-start.33 = (bf16[256,512]{1,0:T(8,128)(2,1)S(1)}, bf16[256,512]{1,0:T(8,128)(2,1)S(1)}, u32[]{:S(2)}, u32[]{:S(2)}) collective-permute-start(bf16[256,512]{1,0:T(8,128)(2,1)S(1)} %get-tuple-element.276), channel_id=1, source_target_pairs={{0,6},{1,7},{2,4},{3,5},{4,2},{5,3},{6,0},{7,1},{8,14},{9,15},{10,... | collective-permute-start | bytes 786440 | tf_op jit(solution)/shard_map/ppermute | solution.py:337
  403.6 7.3 %collective-permute-start.34 = (bf16[4,352,256]{2,1,0:T(8,128)(2,1)S(1)}, bf16[4,352,256]{2,1,0:T(8,128)(2,1)S(1)}, u32[]{:S(2)}, u32[]{:S(2)}) collective-permute-start(bf16[4,352,256]{2,1,0:T(8,128)(2,1)S(1)} %get-tuple-element.196), channel_id=1, source_target_pairs={{0,1},{1,0},{2,3},{3,2},{4,5},{5,4},{6,7},{7,6},{8,9},{9,8},{10,11... | collective-permute-start | bytes 2162696 | tf_op jit(solution)/shard_map/ppermute | solution.py:337
  411.1 7.4 %collective-permute-start.35 = (bf16[352,256]{1,0:T(8,128)(2,1)S(1)}, bf16[352,256]{1,0:T(8,128)(2,1)S(1)}, u32[]{:S(2)}, u32[]{:S(2)}) collective-permute-start(bf16[352,256]{1,0:T(8,128)(2,1)S(1)} %get-tuple-element.280), channel_id=1, source_target_pairs={{0,2},{1,3},{2,0},{3,1},{4,6},{5,7},{6,4},{7,5},{8,10},{9,11},{10,... | collective-permute-start | bytes 540680 | tf_op jit(solution)/shard_map/ppermute | solution.py:337
  412.5 10.5 %collective-permute-start.36 = (bf16[352,256]{1,0:T(8,128)(2,1)S(1)}, bf16[352,256]{1,0:T(8,128)(2,1)S(1)}, u32[]{:S(2)}, u32[]{:S(2)}) collective-permute-start(bf16[352,256]{1,0:T(8,128)(2,1)S(1)} %get-tuple-element.282), channel_id=1, source_target_pairs={{0,4},{1,5},{2,6},{3,7},{4,0},{5,1},{6,2},{7,3},{8,12},{9,13},{10,... | collective-permute-start | bytes 540680 | tf_op jit(solution)/shard_map/ppermute | solution.py:337
  413.0 10.1 %collective-permute-start.37 = (bf16[352,256]{1,0:T(8,128)(2,1)S(1)}, bf16[352,256]{1,0:T(8,128)(2,1)S(1)}, u32[]{:S(2)}, u32[]{:S(2)}) collective-permute-start(bf16[352,256]{1,0:T(8,128)(2,1)S(1)} %get-tuple-element.281), channel_id=1, source_target_pairs={{0,6},{1,7},{2,4},{3,5},{4,2},{5,3},{6,0},{7,1},{8,14},{9,15},{10,... | collective-permute-start | bytes 540680 | tf_op jit(solution)/shard_map/ppermute | solution.py:337
  418.5 21.5 %collective-permute-start.43 = (bf16[96,704]{1,0:T(8,128)(2,1)S(1)}, bf16[96,704]{1,0:T(8,128)(2,1)S(1)}, u32[]{:S(2)}, u32[]{:S(2)}) collective-permute-start(bf16[96,704]{1,0:T(8,128)(2,1)S(1)} %bitcast.125), channel_id=1, source_target_pairs={{0,24},{8,0},{16,8},{24,16},{1,25},{9,1},{17,9},{25,17},{2,26},{10... | collective-permute-start | bytes 405512 | tf_op jit(solution)/shard_map/ppermute | solution.py:913
  423.1 9.4 %collective-permute-start.38 = (bf16[352,256]{1,0:T(8,128)(2,1)S(1)}, bf16[352,256]{1,0:T(8,128)(2,1)S(1)}, u32[]{:S(2)}, u32[]{:S(2)}) collective-permute-start(bf16[352,256]{1,0:T(8,128)(2,1)S(1)} %fusion.35.refs_1_), channel_id=1, source_target_pairs={{0,8},{8,16},{16,24},{24,0},{1,9},{9,17},{17,25},{25,1},{2,10},{10... | collective-permute-start | bytes 540680 | tf_op jit(solution)/shard_map/ppermute | solution.py:913
  424.0 14.5 %collective-permute-start.39 = (bf16[352,256]{1,0:T(8,128)(2,1)S(1)}, bf16[352,256]{1,0:T(8,128)(2,1)S(1)}, u32[]{:S(2)}, u32[]{:S(2)}) collective-permute-start(bf16[352,256]{1,0:T(8,128)(2,1)S(1)} %fusion.35.refs_1_), channel_id=1, source_target_pairs={{0,16},{8,24},{16,0},{24,8},{1,17},{9,25},{17,1},{25,9},{2,18},{10... | collective-permute-start | bytes 540680 | tf_op jit(solution)/shard_map/ppermute | solution.py:913
  432.5 7.5 %collective-permute-start.40 = (bf16[352,256]{1,0:T(8,128)(2,1)S(1)}, bf16[352,256]{1,0:T(8,128)(2,1)S(1)}, u32[]{:S(2)}, u32[]{:S(2)}) collective-permute-start(bf16[352,256]{1,0:T(8,128)(2,1)S(1)} %fusion.35.refs_1_), channel_id=1, source_target_pairs={{0,24},{8,0},{16,8},{24,16},{1,25},{9,1},{17,9},{25,17},{2,26},{10... | collective-permute-start | bytes 540680 | tf_op jit(solution)/shard_map/ppermute | solution.py:913
  (113 other events, 1141.5 us)
Sparse Core Ops, SparseCore 0:
  9.9 94.3 all-gather.2
  106.2 82.1 all-gather.4
  337.3 40.0 reduce-scatter.1
